TPU v7x, 512 devices: a whole 4x4x16 slice. The times are simulated.
512 devices in a mesh: doc: 8 (over y, core), label: 64 (over z, x).
Axes of the slice: x: 4, y: 4, z: 16, core: 2. Of those that a mesh axis runs over, the one named last changes fastest.
Arguments:
- features: float32 [4096, 1024], P('doc'), may hold values from -6 to 6
- doc_labels: int32 [4096, 16], P('doc'), may hold values from 0 to 16383, all different within a row
- tree_perm: int32 [16384], replicated, may hold values from 0 to 16383, as said below
- cluster_sizes: int32 [512], replicated, may hold values from 1 to 4096, 16384 in all
Outputs:
- scores: float32 [4096, 16384], P('doc', 'label')
Inputs may be any that keep to these rules, and one draw needn't show every extreme that they name: `doc_labels`: each document names 16 different labels, and every label is named by some document. `tree_perm`: a permutation; every aligned block of 256 tree positions holds exactly 4 labels of every aligned block of 256 natural indices. `cluster_sizes`: the sizes sum to 16384; the largest is exactly 4096.
All inputs are finite; a program needn't handle non-finite values.
Results may differ from a plain program's by a relative error of at most 0.0001.
Values sent between devices are 32-bit elements; how exact they have to be, the bound alone decides.
No kernel may reach another device: no remote copies, remote signals or barrier semaphores. Data moves between devices by JAX's collectives and lax.ppermute only.
A program may use at most 64 MiB of HBM per device.

v0:
```python
import jax
import jax.numpy as jnp
from jax import lax
from jax.sharding import PartitionSpec as P

L_DEV = 256


EPS = 1e-06


def entering(part, axis, combine, identity, reverse):
    count = lax.axis_size(axis)
    place = lax.axis_index(axis)
    ahead = count - 1 - place if reverse else place
    gathered = jax.tree.map(lambda a: lax.all_gather(a, axis), part)
    state = jax.tree.map(lambda a, e: jnp.zeros_like(a) + jnp.asarray(e, a.dtype), part, identity)

    def one(hop, state):
        source = count - 1 - hop if reverse else hop
        return combine(
            state, jax.tree.map(lambda a: lax.dynamic_index_in_dim(a, source, 0, False), gathered)
        )

    return lax.fori_loop(0, ahead, one, state)


def unit_rows(matrix):
    return matrix * lax.rsqrt(jnp.sum(matrix * matrix, axis=1, keepdims=True) + EPS)


def link(earlier, later):
    empty_later = later[1] < 0.0
    joined = later[0] + jnp.where(earlier[1] == later[1], earlier[0], 0.0)
    return (
        jnp.where(empty_later, earlier[0], joined),
        jnp.where(empty_later, earlier[1], later[1]),
    )


def shards(features, doc_labels, tree_perm, cluster_sizes):
    width = lax.axis_size("label")
    here = lax.axis_index("label")
    total = tree_perm.shape[0]
    depth = features.shape[1]
    per_pair = L_DEV // width
    base = here * L_DEV
    position = jnp.arange(total, dtype=jnp.int32)
    inverse = jnp.zeros((total,), jnp.int32).at[tree_perm].set(position)
    local_ids = doc_labels - base
    slots = jnp.arange(L_DEV, dtype=jnp.int32)
    incidence = jnp.sum((local_ids[:, :, None] == slots[None, None, :]).astype(jnp.float32), axis=1)
    partial_value = lax.dot_general(
        incidence,
        features,
        (((0,), (0,)), ((), ())),
        precision=lax.Precision.HIGHEST,
        preferred_element_type=jnp.float32,
    )
    summed = lax.psum(partial_value, "doc")
    normed = unit_rows(summed)
    own_tree = lax.dynamic_slice_in_dim(inverse, base, L_DEV)
    sending = jnp.argsort(own_tree)
    outgoing = normed[sending].reshape(width, per_pair, depth)
    incoming = lax.all_to_all(outgoing, "label", split_axis=0, concat_axis=0, tiled=True)
    own_perm = lax.dynamic_slice_in_dim(tree_perm, base, L_DEV)
    arrival = jnp.argsort(own_perm // L_DEV * L_DEV + slots)
    label_rows = incoming.reshape(L_DEV, depth)[jnp.argsort(arrival)]
    starts = jnp.cumsum(cluster_sizes) - cluster_sizes
    tree_pos = base + slots
    cluster_ids = jnp.sum((starts[None, 1:] <= tree_pos[:, None]).astype(jnp.int32), axis=1)
    same_cluster = (cluster_ids[:, None] == cluster_ids[None, :]).astype(jnp.float32)
    local_sum = jnp.dot(
        same_cluster,
        label_rows,
        precision=lax.Precision.HIGHEST,
        preferred_element_type=jnp.float32,
    )
    cluster_float = cluster_ids.astype(jnp.float32)
    identity = (jnp.zeros((depth,), jnp.float32), jnp.float32(-1.0))
    below_sum, below_id = entering(
        (local_sum[-1], cluster_float[-1]), "label", link, identity, False
    )
    above_sum, above_id = entering((local_sum[0], cluster_float[0]), "label", link, identity, True)
    cluster_sum = local_sum + jnp.where(
        (cluster_float == below_id)[:, None], below_sum[None, :], 0.0
    )
    cluster_sum = cluster_sum + jnp.where(
        (cluster_float == above_id)[:, None], above_sum[None, :], 0.0
    )
    centroid = unit_rows(cluster_sum)
    combined = label_rows + centroid
    doc_unit = unit_rows(features)
    return lax.dot_general(
        doc_unit,
        combined,
        (((1,), (1,)), ((), ())),
        precision=lax.Precision.HIGHEST,
        preferred_element_type=jnp.float32,
    )


def solution(mesh):
    in_specs = (P("doc", None), P("doc", None), P(), P())
    out_specs = P("doc", "label")
    return jax.shard_map(shards, mesh=mesh, in_specs=in_specs, out_specs=out_specs, check_vma=False)
```

profile of v0, /device:TPU:6, one launch (start us, length us, event | category | flops | bytes accessed | tf_op | source)
XLA Modules:
  0.0 800.1 jit_solution(1050786066250179485)
XLA Ops:
  6.5 0.8 broadcast_subtract_fusion
  7.4 10.8 %convert_reduce_fusion = f32[512,256]{1,0:T(8,128)S(1)} fusion(s32[512,16]{1,0:T(8,128)S(1)} %copy.8), kind=kLoop, calls=%fused_computation.7 | loop fusion | flops 6160384 | bytes 557056 | tf_op jit(solution)/shard_map/reduce_sum | solution.py:52
  18.3 4.5 fusion.18
  22.9 60.3 %scatter_custom_fusion = s32[16384]{0:T(1024)S(1)} fusion(s32[16384]{0:T(1024)S(1)} %compare_select_fusion, s32[16384]{0:T(1024)S(1)} %iota.23, s32[]{:T(128)} %constant.80.clone.1), kind=kCustom, calls=%fused_computation.33 | custom fusion | bytes 65540 | tf_op jit(solution)/shard_map/scatter | solution.py:49
  83.3 3.2 sort.45
  86.5 19.1 %all-reduce.5.cloned.1.call-done = f32[256,1024]{1,0:T(8,128)} async-done(((f32[256,1024]{1,0:T(8,128)}), f32[256,1024]{1,0:T(8,128)}) %all-reduce.5.cloned.1.call-update) | async-done | bytes 1048592 | tf_op jit(solution)/shard_map/psum | solution.py:60
  105.5 1.4 multiply_reduce_fusion.2
  106.9 1.4 broadcast_multiply_fusion
  108.3 1.1 gather_fusion
  109.4 1.3 reshape.55
  110.7 16.0 %all-to-all-start = ((f32[64,4,1024]{2,1,0:T(4,128)}), f32[64,4,1024]{2,1,0:T(4,128)}, u32[]{:S(2)}, u32[]{:S(2)}) async-start(f32[64,4,1024]{2,1,0:T(4,128)} %reshape.55), calls=%async_computation | async-start | bytes 2097152 | tf_op jit(solution)/shard_map/all_to_all | solution.py:65
  127.8 3.2 sort.46
  131.0 3.2 sort.47
  134.1 1.3 dynamic-slice
  136.1 0.8 slice_dynamic-update-slice_fusion.1
  136.9 160.7 %all-reduce.2 = (f32[64]{0:T(128)S(1)}, f32[64]{0:T(128)S(1)}) all-reduce(f32[64]{0:T(128)S(1)} %slice_dynamic-update-slice_fusion, f32[64]{0:T(128)S(1)} %slice_dynamic-update-slice_fusion.1), channel_id=1, replica_groups=mesh['doc'=8,'label'=64] {'label'}, use_global_device_ids=true, to_apply=%add.1 | all-reduce | flops 128 | bytes 1024
  297.9 1.6 reshape.56
  299.5 2.0 gather_fusion.1
  301.5 1.9 fusion.11
  303.5 86.9 %all-gather = f32[64,1,1024]{2,1,0:T(1,128)S(1)} all-gather(f32[1,1,1024]{2,1,0:T(1,128)S(1)} %get-tuple-element.156), channel_id=1, replica_groups=mesh['doc'=8,'label'=64] {'label'}, dimensions={0}, use_global_device_ids=true | all-gather | bytes 266240 | tf_op jit(solution)/shard_map/all_gather | solution.py:16
  390.5 7.8 while.26
  398.3 234.6 %all-gather.1 = f32[64,1,1024]{2,1,0:T(1,128)S(1)} all-gather(f32[1,1,1024]{2,1,0:T(1,128)S(1)} %get-tuple-element.157), channel_id=1, replica_groups=mesh['doc'=8,'label'=64] {'label'}, dimensions={0}, use_global_device_ids=true | all-gather | bytes 266240 | tf_op jit(solution)/shard_map/all_gather | solution.py:16
  632.9 155.8 %while.27 = (s32[]{:T(128)}, f32[1024]{0:T(1024)S(1)}, f32[]{:T(128)}, s32[]{:T(128)}, f32[64]{0:T(128)S(1)}, /*index=5*/f32[64,1024]{1,0:T(8,128)S(1)}, s32[]{:...) while((s32[]{:T(128)}, f32[1024]{0:T(1024)S(1)}, f32[]{:T(128)}, s32[]{:T(128)}, ...), condition=%wide.region_14.15_spmd, body=%wide.region_13.14_spmd.sunk | while | flops 3081 | bytes 20684 | solution.py:25
  789.1 4.1 fusion
  (233 shorter events, 41.0 us)
Async XLA Ops:
  6.5 99.0 %all-reduce.5.cloned.1.call-start = ((), (), s32[]{:S(2)}) async-start(), calls=%async_computation.1 | async-start | bytes 2097152 | tf_op jit(solution)/shard_map/psum | solution.py:60
  18.2 4.6 copy-start.1
  109.4 17.4 %copy-start.2 = (s32[512]{0:T(512)S(1)}, s32[512]{0:T(512)}, u32[]{:S(2)}) copy-start(s32[512]{0:T(512)} %param.11) | copy-start | bytes 6148
  109.4 188.3 %copy-start = (f32[512,1024]{1,0:T(8,128)S(1)}, f32[512,1024]{1,0:T(8,128)}, u32[]{:S(2)}) copy-start(f32[512,1024]{1,0:T(8,128)} %param.8) | copy-start | bytes 6291460
  110.7 187.1 %all-to-all-start = ((f32[64,4,1024]{2,1,0:T(4,128)}), f32[64,4,1024]{2,1,0:T(4,128)}, u32[]{:S(2)}, u32[]{:S(2)}) async-start(f32[64,4,1024]{2,1,0:T(4,128)} %reshape.55), calls=%async_computation | async-start | bytes 2097152 | tf_op jit(solution)/shard_map/all_to_all | solution.py:65
Sparse Core Ops, SparseCore 0:
  22.9 82.5 all-reduce.4
where the time goes:
time: 810 us; the launch traced here: 800 us
  blocking collectives  482 us (60%)
  loops' own time  125 us (15%)
  local copies, waits for them, and re-layouts  108 us (13%)
  other arithmetic  25.6 us (3%)
  waiting for transfers between devices  19.1 us (2%)
  starting transfers between devices  16 us (2%)
  between operations  13.6 us (2%)
  matrix products  10.6 us (1%)
    all_gather x2, blocking collectives, entering(): gathered = jax.tree.map(lambda a: lax.all_gather(a, axis), part)  322 us
    unnamed x1, blocking collectives  161 us
    another operation x2, loops' own time, entering(): return lax.fori_loop(0, ahead, one, state)  125 us
    scatter x1, local copies, waits for them, and re-layouts, shards(): inverse = jnp.zeros((total,), jnp.int32).at[tree_perm].set(position)  60.3 us
    dynamic_slice x126, local copies, waits for them, and re-layouts, one(): lax.dynamic_index_in_dim(a, source, 0, False)  37.8 us
    psum x1, waiting for transfers between devices, shards(): summed = lax.psum(partial_value, 'doc')  19.1 us
  transfers between devices with their start and end apart: 2, of which 1 were waited for; matrix products, arithmetic and copies ran while one was open for 9% of the time, Pallas kernels for 0%

commit v1 on v0

v1 whole, which is shorter than its diff:
```python
import jax
import jax.numpy as jnp
from jax import lax
from jax.sharding import PartitionSpec as P

L_DEV = 256


EPS = 1e-06


def unit_rows(matrix):
    return matrix * lax.rsqrt(jnp.sum(matrix * matrix, axis=1, keepdims=True) + EPS)


def cluster_of(positions, starts):
    return jnp.sum((starts[None, 1:] <= positions[:, None]).astype(jnp.int32), axis=1)


def shards(features, doc_labels, tree_perm, cluster_sizes):
    width = lax.axis_size("label")
    here = lax.axis_index("label")
    base = here * L_DEV
    slots = jnp.arange(L_DEV, dtype=jnp.int32)

    own_perm = lax.dynamic_slice_in_dim(tree_perm, base, L_DEV)
    incidence = jnp.sum(
        (doc_labels[:, :, None] == own_perm[None, None, :]).astype(jnp.float32), axis=1
    )
    partial_value = lax.dot_general(
        incidence,
        features,
        (((0,), (0,)), ((), ())),
        precision=lax.Precision.HIGHEST,
        preferred_element_type=jnp.float32,
    )
    summed = lax.psum(partial_value, "doc")
    label_rows = unit_rows(summed)

    starts = jnp.cumsum(cluster_sizes) - cluster_sizes
    cluster_ids = cluster_of(base + slots, starts)
    shard = jnp.arange(width, dtype=jnp.int32)
    first_id = cluster_of(shard * L_DEV, starts)
    last_id = cluster_of(shard * L_DEV + (L_DEV - 1), starts)

    same_cluster = (cluster_ids[:, None] == cluster_ids[None, :]).astype(jnp.float32)
    local_sum = jnp.dot(
        same_cluster,
        label_rows,
        precision=lax.Precision.HIGHEST,
        preferred_element_type=jnp.float32,
    )
    ends = jnp.stack([local_sum[0], local_sum[-1]])
    gathered = lax.all_gather(ends, "label").reshape(2 * width, -1)

    other = (shard != here)[None, :]
    take_first = (first_id[None, :] == cluster_ids[:, None]) & other
    take_last = (last_id[None, :] == cluster_ids[:, None]) & (first_id != last_id)[None, :] & other
    weights = jnp.stack([take_first, take_last], axis=2).reshape(L_DEV, 2 * width)
    cluster_sum = local_sum + jnp.dot(
        weights.astype(jnp.float32),
        gathered,
        precision=lax.Precision.HIGHEST,
        preferred_element_type=jnp.float32,
    )
    centroid = unit_rows(cluster_sum)
    combined = label_rows + centroid
    doc_unit = unit_rows(features)
    return lax.dot_general(
        doc_unit,
        combined,
        (((1,), (1,)), ((), ())),
        precision=lax.Precision.HIGHEST,
        preferred_element_type=jnp.float32,
    )


def solution(mesh):
    in_specs = (P("doc", None), P("doc", None), P(), P())
    out_specs = P("doc", "label")
    return jax.shard_map(shards, mesh=mesh, in_specs=in_specs, out_specs=out_specs, check_vma=False)
```

time: 810 us -> 221 us (0.27); the launches traced: 800 us -> 221 us
  blocking collectives: 482 us -> 101 us
  loops' own time: 125 us -> 0 us
  local copies, waits for them, and re-layouts: 108 us -> 2.34 us
  waiting for transfers between devices: 19.1 us -> 80.6 us
  starting transfers between devices: 16 us -> 0.01 us
  other arithmetic: 25.6 us -> 13.4 us
    all_gather x2 -> x1, blocking collectives: 322 us -> 101 us  [shards(): gathered = lax.all_gather(ends, 'label').reshape(2 * width, -1)]
    unnamed x1 -> x0, blocking collectives: 161 us -> none
    another operation x2 -> x0, loops' own time: 125 us -> none  [entering(): return lax.fori_loop(0, ahead, one, state)]
    psum x1, waiting for transfers between devices: 19.1 us -> 80.6 us  [shards(): summed = lax.psum(partial_value, 'doc')]
    scatter x1 -> x0, local copies, waits for them, and re-layouts: 60.3 us -> none  [shards(): inverse = jnp.zeros((total,), jnp.int32).at[tree_perm].set(position)]
    dynamic_slice x127 -> x1, local copies, waits for them, and re-layouts: 37.9 us -> 0.77 us  [shards(): own_perm = lax.dynamic_slice_in_dim(tree_perm, base, L_DEV)]
    all_to_all x1 -> x0, starting transfers between devices: 16 us -> none  [shards(): lax.all_to_all(outgoing, 'label', split_axis=0, concat_axis=0, tiled=True)]
    sort x3 -> x0, other arithmetic: 9.5 us -> none  [the longest x1 3.17 us: shards(): arrival = jnp.argsort(own_perm // L_DEV * L_DEV + slots)]
  transfers between devices with their start and end apart: 2 -> 1, of which waited for: 1 -> 1; matrix products, arithmetic and copies ran while one was open for 9% -> 1% of each run, Pallas kernels for 0% -> 0%
where the time goes in v1:
time: 221 us
  blocking collectives  101 us (46%)
  waiting for transfers between devices  80.6 us (36%)
  between operations  13.5 us (6%)
  other arithmetic  13.4 us (6%)
  matrix products  10.4 us (5%)
  local copies, waits for them, and re-layouts  2.34 us (1%)
    all_gather x1, blocking collectives, shards(): gathered = lax.all_gather(ends, 'label').reshape(2 * width, -1)  101 us
    psum x1, waiting for transfers between devices, shards(): summed = lax.psum(partial_value, 'doc')  80.6 us
    reduce_sum x1, other arithmetic, shards(): jnp.sum((doc_labels[:, :, None] == own_perm[None, None, :]).astype(jnp.fl...  10.9 us
    dot_general x1, matrix products, shards(): lax.dot_general(incidence, features, (((0,), (0,)), ((), ())), precision=...  4.64 us
  transfers between devices with their start and end apart: 1, of which 1 were waited for; matrix products, arithmetic and copies ran while one was open for 1% of the time, Pallas kernels for 0%

profile of v1, /device:TPU:6, one launch (start us, length us, event | category | flops | bytes accessed | tf_op | source)
XLA Modules:
  0.0 221.0 jit_solution(827182188428001773)
XLA Ops:
  6.5 0.0 all-reduce.2.cloned.1.call-start
  6.5 0.9 copy.11
  7.4 0.8 dynamic_slice.3
  8.2 10.9 %convert_reduce_fusion = f32[512,256]{1,0:T(8,128)S(1)} fusion(s32[256]{0:T(256)S(1)} %dynamic_slice.3, s32[512,16]{1,0:T(8,128)S(1)} %copy.11), kind=kLoop, calls=%fused_computation | loop fusion | flops 6160384 | bytes 558080 | tf_op jit(solution)/shard_map/reduce_sum | solution.py:27
  19.1 0.0 copy-start
  19.1 4.6 %fusion.21 = f32[256,1024]{1,0:T(8,128)} fusion(f32[512,256]{1,0:T(8,128)S(1)} %convert_reduce_fusion, f32[512,1024]{1,0:T(8,128)} %param.4), kind=kOutput, calls=%fused_computation.41 | convolution fusion | flops 1610612736 | bytes 3670016 | tf_op jit(solution)/shard_map/dot_general | solution.py:30
  23.7 0.0 all-reduce.2.cloned.1.call-update
  23.8 0.2 multiply_reduce_fusion
  24.0 0.4 copy-done.2
  24.4 0.3 reduce-window.9
  24.7 0.1 slice.18
  24.8 0.1 slice_reduce_fusion
  24.9 0.1 bitcast_subtract_fusion
  25.0 0.1 slice.20
  25.1 0.2 convert_reduce_fusion.1
  25.3 0.2 convert_reduce_fusion.3
  25.5 0.1 compare_and_fusion
  25.7 80.6 %all-reduce.2.cloned.1.call-done = f32[256,1024]{1,0:T(8,128)} async-done(((f32[256,1024]{1,0:T(8,128)}), f32[256,1024]{1,0:T(8,128)}) %all-reduce.2.cloned.1.call-update) | async-done | bytes 1048592 | tf_op jit(solution)/shard_map/psum | solution.py:37
  106.2 1.4 multiply_reduce_fusion.2
  107.6 2.1 fusion.7
  109.7 100.7 %all-gather.1 = f32[64,2,1024]{2,1,0:T(2,128)S(1)} all-gather(f32[1,2,1024]{2,1,0:T(2,128)S(1)} %maximum_bitcast_fusion), channel_id=2, replica_groups=mesh['doc'=8,'label'=64] {'label'}, dimensions={0}, use_global_device_ids=true | all-gather | bytes 532480 | tf_op jit(solution)/shard_map/all_gather | solution.py:54
  210.4 0.8 multiply_reduce_fusion.1
  211.3 0.0 copy-done.1
  211.3 2.8 %fusion = f32[512,256]{1,0:T(8,128)} fusion(f32[512,1024]{1,0:T(8,128)S(1)} %copy-done, f32[256,1024]{1,0:T(8,128)S(1)} %get-tuple-element.12, f32[512]{0:T(512)S(1)} %add_rsqrt_fusion, f32[256,1024]{1,0:T(8,128)S(1)} %copy-done.1, f32[256]{0:T(256)S(1)} %add_rsqrt_fusion.1, f32[256]{0:T(256)S(1)} %add_rsqrt_fusion.2), kind=kOutput, calls=%fused_computation.1 | convolution fusion | flops 1611923456 | bytes 4722688 | tf_op jit(solution)/shard_map/dot_general | solution.py:69
  (13 shorter events, 0.1 us)
Async XLA Ops:
  6.5 99.7 %all-reduce.2.cloned.1.call-start = ((), (), s32[]{:S(2)}) async-start(), calls=%async_computation | async-start | bytes 2097152 | tf_op jit(solution)/shard_map/psum | solution.py:37
  19.1 4.7 %copy-start = (f32[512,1024]{1,0:T(8,128)S(1)}, f32[512,1024]{1,0:T(8,128)}, u32[]{:S(2)}) copy-start(f32[512,1024]{1,0:T(8,128)} %param.4) | copy-start | bytes 6291460
  23.7 0.7 copy-start.2
  109.7 101.6 %copy-start.1 = (f32[256,1024]{1,0:T(8,128)S(1)}, f32[256,1024]{1,0:T(8,128)}, u32[]{:S(2)}) copy-start(f32[256,1024]{1,0:T(8,128)} %all-reduce.2.cloned.1.call-done) | copy-start | bytes 3145732
Sparse Core Ops, SparseCore 0:
  23.9 82.3 all-reduce.1

commit v2 on v1

--- a/solution.py
+++ b/solution.py
@@ -34,8 +34,15 @@
         precision=lax.Precision.HIGHEST,
         preferred_element_type=jnp.float32,
     )
-    summed = lax.psum(partial_value, "doc")
-    label_rows = unit_rows(summed)
+    groups = lax.axis_size("doc")
+    depth = features.shape[1]
+    pieces = lax.all_to_all(
+        partial_value.reshape(groups, L_DEV // groups, depth), "doc", 0, 0, tiled=True
+    )
+    mine = unit_rows(jnp.sum(pieces, axis=0))
+    label_rows = lax.all_to_all(
+        jnp.broadcast_to(mine[None], (groups,) + mine.shape), "doc", 0, 0, tiled=True
+    ).reshape(L_DEV, depth)
 
     starts = jnp.cumsum(cluster_sizes) - cluster_sizes
     cluster_ids = cluster_of(base + slots, starts)
@@ -51,7 +58,9 @@
         preferred_element_type=jnp.float32,
     )
     ends = jnp.stack([local_sum[0], local_sum[-1]])
-    gathered = lax.all_gather(ends, "label").reshape(2 * width, -1)
+    gathered = lax.all_to_all(
+        jnp.broadcast_to(ends[None], (width,) + ends.shape), "label", 0, 0, tiled=True
+    ).reshape(2 * width, -1)
 
     other = (shard != here)[None, :]
     take_first = (first_id[None, :] == cluster_ids[:, None]) & other

time: 221 us -> 119 us (0.54)
  blocking collectives: 101 us -> 20.5 us
  waiting for transfers between devices: 80.6 us -> 46.8 us
  starting transfers between devices: 0.01 us -> 22.3 us
  between operations: 13.5 us -> 0.13 us
  local copies, waits for them, and re-layouts: 2.34 us -> 6.09 us
    all_gather x1 -> x0, blocking collectives: 101 us -> none  [shards(): gathered = lax.all_gather(ends, 'label').reshape(2 * width, -1)]
    psum x1 -> x0, waiting for transfers between devices: 80.6 us -> none  [shards(): summed = lax.psum(partial_value, 'doc')]
    all_to_all x0 -> x2, waiting for transfers between devices: none -> 46.8 us  [the longest x1 31.9 us: shards(): lax.all_to_all(jnp.broadcast_to(ends[None], (width,) + ends.shape), 'labe...]
    all_to_all x0 -> x2, starting transfers between devices: none -> 22.3 us  [the longest x1 18.8 us: shards(): lax.all_to_all(jnp.broadcast_to(ends[None], (width,) + ends.shape), 'labe...]
    all_to_all x0 -> x1, blocking collectives: none -> 20.5 us  [shards(): lax.all_to_all(partial_value.reshape(groups, L_DEV // groups, depth), 'do...]
  transfers between devices with their start and end apart: 1 -> 2, of which waited for: 1 -> 2; matrix products, arithmetic and copies ran while one was open for 1% -> 1% of each run, Pallas kernels for 0% -> 0%
where the time goes in v2:
time: 119 us; the launch traced here: 118 us
  waiting for transfers between devices  46.8 us (39%)
  starting transfers between devices  22.3 us (19%)
  blocking collectives  20.5 us (17%)
  other arithmetic  13.6 us (11%)
  matrix products  8.66 us (7%)
  local copies, waits for them, and re-layouts  6.09 us (5%)
    all_to_all x1, waiting for transfers between devices, shards(): lax.all_to_all(jnp.broadcast_to(ends[None], (width,) + ends.shape), 'labe...  31.9 us
    all_to_all x1, blocking collectives, shards(): lax.all_to_all(partial_value.reshape(groups, L_DEV // groups, depth), 'do...  20.5 us
    all_to_all x1, starting transfers between devices, shards(): lax.all_to_all(jnp.broadcast_to(ends[None], (width,) + ends.shape), 'labe...  18.8 us
    all_to_all x1, waiting for transfers between devices, shards(): lax.all_to_all(jnp.broadcast_to(mine[None], (groups,) + mine.shape), 'doc...  15 us
    reduce_sum x1, other arithmetic, shards(): jnp.sum((doc_labels[:, :, None] == own_perm[None, None, :]).astype(jnp.fl...  10.9 us
    all_to_all x1, starting transfers between devices, shards(): lax.all_to_all(jnp.broadcast_to(mine[None], (groups,) + mine.shape), 'doc...  3.56 us
    dot_general x1, matrix products, shards(): lax.dot_general(incidence, features, (((0,), (0,)), ((), ())), precision=...  2.93 us
    dot_general x1, matrix products, shards(): lax.dot_general(doc_unit, combined, (((1,), (1,)), ((), ())), precision=l...  2.79 us
  transfers between devices with their start and end apart: 2, of which 2 were waited for; matrix products, arithmetic and copies ran while one was open for 1% of the time, Pallas kernels for 0%

profile of v2, /device:TPU:6, one launch (start us, length us, event | category | flops | bytes accessed | tf_op | source)
XLA Modules:
  0.0 118.1 jit_solution(6333125169838046619)
XLA Ops:
  0.0 1.0 copy.12
  1.0 0.8 dynamic_slice.3
  1.8 10.9 %convert_reduce_fusion = f32[512,256]{1,0:T(8,128)S(1)} fusion(s32[256]{0:T(256)S(1)} %dynamic_slice.3, s32[512,16]{1,0:T(8,128)S(1)} %copy.12), kind=kLoop, calls=%fused_computation | loop fusion | flops 6160384 | bytes 558080 | tf_op jit(solution)/shard_map/reduce_sum | solution.py:27
  12.7 1.0 copy.13
  13.7 2.9 %fusion = f32[8,32,1024]{2,1,0:T(8,128)S(1)} fusion(f32[8,32,512]{2,1,0:T(8,128)} %bitcast.17, f32[512,1024]{1,0:T(8,128)S(1)} %copy-done), kind=kOutput, calls=%fused_computation.1 | convolution fusion | flops 1610612736 | bytes 3670016 | tf_op jit(solution)/shard_map/dot_general | solution.py:30
  16.6 20.5 %all_to_all.15 = f32[8,32,1024]{2,1,0:T(8,128)} all-to-all(f32[8,32,1024]{2,1,0:T(8,128)S(1)} %fusion), channel_id=1, replica_groups=mesh['doc'=8,'label'=64] {'doc'}, dimensions={0} | all-to-all | bytes 2097152 | tf_op jit(solution)/shard_map/all_to_all | solution.py:39
  37.1 1.3 %reduce_sum.74 = f32[32,1024]{1,0:T(8,128)S(1)} reduce(f32[8,32,1024]{2,1,0:T(8,128)} %all_to_all.15, f32[]{:T(128)} %constant.7.clone.1), dimensions={0}, to_apply=%region_2.0 | reduce | flops 229376 | bytes 1179652 | tf_op jit(solution)/shard_map/reduce_sum | solution.py:42
  38.4 0.1 multiply_reduce_fusion.2
  38.6 1.1 broadcast_in_dim.4
  39.7 3.6 %all-to-all-start.1 = ((f32[8,32,1024]{2,1,0:T(8,128)}), f32[8,32,1024]{2,1,0:T(8,128)S(1)}, u32[]{:S(2)}, u32[]{:S(2)}) async-start(f32[8,32,1024]{2,1,0:T(8,128)} %broadcast_in_dim.4), calls=%async_computation.1 | async-start | bytes 2097152 | tf_op jit(solution)/shard_map/all_to_all | solution.py:43
  43.3 0.3 reduce-window.9
  43.7 0.1 slice_reduce_fusion
  44.0 0.2 convert_reduce_fusion.1
  44.2 15.0 %all-to-all-done.1 = f32[8,32,1024]{2,1,0:T(8,128)S(1)} async-done(((f32[8,32,1024]{2,1,0:T(8,128)}), f32[8,32,1024]{2,1,0:T(8,128)S(1)}, u32[]{:S(2)}, u32[]{:S(2)}) %all-to-all-start.1) | async-done | bytes 1048608 | tf_op jit(solution)/shard_map/all_to_all | solution.py:43
  59.2 0.7 fusion.10
  59.9 1.0 copy-done.1
  60.9 0.9 broadcast_in_dim.5
  61.8 18.8 %all-to-all-start.2 = ((f32[64,2,1024]{2,1,0:T(2,128)}), f32[64,2,1024]{2,1,0:T(2,128)}, u32[]{:S(2)}, u32[]{:S(2)}) async-start(f32[64,2,1024]{2,1,0:T(2,128)} %broadcast_in_dim.5), calls=%async_computation.2 | async-start | bytes 1048576 | tf_op jit(solution)/shard_map/all_to_all | solution.py:61
  80.6 0.2 convert_reduce_fusion.3
  80.9 0.2 multiply_reduce_fusion
  81.1 0.1 compare_and_fusion
  81.2 31.9 %all-to-all-done.2 = f32[64,2,1024]{2,1,0:T(2,128)} async-done(((f32[64,2,1024]{2,1,0:T(2,128)}), f32[64,2,1024]{2,1,0:T(2,128)}, u32[]{:S(2)}, u32[]{:S(2)}) %all-to-all-start.2) | async-done | bytes 524320 | tf_op jit(solution)/shard_map/all_to_all | solution.py:61
  113.1 2.2 %multiply_reduce_fusion.1 = (f32[256]{0:T(256)S(1)}, f32[256,1024]{1,0:T(8,128)S(1)}) fusion(f32[256,1024]{1,0:T(8,128)} %copy-done.1, f32[64,2,1024]{2,1,0:T(2,128)} %all-to-all-done.2, pred[256,64,1]{0,1,2:T(32,128)(4,1)S(1)} %get-tuple-element.10, pred[256,64,1]{0,1,2:T(32,128)(4,1)S(1)} %get-tuple-element.9), kind=kOutput, calls=%fused_computation.10 | convolution fusion | flops 403472128 | bytes 2655232 | tf_op jit(solution)/shard_map/dot_general | solution.py:69
  115.3 2.8 %fusion.2 = f32[512,256]{1,0:T(8,128)} fusion(f32[512,1024]{1,0:T(8,128)S(1)} %copy-done, f32[256,1024]{1,0:T(8,128)S(1)} %bitcast.16, f32[256,1024]{1,0:T(8,128)S(1)} %get-tuple-element.12, f32[512]{0:T(512)S(1)} %add_rsqrt_fusion, f32[256]{0:T(256)S(1)} %add_rsqrt_fusion.1), kind=kOutput, calls=%fused_computation.3 | convolution fusion | flops 1611661312 | bytes 4721664 | tf_op jit(solution)/shard_map/dot_general | solution.py:78
  (19 shorter events, 0.4 us)
Async XLA Ops:
  0.0 13.7 %copy-start = (f32[512,1024]{1,0:T(8,128)S(1)}, f32[512,1024]{1,0:T(8,128)}, u32[]{:S(2)}) copy-start(f32[512,1024]{1,0:T(8,128)} %param.4) | copy-start | bytes 6291460
  38.4 4.9 %copy-start.2 = (s32[512]{0:T(512)S(1)}, s32[512]{0:T(512)}, u32[]{:S(2)}) copy-start(s32[512]{0:T(512)} %param.7) | copy-start | bytes 6148
  39.7 19.4 %all-to-all-start.1 = ((f32[8,32,1024]{2,1,0:T(8,128)}), f32[8,32,1024]{2,1,0:T(8,128)S(1)}, u32[]{:S(2)}, u32[]{:S(2)}) async-start(f32[8,32,1024]{2,1,0:T(8,128)} %broadcast_in_dim.4), calls=%async_computation.1 | async-start | bytes 2097152 | tf_op jit(solution)/shard_map/all_to_all | solution.py:43
  59.9 1.0 copy-start.1
  61.8 51.2 %all-to-all-start.2 = ((f32[64,2,1024]{2,1,0:T(2,128)}), f32[64,2,1024]{2,1,0:T(2,128)}, u32[]{:S(2)}, u32[]{:S(2)}) async-start(f32[64,2,1024]{2,1,0:T(2,128)} %broadcast_in_dim.5), calls=%async_computation.2 | async-start | bytes 1048576 | tf_op jit(solution)/shard_map/all_to_all | solution.py:61

commit v3 on v2

--- a/solution.py
+++ b/solution.py
@@ -25,12 +25,12 @@
 
     own_perm = lax.dynamic_slice_in_dim(tree_perm, base, L_DEV)
     incidence = jnp.sum(
-        (doc_labels[:, :, None] == own_perm[None, None, :]).astype(jnp.float32), axis=1
+        (doc_labels.T[:, None, :] == own_perm[None, :, None]).astype(jnp.float32), axis=0
     )
     partial_value = lax.dot_general(
         incidence,
         features,
-        (((0,), (0,)), ((), ())),
+        (((1,), (0,)), ((), ())),
         precision=lax.Precision.HIGHEST,
         preferred_element_type=jnp.float32,
     )
@@ -62,6 +62,14 @@
         jnp.broadcast_to(ends[None], (width,) + ends.shape), "label", 0, 0, tiled=True
     ).reshape(2 * width, -1)
 
+    doc_unit = unit_rows(features)
+    row_scores = lax.dot_general(
+        doc_unit,
+        label_rows,
+        (((1,), (1,)), ((), ())),
+        precision=lax.Precision.HIGHEST,
+        preferred_element_type=jnp.float32,
+    )
     other = (shard != here)[None, :]
     take_first = (first_id[None, :] == cluster_ids[:, None]) & other
     take_last = (last_id[None, :] == cluster_ids[:, None]) & (first_id != last_id)[None, :] & other
@@ -73,15 +81,13 @@
         preferred_element_type=jnp.float32,
     )
     centroid = unit_rows(cluster_sum)
-    combined = label_rows + centroid
-    doc_unit = unit_rows(features)
     return lax.dot_general(
         doc_unit,
-        combined,
+        centroid,
         (((1,), (1,)), ((), ())),
         precision=lax.Precision.HIGHEST,
         preferred_element_type=jnp.float32,
-    )
+    ) + row_scores
 
 
 def solution(mesh):

time: 119 us -> 107 us (0.90)
  other arithmetic: 13.6 us -> 3.15 us
  matrix products: 8.66 us -> 11.8 us
  waiting for transfers between devices: 46.8 us -> 44.2 us
  local copies, waits for them, and re-layouts: 6.09 us -> 4.09 us
    reduce_sum x1, other arithmetic: 10.9 us -> 1.69 us  [shards(): jnp.sum((doc_labels.T[:, None, :] == own_perm[None, :, None]).astype(jnp....]
    dot_general x2 -> x3, matrix products: 5.72 us -> 8.86 us  [the longest x1 3.48 us: shards(): lax.dot_general(incidence, features, (((1,), (0,)), ((), ())), precision=...]
    all_to_all x1, waiting for transfers between devices: 31.9 us -> 29.2 us  [shards(): lax.all_to_all(jnp.broadcast_to(ends[None], (width,) + ends.shape), 'labe...]
    reduce_sum x1, other arithmetic: 1.29 us -> 0.06 us  [shards(): mine = unit_rows(jnp.sum(pieces, axis=0))]
  transfers between devices with their start and end apart: 2 -> 2, of which waited for: 2 -> 2; matrix products, arithmetic and copies ran while one was open for 1% -> 4% of each run, Pallas kernels for 0% -> 0%
where the time goes in v3:
time: 107 us; the launch traced here: 106 us
  waiting for transfers between devices  44.2 us (41%)
  starting transfers between devices  22.3 us (21%)
  blocking collectives  20.4 us (19%)
  matrix products  11.8 us (11%)
  local copies, waits for them, and re-layouts  4.09 us (4%)
  other arithmetic  3.15 us (3%)
    all_to_all x1, waiting for transfers between devices, shards(): lax.all_to_all(jnp.broadcast_to(ends[None], (width,) + ends.shape), 'labe...  29.2 us
    all_to_all x1, blocking collectives, shards(): lax.all_to_all(partial_value.reshape(groups, L_DEV // groups, depth), 'do...  20.4 us
    all_to_all x1, starting transfers between devices, shards(): lax.all_to_all(jnp.broadcast_to(ends[None], (width,) + ends.shape), 'labe...  18.8 us
    all_to_all x1, waiting for transfers between devices, shards(): lax.all_to_all(jnp.broadcast_to(mine[None], (groups,) + mine.shape), 'doc...  15 us
    all_to_all x1, starting transfers between devices, shards(): lax.all_to_all(jnp.broadcast_to(mine[None], (groups,) + mine.shape), 'doc...  3.56 us
    dot_general x1, matrix products, shards(): lax.dot_general(incidence, features, (((1,), (0,)), ((), ())), precision=...  3.48 us
    dot_general x1, matrix products, shards(): lax.dot_general(doc_unit, centroid, (((1,), (1,)), ((), ())), precision=l...  2.73 us
    dot_general x1, matrix products, shards(): lax.dot_general(doc_unit, label_rows, (((1,), (1,)), ((), ())), precision...  2.65 us
  transfers between devices with their start and end apart: 2, of which 2 were waited for; matrix products, arithmetic and copies ran while one was open for 4% of the time, Pallas kernels for 0%

profile of v3, /device:TPU:6, one launch (start us, length us, event | category | flops | bytes accessed | tf_op | source)
XLA Modules:
  0.0 106.1 jit_solution(15000166133928333938)
XLA Ops:
  0.0 0.8 dynamic_slice.3
  0.8 1.7 %convert_reduce_fusion = f32[256,512]{1,0:T(8,128)S(1)} fusion(s32[16,512]{1,0:T(8,128)} %bitcast.19, s32[256]{0:T(256)S(1)} %dynamic_slice.3), kind=kLoop, calls=%fused_computation | loop fusion | flops 6160384 | bytes 558080 | tf_op jit(solution)/shard_map/reduce_sum | solution.py:27
  2.5 3.5 %fusion = f32[8,32,1024]{2,1,0:T(8,128)S(1)} fusion(f32[8,32,512]{2,1,0:T(8,128)S(1)} %bitcast.18, f32[512,1024]{1,0:T(8,128)} %param.4), kind=kOutput, calls=%fused_computation.1 | convolution fusion | flops 1610612736 | bytes 3670016 | tf_op jit(solution)/shard_map/dot_general | solution.py:30
  6.0 20.4 %all_to_all.15 = f32[8,32,1024]{2,1,0:T(8,128)S(1)} all-to-all(f32[8,32,1024]{2,1,0:T(8,128)S(1)} %fusion), channel_id=1, replica_groups=mesh['doc'=8,'label'=64] {'doc'}, dimensions={0} | all-to-all | bytes 2097152 | tf_op jit(solution)/shard_map/all_to_all | solution.py:39
  26.4 0.1 multiply_reduce_fusion.2
  26.5 0.1 broadcast_multiply_fusion
  26.6 1.1 %broadcast_in_dim.4 = f32[8,32,1024]{2,1,0:T(8,128)} broadcast(f32[32,1024]{1,0:T(8,128)S(1)} %broadcast_multiply_fusion), dimensions={1,2} | broadcast | bytes 1179648 | tf_op jit(solution)/shard_map/broadcast_in_dim | solution.py:44
  27.7 3.6 %all-to-all-start.1 = ((f32[8,32,1024]{2,1,0:T(8,128)}), f32[8,32,1024]{2,1,0:T(8,128)S(1)}, u32[]{:S(2)}, u32[]{:S(2)}) async-start(f32[8,32,1024]{2,1,0:T(8,128)} %broadcast_in_dim.4), calls=%async_computation.1 | async-start | bytes 2097152 | tf_op jit(solution)/shard_map/all_to_all | solution.py:43
  31.3 0.3 reduce-window.9
  31.7 0.1 slice_reduce_fusion
  31.9 0.1 bitcast_subtract_fusion
  32.0 0.2 convert_reduce_fusion.1
  32.2 15.0 %all-to-all-done.1 = f32[8,32,1024]{2,1,0:T(8,128)S(1)} async-done(((f32[8,32,1024]{2,1,0:T(8,128)}), f32[8,32,1024]{2,1,0:T(8,128)S(1)}, u32[]{:S(2)}, u32[]{:S(2)}) %all-to-all-start.1) | async-done | bytes 1048608 | tf_op jit(solution)/shard_map/all_to_all | solution.py:43
  47.2 0.7 fusion.15
  47.9 1.0 copy-done.1
  48.9 0.9 broadcast_in_dim.5
  49.9 18.8 %all-to-all-start.2 = ((f32[64,2,1024]{2,1,0:T(2,128)}), f32[64,2,1024]{2,1,0:T(2,128)}, u32[]{:S(2)}, u32[]{:S(2)}) async-start(f32[64,2,1024]{2,1,0:T(2,128)} %broadcast_in_dim.5), calls=%async_computation.2 | async-start | bytes 1048576 | tf_op jit(solution)/shard_map/all_to_all | solution.py:61
  68.6 0.2 convert_reduce_fusion.3
  68.9 0.2 multiply_reduce_fusion
  69.1 0.1 compare_and_fusion
  69.2 2.6 %fusion.2 = f32[512,256]{1,0:T(8,128)} fusion(f32[256,1024]{1,0:T(8,128)S(1)} %bitcast.17, f32[512,1024]{1,0:T(8,128)S(1)} %copy-done, f32[512]{0:T(512)S(1)} %add_rsqrt_fusion), kind=kOutput, calls=%fused_computation.4 | convolution fusion | flops 1611137024 | bytes 3672064 | tf_op jit(solution)/shard_map/dot_general | solution.py:66
  71.9 29.2 %all-to-all-done.2 = f32[64,2,1024]{2,1,0:T(2,128)} async-done(((f32[64,2,1024]{2,1,0:T(2,128)}), f32[64,2,1024]{2,1,0:T(2,128)}, u32[]{:S(2)}, u32[]{:S(2)}) %all-to-all-start.2) | async-done | bytes 524320 | tf_op jit(solution)/shard_map/all_to_all | solution.py:61
  101.1 2.2 %multiply_reduce_fusion.1 = (f32[256]{0:T(256)S(1)}, f32[256,1024]{1,0:T(8,128)S(1)}) fusion(f32[256,1024]{1,0:T(8,128)} %copy-done.1, f32[64,2,1024]{2,1,0:T(2,128)} %all-to-all-done.2, pred[256,64,1]{0,1,2:T(32,128)(4,1)S(1)} %get-tuple-element.10, pred[256,64,1]{0,1,2:T(32,128)(4,1)S(1)} %get-tuple-element.9), kind=kOutput, calls=%fused_computation.12 | convolution fusion | flops 403472128 | bytes 2655232 | tf_op jit(solution)/shard_map/dot_general | solution.py:77
  103.3 2.7 %fusion.7 = f32[512,256]{1,0:T(8,128)} fusion(f32[512,256]{1,0:T(8,128)S(1)} %copy-done.2, f32[512,1024]{1,0:T(8,128)S(1)} %copy-done, f32[256,1024]{1,0:T(8,128)S(1)} %get-tuple-element.12, f32[512]{0:T(512)S(1)} %add_rsqrt_fusion, f32[256]{0:T(256)S(1)} %add_rsqrt_fusion.1), kind=kOutput, calls=%fused_computation.10 | convolution fusion | flops 1611530240 | bytes 4197376 | tf_op jit(solution)/shard_map/dot_general | solution.py:84
  (20 shorter events, 0.3 us)
Async XLA Ops:
  26.4 4.9 %copy-start.3 = (s32[512]{0:T(512)S(1)}, s32[512]{0:T(512)}, u32[]{:S(2)}) copy-start(s32[512]{0:T(512)} %param.7) | copy-start | bytes 6148
  27.7 19.4 %all-to-all-start.1 = ((f32[8,32,1024]{2,1,0:T(8,128)}), f32[8,32,1024]{2,1,0:T(8,128)S(1)}, u32[]{:S(2)}, u32[]{:S(2)}) async-start(f32[8,32,1024]{2,1,0:T(8,128)} %broadcast_in_dim.4), calls=%async_computation.1 | async-start | bytes 2097152 | tf_op jit(solution)/shard_map/all_to_all | solution.py:43
  31.3 37.6 %copy-start = (f32[512,1024]{1,0:T(8,128)S(1)}, f32[512,1024]{1,0:T(8,128)}, u32[]{:S(2)}) copy-start(f32[512,1024]{1,0:T(8,128)} %param.4) | copy-start | bytes 6291460
  47.9 1.0 copy-start.1
  49.9 51.2 %all-to-all-start.2 = ((f32[64,2,1024]{2,1,0:T(2,128)}), f32[64,2,1024]{2,1,0:T(2,128)}, u32[]{:S(2)}, u32[]{:S(2)}) async-start(f32[64,2,1024]{2,1,0:T(2,128)} %broadcast_in_dim.5), calls=%async_computation.2 | async-start | bytes 1048576 | tf_op jit(solution)/shard_map/all_to_all | solution.py:61
  71.9 31.4 %copy-start.2 = (f32[512,256]{1,0:T(8,128)S(1)}, f32[512,256]{1,0:T(8,128)}, u32[]{:S(2)}) copy-start(f32[512,256]{1,0:T(8,128)} %fusion.2) | copy-start | bytes 1572868

commit v4 on v3

--- a/solution.py
+++ b/solution.py
@@ -58,9 +58,6 @@
         preferred_element_type=jnp.float32,
     )
     ends = jnp.stack([local_sum[0], local_sum[-1]])
-    gathered = lax.all_to_all(
-        jnp.broadcast_to(ends[None], (width,) + ends.shape), "label", 0, 0, tiled=True
-    ).reshape(2 * width, -1)
 
     doc_unit = unit_rows(features)
     row_scores = lax.dot_general(
@@ -70,16 +67,42 @@
         precision=lax.Precision.HIGHEST,
         preferred_element_type=jnp.float32,
     )
-    other = (shard != here)[None, :]
-    take_first = (first_id[None, :] == cluster_ids[:, None]) & other
-    take_last = (last_id[None, :] == cluster_ids[:, None]) & (first_id != last_id)[None, :] & other
-    weights = jnp.stack([take_first, take_last], axis=2).reshape(L_DEV, 2 * width)
-    cluster_sum = local_sum + jnp.dot(
-        weights.astype(jnp.float32),
-        gathered,
-        precision=lax.Precision.HIGHEST,
-        preferred_element_type=jnp.float32,
+
+    lane = lax.axis_index("doc")
+    my_first = first_id[here]
+    my_last = last_id[here]
+    extra = jnp.zeros_like(ends)
+    for near in (1, groups + 1):
+        for sign in (1, -1):
+            pairs = []
+            for i in range(groups):
+                step = sign * (i + near)
+                for j in range(width):
+                    if 0 <= j + step < width:
+                        pairs.append((i * width + j, i * width + j + step))
+            got = lax.ppermute(ends, ("doc", "label"), pairs)
+            source = here - sign * (lane + near)
+            valid = (source >= 0) & (source < width)
+            source = jnp.clip(source, 0, width - 1)
+            src_first = first_id[source]
+            src_last = last_id[source]
+            parts = []
+            for target in (my_first, my_last):
+                part = jnp.where(
+                    src_first == target, got[0], jnp.where(src_last == target, got[1], 0.0)
+                )
+                parts.append(jnp.where(valid, part, 0.0))
+            extra = extra + jnp.stack(parts)
+    extra = jnp.sum(
+        lax.all_to_all(
+            jnp.broadcast_to(extra[None], (groups,) + extra.shape), "doc", 0, 0, tiled=True
+        ),
+        axis=0,
     )
+    in_first = (cluster_ids == my_first)[:, None]
+    in_last = ((cluster_ids == my_last) & (my_last != my_first))[:, None]
+    cluster_sum = local_sum + jnp.where(in_first, extra[0][None, :], 0.0)
+    cluster_sum = cluster_sum + jnp.where(in_last, extra[1][None, :], 0.0)
     centroid = unit_rows(cluster_sum)
     return lax.dot_general(
         doc_unit,

time: 107 us -> 116 us (1.084)
  between operations: 0.15 us -> 21.2 us
  blocking collectives: 20.4 us -> 0 us
  starting transfers between devices: 22.3 us -> 32.3 us
  waiting for transfers between devices: 44.2 us -> 38.4 us
  matrix products: 11.8 us -> 14.2 us
  other arithmetic: 3.15 us -> 4.73 us
    all_to_all x1 -> x0, blocking collectives: 20.4 us -> none  [shards(): lax.all_to_all(partial_value.reshape(groups, L_DEV // groups, depth), 'do...]
    ppermute x0 -> x4, starting transfers between devices: none -> 15.7 us  [shards(): got = lax.ppermute(ends, ('doc', 'label'), pairs)]
    all_to_all x1 -> x2, waiting for transfers between devices: 29.2 us -> 17.1 us  [the longest x1 15.3 us: shards(): lax.all_to_all(partial_value.reshape(groups, L_DEV // groups, depth), 'do...]
    ppermute x0 -> x4, waiting for transfers between devices: none -> 8.06 us  [shards(): got = lax.ppermute(ends, ('doc', 'label'), pairs)]
    all_to_all x1 -> x2, starting transfers between devices: 18.8 us -> 13 us  [the longest x1 8.58 us: shards(): lax.all_to_all(jnp.broadcast_to(extra[None], (groups,) + extra.shape), 'd...]
    dot_general x1 -> x0, matrix products: 2.23 us -> none  [shards(): jnp.dot(weights.astype(jnp.float32), gathered, precision=lax.Precision.HI...]
    all_to_all x1, waiting for transfers between devices: 15 us -> 13.2 us  [shards(): lax.all_to_all(jnp.broadcast_to(mine[None], (groups,) + mine.shape), 'doc...]
    dot_general x1, matrix products: 2.65 us -> 3.87 us  [shards(): lax.dot_general(doc_unit, label_rows, (((1,), (1,)), ((), ())), precision...]
  transfers between devices with their start and end apart: 2 -> 7, of which waited for: 2 -> 4; matrix products, arithmetic and copies ran while one was open for 4% -> 6% of each run, Pallas kernels for 0% -> 0%
where the time goes in v4:
time: 116 us; the launch traced here: 115 us
  waiting for transfers between devices  38.4 us (33%)
  starting transfers between devices  32.3 us (28%)
  between operations  21.2 us (18%)
  matrix products  14.2 us (12%)
  other arithmetic  4.73 us (4%)
  local copies, waits for them, and re-layouts  4.48 us (4%)
    ppermute x4, starting transfers between devices, shards(): got = lax.ppermute(ends, ('doc', 'label'), pairs)  15.7 us
    all_to_all x1, waiting for transfers between devices, shards(): lax.all_to_all(partial_value.reshape(groups, L_DEV // groups, depth), 'do...  15.3 us
    all_to_all x1, waiting for transfers between devices, shards(): lax.all_to_all(jnp.broadcast_to(mine[None], (groups,) + mine.shape), 'doc...  13.2 us
    all_to_all x1, starting transfers between devices, shards(): lax.all_to_all(jnp.broadcast_to(extra[None], (groups,) + extra.shape), 'd...  8.58 us
    ppermute x4, waiting for transfers between devices, shards(): got = lax.ppermute(ends, ('doc', 'label'), pairs)  8.06 us
    dot_general x1, matrix products, shards(): lax.dot_general(incidence, features, (((1,), (0,)), ((), ())), precision=...  4.48 us
    all_to_all x1, starting transfers between devices, shards(): lax.all_to_all(partial_value.reshape(groups, L_DEV // groups, depth), 'do...  4.47 us
    dot_general x1, matrix products, shards(): lax.dot_general(doc_unit, centroid, (((1,), (1,)), ((), ())), precision=l...  3.91 us
  transfers between devices with their start and end apart: 7, of which 4 were waited for; matrix products, arithmetic and copies ran while one was open for 6% of the time, Pallas kernels for 0%

profile of v4, /device:TPU:6, one launch (start us, length us, event | category | flops | bytes accessed | tf_op | source)
XLA Modules:
  0.0 115.3 jit_solution(10038871514347573838)
XLA Ops:
  0.0 0.8 dynamic_slice.33
  0.8 1.7 %convert_reduce_fusion = f32[256,512]{1,0:T(8,128)S(1)} fusion(s32[16,512]{1,0:T(8,128)} %bitcast.31, s32[256]{0:T(256)S(1)} %dynamic_slice.33), kind=kLoop, calls=%fused_computation | loop fusion | flops 6160384 | bytes 558080 | tf_op jit(solution)/shard_map/reduce_sum | solution.py:27
  2.5 4.5 %fusion = f32[8,32,1024]{2,1,0:T(8,128)} fusion(f32[8,32,512]{2,1,0:T(8,128)S(1)} %bitcast.26, f32[512,1024]{1,0:T(8,128)} %param.4), kind=kOutput, calls=%fused_computation.1 | convolution fusion | flops 1610612736 | bytes 3670016 | tf_op jit(solution)/shard_map/dot_general | solution.py:30
  7.0 4.5 %all-to-all-start = ((f32[8,32,1024]{2,1,0:T(8,128)}), f32[8,32,1024]{2,1,0:T(8,128)S(1)}, u32[]{:S(2)}, u32[]{:S(2)}) async-start(f32[8,32,1024]{2,1,0:T(8,128)} %fusion), calls=%async_computation | async-start | bytes 2097152 | tf_op jit(solution)/shard_map/all_to_all | solution.py:39
  11.4 0.3 reduce-window.9
  12.0 15.3 %all-to-all-done = f32[8,32,1024]{2,1,0:T(8,128)S(1)} async-done(((f32[8,32,1024]{2,1,0:T(8,128)}), f32[8,32,1024]{2,1,0:T(8,128)S(1)}, u32[]{:S(2)}, u32[]{:S(2)}) %all-to-all-start) | async-done | bytes 1048608 | tf_op jit(solution)/shard_map/all_to_all | solution.py:39
  27.7 1.1 broadcast_in_dim.81
  28.8 3.6 %all-to-all-start.1 = ((f32[8,32,1024]{2,1,0:T(8,128)}), f32[8,32,1024]{2,1,0:T(8,128)S(1)}, u32[]{:S(2)}, u32[]{:S(2)}) async-start(f32[8,32,1024]{2,1,0:T(8,128)} %broadcast_in_dim.81), calls=%async_computation.1 | async-start | bytes 2097152 | tf_op jit(solution)/shard_map/all_to_all | solution.py:43
  32.7 0.7 fusion.27
  35.0 13.2 %all-to-all-done.1 = f32[8,32,1024]{2,1,0:T(8,128)S(1)} async-done(((f32[8,32,1024]{2,1,0:T(8,128)}), f32[8,32,1024]{2,1,0:T(8,128)S(1)}, u32[]{:S(2)}, u32[]{:S(2)}) %all-to-all-start.1) | async-done | bytes 1048608 | tf_op jit(solution)/shard_map/all_to_all | solution.py:43
  48.2 1.0 copy-done.1
  49.2 1.9 %fusion.18 = f32[256,1024]{1,0:T(8,128)S(1)} fusion(f32[256,1024]{1,0:T(8,128)} %bitcast.24, s32[256]{0:T(256)S(1)} %convert_reduce_fusion.1), kind=kOutput, calls=%fused_computation.21 | convolution fusion | flops 805371904 | bytes 2098176 | tf_op jit(solution)/shard_map/dot_general | solution.py:54
  51.2 3.7 %collective-permute-start = (f32[2,1024]{1,0:T(2,128)S(1)}, f32[2,1024]{1,0:T(2,128)S(1)}, u32[]{:S(2)}, u32[]{:S(2)}) collective-permute-start(f32[2,1024]{1,0:T(2,128)S(1)} %pad_maximum_fusion), channel_id=1, source_target_pairs={{0,1},{1,2},{2,3},{3,4},{4,5},{5,6},{6,7},{7,8},{8,9},{9,10},{10,1... | collective-permute-start | bytes 24584 | tf_op jit(solution)/shard_map/ppermute | solution.py:83
  55.0 1.2 %broadcast_compare_fusion = (pred[256]{0:T(512)(128)(4,1)S(1)}, pred[256]{0:T(512)(128)(4,1)S(1)}) fusion(s32[256]{0:T(256)S(1)} %convert_reduce_fusion.1, s32[]{:T(128)} %bitcast.6, pred[]{:T(512)S(6)} %ne.3, s32[]{:T(128)} %bitcast.9), kind=kLoop, calls=%fused_computation.63 | loop fusion | flops 768 | bytes 1545 | tf_op jit(solution)/shard_map/eq | solution.py:102
  76.0 2.1 %collective-permute-start.1 = (f32[2,1024]{1,0:T(2,128)S(1)}, f32[2,1024]{1,0:T(2,128)S(1)}, u32[]{:S(2)}, u32[]{:S(2)}) collective-permute-start(f32[2,1024]{1,0:T(2,128)S(1)} %pad_maximum_fusion), channel_id=1, source_target_pairs={{1,0},{2,1},{3,2},{4,3},{5,4},{6,5},{7,6},{8,7},{9,8},{10,9},{11,1... | collective-permute-start | bytes 24584 | tf_op jit(solution)/shard_map/ppermute | solution.py:83
  78.1 8.6 %collective-permute-start.2 = (f32[2,1024]{1,0:T(2,128)S(1)}, f32[2,1024]{1,0:T(2,128)S(1)}, u32[]{:S(2)}, u32[]{:S(2)}) collective-permute-start(f32[2,1024]{1,0:T(2,128)S(1)} %pad_maximum_fusion), channel_id=1, source_target_pairs={{0,9},{1,10},{2,11},{3,12},{4,13},{5,14},{6,15},{7,16},{8,17},{9,1... | collective-permute-start | bytes 24584 | tf_op jit(solution)/shard_map/ppermute | solution.py:83
  86.6 1.3 %collective-permute-start.3 = (f32[2,1024]{1,0:T(2,128)S(1)}, f32[2,1024]{1,0:T(2,128)S(1)}, u32[]{:S(2)}, u32[]{:S(2)}) collective-permute-start(f32[2,1024]{1,0:T(2,128)S(1)} %pad_maximum_fusion), channel_id=1, source_target_pairs={{9,0},{10,1},{11,2},{12,3},{13,4},{14,5},{15,6},{16,7},{17,8},{18,... | collective-permute-start | bytes 24584 | tf_op jit(solution)/shard_map/ppermute | solution.py:83
  88.0 8.0 %collective-permute-done.3 = f32[2,1024]{1,0:T(2,128)S(1)} collective-permute-done((f32[2,1024]{1,0:T(2,128)S(1)}, f32[2,1024]{1,0:T(2,128)S(1)}, u32[]{:S(2)}, u32[]{:S(2)}) %collective-permute-start.3) | collective-permute-done | bytes 8224 | tf_op jit(solution)/shard_map/ppermute | solution.py:83
  96.1 0.6 broadcast_in_dim.84
  96.8 8.6 %all-to-all-start.2 = ((f32[8,2,1024]{2,1,0:T(2,128)}), f32[8,2,1024]{2,1,0:T(2,128)S(1)}, u32[]{:S(2)}, u32[]{:S(2)}) async-start(f32[8,2,1024]{2,1,0:T(2,128)} %broadcast_in_dim.84), calls=%async_computation.2 | async-start | bytes 131072 | tf_op jit(solution)/shard_map/all_to_all | solution.py:97
  105.4 3.9 %fusion.2 = f32[512,256]{1,0:T(8,128)} fusion(f32[256,1024]{1,0:T(8,128)} %bitcast.25, f32[512,1024]{1,0:T(8,128)S(1)} %copy-done, f32[512]{0:T(512)S(1)} %add_rsqrt_fusion), kind=kOutput, calls=%fused_computation.4 | convolution fusion | flops 1611137024 | bytes 3672064 | tf_op jit(solution)/shard_map/dot_general | solution.py:63
  109.2 1.8 %all-to-all-done.2 = f32[8,2,1024]{2,1,0:T(2,128)S(1)} async-done(((f32[8,2,1024]{2,1,0:T(2,128)}), f32[8,2,1024]{2,1,0:T(2,128)S(1)}, u32[]{:S(2)}, u32[]{:S(2)}) %all-to-all-start.2) | async-done | bytes 65568 | tf_op jit(solution)/shard_map/all_to_all | solution.py:97
  111.0 0.4 multiply_reduce_fusion.1
  111.4 3.9 %fusion.6 = f32[512,256]{1,0:T(8,128)} fusion(f32[512,256]{1,0:T(8,128)} %fusion.2, f32[512,1024]{1,0:T(8,128)S(1)} %copy-done, f32[512]{0:T(512)S(1)} %add_rsqrt_fusion, f32[256,1024]{1,0:T(8,128)S(1)} %fusion.18, f32[256]{0:T(256)S(1)} %add_rsqrt_fusion.1, f32[1024]{0:T(1024)S(1)} %bitcast.30, f32[1024]{0:T(1024)S(1)} %bitcast.28, ...), kind=kOutput, calls=%fused_computation.8 | convolution fusion | flops 1612578816 | bytes 4206080 | tf_op jit(solution)/shard_map/dot_general | solution.py:107
  (34 shorter events, 1.5 us)
Async XLA Ops:
  2.5 9.0 %copy-start.2 = (s32[512]{0:T(512)S(1)}, s32[512]{0:T(512)}, u32[]{:S(2)}) copy-start(s32[512]{0:T(512)} %param.7) | copy-start | bytes 6148
  7.0 20.4 %all-to-all-start = ((f32[8,32,1024]{2,1,0:T(8,128)}), f32[8,32,1024]{2,1,0:T(8,128)S(1)}, u32[]{:S(2)}, u32[]{:S(2)}) async-start(f32[8,32,1024]{2,1,0:T(8,128)} %fusion), calls=%async_computation | async-start | bytes 2097152 | tf_op jit(solution)/shard_map/all_to_all | solution.py:39
  27.5 7.3 %copy-start = (f32[512,1024]{1,0:T(8,128)S(1)}, f32[512,1024]{1,0:T(8,128)}, u32[]{:S(2)}) copy-start(f32[512,1024]{1,0:T(8,128)} %param.4) | copy-start | bytes 6291460
  28.8 19.4 %all-to-all-start.1 = ((f32[8,32,1024]{2,1,0:T(8,128)}), f32[8,32,1024]{2,1,0:T(8,128)S(1)}, u32[]{:S(2)}, u32[]{:S(2)}) async-start(f32[8,32,1024]{2,1,0:T(8,128)} %broadcast_in_dim.81), calls=%async_computation.1 | async-start | bytes 2097152 | tf_op jit(solution)/shard_map/all_to_all | solution.py:43
  48.2 1.0 copy-start.1
  51.2 36.7 %collective-permute-start = (f32[2,1024]{1,0:T(2,128)S(1)}, f32[2,1024]{1,0:T(2,128)S(1)}, u32[]{:S(2)}, u32[]{:S(2)}) collective-permute-start(f32[2,1024]{1,0:T(2,128)S(1)} %pad_maximum_fusion), channel_id=1, source_target_pairs={{0,1},{1,2},{2,3},{3,4},{4,5},{5,6},{6,7},{7,8},{8,9},{9,10},{10,1... | collective-permute-start | bytes 24584 | tf_op jit(solution)/shard_map/ppermute | solution.py:83
  76.0 12.0 %collective-permute-start.1 = (f32[2,1024]{1,0:T(2,128)S(1)}, f32[2,1024]{1,0:T(2,128)S(1)}, u32[]{:S(2)}, u32[]{:S(2)}) collective-permute-start(f32[2,1024]{1,0:T(2,128)S(1)} %pad_maximum_fusion), channel_id=1, source_target_pairs={{1,0},{2,1},{3,2},{4,3},{5,4},{6,5},{7,6},{8,7},{9,8},{10,9},{11,1... | collective-permute-start | bytes 24584 | tf_op jit(solution)/shard_map/ppermute | solution.py:83
  78.1 9.9 %collective-permute-start.2 = (f32[2,1024]{1,0:T(2,128)S(1)}, f32[2,1024]{1,0:T(2,128)S(1)}, u32[]{:S(2)}, u32[]{:S(2)}) collective-permute-start(f32[2,1024]{1,0:T(2,128)S(1)} %pad_maximum_fusion), channel_id=1, source_target_pairs={{0,9},{1,10},{2,11},{3,12},{4,13},{5,14},{6,15},{7,16},{8,17},{9,1... | collective-permute-start | bytes 24584 | tf_op jit(solution)/shard_map/ppermute | solution.py:83
  86.6 9.5 %collective-permute-start.3 = (f32[2,1024]{1,0:T(2,128)S(1)}, f32[2,1024]{1,0:T(2,128)S(1)}, u32[]{:S(2)}, u32[]{:S(2)}) collective-permute-start(f32[2,1024]{1,0:T(2,128)S(1)} %pad_maximum_fusion), channel_id=1, source_target_pairs={{9,0},{10,1},{11,2},{12,3},{13,4},{14,5},{15,6},{16,7},{17,8},{18,... | collective-permute-start | bytes 24584 | tf_op jit(solution)/shard_map/ppermute | solution.py:83
  96.8 14.2 %all-to-all-start.2 = ((f32[8,2,1024]{2,1,0:T(2,128)}), f32[8,2,1024]{2,1,0:T(2,128)S(1)}, u32[]{:S(2)}, u32[]{:S(2)}) async-start(f32[8,2,1024]{2,1,0:T(2,128)} %broadcast_in_dim.84), calls=%async_computation.2 | async-start | bytes 131072 | tf_op jit(solution)/shard_map/all_to_all | solution.py:97

commit v5 on v3

--- a/solution.py
+++ b/solution.py
@@ -1,7 +1,46 @@
 import jax
 import jax.numpy as jnp
 from jax import lax
+from jax.experimental import pallas as pl
+from jax.experimental.pallas import tpu as pltpu
 from jax.sharding import PartitionSpec as P
+
+def split3(x):
+    hi = x.astype(jnp.bfloat16)
+    r1 = x - hi.astype(jnp.float32)
+    mid = r1.astype(jnp.bfloat16)
+    lo = (r1 - mid.astype(jnp.float32)).astype(jnp.bfloat16)
+    return hi, mid, lo
+
+
+def pifa_kernel(here_ref, perm_ref, lab_ref, feat_ref, out_ref):
+    row = perm_ref[pl.ds(here_ref[0], 1), :]
+    lab = lab_ref[...]
+    inc_t = jnp.zeros((lab.shape[0], row.shape[1]), jnp.float32)
+    for k in range(lab.shape[1]):
+        inc_t = inc_t + (lab[:, k : k + 1] == row).astype(jnp.float32)
+    inc = inc_t.T.astype(jnp.bfloat16)
+    acc = None
+    for piece in split3(feat_ref[...]):
+        part = jnp.dot(inc, piece, preferred_element_type=jnp.float32)
+        acc = part if acc is None else acc + part
+    out_ref[...] = acc
+
+
+def pifa_partial(here, perm_blocks, doc_labels, features):
+    n_slots = perm_blocks.shape[1]
+    return pl.pallas_call(
+        pifa_kernel,
+        out_shape=jax.ShapeDtypeStruct((n_slots, features.shape[1]), jnp.float32),
+        in_specs=[
+            pl.BlockSpec(memory_space=pltpu.SMEM),
+            pl.BlockSpec(memory_space=pltpu.VMEM),
+            pl.BlockSpec(memory_space=pltpu.VMEM),
+            pl.BlockSpec(memory_space=pltpu.VMEM),
+        ],
+        out_specs=pl.BlockSpec(memory_space=pltpu.VMEM),
+    )(here, perm_blocks, doc_labels, features)
+
 
 L_DEV = 256
 
@@ -23,16 +62,8 @@
     base = here * L_DEV
     slots = jnp.arange(L_DEV, dtype=jnp.int32)
 
-    own_perm = lax.dynamic_slice_in_dim(tree_perm, base, L_DEV)
-    incidence = jnp.sum(
-        (doc_labels.T[:, None, :] == own_perm[None, :, None]).astype(jnp.float32), axis=0
-    )
-    partial_value = lax.dot_general(
-        incidence,
-        features,
-        (((1,), (0,)), ((), ())),
-        precision=lax.Precision.HIGHEST,
-        preferred_element_type=jnp.float32,
+    partial_value = pifa_partial(
+        here.astype(jnp.int32)[None], tree_perm.reshape(width, L_DEV), doc_labels, features
     )
     groups = lax.axis_size("doc")
     depth = features.shape[1]

time: 107 us -> 109 us (1.019)
  Pallas kernels: 0 us -> 5.19 us
  matrix products: 11.8 us -> 8.37 us
  local copies, waits for them, and re-layouts: 4.09 us -> 6.4 us
  other arithmetic: 3.15 us -> 1.46 us
    pallas_call x0 -> x1, Pallas kernels: none -> 5.19 us  [pifa_partial(): pl.pallas_call(pifa_kernel, out_shape=jax.ShapeDtypeStruct((n_slots, feat...]
    dot_general x1 -> x0, matrix products: 3.48 us -> none  [shards(): lax.dot_general(incidence, features, (((1,), (0,)), ((), ())), precision=...]
    reduce_sum x1 -> x0, other arithmetic: 1.69 us -> none  [shards(): jnp.sum((doc_labels.T[:, None, :] == own_perm[None, :, None]).astype(jnp....]
    unnamed x8 -> x9, local copies, waits for them, and re-layouts: 1 us -> 2.59 us
    reshape x0 -> x1, local copies, waits for them, and re-layouts: none -> 1.47 us  [shards(): tree_perm.reshape(width, L_DEV)]
where the time goes in v5:
time: 109 us
  waiting for transfers between devices  44.2 us (41%)
  starting transfers between devices  22.3 us (20%)
  blocking collectives  20.6 us (19%)
  matrix products  8.37 us (8%)
  local copies, waits for them, and re-layouts  6.4 us (6%)
  Pallas kernels  5.19 us (5%)
  other arithmetic  1.46 us (1%)
    all_to_all x1, waiting for transfers between devices, shards(): lax.all_to_all(jnp.broadcast_to(ends[None], (width,) + ends.shape), 'labe...  29.2 us
    all_to_all x1, blocking collectives, shards(): lax.all_to_all(partial_value.reshape(groups, L_DEV // groups, depth), 'do...  20.6 us
    all_to_all x1, starting transfers between devices, shards(): lax.all_to_all(jnp.broadcast_to(ends[None], (width,) + ends.shape), 'labe...  18.8 us
    all_to_all x1, waiting for transfers between devices, shards(): lax.all_to_all(jnp.broadcast_to(mine[None], (groups,) + mine.shape), 'doc...  15 us
    pallas_call x1, Pallas kernels, pifa_partial(): pl.pallas_call(pifa_kernel, out_shape=jax.ShapeDtypeStruct((n_slots, feat...  5.19 us
    all_to_all x1, starting transfers between devices, shards(): lax.all_to_all(jnp.broadcast_to(mine[None], (groups,) + mine.shape), 'doc...  3.56 us
    dot_general x1, matrix products, shards(): lax.dot_general(doc_unit, centroid, (((1,), (1,)), ((), ())), precision=l...  2.73 us
    dot_general x1, matrix products, shards(): lax.dot_general(doc_unit, label_rows, (((1,), (1,)), ((), ())), precision...  2.65 us
  transfers between devices with their start and end apart: 2, of which 2 were waited for; matrix products, arithmetic and copies ran while one was open for 4% of the time, Pallas kernels for 0%

profile of v5, /device:TPU:6, one launch (start us, length us, event | category | flops | bytes accessed | tf_op | source)
XLA Modules:
  0.0 108.6 jit_solution(1704257233736302335)
XLA Ops:
  0.0 1.5 %reshape.232.perm_ref = s32[64,256]{1,0:T(8,128)} reshape(s32[16384]{0:T(1024)} %param.6) | data formatting | bytes 131072 | tf_op jit(solution)/shard_map/reshape | solution.py:66
  1.5 1.6 %copy.9.lab_ref = s32[512,16]{1,0:T(8,128)} copy(s32[512,16]{0,1:T(8,128)} %param.5) | data formatting | bytes 65536 | tf_op args[1]
  3.1 5.2 %shard_map.46 = f32[256,1024]{1,0:T(8,128)} custom-call(s32[1]{0:T(128)} %bitcast.2.here_ref, s32[64,256]{1,0:T(8,128)} %reshape.232.perm_ref, s32[512,16]{1,0:T(8,128)} %copy.9.lab_ref, f32[512,1024]{1,0:T(8,128)} %feat_ref.1), custom_call_target="tpu_custom_call" | custom-call | tf_op jit(solution)/shard_map/pallas_call | solution.py:32
  8.3 20.6 %all_to_all.15 = f32[8,32,1024]{2,1,0:T(8,128)S(1)} all-to-all(f32[8,32,1024]{2,1,0:T(8,128)} %bitcast.14), channel_id=1, replica_groups=mesh['doc'=8,'label'=64] {'doc'}, dimensions={0} | all-to-all | bytes 2097152 | tf_op jit(solution)/shard_map/all_to_all | solution.py:70
  28.9 0.1 multiply_reduce_fusion.2
  29.0 0.1 broadcast_multiply_fusion
  29.1 1.1 %broadcast_in_dim.7 = f32[8,32,1024]{2,1,0:T(8,128)} broadcast(f32[32,1024]{1,0:T(8,128)S(1)} %broadcast_multiply_fusion), dimensions={1,2} | broadcast | bytes 1179648 | tf_op jit(solution)/shard_map/broadcast_in_dim | solution.py:75
  30.2 3.6 %all-to-all-start.1 = ((f32[8,32,1024]{2,1,0:T(8,128)}), f32[8,32,1024]{2,1,0:T(8,128)S(1)}, u32[]{:S(2)}, u32[]{:S(2)}) async-start(f32[8,32,1024]{2,1,0:T(8,128)} %broadcast_in_dim.7), calls=%async_computation.1 | async-start | bytes 2097152 | tf_op jit(solution)/shard_map/all_to_all | solution.py:74
  33.8 0.3 reduce-window.9
  34.1 0.1 slice.18
  34.2 0.1 slice_reduce_fusion
  34.5 0.2 convert_reduce_fusion
  34.7 15.0 %all-to-all-done.1 = f32[8,32,1024]{2,1,0:T(8,128)S(1)} async-done(((f32[8,32,1024]{2,1,0:T(8,128)}), f32[8,32,1024]{2,1,0:T(8,128)S(1)}, u32[]{:S(2)}, u32[]{:S(2)}) %all-to-all-start.1) | async-done | bytes 1048608 | tf_op jit(solution)/shard_map/all_to_all | solution.py:74
  49.7 0.7 fusion.13
  50.4 1.0 copy-done.1
  51.4 0.9 broadcast_in_dim.8
  52.4 18.8 %all-to-all-start.2 = ((f32[64,2,1024]{2,1,0:T(2,128)}), f32[64,2,1024]{2,1,0:T(2,128)}, u32[]{:S(2)}, u32[]{:S(2)}) async-start(f32[64,2,1024]{2,1,0:T(2,128)} %broadcast_in_dim.8), calls=%async_computation.2 | async-start | bytes 1048576 | tf_op jit(solution)/shard_map/all_to_all | solution.py:92
  71.1 0.2 convert_reduce_fusion.2
  71.4 0.2 multiply_reduce_fusion
  71.6 0.1 compare_and_fusion
  71.7 2.6 %fusion = f32[512,256]{1,0:T(8,128)} fusion(f32[256,1024]{1,0:T(8,128)S(1)} %bitcast.13, f32[512,1024]{1,0:T(8,128)S(1)} %copy-done, f32[512]{0:T(512)S(1)} %add_rsqrt_fusion), kind=kOutput, calls=%fused_computation.1 | convolution fusion | flops 1611137024 | bytes 3672064 | tf_op jit(solution)/shard_map/dot_general | solution.py:97
  74.4 29.2 %all-to-all-done.2 = f32[64,2,1024]{2,1,0:T(2,128)} async-done(((f32[64,2,1024]{2,1,0:T(2,128)}), f32[64,2,1024]{2,1,0:T(2,128)}, u32[]{:S(2)}, u32[]{:S(2)}) %all-to-all-start.2) | async-done | bytes 524320 | tf_op jit(solution)/shard_map/all_to_all | solution.py:92
  103.6 2.3 %multiply_reduce_fusion.1 = (f32[256]{0:T(256)S(1)}, f32[256,1024]{1,0:T(8,128)S(1)}) fusion(f32[256,1024]{1,0:T(8,128)} %copy-done.1, f32[64,2,1024]{2,1,0:T(2,128)} %all-to-all-done.2, pred[256,64,1]{0,1,2:T(32,128)(4,1)S(1)} %get-tuple-element.10, pred[256,64,1]{0,1,2:T(32,128)(4,1)S(1)} %get-tuple-element.9), kind=kOutput, calls=%fused_computation.9 | convolution fusion | flops 403472128 | bytes 2655232 | tf_op jit(solution)/shard_map/dot_general | solution.py:108
  105.9 2.7 %fusion.5 = f32[512,256]{1,0:T(8,128)} fusion(f32[512,256]{1,0:T(8,128)S(1)} %copy-done.2, f32[512,1024]{1,0:T(8,128)S(1)} %copy-done, f32[256,1024]{1,0:T(8,128)S(1)} %get-tuple-element.12, f32[512]{0:T(512)S(1)} %add_rsqrt_fusion, f32[256]{0:T(256)S(1)} %add_rsqrt_fusion.1), kind=kOutput, calls=%fused_computation.7 | convolution fusion | flops 1611530240 | bytes 4197376 | tf_op jit(solution)/shard_map/dot_general | solution.py:115
  (20 shorter events, 0.3 us)
Async XLA Ops:
  28.9 4.9 %copy-start.3 = (s32[512]{0:T(512)S(1)}, s32[512]{0:T(512)}, u32[]{:S(2)}) copy-start(s32[512]{0:T(512)} %param.7) | copy-start | bytes 6148
  30.2 19.4 %all-to-all-start.1 = ((f32[8,32,1024]{2,1,0:T(8,128)}), f32[8,32,1024]{2,1,0:T(8,128)S(1)}, u32[]{:S(2)}, u32[]{:S(2)}) async-start(f32[8,32,1024]{2,1,0:T(8,128)} %broadcast_in_dim.7), calls=%async_computation.1 | async-start | bytes 2097152 | tf_op jit(solution)/shard_map/all_to_all | solution.py:74
  33.8 37.6 %copy-start = (f32[512,1024]{1,0:T(8,128)S(1)}, f32[512,1024]{1,0:T(8,128)}, u32[]{:S(2)}) copy-start(f32[512,1024]{1,0:T(8,128)} %feat_ref.1) | copy-start | bytes 6291460
  50.4 1.0 copy-start.1
  52.4 51.2 %all-to-all-start.2 = ((f32[64,2,1024]{2,1,0:T(2,128)}), f32[64,2,1024]{2,1,0:T(2,128)}, u32[]{:S(2)}, u32[]{:S(2)}) async-start(f32[64,2,1024]{2,1,0:T(2,128)} %broadcast_in_dim.8), calls=%async_computation.2 | async-start | bytes 1048576 | tf_op jit(solution)/shard_map/all_to_all | solution.py:92
  103.6 2.3 %copy-start.2 = (f32[512,256]{1,0:T(8,128)S(1)}, f32[512,256]{1,0:T(8,128)}, u32[]{:S(2)}) copy-start(f32[512,256]{1,0:T(8,128)} %fusion) | copy-start | bytes 1572868

commit v6 on v5

--- a/solution.py
+++ b/solution.py
@@ -13,33 +13,26 @@
     return hi, mid, lo
 
 
-def pifa_kernel(here_ref, perm_ref, lab_ref, feat_ref, out_ref):
-    row = perm_ref[pl.ds(here_ref[0], 1), :]
+def pifa_kernel(perm_ref, lab_ref, feat_ref, out_ref):
+    column = perm_ref[...]
     lab = lab_ref[...]
-    inc_t = jnp.zeros((lab.shape[0], row.shape[1]), jnp.float32)
-    for k in range(lab.shape[1]):
-        inc_t = inc_t + (lab[:, k : k + 1] == row).astype(jnp.float32)
-    inc = inc_t.T.astype(jnp.bfloat16)
+    inc = jnp.zeros((column.shape[0], lab.shape[1]), jnp.int32)
+    for k in range(lab.shape[0]):
+        inc = inc + (column == lab[k : k + 1, :]).astype(jnp.int32)
+    inc = inc.astype(jnp.float32).astype(jnp.bfloat16)
     acc = None
     for piece in split3(feat_ref[...]):
         part = jnp.dot(inc, piece, preferred_element_type=jnp.float32)
         acc = part if acc is None else acc + part
     out_ref[...] = acc
 
-
-def pifa_partial(here, perm_blocks, doc_labels, features):
-    n_slots = perm_blocks.shape[1]
+def pifa_partial(own_perm, doc_labels, features):
     return pl.pallas_call(
         pifa_kernel,
-        out_shape=jax.ShapeDtypeStruct((n_slots, features.shape[1]), jnp.float32),
-        in_specs=[
-            pl.BlockSpec(memory_space=pltpu.SMEM),
-            pl.BlockSpec(memory_space=pltpu.VMEM),
-            pl.BlockSpec(memory_space=pltpu.VMEM),
-            pl.BlockSpec(memory_space=pltpu.VMEM),
-        ],
+        out_shape=jax.ShapeDtypeStruct((own_perm.shape[0], features.shape[1]), jnp.float32),
+        in_specs=[pl.BlockSpec(memory_space=pltpu.VMEM)] * 3,
         out_specs=pl.BlockSpec(memory_space=pltpu.VMEM),
-    )(here, perm_blocks, doc_labels, features)
+    )(own_perm[:, None], doc_labels.T, features)
 
 
 L_DEV = 256
@@ -62,9 +55,8 @@
     base = here * L_DEV
     slots = jnp.arange(L_DEV, dtype=jnp.int32)
 
-    partial_value = pifa_partial(
-        here.astype(jnp.int32)[None], tree_perm.reshape(width, L_DEV), doc_labels, features
-    )
+    own_perm = lax.dynamic_slice_in_dim(tree_perm, base, L_DEV)
+    partial_value = pifa_partial(own_perm, doc_labels, features)
     groups = lax.axis_size("doc")
     depth = features.shape[1]
     pieces = lax.all_to_all(

time: 109 us -> 107 us (0.982)
  local copies, waits for them, and re-layouts: 6.4 us -> 4.89 us
    unnamed x9 -> x8, local copies, waits for them, and re-layouts: 2.59 us -> 1 us
    reshape x1 -> x0, local copies, waits for them, and re-layouts: 1.47 us -> none  [shards(): tree_perm.reshape(width, L_DEV)]
where the time goes in v6:
time: 107 us; the launch traced here: 106 us
  waiting for transfers between devices  44.2 us (41%)
  starting transfers between devices  22.3 us (21%)
  blocking collectives  20.6 us (19%)
  matrix products  8.31 us (8%)
  local copies, waits for them, and re-layouts  4.89 us (5%)
  Pallas kernels  4.54 us (4%)
  other arithmetic  1.46 us (1%)
    all_to_all x1, waiting for transfers between devices, shards(): lax.all_to_all(jnp.broadcast_to(ends[None], (width,) + ends.shape), 'labe...  29.2 us
    all_to_all x1, blocking collectives, shards(): lax.all_to_all(partial_value.reshape(groups, L_DEV // groups, depth), 'do...  20.6 us
    all_to_all x1, starting transfers between devices, shards(): lax.all_to_all(jnp.broadcast_to(ends[None], (width,) + ends.shape), 'labe...  18.8 us
    all_to_all x1, waiting for transfers between devices, shards(): lax.all_to_all(jnp.broadcast_to(mine[None], (groups,) + mine.shape), 'doc...  15 us
    pallas_call x1, Pallas kernels, pifa_partial(): pl.pallas_call(pifa_kernel, out_shape=jax.ShapeDtypeStruct((own_perm.shap...  4.54 us
    all_to_all x1, starting transfers between devices, shards(): lax.all_to_all(jnp.broadcast_to(mine[None], (groups,) + mine.shape), 'doc...  3.56 us
    dot_general x1, matrix products, shards(): lax.dot_general(doc_unit, centroid, (((1,), (1,)), ((), ())), precision=l...  2.73 us
    dot_general x1, matrix products, shards(): lax.dot_general(doc_unit, label_rows, (((1,), (1,)), ((), ())), precision...  2.65 us
  transfers between devices with their start and end apart: 2, of which 2 were waited for; matrix products, arithmetic and copies ran while one was open for 4% of the time, Pallas kernels for 0%

profile of v6, /device:TPU:6, one launch (start us, length us, event | category | flops | bytes accessed | tf_op | source)
XLA Modules:
  0.0 106.4 jit_solution(11008886646478449472)
XLA Ops:
  0.0 0.8 dynamic_slice.3
  0.8 0.8 copy.8.perm_ref
  1.6 4.5 %shard_map.46 = f32[256,1024]{1,0:T(8,128)} custom-call(s32[256,1]{1,0:T(8,128)} %copy.8.perm_ref, s32[16,512]{1,0:T(8,128)} %bitcast.16, f32[512,1024]{1,0:T(8,128)} %feat_ref.1), custom_call_target="tpu_custom_call" | custom-call | tf_op jit(solution)/shard_map/pallas_call | solution.py:30
  6.1 20.6 %all_to_all.15 = f32[8,32,1024]{2,1,0:T(8,128)S(1)} all-to-all(f32[8,32,1024]{2,1,0:T(8,128)} %bitcast.15), channel_id=1, replica_groups=mesh['doc'=8,'label'=64] {'doc'}, dimensions={0} | all-to-all | bytes 2097152 | tf_op jit(solution)/shard_map/all_to_all | solution.py:62
  26.7 0.1 multiply_reduce_fusion.2
  26.9 0.1 broadcast_multiply_fusion
  27.0 1.1 %broadcast_in_dim.7 = f32[8,32,1024]{2,1,0:T(8,128)} broadcast(f32[32,1024]{1,0:T(8,128)S(1)} %broadcast_multiply_fusion), dimensions={1,2} | broadcast | bytes 1179648 | tf_op jit(solution)/shard_map/broadcast_in_dim | solution.py:67
  28.1 3.6 %all-to-all-start.1 = ((f32[8,32,1024]{2,1,0:T(8,128)}), f32[8,32,1024]{2,1,0:T(8,128)S(1)}, u32[]{:S(2)}, u32[]{:S(2)}) async-start(f32[8,32,1024]{2,1,0:T(8,128)} %broadcast_in_dim.7), calls=%async_computation.1 | async-start | bytes 2097152 | tf_op jit(solution)/shard_map/all_to_all | solution.py:66
  31.6 0.3 reduce-window.9
  32.0 0.1 slice.18
  32.1 0.1 slice_reduce_fusion
  32.3 0.2 convert_reduce_fusion
  32.5 15.0 %all-to-all-done.1 = f32[8,32,1024]{2,1,0:T(8,128)S(1)} async-done(((f32[8,32,1024]{2,1,0:T(8,128)}), f32[8,32,1024]{2,1,0:T(8,128)S(1)}, u32[]{:S(2)}, u32[]{:S(2)}) %all-to-all-start.1) | async-done | bytes 1048608 | tf_op jit(solution)/shard_map/all_to_all | solution.py:66
  47.5 0.7 fusion.13
  48.2 1.0 copy-done.1
  49.2 0.9 broadcast_in_dim.8
  50.2 18.8 %all-to-all-start.2 = ((f32[64,2,1024]{2,1,0:T(2,128)}), f32[64,2,1024]{2,1,0:T(2,128)}, u32[]{:S(2)}, u32[]{:S(2)}) async-start(f32[64,2,1024]{2,1,0:T(2,128)} %broadcast_in_dim.8), calls=%async_computation.2 | async-start | bytes 1048576 | tf_op jit(solution)/shard_map/all_to_all | solution.py:84
  69.0 0.2 convert_reduce_fusion.2
  69.2 0.2 multiply_reduce_fusion
  69.4 0.1 compare_and_fusion
  69.6 2.6 %fusion = f32[512,256]{1,0:T(8,128)} fusion(f32[256,1024]{1,0:T(8,128)S(1)} %bitcast.14, f32[512,1024]{1,0:T(8,128)S(1)} %copy-done, f32[512]{0:T(512)S(1)} %add_rsqrt_fusion), kind=kOutput, calls=%fused_computation.1 | convolution fusion | flops 1611137024 | bytes 3672064 | tf_op jit(solution)/shard_map/dot_general | solution.py:89
  72.2 29.2 %all-to-all-done.2 = f32[64,2,1024]{2,1,0:T(2,128)} async-done(((f32[64,2,1024]{2,1,0:T(2,128)}), f32[64,2,1024]{2,1,0:T(2,128)}, u32[]{:S(2)}, u32[]{:S(2)}) %all-to-all-start.2) | async-done | bytes 524320 | tf_op jit(solution)/shard_map/all_to_all | solution.py:84
  101.4 2.2 %multiply_reduce_fusion.1 = (f32[256]{0:T(256)S(1)}, f32[256,1024]{1,0:T(8,128)S(1)}) fusion(f32[256,1024]{1,0:T(8,128)} %copy-done.1, f32[64,2,1024]{2,1,0:T(2,128)} %all-to-all-done.2, pred[256,64,1]{0,1,2:T(32,128)(4,1)S(1)} %get-tuple-element.10, pred[256,64,1]{0,1,2:T(32,128)(4,1)S(1)} %get-tuple-element.9), kind=kOutput, calls=%fused_computation.9 | convolution fusion | flops 403472128 | bytes 2655232 | tf_op jit(solution)/shard_map/dot_general | solution.py:100
  103.7 2.7 %fusion.5 = f32[512,256]{1,0:T(8,128)} fusion(f32[512,256]{1,0:T(8,128)S(1)} %copy-done.2, f32[512,1024]{1,0:T(8,128)S(1)} %copy-done, f32[256,1024]{1,0:T(8,128)S(1)} %get-tuple-element.12, f32[512]{0:T(512)S(1)} %add_rsqrt_fusion, f32[256]{0:T(256)S(1)} %add_rsqrt_fusion.1), kind=kOutput, calls=%fused_computation.7 | convolution fusion | flops 1611530240 | bytes 4197376 | tf_op jit(solution)/shard_map/dot_general | solution.py:107
  (20 shorter events, 0.3 us)
Async XLA Ops:
  26.7 4.9 %copy-start.3 = (s32[512]{0:T(512)S(1)}, s32[512]{0:T(512)}, u32[]{:S(2)}) copy-start(s32[512]{0:T(512)} %param.7) | copy-start | bytes 6148
  28.1 19.4 %all-to-all-start.1 = ((f32[8,32,1024]{2,1,0:T(8,128)}), f32[8,32,1024]{2,1,0:T(8,128)S(1)}, u32[]{:S(2)}, u32[]{:S(2)}) async-start(f32[8,32,1024]{2,1,0:T(8,128)} %broadcast_in_dim.7), calls=%async_computation.1 | async-start | bytes 2097152 | tf_op jit(solution)/shard_map/all_to_all | solution.py:66
  31.6 37.6 %copy-start = (f32[512,1024]{1,0:T(8,128)S(1)}, f32[512,1024]{1,0:T(8,128)}, u32[]{:S(2)}) copy-start(f32[512,1024]{1,0:T(8,128)} %feat_ref.1) | copy-start | bytes 6291460
  48.2 1.0 copy-start.1
  50.2 51.2 %all-to-all-start.2 = ((f32[64,2,1024]{2,1,0:T(2,128)}), f32[64,2,1024]{2,1,0:T(2,128)}, u32[]{:S(2)}, u32[]{:S(2)}) async-start(f32[64,2,1024]{2,1,0:T(2,128)} %broadcast_in_dim.8), calls=%async_computation.2 | async-start | bytes 1048576 | tf_op jit(solution)/shard_map/all_to_all | solution.py:84
  72.2 31.5 %copy-start.2 = (f32[512,256]{1,0:T(8,128)S(1)}, f32[512,256]{1,0:T(8,128)}, u32[]{:S(2)}) copy-start(f32[512,256]{1,0:T(8,128)} %fusion) | copy-start | bytes 1572868

commit v7 on v6

--- a/solution.py
+++ b/solution.py
@@ -13,27 +13,39 @@
     return hi, mid, lo
 
 
-def pifa_kernel(perm_ref, lab_ref, feat_ref, out_ref):
-    column = perm_ref[...]
-    lab = lab_ref[...]
-    inc = jnp.zeros((column.shape[0], lab.shape[1]), jnp.int32)
-    for k in range(lab.shape[0]):
-        inc = inc + (column == lab[k : k + 1, :]).astype(jnp.int32)
-    inc = inc.astype(jnp.float32).astype(jnp.bfloat16)
+def pifa_kernel(perm_ref, lab_ref, feat_ref, out_ref, inc_ref):
+    @pl.when(pl.program_id(0) == 0)
+    def _():
+        column = perm_ref[...]
+        lab = lab_ref[...]
+        inc = jnp.zeros((column.shape[0], lab.shape[1]), jnp.int32)
+        for k in range(lab.shape[0]):
+            inc = inc + (column == lab[k : k + 1, :]).astype(jnp.int32)
+        inc_ref[...] = inc.astype(jnp.float32).astype(jnp.bfloat16)
+
+    inc = inc_ref[...]
     acc = None
     for piece in split3(feat_ref[...]):
         part = jnp.dot(inc, piece, preferred_element_type=jnp.float32)
         acc = part if acc is None else acc + part
     out_ref[...] = acc
 
-def pifa_partial(own_perm, doc_labels, features):
+
+def pifa_partial(own_perm, doc_labels, features, block=256):
+    slots = own_perm.shape[0]
+    docs, depth = features.shape
     return pl.pallas_call(
         pifa_kernel,
-        out_shape=jax.ShapeDtypeStruct((own_perm.shape[0], features.shape[1]), jnp.float32),
-        in_specs=[pl.BlockSpec(memory_space=pltpu.VMEM)] * 3,
-        out_specs=pl.BlockSpec(memory_space=pltpu.VMEM),
+        out_shape=jax.ShapeDtypeStruct((slots, depth), jnp.float32),
+        grid=(depth // block,),
+        in_specs=[
+            pl.BlockSpec((slots, 1), lambda c: (0, 0)),
+            pl.BlockSpec((doc_labels.shape[1], docs), lambda c: (0, 0)),
+            pl.BlockSpec((docs, block), lambda c: (0, c)),
+        ],
+        out_specs=pl.BlockSpec((slots, block), lambda c: (0, c)),
+        scratch_shapes=[pltpu.VMEM((slots, docs), jnp.bfloat16)],
     )(own_perm[:, None], doc_labels.T, features)
-
 
 L_DEV = 256
 

time: 107 us -> 108 us (level)
  no operation moved by 1% of the time
where the time goes in v7:
time: 108 us; the launch traced here: 107 us
  waiting for transfers between devices  44.2 us (41%)
  starting transfers between devices  22.3 us (21%)
  blocking collectives  20.6 us (19%)
  matrix products  8.32 us (8%)
  Pallas kernels  5.32 us (5%)
  local copies, waits for them, and re-layouts  4.89 us (5%)
  other arithmetic  1.46 us (1%)
    all_to_all x1, waiting for transfers between devices, shards(): lax.all_to_all(jnp.broadcast_to(ends[None], (width,) + ends.shape), 'labe...  29.2 us
    all_to_all x1, blocking collectives, shards(): lax.all_to_all(partial_value.reshape(groups, L_DEV // groups, depth), 'do...  20.6 us
    all_to_all x1, starting transfers between devices, shards(): lax.all_to_all(jnp.broadcast_to(ends[None], (width,) + ends.shape), 'labe...  18.8 us
    all_to_all x1, waiting for transfers between devices, shards(): lax.all_to_all(jnp.broadcast_to(mine[None], (groups,) + mine.shape), 'doc...  15 us
    pallas_call x1, Pallas kernels, pifa_partial(): pl.pallas_call(pifa_kernel, out_shape=jax.ShapeDtypeStruct((slots, depth)...  5.32 us
    all_to_all x1, starting transfers between devices, shards(): lax.all_to_all(jnp.broadcast_to(mine[None], (groups,) + mine.shape), 'doc...  3.56 us
    dot_general x1, matrix products, shards(): lax.dot_general(doc_unit, centroid, (((1,), (1,)), ((), ())), precision=l...  2.73 us
    dot_general x1, matrix products, shards(): lax.dot_general(doc_unit, label_rows, (((1,), (1,)), ((), ())), precision...  2.65 us
  transfers between devices with their start and end apart: 2, of which 2 were waited for; matrix products, arithmetic and copies ran while one was open for 4% of the time, Pallas kernels for 0%

profile of v7, /device:TPU:6, one launch (start us, length us, event | category | flops | bytes accessed | tf_op | source)
XLA Modules:
  0.0 107.2 jit_solution(2537824230308839306)
XLA Ops:
  0.0 0.8 dynamic_slice.3
  0.8 0.8 copy.8.perm_ref
  1.6 5.3 %shard_map.46 = f32[256,1024]{1,0:T(8,128)} custom-call(s32[256,1]{1,0:T(8,128)} %copy.8.perm_ref, s32[16,512]{1,0:T(8,128)} %bitcast.16, f32[512,1024]{1,0:T(8,128)} %feat_ref.1), custom_call_target="tpu_custom_call" | custom-call | tf_op jit(solution)/shard_map/pallas_call | solution.py:37
  6.9 20.6 %all_to_all.15 = f32[8,32,1024]{2,1,0:T(8,128)S(1)} all-to-all(f32[8,32,1024]{2,1,0:T(8,128)} %bitcast.15), channel_id=1, replica_groups=mesh['doc'=8,'label'=64] {'doc'}, dimensions={0} | all-to-all | bytes 2097152 | tf_op jit(solution)/shard_map/all_to_all | solution.py:74
  27.5 0.1 multiply_reduce_fusion.2
  27.7 0.1 broadcast_multiply_fusion
  27.8 1.1 %broadcast_in_dim.7 = f32[8,32,1024]{2,1,0:T(8,128)} broadcast(f32[32,1024]{1,0:T(8,128)S(1)} %broadcast_multiply_fusion), dimensions={1,2} | broadcast | bytes 1179648 | tf_op jit(solution)/shard_map/broadcast_in_dim | solution.py:79
  28.9 3.6 %all-to-all-start.1 = ((f32[8,32,1024]{2,1,0:T(8,128)}), f32[8,32,1024]{2,1,0:T(8,128)S(1)}, u32[]{:S(2)}, u32[]{:S(2)}) async-start(f32[8,32,1024]{2,1,0:T(8,128)} %broadcast_in_dim.7), calls=%async_computation.1 | async-start | bytes 2097152 | tf_op jit(solution)/shard_map/all_to_all | solution.py:78
  32.4 0.3 reduce-window.9
  32.8 0.1 slice.18
  32.9 0.1 slice_reduce_fusion
  33.1 0.2 convert_reduce_fusion
  33.3 15.0 %all-to-all-done.1 = f32[8,32,1024]{2,1,0:T(8,128)S(1)} async-done(((f32[8,32,1024]{2,1,0:T(8,128)}), f32[8,32,1024]{2,1,0:T(8,128)S(1)}, u32[]{:S(2)}, u32[]{:S(2)}) %all-to-all-start.1) | async-done | bytes 1048608 | tf_op jit(solution)/shard_map/all_to_all | solution.py:78
  48.3 0.7 fusion.13
  49.0 1.0 copy-done.1
  50.0 0.9 broadcast_in_dim.8
  51.0 18.8 %all-to-all-start.2 = ((f32[64,2,1024]{2,1,0:T(2,128)}), f32[64,2,1024]{2,1,0:T(2,128)}, u32[]{:S(2)}, u32[]{:S(2)}) async-start(f32[64,2,1024]{2,1,0:T(2,128)} %broadcast_in_dim.8), calls=%async_computation.2 | async-start | bytes 1048576 | tf_op jit(solution)/shard_map/all_to_all | solution.py:96
  69.8 0.2 convert_reduce_fusion.2
  70.0 0.2 multiply_reduce_fusion
  70.2 0.1 compare_and_fusion
  70.4 2.6 %fusion = f32[512,256]{1,0:T(8,128)} fusion(f32[256,1024]{1,0:T(8,128)S(1)} %bitcast.14, f32[512,1024]{1,0:T(8,128)S(1)} %copy-done, f32[512]{0:T(512)S(1)} %add_rsqrt_fusion), kind=kOutput, calls=%fused_computation.1 | convolution fusion | flops 1611137024 | bytes 3672064 | tf_op jit(solution)/shard_map/dot_general | solution.py:101
  73.0 29.2 %all-to-all-done.2 = f32[64,2,1024]{2,1,0:T(2,128)} async-done(((f32[64,2,1024]{2,1,0:T(2,128)}), f32[64,2,1024]{2,1,0:T(2,128)}, u32[]{:S(2)}, u32[]{:S(2)}) %all-to-all-start.2) | async-done | bytes 524320 | tf_op jit(solution)/shard_map/all_to_all | solution.py:96
  102.2 2.2 %multiply_reduce_fusion.1 = (f32[256]{0:T(256)S(1)}, f32[256,1024]{1,0:T(8,128)S(1)}) fusion(f32[256,1024]{1,0:T(8,128)} %copy-done.1, f32[64,2,1024]{2,1,0:T(2,128)} %all-to-all-done.2, pred[256,64,1]{0,1,2:T(32,128)(4,1)S(1)} %get-tuple-element.10, pred[256,64,1]{0,1,2:T(32,128)(4,1)S(1)} %get-tuple-element.9), kind=kOutput, calls=%fused_computation.9 | convolution fusion | flops 403472128 | bytes 2655232 | tf_op jit(solution)/shard_map/dot_general | solution.py:112
  104.5 2.7 %fusion.5 = f32[512,256]{1,0:T(8,128)} fusion(f32[512,256]{1,0:T(8,128)S(1)} %copy-done.2, f32[512,1024]{1,0:T(8,128)S(1)} %copy-done, f32[256,1024]{1,0:T(8,128)S(1)} %get-tuple-element.12, f32[512]{0:T(512)S(1)} %add_rsqrt_fusion, f32[256]{0:T(256)S(1)} %add_rsqrt_fusion.1), kind=kOutput, calls=%fused_computation.7 | convolution fusion | flops 1611530240 | bytes 4197376 | tf_op jit(solution)/shard_map/dot_general | solution.py:119
  (20 shorter events, 0.3 us)
Async XLA Ops:
  27.5 4.9 %copy-start.3 = (s32[512]{0:T(512)S(1)}, s32[512]{0:T(512)}, u32[]{:S(2)}) copy-start(s32[512]{0:T(512)} %param.7) | copy-start | bytes 6148
  28.9 19.4 %all-to-all-start.1 = ((f32[8,32,1024]{2,1,0:T(8,128)}), f32[8,32,1024]{2,1,0:T(8,128)S(1)}, u32[]{:S(2)}, u32[]{:S(2)}) async-start(f32[8,32,1024]{2,1,0:T(8,128)} %broadcast_in_dim.7), calls=%async_computation.1 | async-start | bytes 2097152 | tf_op jit(solution)/shard_map/all_to_all | solution.py:78
  32.4 37.6 %copy-start = (f32[512,1024]{1,0:T(8,128)S(1)}, f32[512,1024]{1,0:T(8,128)}, u32[]{:S(2)}) copy-start(f32[512,1024]{1,0:T(8,128)} %feat_ref.1) | copy-start | bytes 6291460
  49.0 1.0 copy-start.1
  51.0 51.2 %all-to-all-start.2 = ((f32[64,2,1024]{2,1,0:T(2,128)}), f32[64,2,1024]{2,1,0:T(2,128)}, u32[]{:S(2)}, u32[]{:S(2)}) async-start(f32[64,2,1024]{2,1,0:T(2,128)} %broadcast_in_dim.8), calls=%async_computation.2 | async-start | bytes 1048576 | tf_op jit(solution)/shard_map/all_to_all | solution.py:96
  73.0 31.4 %copy-start.2 = (f32[512,256]{1,0:T(8,128)S(1)}, f32[512,256]{1,0:T(8,128)}, u32[]{:S(2)}) copy-start(f32[512,256]{1,0:T(8,128)} %fusion) | copy-start | bytes 1572868

commit v8 on v7

--- a/solution.py
+++ b/solution.py
@@ -97,32 +97,38 @@
         jnp.broadcast_to(ends[None], (width,) + ends.shape), "label", 0, 0, tiled=True
     ).reshape(2 * width, -1)
 
+    other = (shard != here)[None, :]
+    take_first = (first_id[None, :] == cluster_ids[:, None]) & other
+    take_last = (last_id[None, :] == cluster_ids[:, None]) & (first_id != last_id)[None, :] & other
+    weights = jnp.stack([take_first, take_last], axis=2).reshape(L_DEV, 2 * width)
     doc_unit = unit_rows(features)
-    row_scores = lax.dot_general(
+    both = lax.dot_general(
         doc_unit,
-        label_rows,
+        jnp.concatenate([label_rows, local_sum]),
         (((1,), (1,)), ((), ())),
         precision=lax.Precision.HIGHEST,
         preferred_element_type=jnp.float32,
     )
-    other = (shard != here)[None, :]
-    take_first = (first_id[None, :] == cluster_ids[:, None]) & other
-    take_last = (last_id[None, :] == cluster_ids[:, None]) & (first_id != last_id)[None, :] & other
-    weights = jnp.stack([take_first, take_last], axis=2).reshape(L_DEV, 2 * width)
+    row_scores = both[:, :L_DEV]
+    near_scores = both[:, L_DEV:]
+    weights = weights.astype(jnp.float32)
     cluster_sum = local_sum + jnp.dot(
-        weights.astype(jnp.float32),
-        gathered,
+        weights, gathered, precision=lax.Precision.HIGHEST, preferred_element_type=jnp.float32
+    )
+    scale = lax.rsqrt(jnp.sum(cluster_sum * cluster_sum, axis=1) + EPS)
+    far_scores = jnp.dot(
+        lax.dot_general(
+            doc_unit,
+            gathered,
+            (((1,), (1,)), ((), ())),
+            precision=lax.Precision.HIGHEST,
+            preferred_element_type=jnp.float32,
+        ),
+        weights.T,
         precision=lax.Precision.HIGHEST,
         preferred_element_type=jnp.float32,
     )
-    centroid = unit_rows(cluster_sum)
-    return lax.dot_general(
-        doc_unit,
-        centroid,
-        (((1,), (1,)), ((), ())),
-        precision=lax.Precision.HIGHEST,
-        preferred_element_type=jnp.float32,
-    ) + row_scores
+    return row_scores + (near_scores + far_scores) * scale[None, :]
 
 
 def solution(mesh):

time: 108 us -> 112 us (1.037)
  matrix products: 8.32 us -> 12.5 us
  local copies, waits for them, and re-layouts: 4.89 us -> 8.22 us
  waiting for transfers between devices: 44.2 us -> 41 us
    all_to_all x1, waiting for transfers between devices: 29.2 us -> 26.1 us  [shards(): lax.all_to_all(jnp.broadcast_to(ends[None], (width,) + ends.shape), 'labe...]
    dot_general x3 -> x4, matrix products: 7.61 us -> 10.6 us  [the longest x1 4.59 us: shards(): lax.dot_general(doc_unit, jnp.concatenate([label_rows, local_sum]), (((1,...]
    reshape x0 -> x2, local copies, waits for them, and re-layouts: none -> 2.27 us  [the longest x1 2.19 us: shards(): gathered = lax.all_to_all(jnp.broadcast_to(ends[None], (width,) + ends.sh...]
    dot_general x1, matrix products: 0.71 us -> 1.92 us  [shards(): jnp.dot(same_cluster, label_rows, precision=lax.Precision.HIGHEST, prefer...]
  transfers between devices with their start and end apart: 2 -> 2, of which waited for: 2 -> 2; matrix products, arithmetic and copies ran while one was open for 4% -> 6% of each run, Pallas kernels for 0% -> 0%
where the time goes in v8:
time: 112 us
  waiting for transfers between devices  41 us (37%)
  starting transfers between devices  22.3 us (20%)
  blocking collectives  20.6 us (18%)
  matrix products  12.5 us (11%)
  local copies, waits for them, and re-layouts  8.22 us (7%)
  Pallas kernels  5.32 us (5%)
  other arithmetic  1.47 us (1%)
    all_to_all x1, waiting for transfers between devices, shards(): lax.all_to_all(jnp.broadcast_to(ends[None], (width,) + ends.shape), 'labe...  26.1 us
    all_to_all x1, blocking collectives, shards(): lax.all_to_all(partial_value.reshape(groups, L_DEV // groups, depth), 'do...  20.6 us
    all_to_all x1, starting transfers between devices, shards(): lax.all_to_all(jnp.broadcast_to(ends[None], (width,) + ends.shape), 'labe...  18.8 us
    all_to_all x1, waiting for transfers between devices, shards(): lax.all_to_all(jnp.broadcast_to(mine[None], (groups,) + mine.shape), 'doc...  15 us
    pallas_call x1, Pallas kernels, pifa_partial(): pl.pallas_call(pifa_kernel, out_shape=jax.ShapeDtypeStruct((slots, depth)...  5.32 us
    dot_general x1, matrix products, shards(): lax.dot_general(doc_unit, jnp.concatenate([label_rows, local_sum]), (((1,...  4.59 us
    all_to_all x1, starting transfers between devices, shards(): lax.all_to_all(jnp.broadcast_to(mine[None], (groups,) + mine.shape), 'doc...  3.56 us
    dot_general x1, matrix products, shards(): lax.dot_general(doc_unit, gathered, (((1,), (1,)), ((), ())), precision=l...  2.95 us
  transfers between devices with their start and end apart: 2, of which 2 were waited for; matrix products, arithmetic and copies ran while one was open for 6% of the time, Pallas kernels for 0%

profile of v8, /device:TPU:6, one launch (start us, length us, event | category | flops | bytes accessed | tf_op | source)
XLA Modules:
  0.0 111.6 jit_solution(4482961955580855587)
XLA Ops:
  0.0 0.8 dynamic_slice.3
  0.8 0.8 copy.11.perm_ref
  1.6 5.3 %shard_map.46 = f32[256,1024]{1,0:T(8,128)} custom-call(s32[256,1]{1,0:T(8,128)} %copy.11.perm_ref, s32[16,512]{1,0:T(8,128)} %bitcast.24, f32[512,1024]{1,0:T(8,128)} %feat_ref.1), custom_call_target="tpu_custom_call" | custom-call | tf_op jit(solution)/shard_map/pallas_call | solution.py:37
  6.9 20.6 %all_to_all.15 = f32[8,32,1024]{2,1,0:T(8,128)S(1)} all-to-all(f32[8,32,1024]{2,1,0:T(8,128)} %bitcast.23), channel_id=1, replica_groups=mesh['doc'=8,'label'=64] {'doc'}, dimensions={0} | all-to-all | bytes 2097152 | tf_op jit(solution)/shard_map/all_to_all | solution.py:74
  27.5 0.1 multiply_reduce_fusion.1
  27.8 1.1 broadcast_in_dim.7
  28.9 3.6 %all-to-all-start.1 = ((f32[8,32,1024]{2,1,0:T(8,128)}), f32[8,32,1024]{2,1,0:T(8,128)S(1)}, u32[]{:S(2)}, u32[]{:S(2)}) async-start(f32[8,32,1024]{2,1,0:T(8,128)} %broadcast_in_dim.7), calls=%async_computation.1 | async-start | bytes 2097152 | tf_op jit(solution)/shard_map/all_to_all | solution.py:78
  32.4 0.3 reduce-window.9
  32.9 0.1 slice_reduce_fusion
  33.1 0.2 convert_reduce_fusion
  33.3 15.0 %all-to-all-done.1 = f32[8,32,1024]{2,1,0:T(8,128)S(1)} async-done(((f32[8,32,1024]{2,1,0:T(8,128)}), f32[8,32,1024]{2,1,0:T(8,128)S(1)}, u32[]{:S(2)}, u32[]{:S(2)}) %all-to-all-start.1) | async-done | bytes 1048608 | tf_op jit(solution)/shard_map/all_to_all | solution.py:78
  48.3 1.0 copy-done.1
  49.3 1.9 %fusion.15 = f32[256,1024]{1,0:T(8,128)S(1)} fusion(f32[256,1024]{1,0:T(8,128)} %bitcast.21, s32[256]{0:T(256)S(1)} %convert_reduce_fusion), kind=kOutput, calls=%fused_computation.19 | convolution fusion | flops 805371904 | bytes 2098176 | tf_op jit(solution)/shard_map/dot_general | solution.py:89
  51.3 0.9 broadcast_in_dim.8
  52.2 18.8 %all-to-all-start.2 = ((f32[64,2,1024]{2,1,0:T(2,128)}), f32[64,2,1024]{2,1,0:T(2,128)}, u32[]{:S(2)}, u32[]{:S(2)}) async-start(f32[64,2,1024]{2,1,0:T(2,128)} %broadcast_in_dim.8), calls=%async_computation.2 | async-start | bytes 1048576 | tf_op jit(solution)/shard_map/all_to_all | solution.py:96
  71.0 0.2 convert_reduce_fusion.2
  71.5 0.2 multiply_reduce_fusion
  71.8 1.0 copy-done.2
  72.7 4.6 %fusion = f32[512,512]{1,0:T(8,128)} fusion(f32[256,1024]{1,0:T(8,128)S(1)} %fusion.15, f32[256,1024]{1,0:T(8,128)S(1)} %bitcast.22, f32[512,1024]{1,0:T(8,128)S(1)} %copy-done, f32[512]{0:T(512)S(1)} %add_rsqrt_fusion), kind=kOutput, calls=%fused_computation | convolution fusion | flops 3222274048 | bytes 5244928 | tf_op jit(solution)/shard_map/dot_general | solution.py:105
  77.3 26.1 %all-to-all-done.2 = f32[64,2,1024]{2,1,0:T(2,128)} async-done(((f32[64,2,1024]{2,1,0:T(2,128)}), f32[64,2,1024]{2,1,0:T(2,128)}, u32[]{:S(2)}, u32[]{:S(2)}) %all-to-all-start.2) | async-done | bytes 524320 | tf_op jit(solution)/shard_map/all_to_all | solution.py:96
  103.4 2.2 %reshape.233 = f32[128,1024]{1,0:T(8,128)} reshape(f32[64,2,1024]{2,1,0:T(2,128)} %all-to-all-done.2) | data formatting | bytes 1048576 | tf_op jit(solution)/shard_map/reshape | solution.py:98
  105.6 3.0 %fusion.4 = f32[512,128]{1,0:T(8,128)S(1)} fusion(f32[128,1024]{1,0:T(8,128)} %reshape.233, f32[512,1024]{1,0:T(8,128)S(1)} %copy-done, f32[512]{0:T(512)S(1)} %add_rsqrt_fusion), kind=kOutput, calls=%fused_computation.5 | convolution fusion | flops 805830656 | bytes 2885632 | tf_op jit(solution)/shard_map/dot_general | solution.py:120
  108.6 1.9 %fusion.9 = f32[256]{0:T(256)S(1)} fusion(f32[256,1024]{1,0:T(8,128)S(1)} %fusion.15, f32[64,2,1024]{2,1,0:T(2,128)} %all-to-all-done.2, pred[256,64,1]{0,1,2:T(32,128)(4,1)S(1)} %get-tuple-element.10, pred[256,64,1]{0,1,2:T(32,128)(4,1)S(1)} %get-tuple-element.9), kind=kOutput, calls=%fused_computation.11 | convolution fusion | flops 403472128 | bytes 1606656 | tf_op jit(solution)/shard_map/dot_general | solution.py:115
  110.4 1.2 %fusion.11 = f32[512,256]{1,0:T(8,128)} fusion(f32[512,128]{1,0:T(8,128)S(1)} %fusion.4, pred[256,128]{0,1:T(32,128)(4,1)S(1)} %reshape.234, f32[512,512]{1,0:T(8,128)S(1)} %copy-done.3, f32[256]{0:T(256)S(1)} %add_rsqrt_fusion.1), kind=kOutput, calls=%fused_computation.14 | convolution fusion | flops 201719808 | bytes 1868800 | tf_op jit(solution)/shard_map/dot_general | solution.py:119
  (27 shorter events, 0.8 us)
Async XLA Ops:
  27.5 4.9 %copy-start.4 = (s32[512]{0:T(512)S(1)}, s32[512]{0:T(512)}, u32[]{:S(2)}) copy-start(s32[512]{0:T(512)} %param.7) | copy-start | bytes 6148
  28.9 19.4 %all-to-all-start.1 = ((f32[8,32,1024]{2,1,0:T(8,128)}), f32[8,32,1024]{2,1,0:T(8,128)S(1)}, u32[]{:S(2)}, u32[]{:S(2)}) async-start(f32[8,32,1024]{2,1,0:T(8,128)} %broadcast_in_dim.7), calls=%async_computation.1 | async-start | bytes 2097152 | tf_op jit(solution)/shard_map/all_to_all | solution.py:78
  32.4 39.1 %copy-start = (f32[512,1024]{1,0:T(8,128)S(1)}, f32[512,1024]{1,0:T(8,128)}, u32[]{:S(2)}) copy-start(f32[512,1024]{1,0:T(8,128)} %feat_ref.1) | copy-start | bytes 6291460
  48.3 1.0 copy-start.1
  52.2 51.2 %all-to-all-start.2 = ((f32[64,2,1024]{2,1,0:T(2,128)}), f32[64,2,1024]{2,1,0:T(2,128)}, u32[]{:S(2)}, u32[]{:S(2)}) async-start(f32[64,2,1024]{2,1,0:T(2,128)} %broadcast_in_dim.8), calls=%async_computation.2 | async-start | bytes 1048576 | tf_op jit(solution)/shard_map/all_to_all | solution.py:96
  71.5 1.2 %copy-start.2 = (f32[8,32,1024]{2,1,0:T(8,128)S(1)}, f32[8,32,1024]{2,1,0:T(8,128)}, u32[]{:S(2)}) copy-start(f32[8,32,1024]{2,1,0:T(8,128)} %copy-done.1) | copy-start | bytes 3145732
  105.6 4.8 %copy-start.3 = (f32[512,512]{1,0:T(8,128)S(1)}, f32[512,512]{1,0:T(8,128)}, u32[]{:S(2)}) copy-start(f32[512,512]{1,0:T(8,128)} %fusion) | copy-start | bytes 3145732

commit v9 on v6

--- a/solution.py
+++ b/solution.py
@@ -63,15 +63,46 @@
         partial_value.reshape(groups, L_DEV // groups, depth), "doc", 0, 0, tiled=True
     )
     mine = unit_rows(jnp.sum(pieces, axis=0))
-    label_rows = lax.all_to_all(
-        jnp.broadcast_to(mine[None], (groups,) + mine.shape), "doc", 0, 0, tiled=True
-    ).reshape(L_DEV, depth)
+    label_rows = lax.all_gather(mine, "doc", tiled=True)
 
     starts = jnp.cumsum(cluster_sizes) - cluster_sizes
     cluster_ids = cluster_of(base + slots, starts)
     shard = jnp.arange(width, dtype=jnp.int32)
     first_id = cluster_of(shard * L_DEV, starts)
     last_id = cluster_of(shard * L_DEV + (L_DEV - 1), starts)
+    my_first = first_id[here]
+    my_last = last_id[here]
+
+    chunk = L_DEV // groups
+    chunk_ids = cluster_of(base + lax.axis_index("doc") * chunk + jnp.arange(chunk), starts)
+    ends = jnp.stack(
+        [
+            jnp.sum(jnp.where((chunk_ids == my_first)[:, None], mine, 0.0), axis=0),
+            jnp.sum(jnp.where((chunk_ids == my_last)[:, None], mine, 0.0), axis=0),
+        ]
+    )
+    gathered = lax.all_to_all(
+        jnp.broadcast_to(ends[None], (width,) + ends.shape), "label", 0, 0, tiled=True
+    )
+    other = shard != here
+    parts = []
+    for target in (my_first, my_last):
+        use_first = (first_id == target) & other
+        use_last = (last_id == target) & (first_id != last_id) & other
+        parts.append(
+            jnp.sum(
+                jnp.where(use_first[:, None], gathered[:, 0], 0.0)
+                + jnp.where(use_last[:, None], gathered[:, 1], 0.0),
+                axis=0,
+            )
+        )
+    extra = jnp.stack(parts)
+    extra = jnp.sum(
+        lax.all_to_all(
+            jnp.broadcast_to(extra[None], (groups,) + extra.shape), "doc", 0, 0, tiled=True
+        ),
+        axis=0,
+    )
 
     same_cluster = (cluster_ids[:, None] == cluster_ids[None, :]).astype(jnp.float32)
     local_sum = jnp.dot(
@@ -80,11 +111,6 @@
         precision=lax.Precision.HIGHEST,
         preferred_element_type=jnp.float32,
     )
-    ends = jnp.stack([local_sum[0], local_sum[-1]])
-    gathered = lax.all_to_all(
-        jnp.broadcast_to(ends[None], (width,) + ends.shape), "label", 0, 0, tiled=True
-    ).reshape(2 * width, -1)
-
     doc_unit = unit_rows(features)
     row_scores = lax.dot_general(
         doc_unit,
@@ -93,16 +119,10 @@
         precision=lax.Precision.HIGHEST,
         preferred_element_type=jnp.float32,
     )
-    other = (shard != here)[None, :]
-    take_first = (first_id[None, :] == cluster_ids[:, None]) & other
-    take_last = (last_id[None, :] == cluster_ids[:, None]) & (first_id != last_id)[None, :] & other
-    weights = jnp.stack([take_first, take_last], axis=2).reshape(L_DEV, 2 * width)
-    cluster_sum = local_sum + jnp.dot(
-        weights.astype(jnp.float32),
-        gathered,
-        precision=lax.Precision.HIGHEST,
-        preferred_element_type=jnp.float32,
-    )
+    in_first = (cluster_ids == my_first)[:, None]
+    in_last = ((cluster_ids == my_last) & (my_last != my_first))[:, None]
+    cluster_sum = local_sum + jnp.where(in_first, extra[0][None, :], 0.0)
+    cluster_sum = cluster_sum + jnp.where(in_last, extra[1][None, :], 0.0)
     centroid = unit_rows(cluster_sum)
     return lax.dot_general(
         doc_unit,

time: 107 us -> 109 us (1.019)
  blocking collectives: 20.6 us -> 0 us
  between operations: 0.14 us -> 14.8 us
  other arithmetic: 1.46 us -> 6.13 us
  starting transfers between devices: 22.3 us -> 26.5 us
  waiting for transfers between devices: 44.2 us -> 43.1 us
    all_to_all x1 -> x0, blocking collectives: 20.6 us -> none  [shards(): lax.all_to_all(partial_value.reshape(groups, L_DEV // groups, depth), 'do...]
    all_to_all x1 -> x2, starting transfers between devices: 3.56 us -> 7.83 us  [the longest x1 4.47 us: shards(): lax.all_to_all(partial_value.reshape(groups, L_DEV // groups, depth), 'do...]
    eq x0 -> x2, other arithmetic: none -> 2.49 us  [the longest x1 1.25 us: shards(): chunk_ids == my_last]
    dot_general x1 -> x0, matrix products: 2.23 us -> none  [shards(): jnp.dot(weights.astype(jnp.float32), gathered, precision=lax.Precision.HI...]
    all_to_all x1, waiting for transfers between devices: 29.2 us -> 27.6 us  [shards(): lax.all_to_all(jnp.broadcast_to(ends[None], (width,) + ends.shape), 'labe...]
    dot_general x1, matrix products: 0.7 us -> 2.2 us  [shards(): jnp.dot(same_cluster, label_rows, precision=lax.Precision.HIGHEST, prefer...]
    dynamic_slice x0 -> x2, local copies, waits for them, and re-layouts: none -> 1.25 us  [the longest x1 0.64 us: shards(): my_last = last_id[here]]
    and x1, other arithmetic: 0.11 us -> 1.24 us  [shards(): use_last = (last_id == target) & (first_id != last_id) & other]
  transfers between devices with their start and end apart: 2 -> 4, of which waited for: 2 -> 3; matrix products, arithmetic and copies ran while one was open for 4% -> 10% of each run, Pallas kernels for 0% -> 0%
where the time goes in v9:
time: 109 us; the launch traced here: 108 us
  waiting for transfers between devices  43.1 us (40%)
  starting transfers between devices  26.5 us (24%)
  between operations  14.8 us (14%)
  matrix products  8.01 us (7%)
  other arithmetic  6.13 us (6%)
  local copies, waits for them, and re-layouts  5.07 us (5%)
  Pallas kernels  4.54 us (4%)
    all_to_all x1, waiting for transfers between devices, shards(): lax.all_to_all(jnp.broadcast_to(ends[None], (width,) + ends.shape), 'labe...  27.6 us
    all_to_all x1, starting transfers between devices, shards(): lax.all_to_all(jnp.broadcast_to(ends[None], (width,) + ends.shape), 'labe...  18.6 us
    all_to_all x1, waiting for transfers between devices, shards(): lax.all_to_all(partial_value.reshape(groups, L_DEV // groups, depth), 'do...  12.4 us
    pallas_call x1, Pallas kernels, pifa_partial(): pl.pallas_call(pifa_kernel, out_shape=jax.ShapeDtypeStruct((own_perm.shap...  4.54 us
    all_to_all x1, starting transfers between devices, shards(): lax.all_to_all(partial_value.reshape(groups, L_DEV // groups, depth), 'do...  4.47 us
    all_to_all x1, starting transfers between devices, shards(): lax.all_to_all(jnp.broadcast_to(extra[None], (groups,) + extra.shape), 'd...  3.35 us
    dot_general x1, matrix products, shards(): lax.dot_general(doc_unit, label_rows, (((1,), (1,)), ((), ())), precision...  3.07 us
    dot_general x1, matrix products, shards(): lax.dot_general(doc_unit, centroid, (((1,), (1,)), ((), ())), precision=l...  2.74 us
  transfers between devices with their start and end apart: 4, of which 3 were waited for; matrix products, arithmetic and copies ran while one was open for 10% of the time, Pallas kernels for 0%

profile of v9, /device:TPU:6, one launch (start us, length us, event | category | flops | bytes accessed | tf_op | source)
XLA Modules:
  0.0 108.1 jit_solution(11167997980361010978)
XLA Ops:
  6.5 0.8 dynamic_slice.9
  7.3 0.8 copy.10.perm_ref
  8.1 4.5 %shard_map.46 = f32[256,1024]{1,0:T(8,128)} custom-call(s32[256,1]{1,0:T(8,128)} %copy.10.perm_ref, s32[16,512]{1,0:T(8,128)} %bitcast.34, f32[512,1024]{1,0:T(8,128)} %feat_ref.1), custom_call_target="tpu_custom_call" | custom-call | tf_op jit(solution)/shard_map/pallas_call | solution.py:30
  12.6 4.5 %all-to-all-start = ((f32[8,32,1024]{2,1,0:T(8,128)}), f32[8,32,1024]{2,1,0:T(8,128)S(1)}, u32[]{:S(2)}, u32[]{:S(2)}) async-start(f32[8,32,1024]{2,1,0:T(8,128)} %bitcast.33), calls=%async_computation | async-start | bytes 2097152 | tf_op jit(solution)/shard_map/all_to_all | solution.py:62
  17.1 0.3 reduce-window.9
  18.0 0.6 dynamic_slice.10
  18.6 0.6 dynamic_slice.11
  19.5 1.2 %broadcast_compare_fusion.1 = (pred[32]{0:T(512)(128)(4,1)S(1)}, pred[32]{0:T(512)(128)(4,1)S(1)}) fusion(s32[32]{0:T(128)S(1)} %convert_reduce_fusion.3, s32[]{:T(128)} %bitcast.7, s32[]{:T(128)} %bitcast.5), kind=kLoop, calls=%fused_computation.48 | loop fusion | flops 64 | bytes 200 | tf_op jit(solution)/shard_map/eq | solution.py:81
  20.7 12.4 %all-to-all-done = f32[8,32,1024]{2,1,0:T(8,128)S(1)} async-done(((f32[8,32,1024]{2,1,0:T(8,128)}), f32[8,32,1024]{2,1,0:T(8,128)S(1)}, u32[]{:S(2)}, u32[]{:S(2)}) %all-to-all-start) | async-done | bytes 1048608 | tf_op jit(solution)/shard_map/all_to_all | solution.py:62
  33.3 0.7 select_reduce_fusion.1
  34.0 0.9 broadcast_in_dim.125
  35.0 18.6 %all-to-all-start.1 = ((f32[64,2,1024]{2,1,0:T(2,128)}), f32[64,2,1024]{2,1,0:T(2,128)S(1)}, u32[]{:S(2)}, u32[]{:S(2)}) async-start(f32[64,2,1024]{2,1,0:T(2,128)} %broadcast_in_dim.125), calls=%async_computation.1 | async-start | bytes 1048576 | tf_op jit(solution)/shard_map/all_to_all | solution.py:84
  53.6 0.7 all-gather.2.cloned.1.call-update
  55.8 0.2 multiply_reduce_fusion
  56.0 1.2 %broadcast_compare_fusion = (pred[256]{0:T(512)(128)(4,1)S(1)}, pred[256]{0:T(512)(128)(4,1)S(1)}) fusion(s32[256]{0:T(256)S(1)} %convert_reduce_fusion, s32[]{:T(128)} %bitcast.5, pred[]{:T(512)S(6)} %ne.36, s32[]{:T(128)} %bitcast.7), kind=kLoop, calls=%fused_computation.45 | loop fusion | flops 768 | bytes 1545 | tf_op jit(solution)/shard_map/eq | solution.py:122
  57.2 1.2 %and_and_fusion = (pred[64]{0:T(512)(128)(4,1)S(1)}, pred[64]{0:T(512)(128)(4,1)S(1)}, pred[64]{0:T(512)(128)(4,1)S(1)}, pred[64]{0:T(512)(128)(4,1)S(1)}) fusion(s32[64]{0:T(128)S(1)} %get-tuple-element.10, s32[]{:T(128)} %bitcast.7, s32[]{:T(128)S(6)} %axis_index.22, s32[64]{0:T(128)S(1)} %get-tuple-element.9, s32[]{:T(128)} %bitcast.5), kind=kLoop, calls=%fused_computation.37 | loop fusion | flops 768 | bytes 780 | tf_op jit(solution)/shard_map/and | solution.py:91
  58.5 27.6 %all-to-all-done.1 = f32[64,2,1024]{2,1,0:T(2,128)S(1)} async-done(((f32[64,2,1024]{2,1,0:T(2,128)}), f32[64,2,1024]{2,1,0:T(2,128)S(1)}, u32[]{:S(2)}, u32[]{:S(2)}) %all-to-all-start.1) | async-done | bytes 524320 | tf_op jit(solution)/shard_map/all_to_all | solution.py:84
  86.1 0.4 fusion.19
  86.7 0.6 broadcast_in_dim.130
  87.3 3.4 %all-to-all-start.2 = ((f32[8,2,1024]{2,1,0:T(2,128)}), f32[8,2,1024]{2,1,0:T(2,128)S(1)}, u32[]{:S(2)}, u32[]{:S(2)}) async-start(f32[8,2,1024]{2,1,0:T(2,128)} %broadcast_in_dim.130), calls=%async_computation.2 | async-start | bytes 131072 | tf_op jit(solution)/shard_map/all_to_all | solution.py:101
  90.7 3.1 %fusion = f32[512,256]{1,0:T(8,128)S(1)} fusion(f32[256,1024]{1,0:T(8,128)} %all-gather.2.cloned.1.call-done, f32[512,1024]{1,0:T(8,128)S(1)} %copy-done, f32[512]{0:T(512)S(1)} %add_rsqrt_fusion), kind=kOutput, calls=%fused_computation.1 | convolution fusion | flops 1611137024 | bytes 3672064 | tf_op jit(solution)/shard_map/dot_general | solution.py:115
  93.8 2.4 %all-to-all-done.2 = f32[8,2,1024]{2,1,0:T(2,128)S(1)} async-done(((f32[8,2,1024]{2,1,0:T(2,128)}), f32[8,2,1024]{2,1,0:T(2,128)S(1)}, u32[]{:S(2)}, u32[]{:S(2)}) %all-to-all-start.2) | async-done | bytes 65568 | tf_op jit(solution)/shard_map/all_to_all | solution.py:101
  96.3 2.2 %multiply_reduce_fusion.1 = (f32[256]{0:T(256)S(1)}, f32[256,1024]{1,0:T(8,128)S(1)}) fusion(f32[1024]{0:T(1024)S(1)} %bitcast.42, pred[256]{0:T(512)(128)(4,1)S(1)} %get-tuple-element.17, f32[1024]{0:T(1024)S(1)} %bitcast.41, pred[256]{0:T(512)(128)(4,1)S(1)} %get-tuple-element.16, f32[256,1024]{1,0:T(8,128)} %all-gather.2.cloned.1.call-done, ...), kind=kOutput, calls=%fused_computation.9 | convolution fusion | flops 806944512 | bytes 2107904 | tf_op jit(solution)/shard_map/dot_general | solution.py:108
  98.5 2.7 %fusion.5 = f32[512,256]{1,0:T(8,128)} fusion(f32[512,256]{1,0:T(8,128)S(1)} %fusion, f32[512,1024]{1,0:T(8,128)S(1)} %copy-done, f32[256,1024]{1,0:T(8,128)S(1)} %get-tuple-element.25, f32[512]{0:T(512)S(1)} %add_rsqrt_fusion, f32[256]{0:T(256)S(1)} %add_rsqrt_fusion.1), kind=kOutput, calls=%fused_computation.7 | convolution fusion | flops 1611530240 | bytes 4197376 | tf_op jit(solution)/shard_map/dot_general | solution.py:127
  (27 shorter events, 1.5 us)
Async XLA Ops:
  8.1 9.0 %copy-start.1 = (s32[512]{0:T(512)S(1)}, s32[512]{0:T(512)}, u32[]{:S(2)}) copy-start(s32[512]{0:T(512)} %param.7) | copy-start | bytes 6148
  12.6 20.4 %all-to-all-start = ((f32[8,32,1024]{2,1,0:T(8,128)}), f32[8,32,1024]{2,1,0:T(8,128)S(1)}, u32[]{:S(2)}, u32[]{:S(2)}) async-start(f32[8,32,1024]{2,1,0:T(8,128)} %bitcast.33), calls=%async_computation | async-start | bytes 2097152 | tf_op jit(solution)/shard_map/all_to_all | solution.py:62
  17.1 38.6 %copy-start = (f32[512,1024]{1,0:T(8,128)S(1)}, f32[512,1024]{1,0:T(8,128)}, u32[]{:S(2)}) copy-start(f32[512,1024]{1,0:T(8,128)} %feat_ref.1) | copy-start | bytes 6291460
  35.0 51.1 %all-to-all-start.1 = ((f32[64,2,1024]{2,1,0:T(2,128)}), f32[64,2,1024]{2,1,0:T(2,128)S(1)}, u32[]{:S(2)}, u32[]{:S(2)}) async-start(f32[64,2,1024]{2,1,0:T(2,128)} %broadcast_in_dim.125), calls=%async_computation.1 | async-start | bytes 1048576 | tf_op jit(solution)/shard_map/all_to_all | solution.py:84
  53.6 37.2 %all-gather.2.cloned.1.call-start = ((), (), s32[]{:S(2)}) async-start(), calls=%async_computation.3 | async-start | bytes 1179648 | tf_op jit(solution)/shard_map/all_gather | solution.py:66
  87.3 8.9 %all-to-all-start.2 = ((f32[8,2,1024]{2,1,0:T(2,128)}), f32[8,2,1024]{2,1,0:T(2,128)S(1)}, u32[]{:S(2)}, u32[]{:S(2)}) async-start(f32[8,2,1024]{2,1,0:T(2,128)} %broadcast_in_dim.130), calls=%async_computation.2 | async-start | bytes 131072 | tf_op jit(solution)/shard_map/all_to_all | solution.py:101
Sparse Core Ops, SparseCore 0:
  56.5 29.9 all-gather.1

commit v10 on v6

--- a/solution.py
+++ b/solution.py
@@ -77,7 +77,7 @@
     local_sum = jnp.dot(
         same_cluster,
         label_rows,
-        precision=lax.Precision.HIGHEST,
+        precision=lax.Precision.HIGH,
         preferred_element_type=jnp.float32,
     )
     ends = jnp.stack([local_sum[0], local_sum[-1]])
@@ -90,7 +90,7 @@
         doc_unit,
         label_rows,
         (((1,), (1,)), ((), ())),
-        precision=lax.Precision.HIGHEST,
+        precision=lax.Precision.HIGH,
         preferred_element_type=jnp.float32,
     )
     other = (shard != here)[None, :]
@@ -100,7 +100,7 @@
     cluster_sum = local_sum + jnp.dot(
         weights.astype(jnp.float32),
         gathered,
-        precision=lax.Precision.HIGHEST,
+        precision=lax.Precision.HIGH,
         preferred_element_type=jnp.float32,
     )
     centroid = unit_rows(cluster_sum)
@@ -108,7 +108,7 @@
         doc_unit,
         centroid,
         (((1,), (1,)), ((), ())),
-        precision=lax.Precision.HIGHEST,
+        precision=lax.Precision.HIGH,
         preferred_element_type=jnp.float32,
     ) + row_scores
 

time: 107 us -> 106 us (level)
  matrix products: 8.31 us -> 6.27 us
  transfers between devices with their start and end apart: 2 -> 2, of which waited for: 2 -> 2; matrix products, arithmetic and copies ran while one was open for 4% -> 3% of each run, Pallas kernels for 0% -> 0%
where the time goes in v10:
time: 106 us; the launch traced here: 105 us
  waiting for transfers between devices  45 us (42%)
  starting transfers between devices  22.3 us (21%)
  blocking collectives  20.6 us (19%)
  matrix products  6.27 us (6%)
  local copies, waits for them, and re-layouts  4.89 us (5%)
  Pallas kernels  4.54 us (4%)
  other arithmetic  1.46 us (1%)
    all_to_all x1, waiting for transfers between devices, shards(): lax.all_to_all(jnp.broadcast_to(ends[None], (width,) + ends.shape), 'labe...  30 us
    all_to_all x1, blocking collectives, shards(): lax.all_to_all(partial_value.reshape(groups, L_DEV // groups, depth), 'do...  20.6 us
    all_to_all x1, starting transfers between devices, shards(): lax.all_to_all(jnp.broadcast_to(ends[None], (width,) + ends.shape), 'labe...  18.8 us
    all_to_all x1, waiting for transfers between devices, shards(): lax.all_to_all(jnp.broadcast_to(mine[None], (groups,) + mine.shape), 'doc...  15 us
    pallas_call x1, Pallas kernels, pifa_partial(): pl.pallas_call(pifa_kernel, out_shape=jax.ShapeDtypeStruct((own_perm.shap...  4.54 us
    all_to_all x1, starting transfers between devices, shards(): lax.all_to_all(jnp.broadcast_to(mine[None], (groups,) + mine.shape), 'doc...  3.56 us
  transfers between devices with their start and end apart: 2, of which 2 were waited for; matrix products, arithmetic and copies ran while one was open for 3% of the time, Pallas kernels for 0%

profile of v10, /device:TPU:6, one launch (start us, length us, event | category | flops | bytes accessed | tf_op | source)
XLA Modules:
  0.0 105.2 jit_solution(7848717351493594842)
XLA Ops:
  0.0 0.8 dynamic_slice.3
  0.8 0.8 copy.8.perm_ref
  1.6 4.5 %shard_map.46 = f32[256,1024]{1,0:T(8,128)} custom-call(s32[256,1]{1,0:T(8,128)} %copy.8.perm_ref, s32[16,512]{1,0:T(8,128)} %bitcast.16, f32[512,1024]{1,0:T(8,128)} %feat_ref.1), custom_call_target="tpu_custom_call" | custom-call | tf_op jit(solution)/shard_map/pallas_call | solution.py:30
  6.1 20.6 %all_to_all.15 = f32[8,32,1024]{2,1,0:T(8,128)S(1)} all-to-all(f32[8,32,1024]{2,1,0:T(8,128)} %bitcast.15), channel_id=1, replica_groups=mesh['doc'=8,'label'=64] {'doc'}, dimensions={0} | all-to-all | bytes 2097152 | tf_op jit(solution)/shard_map/all_to_all | solution.py:62
  26.7 0.1 multiply_reduce_fusion.2
  26.9 0.1 broadcast_multiply_fusion
  27.0 1.1 %broadcast_in_dim.7 = f32[8,32,1024]{2,1,0:T(8,128)} broadcast(f32[32,1024]{1,0:T(8,128)S(1)} %broadcast_multiply_fusion), dimensions={1,2} | broadcast | bytes 1179648 | tf_op jit(solution)/shard_map/broadcast_in_dim | solution.py:67
  28.1 3.6 %all-to-all-start.1 = ((f32[8,32,1024]{2,1,0:T(8,128)}), f32[8,32,1024]{2,1,0:T(8,128)S(1)}, u32[]{:S(2)}, u32[]{:S(2)}) async-start(f32[8,32,1024]{2,1,0:T(8,128)} %broadcast_in_dim.7), calls=%async_computation.1 | async-start | bytes 2097152 | tf_op jit(solution)/shard_map/all_to_all | solution.py:66
  31.6 0.3 reduce-window.9
  32.0 0.1 slice.18
  32.1 0.1 slice_reduce_fusion
  32.3 0.2 convert_reduce_fusion
  32.5 15.0 %all-to-all-done.1 = f32[8,32,1024]{2,1,0:T(8,128)S(1)} async-done(((f32[8,32,1024]{2,1,0:T(8,128)}), f32[8,32,1024]{2,1,0:T(8,128)S(1)}, u32[]{:S(2)}, u32[]{:S(2)}) %all-to-all-start.1) | async-done | bytes 1048608 | tf_op jit(solution)/shard_map/all_to_all | solution.py:66
  47.5 0.5 fusion.13
  48.0 1.0 copy-done.1
  49.0 0.9 broadcast_in_dim.8
  50.0 18.8 %all-to-all-start.2 = ((f32[64,2,1024]{2,1,0:T(2,128)}), f32[64,2,1024]{2,1,0:T(2,128)}, u32[]{:S(2)}, u32[]{:S(2)}) async-start(f32[64,2,1024]{2,1,0:T(2,128)} %broadcast_in_dim.8), calls=%async_computation.2 | async-start | bytes 1048576 | tf_op jit(solution)/shard_map/all_to_all | solution.py:84
  68.8 0.2 convert_reduce_fusion.2
  69.0 0.2 multiply_reduce_fusion
  69.2 0.1 compare_and_fusion
  69.3 1.8 %fusion = f32[512,256]{1,0:T(8,128)} fusion(f32[256,1024]{1,0:T(8,128)S(1)} %bitcast.14, f32[512,1024]{1,0:T(8,128)S(1)} %copy-done, f32[512]{0:T(512)S(1)} %add_rsqrt_fusion), kind=kOutput, calls=%fused_computation.1 | convolution fusion | flops 805830656 | bytes 3672064 | tf_op jit(solution)/shard_map/dot_general | solution.py:89
  71.2 30.0 %all-to-all-done.2 = f32[64,2,1024]{2,1,0:T(2,128)} async-done(((f32[64,2,1024]{2,1,0:T(2,128)}), f32[64,2,1024]{2,1,0:T(2,128)}, u32[]{:S(2)}, u32[]{:S(2)}) %all-to-all-start.2) | async-done | bytes 524320 | tf_op jit(solution)/shard_map/all_to_all | solution.py:84
  101.2 2.0 %multiply_reduce_fusion.1 = (f32[256]{0:T(256)S(1)}, f32[256,1024]{1,0:T(8,128)S(1)}) fusion(f32[256,1024]{1,0:T(8,128)} %copy-done.1, f32[64,2,1024]{2,1,0:T(2,128)} %all-to-all-done.2, pred[256,64,1]{0,1,2:T(32,128)(4,1)S(1)} %get-tuple-element.10, pred[256,64,1]{0,1,2:T(32,128)(4,1)S(1)} %get-tuple-element.9), kind=kOutput, calls=%fused_computation.9 | convolution fusion | flops 202145536 | bytes 2655232 | tf_op jit(solution)/shard_map/dot_general | solution.py:100
  103.3 1.9 %fusion.5 = f32[512,256]{1,0:T(8,128)} fusion(f32[512,256]{1,0:T(8,128)S(1)} %copy-done.2, f32[512,1024]{1,0:T(8,128)S(1)} %copy-done, f32[256,1024]{1,0:T(8,128)S(1)} %get-tuple-element.12, f32[512]{0:T(512)S(1)} %add_rsqrt_fusion, f32[256]{0:T(256)S(1)} %add_rsqrt_fusion.1), kind=kOutput, calls=%fused_computation.7 | convolution fusion | flops 806223872 | bytes 4197376 | tf_op jit(solution)/shard_map/dot_general | solution.py:107
  (20 shorter events, 0.3 us)
Async XLA Ops:
  26.7 4.9 %copy-start.3 = (s32[512]{0:T(512)S(1)}, s32[512]{0:T(512)}, u32[]{:S(2)}) copy-start(s32[512]{0:T(512)} %param.7) | copy-start | bytes 6148
  28.1 19.4 %all-to-all-start.1 = ((f32[8,32,1024]{2,1,0:T(8,128)}), f32[8,32,1024]{2,1,0:T(8,128)S(1)}, u32[]{:S(2)}, u32[]{:S(2)}) async-start(f32[8,32,1024]{2,1,0:T(8,128)} %broadcast_in_dim.7), calls=%async_computation.1 | async-start | bytes 2097152 | tf_op jit(solution)/shard_map/all_to_all | solution.py:66
  31.6 37.4 %copy-start = (f32[512,1024]{1,0:T(8,128)S(1)}, f32[512,1024]{1,0:T(8,128)}, u32[]{:S(2)}) copy-start(f32[512,1024]{1,0:T(8,128)} %feat_ref.1) | copy-start | bytes 6291460
  48.0 1.0 copy-start.1
  50.0 51.2 %all-to-all-start.2 = ((f32[64,2,1024]{2,1,0:T(2,128)}), f32[64,2,1024]{2,1,0:T(2,128)}, u32[]{:S(2)}, u32[]{:S(2)}) async-start(f32[64,2,1024]{2,1,0:T(2,128)} %broadcast_in_dim.8), calls=%async_computation.2 | async-start | bytes 1048576 | tf_op jit(solution)/shard_map/all_to_all | solution.py:84
  71.2 32.1 %copy-start.2 = (f32[512,256]{1,0:T(8,128)S(1)}, f32[512,256]{1,0:T(8,128)}, u32[]{:S(2)}) copy-start(f32[512,256]{1,0:T(8,128)} %fusion) | copy-start | bytes 1572868

commit v11 on v10

--- a/solution.py
+++ b/solution.py
@@ -80,10 +80,9 @@
         precision=lax.Precision.HIGH,
         preferred_element_type=jnp.float32,
     )
-    ends = jnp.stack([local_sum[0], local_sum[-1]])
-    gathered = lax.all_to_all(
-        jnp.broadcast_to(ends[None], (width,) + ends.shape), "label", 0, 0, tiled=True
-    ).reshape(2 * width, -1)
+    above = shard > here
+    sending = jnp.where(above[:, None], local_sum[-1][None, :], local_sum[0][None, :])
+    gathered = lax.all_to_all(sending, "label", 0, 0, tiled=True)
 
     doc_unit = unit_rows(features)
     row_scores = lax.dot_general(
@@ -93,10 +92,10 @@
         precision=lax.Precision.HIGH,
         preferred_element_type=jnp.float32,
     )
-    other = (shard != here)[None, :]
-    take_first = (first_id[None, :] == cluster_ids[:, None]) & other
-    take_last = (last_id[None, :] == cluster_ids[:, None]) & (first_id != last_id)[None, :] & other
-    weights = jnp.stack([take_first, take_last], axis=2).reshape(L_DEV, 2 * width)
+    below = shard < here
+    take_below = (last_id[None, :] == cluster_ids[:, None]) & below[None, :]
+    take_above = (first_id[None, :] == cluster_ids[:, None]) & above[None, :]
+    weights = take_below | take_above
     cluster_sum = local_sum + jnp.dot(
         weights.astype(jnp.float32),
         gathered,

time: 106 us -> 94.2 us (0.89)
  waiting for transfers between devices: 45 us -> 34 us
    all_to_all x1, waiting for transfers between devices: 30 us -> 19 us  [shards(): gathered = lax.all_to_all(sending, 'label', 0, 0, tiled=True)]
where the time goes in v11:
time: 94.2 us; the launch traced here: 93.7 us
  waiting for transfers between devices  34 us (36%)
  starting transfers between devices  22.3 us (24%)
  blocking collectives  20.6 us (22%)
  matrix products  6.07 us (6%)
  Pallas kernels  4.54 us (5%)
  local copies, waits for them, and re-layouts  3.94 us (4%)
  other arithmetic  2.26 us (2%)
    all_to_all x1, blocking collectives, shards(): lax.all_to_all(partial_value.reshape(groups, L_DEV // groups, depth), 'do...  20.6 us
    all_to_all x1, waiting for transfers between devices, shards(): gathered = lax.all_to_all(sending, 'label', 0, 0, tiled=True)  19 us
    all_to_all x1, starting transfers between devices, shards(): gathered = lax.all_to_all(sending, 'label', 0, 0, tiled=True)  18.6 us
    all_to_all x1, waiting for transfers between devices, shards(): lax.all_to_all(jnp.broadcast_to(mine[None], (groups,) + mine.shape), 'doc...  15 us
    pallas_call x1, Pallas kernels, pifa_partial(): pl.pallas_call(pifa_kernel, out_shape=jax.ShapeDtypeStruct((own_perm.shap...  4.54 us
    all_to_all x1, starting transfers between devices, shards(): lax.all_to_all(jnp.broadcast_to(mine[None], (groups,) + mine.shape), 'doc...  3.69 us
    dot_general x1, matrix products, shards(): lax.dot_general(doc_unit, centroid, (((1,), (1,)), ((), ())), precision=l...  1.92 us
  transfers between devices with their start and end apart: 2, of which 2 were waited for; matrix products, arithmetic and copies ran while one was open for 3% of the time, Pallas kernels for 0%

profile of v11, /device:TPU:6, one launch (start us, length us, event | category | flops | bytes accessed | tf_op | source)
XLA Modules:
  0.0 93.7 jit_solution(12259784101179232368)
XLA Ops:
  0.0 0.8 dynamic_slice.3
  0.8 0.8 copy.6.perm_ref
  1.6 4.5 %shard_map.46 = f32[256,1024]{1,0:T(8,128)} custom-call(s32[256,1]{1,0:T(8,128)} %copy.6.perm_ref, s32[16,512]{1,0:T(8,128)} %bitcast.19, f32[512,1024]{1,0:T(8,128)} %feat_ref.1), custom_call_target="tpu_custom_call" | custom-call | tf_op jit(solution)/shard_map/pallas_call | solution.py:30
  6.1 20.6 %all_to_all.19 = f32[8,32,1024]{2,1,0:T(8,128)S(1)} all-to-all(f32[8,32,1024]{2,1,0:T(8,128)} %bitcast.18), channel_id=1, replica_groups=mesh['doc'=8,'label'=64] {'doc'}, dimensions={0} | all-to-all | bytes 2097152 | tf_op jit(solution)/shard_map/all_to_all | solution.py:62
  26.7 0.1 multiply_reduce_fusion.2
  26.9 0.1 broadcast_multiply_fusion
  27.0 1.1 %broadcast_in_dim.20 = f32[8,32,1024]{2,1,0:T(8,128)} broadcast(f32[32,1024]{1,0:T(8,128)S(1)} %broadcast_multiply_fusion), dimensions={1,2} | broadcast | bytes 1179648 | tf_op jit(solution)/shard_map/broadcast_in_dim | solution.py:67
  28.1 3.7 %all-to-all-start.1 = ((f32[8,32,1024]{2,1,0:T(8,128)}), f32[8,32,1024]{2,1,0:T(8,128)S(1)}, u32[]{:S(2)}, u32[]{:S(2)}) async-start(f32[8,32,1024]{2,1,0:T(8,128)} %broadcast_in_dim.20), calls=%async_computation.1 | async-start | bytes 2097152 | tf_op jit(solution)/shard_map/all_to_all | solution.py:66
  31.8 0.3 reduce-window.9
  32.1 0.1 slice.22
  32.2 0.1 slice_reduce_fusion
  32.3 0.1 bitcast_subtract_fusion
  32.5 0.2 convert_reduce_fusion
  32.7 15.0 %all-to-all-done.1 = f32[8,32,1024]{2,1,0:T(8,128)S(1)} async-done(((f32[8,32,1024]{2,1,0:T(8,128)}), f32[8,32,1024]{2,1,0:T(8,128)S(1)}, u32[]{:S(2)}, u32[]{:S(2)}) %all-to-all-start.1) | async-done | bytes 1048608 | tf_op jit(solution)/shard_map/all_to_all | solution.py:66
  47.6 0.5 fusion.13
  48.1 1.0 %copy-done.1 = f32[256,1024]{1,0:T(8,128)} copy-done((f32[256,1024]{1,0:T(8,128)}, f32[256,1024]{1,0:T(8,128)S(1)}, u32[]{:S(2)}) %copy-start.1) | copy-done | bytes 1048600
  49.1 0.9 broadcast_select_fusion
  50.1 18.6 %all-to-all-start.2 = ((f32[64,1,1024]{2,1,0:T(1,128)}), f32[64,1,1024]{2,1,0:T(1,128)S(1)}, u32[]{:S(2)}, u32[]{:S(2)}) async-start(f32[64,1,1024]{2,1,0:T(1,128)} %broadcast_select_fusion), calls=%async_computation.2 | async-start | bytes 524288 | tf_op jit(solution)/shard_map/all_to_all | solution.py:85
  68.7 0.2 convert_reduce_fusion.2
  68.9 0.2 multiply_reduce_fusion
  69.1 1.8 %fusion = f32[512,256]{1,0:T(8,128)} fusion(f32[256,1024]{1,0:T(8,128)S(1)} %bitcast.17, f32[512,1024]{1,0:T(8,128)S(1)} %copy-done, f32[512]{0:T(512)S(1)} %add_rsqrt_fusion), kind=kOutput, calls=%fused_computation.1 | convolution fusion | flops 805830656 | bytes 3672064 | tf_op jit(solution)/shard_map/dot_general | solution.py:88
  70.9 19.0 %all-to-all-done.2 = f32[64,1,1024]{2,1,0:T(1,128)S(1)} async-done(((f32[64,1,1024]{2,1,0:T(1,128)}), f32[64,1,1024]{2,1,0:T(1,128)S(1)}, u32[]{:S(2)}, u32[]{:S(2)}) %all-to-all-start.2) | async-done | bytes 262176 | tf_op jit(solution)/shard_map/all_to_all | solution.py:85
  89.9 1.8 %multiply_reduce_fusion.1 = (f32[256]{0:T(256)S(1)}, f32[256,1024]{1,0:T(8,128)S(1)}) fusion(f32[256,1024]{1,0:T(8,128)} %copy-done.1, f32[64,1,1024]{2,1,0:T(1,128)S(1)} %all-to-all-done.2, s32[64]{0:T(128)S(1)} %get-tuple-element.6, s32[64]{0:T(128)S(1)} %get-tuple-element.5, s32[256]{0:T(256)S(1)} %convert_reduce_fusion, ...), kind=kOutput, calls=%fused_computation.8 | convolution fusion | flops 101531392 | bytes 2361984 | tf_op jit(solution)/shard_map/dot_general | solution.py:99
  91.8 1.9 %fusion.4 = f32[512,256]{1,0:T(8,128)} fusion(f32[512,256]{1,0:T(8,128)S(1)} %copy-done.2, f32[512,1024]{1,0:T(8,128)S(1)} %copy-done, f32[256,1024]{1,0:T(8,128)S(1)} %get-tuple-element.10, f32[512]{0:T(512)S(1)} %add_rsqrt_fusion, f32[256]{0:T(256)S(1)} %add_rsqrt_fusion.1), kind=kOutput, calls=%fused_computation.6 | convolution fusion | flops 806223872 | bytes 4197376 | tf_op jit(solution)/shard_map/dot_general | solution.py:106
  (18 shorter events, 0.2 us)
Async XLA Ops:
  26.7 5.0 %copy-start.3 = (s32[512]{0:T(512)S(1)}, s32[512]{0:T(512)}, u32[]{:S(2)}) copy-start(s32[512]{0:T(512)} %param.7) | copy-start | bytes 6148
  28.1 40.8 %copy-start = (f32[512,1024]{1,0:T(8,128)S(1)}, f32[512,1024]{1,0:T(8,128)}, u32[]{:S(2)}) copy-start(f32[512,1024]{1,0:T(8,128)} %feat_ref.1) | copy-start | bytes 6291460
  28.1 19.6 %all-to-all-start.1 = ((f32[8,32,1024]{2,1,0:T(8,128)}), f32[8,32,1024]{2,1,0:T(8,128)S(1)}, u32[]{:S(2)}, u32[]{:S(2)}) async-start(f32[8,32,1024]{2,1,0:T(8,128)} %broadcast_in_dim.20), calls=%async_computation.1 | async-start | bytes 2097152 | tf_op jit(solution)/shard_map/all_to_all | solution.py:66
  48.1 1.0 %copy-start.1 = (f32[256,1024]{1,0:T(8,128)}, f32[256,1024]{1,0:T(8,128)S(1)}, u32[]{:S(2)}) copy-start(f32[256,1024]{1,0:T(8,128)S(1)} %fusion.13) | copy-start | bytes 3145732
  50.1 39.9 %all-to-all-start.2 = ((f32[64,1,1024]{2,1,0:T(1,128)}), f32[64,1,1024]{2,1,0:T(1,128)S(1)}, u32[]{:S(2)}, u32[]{:S(2)}) async-start(f32[64,1,1024]{2,1,0:T(1,128)} %broadcast_select_fusion), calls=%async_computation.2 | async-start | bytes 524288 | tf_op jit(solution)/shard_map/all_to_all | solution.py:85
  70.9 20.8 %copy-start.2 = (f32[512,256]{1,0:T(8,128)S(1)}, f32[512,256]{1,0:T(8,128)}, u32[]{:S(2)}) copy-start(f32[512,256]{1,0:T(8,128)} %fusion) | copy-start | bytes 1572868

commit v12 on v3

--- a/solution.py
+++ b/solution.py
@@ -27,12 +27,8 @@
     incidence = jnp.sum(
         (doc_labels.T[:, None, :] == own_perm[None, :, None]).astype(jnp.float32), axis=0
     )
-    partial_value = lax.dot_general(
-        incidence,
-        features,
-        (((1,), (0,)), ((), ())),
-        precision=lax.Precision.HIGHEST,
-        preferred_element_type=jnp.float32,
+    partial_value = jnp.dot(
+        incidence, features, precision=lax.Precision.HIGH, preferred_element_type=jnp.float32
     )
     groups = lax.axis_size("doc")
     depth = features.shape[1]
@@ -54,30 +50,29 @@
     local_sum = jnp.dot(
         same_cluster,
         label_rows,
-        precision=lax.Precision.HIGHEST,
+        precision=lax.Precision.HIGH,
         preferred_element_type=jnp.float32,
     )
-    ends = jnp.stack([local_sum[0], local_sum[-1]])
-    gathered = lax.all_to_all(
-        jnp.broadcast_to(ends[None], (width,) + ends.shape), "label", 0, 0, tiled=True
-    ).reshape(2 * width, -1)
+    above = shard > here
+    sending = jnp.where(above[:, None], local_sum[-1][None, :], local_sum[0][None, :])
+    gathered = lax.all_to_all(sending, "label", 0, 0, tiled=True)
 
     doc_unit = unit_rows(features)
     row_scores = lax.dot_general(
         doc_unit,
         label_rows,
         (((1,), (1,)), ((), ())),
-        precision=lax.Precision.HIGHEST,
+        precision=lax.Precision.HIGH,
         preferred_element_type=jnp.float32,
     )
-    other = (shard != here)[None, :]
-    take_first = (first_id[None, :] == cluster_ids[:, None]) & other
-    take_last = (last_id[None, :] == cluster_ids[:, None]) & (first_id != last_id)[None, :] & other
-    weights = jnp.stack([take_first, take_last], axis=2).reshape(L_DEV, 2 * width)
+    below = shard < here
+    take_below = (last_id[None, :] == cluster_ids[:, None]) & below[None, :]
+    take_above = (first_id[None, :] == cluster_ids[:, None]) & above[None, :]
+    weights = take_below | take_above
     cluster_sum = local_sum + jnp.dot(
         weights.astype(jnp.float32),
         gathered,
-        precision=lax.Precision.HIGHEST,
+        precision=lax.Precision.HIGH,
         preferred_element_type=jnp.float32,
     )
     centroid = unit_rows(cluster_sum)
@@ -85,7 +80,7 @@
         doc_unit,
         centroid,
         (((1,), (1,)), ((), ())),
-        precision=lax.Precision.HIGHEST,
+        precision=lax.Precision.HIGH,
         preferred_element_type=jnp.float32,
     ) + row_scores
 

time: 107 us -> 93.1 us (0.87)
  waiting for transfers between devices: 44.2 us -> 34 us
  matrix products: 11.8 us -> 8.73 us
    all_to_all x1, waiting for transfers between devices: 29.2 us -> 19 us  [shards(): gathered = lax.all_to_all(sending, 'label', 0, 0, tiled=True)]
  transfers between devices with their start and end apart: 2 -> 2, of which waited for: 2 -> 2; matrix products, arithmetic and copies ran while one was open for 4% -> 3% of each run, Pallas kernels for 0% -> 0%
where the time goes in v12:
time: 93.1 us; the launch traced here: 92.6 us
  waiting for transfers between devices  34 us (37%)
  starting transfers between devices  22.3 us (24%)
  blocking collectives  20.4 us (22%)
  matrix products  8.73 us (9%)
  other arithmetic  3.95 us (4%)
  local copies, waits for them, and re-layouts  3.14 us (3%)
    all_to_all x1, blocking collectives, shards(): lax.all_to_all(partial_value.reshape(groups, L_DEV // groups, depth), 'do...  20.4 us
    all_to_all x1, waiting for transfers between devices, shards(): gathered = lax.all_to_all(sending, 'label', 0, 0, tiled=True)  19 us
    all_to_all x1, starting transfers between devices, shards(): gathered = lax.all_to_all(sending, 'label', 0, 0, tiled=True)  18.6 us
    all_to_all x1, waiting for transfers between devices, shards(): lax.all_to_all(jnp.broadcast_to(mine[None], (groups,) + mine.shape), 'doc...  15 us
    all_to_all x1, starting transfers between devices, shards(): lax.all_to_all(jnp.broadcast_to(mine[None], (groups,) + mine.shape), 'doc...  3.69 us
    dot_general x1, matrix products, shards(): jnp.dot(incidence, features, precision=lax.Precision.HIGH, preferred_elem...  2.66 us
    dot_general x1, matrix products, shards(): lax.dot_general(doc_unit, centroid, (((1,), (1,)), ((), ())), precision=l...  1.92 us
  transfers between devices with their start and end apart: 2, of which 2 were waited for; matrix products, arithmetic and copies ran while one was open for 3% of the time, Pallas kernels for 0%

profile of v12, /device:TPU:6, one launch (start us, length us, event | category | flops | bytes accessed | tf_op | source)
XLA Modules:
  0.0 92.6 jit_solution(5715986689118082779)
XLA Ops:
  0.0 0.8 dynamic_slice.3
  0.8 1.7 %convert_reduce_fusion = f32[256,512]{1,0:T(8,128)S(1)} fusion(s32[16,512]{1,0:T(8,128)} %bitcast.22, s32[256]{0:T(256)S(1)} %dynamic_slice.3), kind=kLoop, calls=%fused_computation | loop fusion | flops 6160384 | bytes 558080 | tf_op jit(solution)/shard_map/reduce_sum | solution.py:27
  2.5 2.7 %fusion = f32[8,32,1024]{2,1,0:T(8,128)S(1)} fusion(f32[8,32,512]{2,1,0:T(8,128)S(1)} %bitcast.21, f32[512,1024]{1,0:T(8,128)} %param.4), kind=kOutput, calls=%fused_computation.1 | convolution fusion | flops 805306368 | bytes 3670016 | tf_op jit(solution)/shard_map/dot_general | solution.py:30
  5.1 20.4 %all_to_all.19 = f32[8,32,1024]{2,1,0:T(8,128)S(1)} all-to-all(f32[8,32,1024]{2,1,0:T(8,128)S(1)} %fusion), channel_id=1, replica_groups=mesh['doc'=8,'label'=64] {'doc'}, dimensions={0} | all-to-all | bytes 2097152 | tf_op jit(solution)/shard_map/all_to_all | solution.py:35
  25.6 0.1 multiply_reduce_fusion.2
  25.7 0.1 broadcast_multiply_fusion
  25.8 1.1 %broadcast_in_dim.17 = f32[8,32,1024]{2,1,0:T(8,128)} broadcast(f32[32,1024]{1,0:T(8,128)S(1)} %broadcast_multiply_fusion), dimensions={1,2} | broadcast | bytes 1179648 | tf_op jit(solution)/shard_map/broadcast_in_dim | solution.py:40
  26.9 3.7 %all-to-all-start.1 = ((f32[8,32,1024]{2,1,0:T(8,128)}), f32[8,32,1024]{2,1,0:T(8,128)S(1)}, u32[]{:S(2)}, u32[]{:S(2)}) async-start(f32[8,32,1024]{2,1,0:T(8,128)} %broadcast_in_dim.17), calls=%async_computation.1 | async-start | bytes 2097152 | tf_op jit(solution)/shard_map/all_to_all | solution.py:39
  30.6 0.3 reduce-window.9
  30.9 0.1 slice.22
  31.0 0.1 slice_reduce_fusion
  31.2 0.1 slice.24
  31.3 0.2 convert_reduce_fusion.1
  31.5 15.0 %all-to-all-done.1 = f32[8,32,1024]{2,1,0:T(8,128)S(1)} async-done(((f32[8,32,1024]{2,1,0:T(8,128)}), f32[8,32,1024]{2,1,0:T(8,128)S(1)}, u32[]{:S(2)}, u32[]{:S(2)}) %all-to-all-start.1) | async-done | bytes 1048608 | tf_op jit(solution)/shard_map/all_to_all | solution.py:39
  46.5 0.5 fusion.15
  47.0 1.0 %copy-done.1 = f32[256,1024]{1,0:T(8,128)} copy-done((f32[256,1024]{1,0:T(8,128)}, f32[256,1024]{1,0:T(8,128)S(1)}, u32[]{:S(2)}) %copy-start.1) | copy-done | bytes 1048600
  48.0 0.9 broadcast_select_fusion
  48.9 18.6 %all-to-all-start.2 = ((f32[64,1,1024]{2,1,0:T(1,128)}), f32[64,1,1024]{2,1,0:T(1,128)S(1)}, u32[]{:S(2)}, u32[]{:S(2)}) async-start(f32[64,1,1024]{2,1,0:T(1,128)} %broadcast_select_fusion), calls=%async_computation.2 | async-start | bytes 524288 | tf_op jit(solution)/shard_map/all_to_all | solution.py:58
  67.5 0.2 convert_reduce_fusion.3
  67.7 0.2 multiply_reduce_fusion
  67.9 1.8 %fusion.2 = f32[512,256]{1,0:T(8,128)} fusion(f32[256,1024]{1,0:T(8,128)S(1)} %bitcast.20, f32[512,1024]{1,0:T(8,128)S(1)} %copy-done, f32[512]{0:T(512)S(1)} %add_rsqrt_fusion), kind=kOutput, calls=%fused_computation.4 | convolution fusion | flops 805830656 | bytes 3672064 | tf_op jit(solution)/shard_map/dot_general | solution.py:61
  69.8 19.0 %all-to-all-done.2 = f32[64,1,1024]{2,1,0:T(1,128)S(1)} async-done(((f32[64,1,1024]{2,1,0:T(1,128)}), f32[64,1,1024]{2,1,0:T(1,128)S(1)}, u32[]{:S(2)}, u32[]{:S(2)}) %all-to-all-start.2) | async-done | bytes 262176 | tf_op jit(solution)/shard_map/all_to_all | solution.py:58
  88.8 1.8 %multiply_reduce_fusion.1 = (f32[256]{0:T(256)S(1)}, f32[256,1024]{1,0:T(8,128)S(1)}) fusion(f32[256,1024]{1,0:T(8,128)} %copy-done.1, f32[64,1,1024]{2,1,0:T(1,128)S(1)} %all-to-all-done.2, s32[64]{0:T(128)S(1)} %get-tuple-element.6, s32[64]{0:T(128)S(1)} %get-tuple-element.5, s32[256]{0:T(256)S(1)} %convert_reduce_fusion.1, ...), kind=kOutput, calls=%fused_computation.11 | convolution fusion | flops 101531392 | bytes 2361984 | tf_op jit(solution)/shard_map/dot_general | solution.py:72
  90.6 1.9 %fusion.6 = f32[512,256]{1,0:T(8,128)} fusion(f32[512,256]{1,0:T(8,128)S(1)} %copy-done.2, f32[512,1024]{1,0:T(8,128)S(1)} %copy-done, f32[256,1024]{1,0:T(8,128)S(1)} %get-tuple-element.10, f32[512]{0:T(512)S(1)} %add_rsqrt_fusion, f32[256]{0:T(256)S(1)} %add_rsqrt_fusion.1), kind=kOutput, calls=%fused_computation.9 | convolution fusion | flops 806223872 | bytes 4197376 | tf_op jit(solution)/shard_map/dot_general | solution.py:79
  (18 shorter events, 0.2 us)
Async XLA Ops:
  25.6 5.0 %copy-start.3 = (s32[512]{0:T(512)S(1)}, s32[512]{0:T(512)}, u32[]{:S(2)}) copy-start(s32[512]{0:T(512)} %param.7) | copy-start | bytes 6148
  26.9 40.8 %copy-start = (f32[512,1024]{1,0:T(8,128)S(1)}, f32[512,1024]{1,0:T(8,128)}, u32[]{:S(2)}) copy-start(f32[512,1024]{1,0:T(8,128)} %param.4) | copy-start | bytes 6291460
  26.9 19.6 %all-to-all-start.1 = ((f32[8,32,1024]{2,1,0:T(8,128)}), f32[8,32,1024]{2,1,0:T(8,128)S(1)}, u32[]{:S(2)}, u32[]{:S(2)}) async-start(f32[8,32,1024]{2,1,0:T(8,128)} %broadcast_in_dim.17), calls=%async_computation.1 | async-start | bytes 2097152 | tf_op jit(solution)/shard_map/all_to_all | solution.py:39
  47.0 1.0 %copy-start.1 = (f32[256,1024]{1,0:T(8,128)}, f32[256,1024]{1,0:T(8,128)S(1)}, u32[]{:S(2)}) copy-start(f32[256,1024]{1,0:T(8,128)S(1)} %fusion.15) | copy-start | bytes 3145732
  48.9 39.9 %all-to-all-start.2 = ((f32[64,1,1024]{2,1,0:T(1,128)}), f32[64,1,1024]{2,1,0:T(1,128)S(1)}, u32[]{:S(2)}, u32[]{:S(2)}) async-start(f32[64,1,1024]{2,1,0:T(1,128)} %broadcast_select_fusion), calls=%async_computation.2 | async-start | bytes 524288 | tf_op jit(solution)/shard_map/all_to_all | solution.py:58
  69.8 20.8 %copy-start.2 = (f32[512,256]{1,0:T(8,128)S(1)}, f32[512,256]{1,0:T(8,128)}, u32[]{:S(2)}) copy-start(f32[512,256]{1,0:T(8,128)} %fusion.2) | copy-start | bytes 1572868

commit v13 on v12

--- a/solution.py
+++ b/solution.py
@@ -54,7 +54,9 @@
         preferred_element_type=jnp.float32,
     )
     above = shard > here
-    sending = jnp.where(above[:, None], local_sum[-1][None, :], local_sum[0][None, :])
+    first_sum = jnp.sum(jnp.where((cluster_ids == first_id[here])[:, None], label_rows, 0.0), axis=0)
+    last_sum = jnp.sum(jnp.where((cluster_ids == last_id[here])[:, None], label_rows, 0.0), axis=0)
+    sending = jnp.where(above[:, None], last_sum[None, :], first_sum[None, :])
     gathered = lax.all_to_all(sending, "label", 0, 0, tiled=True)
 
     doc_unit = unit_rows(features)

time: 93.1 us -> 92.2 us (level)
  blocking collectives: 20.4 us -> 0 us
  waiting for transfers between devices: 34 us -> 47.2 us
  starting transfers between devices: 22.3 us -> 26.7 us
  other arithmetic: 3.95 us -> 5.49 us
    all_to_all x1 -> x0, blocking collectives: 20.4 us -> none  [shards(): lax.all_to_all(partial_value.reshape(groups, L_DEV // groups, depth), 'do...]
    all_to_all x0 -> x1, waiting for transfers between devices: none -> 15.4 us  [shards(): lax.all_to_all(partial_value.reshape(groups, L_DEV // groups, depth), 'do...]
    all_to_all x0 -> x1, starting transfers between devices: none -> 4.47 us  [shards(): lax.all_to_all(partial_value.reshape(groups, L_DEV // groups, depth), 'do...]
    all_to_all x1, waiting for transfers between devices: 15 us -> 12.5 us  [shards(): lax.all_to_all(jnp.broadcast_to(mine[None], (groups,) + mine.shape), 'doc...]
    dot_general x1, matrix products: 1.83 us -> 0.48 us  [shards(): jnp.dot(weights.astype(jnp.float32), gathered, precision=lax.Precision.HI...]
    eq x0 -> x1, other arithmetic: none -> 1.34 us  [shards(): cluster_ids == first_id[here]]
    dynamic_slice x0 -> x2, local copies, waits for them, and re-layouts: none -> 1.25 us  [the longest x1 0.67 us: shards(): last_id[here]]
    dot_general x1, matrix products: 2.66 us -> 3.66 us  [shards(): jnp.dot(incidence, features, precision=lax.Precision.HIGH, preferred_elem...]
  transfers between devices with their start and end apart: 2 -> 3, of which waited for: 2 -> 3; matrix products, arithmetic and copies ran while one was open for 3% -> 6% of each run, Pallas kernels for 0% -> 0%
where the time goes in v13:
time: 92.2 us; the launch traced here: 91.6 us
  waiting for transfers between devices  47.2 us (51%)
  starting transfers between devices  26.7 us (29%)
  matrix products  8.53 us (9%)
  other arithmetic  5.49 us (6%)
  local copies, waits for them, and re-layouts  3.57 us (4%)
    all_to_all x1, waiting for transfers between devices, shards(): gathered = lax.all_to_all(sending, 'label', 0, 0, tiled=True)  19.2 us
    all_to_all x1, starting transfers between devices, shards(): gathered = lax.all_to_all(sending, 'label', 0, 0, tiled=True)  18.6 us
    all_to_all x1, waiting for transfers between devices, shards(): lax.all_to_all(partial_value.reshape(groups, L_DEV // groups, depth), 'do...  15.4 us
    all_to_all x1, waiting for transfers between devices, shards(): lax.all_to_all(jnp.broadcast_to(mine[None], (groups,) + mine.shape), 'doc...  12.5 us
    all_to_all x1, starting transfers between devices, shards(): lax.all_to_all(partial_value.reshape(groups, L_DEV // groups, depth), 'do...  4.47 us
    all_to_all x1, starting transfers between devices, shards(): lax.all_to_all(jnp.broadcast_to(mine[None], (groups,) + mine.shape), 'doc...  3.69 us
    dot_general x1, matrix products, shards(): jnp.dot(incidence, features, precision=lax.Precision.HIGH, preferred_elem...  3.66 us
    dot_general x1, matrix products, shards(): lax.dot_general(doc_unit, centroid, (((1,), (1,)), ((), ())), precision=l...  1.92 us
  transfers between devices with their start and end apart: 3, of which 3 were waited for; matrix products, arithmetic and copies ran while one was open for 6% of the time, Pallas kernels for 0%

profile of v13, /device:TPU:6, one launch (start us, length us, event | category | flops | bytes accessed | tf_op | source)
XLA Modules:
  0.0 91.6 jit_solution(653901666063127458)
XLA Ops:
  0.0 0.8 dynamic_slice.9
  0.8 1.7 %convert_reduce_fusion = f32[256,512]{1,0:T(8,128)S(1)} fusion(s32[16,512]{1,0:T(8,128)} %bitcast.20, s32[256]{0:T(256)S(1)} %dynamic_slice.9), kind=kLoop, calls=%fused_computation | loop fusion | flops 6160384 | bytes 558080 | tf_op jit(solution)/shard_map/reduce_sum | solution.py:27
  2.5 3.7 %fusion = f32[8,32,1024]{2,1,0:T(8,128)} fusion(f32[8,32,512]{2,1,0:T(8,128)S(1)} %bitcast.19, f32[512,1024]{1,0:T(8,128)} %param.4), kind=kOutput, calls=%fused_computation.1 | convolution fusion | flops 805306368 | bytes 3670016 | tf_op jit(solution)/shard_map/dot_general | solution.py:30
  6.1 4.5 %all-to-all-start = ((f32[8,32,1024]{2,1,0:T(8,128)}), f32[8,32,1024]{2,1,0:T(8,128)S(1)}, u32[]{:S(2)}, u32[]{:S(2)}) async-start(f32[8,32,1024]{2,1,0:T(8,128)} %fusion), calls=%async_computation | async-start | bytes 2097152 | tf_op jit(solution)/shard_map/all_to_all | solution.py:35
  10.6 0.3 reduce-window.9
  11.1 15.4 %all-to-all-done = f32[8,32,1024]{2,1,0:T(8,128)S(1)} async-done(((f32[8,32,1024]{2,1,0:T(8,128)}), f32[8,32,1024]{2,1,0:T(8,128)S(1)}, u32[]{:S(2)}, u32[]{:S(2)}) %all-to-all-start) | async-done | bytes 1048608 | tf_op jit(solution)/shard_map/all_to_all | solution.py:35
  26.6 0.1 multiply_reduce_fusion.2
  26.9 1.1 %broadcast_in_dim.35 = f32[8,32,1024]{2,1,0:T(8,128)} broadcast(f32[32,1024]{1,0:T(8,128)S(1)} %broadcast_multiply_fusion), dimensions={1,2} | broadcast | bytes 1179648 | tf_op jit(solution)/shard_map/broadcast_in_dim | solution.py:40
  28.0 3.7 %all-to-all-start.1 = ((f32[8,32,1024]{2,1,0:T(8,128)}), f32[8,32,1024]{2,1,0:T(8,128)S(1)}, u32[]{:S(2)}, u32[]{:S(2)}) async-start(f32[8,32,1024]{2,1,0:T(8,128)} %broadcast_in_dim.35), calls=%async_computation.1 | async-start | bytes 2097152 | tf_op jit(solution)/shard_map/all_to_all | solution.py:39
  31.8 0.2 convert_reduce_fusion.3
  32.0 0.7 dynamic_slice.10
  32.7 0.6 dynamic_slice.11
  33.3 0.2 convert_reduce_fusion.1
  33.5 1.3 %broadcast_compare_fusion = (pred[256]{0:T(512)(128)(4,1)S(1)}, pred[256]{0:T(512)(128)(4,1)S(1)}) fusion(s32[256]{0:T(256)S(1)} %convert_reduce_fusion.1, s32[]{:T(128)} %bitcast.7, s32[]{:T(128)} %bitcast.6), kind=kLoop, calls=%fused_computation.44 | loop fusion | flops 512 | bytes 1544 | tf_op jit(solution)/shard_map/eq | solution.py:57
  35.0 12.5 %all-to-all-done.1 = f32[8,32,1024]{2,1,0:T(8,128)S(1)} async-done(((f32[8,32,1024]{2,1,0:T(8,128)}), f32[8,32,1024]{2,1,0:T(8,128)S(1)}, u32[]{:S(2)}, u32[]{:S(2)}) %all-to-all-start.1) | async-done | bytes 1048608 | tf_op jit(solution)/shard_map/all_to_all | solution.py:39
  47.5 0.2 select_reduce_fusion.1
  47.8 0.9 broadcast_select_fusion
  48.7 18.6 %all-to-all-start.2 = ((f32[64,1,1024]{2,1,0:T(1,128)}), f32[64,1,1024]{2,1,0:T(1,128)S(1)}, u32[]{:S(2)}, u32[]{:S(2)}) async-start(f32[64,1,1024]{2,1,0:T(1,128)} %broadcast_select_fusion), calls=%async_computation.2 | async-start | bytes 524288 | tf_op jit(solution)/shard_map/all_to_all | solution.py:60
  67.3 0.2 multiply_reduce_fusion
  67.5 1.8 %fusion.2 = f32[512,256]{1,0:T(8,128)} fusion(f32[256,1024]{1,0:T(8,128)S(1)} %bitcast.17, f32[512,1024]{1,0:T(8,128)S(1)} %copy-done, f32[512]{0:T(512)S(1)} %add_rsqrt_fusion), kind=kOutput, calls=%fused_computation.4 | convolution fusion | flops 805830656 | bytes 3672064 | tf_op jit(solution)/shard_map/dot_general | solution.py:63
  69.4 19.2 %all-to-all-done.2 = f32[64,1,1024]{2,1,0:T(1,128)S(1)} async-done(((f32[64,1,1024]{2,1,0:T(1,128)}), f32[64,1,1024]{2,1,0:T(1,128)S(1)}, u32[]{:S(2)}, u32[]{:S(2)}) %all-to-all-start.2) | async-done | bytes 262176 | tf_op jit(solution)/shard_map/all_to_all | solution.py:60
  88.6 0.5 fusion.13
  89.1 0.6 multiply_reduce_fusion.1
  89.7 1.9 %fusion.6 = f32[512,256]{1,0:T(8,128)} fusion(f32[512,256]{1,0:T(8,128)S(1)} %copy-done.1, f32[512,1024]{1,0:T(8,128)S(1)} %copy-done, f32[256,1024]{1,0:T(8,128)S(1)} %get-tuple-element.12, f32[512]{0:T(512)S(1)} %add_rsqrt_fusion, f32[256]{0:T(256)S(1)} %add_rsqrt_fusion.1), kind=kOutput, calls=%fused_computation.9 | convolution fusion | flops 806223872 | bytes 4197376 | tf_op jit(solution)/shard_map/dot_general | solution.py:81
  (22 shorter events, 0.7 us)
Async XLA Ops:
  2.5 8.1 %copy-start.2 = (s32[512]{0:T(512)S(1)}, s32[512]{0:T(512)}, u32[]{:S(2)}) copy-start(s32[512]{0:T(512)} %param.7) | copy-start | bytes 6148
  6.1 20.4 %all-to-all-start = ((f32[8,32,1024]{2,1,0:T(8,128)}), f32[8,32,1024]{2,1,0:T(8,128)S(1)}, u32[]{:S(2)}, u32[]{:S(2)}) async-start(f32[8,32,1024]{2,1,0:T(8,128)} %fusion), calls=%async_computation | async-start | bytes 2097152 | tf_op jit(solution)/shard_map/all_to_all | solution.py:35
  28.0 39.3 %copy-start = (f32[512,1024]{1,0:T(8,128)S(1)}, f32[512,1024]{1,0:T(8,128)}, u32[]{:S(2)}) copy-start(f32[512,1024]{1,0:T(8,128)} %param.4) | copy-start | bytes 6291460
  28.0 19.6 %all-to-all-start.1 = ((f32[8,32,1024]{2,1,0:T(8,128)}), f32[8,32,1024]{2,1,0:T(8,128)S(1)}, u32[]{:S(2)}, u32[]{:S(2)}) async-start(f32[8,32,1024]{2,1,0:T(8,128)} %broadcast_in_dim.35), calls=%async_computation.1 | async-start | bytes 2097152 | tf_op jit(solution)/shard_map/all_to_all | solution.py:39
  48.7 39.9 %all-to-all-start.2 = ((f32[64,1,1024]{2,1,0:T(1,128)}), f32[64,1,1024]{2,1,0:T(1,128)S(1)}, u32[]{:S(2)}, u32[]{:S(2)}) async-start(f32[64,1,1024]{2,1,0:T(1,128)} %broadcast_select_fusion), calls=%async_computation.2 | async-start | bytes 524288 | tf_op jit(solution)/shard_map/all_to_all | solution.py:60
  88.6 1.1 %copy-start.1 = (f32[512,256]{1,0:T(8,128)S(1)}, f32[512,256]{1,0:T(8,128)}, u32[]{:S(2)}) copy-start(f32[512,256]{1,0:T(8,128)} %fusion.2) | copy-start | bytes 1572868

commit v14 on v13

--- a/solution.py
+++ b/solution.py
@@ -1,7 +1,7 @@
 import jax
 import jax.numpy as jnp
 from jax import lax
-from jax.sharding import PartitionSpec as P
+from jax.sharding import Mesh, PartitionSpec as P
 
 L_DEV = 256
 
@@ -30,15 +30,28 @@
     partial_value = jnp.dot(
         incidence, features, precision=lax.Precision.HIGH, preferred_element_type=jnp.float32
     )
-    groups = lax.axis_size("doc")
+    chips = lax.axis_size("dy")
     depth = features.shape[1]
+    half = L_DEV // 2
+    core = lax.axis_index("dc")
+    sibling = [(0, 1), (1, 0)]
+    halves = partial_value.reshape(2, half, depth)
+    keep = jnp.where(core == 0, halves[0], halves[1])
+    give = jnp.where(core == 0, halves[1], halves[0])
+    chip_half = keep + lax.ppermute(give, "dc", sibling)
     pieces = lax.all_to_all(
-        partial_value.reshape(groups, L_DEV // groups, depth), "doc", 0, 0, tiled=True
+        chip_half.reshape(chips, half // chips, depth), "dy", 0, 0, tiled=True
     )
     mine = unit_rows(jnp.sum(pieces, axis=0))
-    label_rows = lax.all_to_all(
-        jnp.broadcast_to(mine[None], (groups,) + mine.shape), "doc", 0, 0, tiled=True
-    ).reshape(L_DEV, depth)
+    own_half = lax.all_to_all(
+        jnp.broadcast_to(mine[None], (chips,) + mine.shape), "dy", 0, 0, tiled=True
+    ).reshape(half, depth)
+    other_half = lax.ppermute(own_half, "dc", sibling)
+    label_rows = jnp.where(
+        core == 0,
+        jnp.concatenate([own_half, other_half]),
+        jnp.concatenate([other_half, own_half]),
+    )
 
     starts = jnp.cumsum(cluster_sizes) - cluster_sizes
     cluster_ids = cluster_of(base + slots, starts)
@@ -88,6 +101,9 @@
 
 
 def solution(mesh):
-    in_specs = (P("doc", None), P("doc", None), P(), P())
-    out_specs = P("doc", "label")
-    return jax.shard_map(shards, mesh=mesh, in_specs=in_specs, out_specs=out_specs, check_vma=False)
+    doc = mesh.shape["doc"]
+    split = Mesh(mesh.devices.reshape(doc // 2, 2, -1), ("dy", "dc", "label"))
+    docs = ("dy", "dc")
+    in_specs = (P(docs, None), P(docs, None), P(), P())
+    out_specs = P(docs, "label")
+    return jax.shard_map(shards, mesh=split, in_specs=in_specs, out_specs=out_specs, check_vma=False)

time: 92.2 us -> 87.7 us (0.951)
  waiting for transfers between devices: 47.2 us -> 40.3 us
  starting transfers between devices: 26.7 us -> 30.3 us
  matrix products: 8.53 us -> 6.81 us
    all_to_all x2, waiting for transfers between devices: 28 us -> 16.5 us  [the longest x1 9.24 us: shards(): lax.all_to_all(chip_half.reshape(chips, half // chips, depth), 'dy', 0, 0...]
    ppermute x0 -> x2, starting transfers between devices: none -> 3.83 us  [the longest x1 1.92 us: shards(): chip_half = keep + lax.ppermute(give, 'dc', sibling)]
    all_to_all x1, waiting for transfers between devices: 19.2 us -> 21.5 us  [shards(): gathered = lax.all_to_all(sending, 'label', 0, 0, tiled=True)]
    ppermute x0 -> x2, waiting for transfers between devices: none -> 2.26 us  [the longest x1 1.88 us: shards(): chip_half = keep + lax.ppermute(give, 'dc', sibling)]
    dot_general x1, matrix products: 3.66 us -> 2.67 us  [shards(): jnp.dot(incidence, features, precision=lax.Precision.HIGH, preferred_elem...]
  transfers between devices with their start and end apart: 3 -> 5, of which waited for: 3 -> 5; matrix products, arithmetic and copies ran while one was open for 6% -> 4% of each run, Pallas kernels for 0% -> 0%
where the time goes in v14:
time: 87.7 us; the launch traced here: 87.1 us
  waiting for transfers between devices  40.3 us (46%)
  starting transfers between devices  30.3 us (35%)
  matrix products  6.81 us (8%)
  other arithmetic  6.36 us (7%)
  local copies, waits for them, and re-layouts  3.13 us (4%)
    all_to_all x1, waiting for transfers between devices, shards(): gathered = lax.all_to_all(sending, 'label', 0, 0, tiled=True)  21.5 us
    all_to_all x1, starting transfers between devices, shards(): gathered = lax.all_to_all(sending, 'label', 0, 0, tiled=True)  18.6 us
    all_to_all x1, waiting for transfers between devices, shards(): lax.all_to_all(chip_half.reshape(chips, half // chips, depth), 'dy', 0, 0...  9.24 us
    all_to_all x1, waiting for transfers between devices, shards(): lax.all_to_all(jnp.broadcast_to(mine[None], (chips,) + mine.shape), 'dy',...  7.27 us
    all_to_all x1, starting transfers between devices, shards(): lax.all_to_all(chip_half.reshape(chips, half // chips, depth), 'dy', 0, 0...  4.47 us
    all_to_all x1, starting transfers between devices, shards(): lax.all_to_all(jnp.broadcast_to(mine[None], (chips,) + mine.shape), 'dy',...  3.47 us
    dot_general x1, matrix products, shards(): jnp.dot(incidence, features, precision=lax.Precision.HIGH, preferred_elem...  2.67 us
    ppermute x1, starting transfers between devices, shards(): chip_half = keep + lax.ppermute(give, 'dc', sibling)  1.92 us
  transfers between devices with their start and end apart: 5, of which 5 were waited for; matrix products, arithmetic and copies ran while one was open for 4% of the time, Pallas kernels for 0%

profile of v14, /device:TPU:6, one launch (start us, length us, event | category | flops | bytes accessed | tf_op | source)
XLA Modules:
  0.0 87.1 jit_solution(10315395060800893371)
XLA Ops:
  0.0 0.8 dynamic_slice.9
  0.8 1.7 %convert_reduce_fusion = f32[256,512]{1,0:T(8,128)S(1)} fusion(s32[16,512]{1,0:T(8,128)} %bitcast.17, s32[256]{0:T(256)S(1)} %dynamic_slice.9), kind=kLoop, calls=%fused_computation | loop fusion | flops 6160384 | bytes 558080 | tf_op jit(solution)/shard_map/reduce_sum | solution.py:27
  2.5 2.7 %fusion.27 = f32[256,1024]{1,0:T(8,128)S(1)} fusion(f32[256,512]{1,0:T(8,128)S(1)} %convert_reduce_fusion, f32[512,1024]{1,0:T(8,128)} %param.4), kind=kOutput, calls=%fused_computation.52 | convolution fusion | flops 805306368 | bytes 3670016 | tf_op jit(solution)/shard_map/dot_general | solution.py:30
  5.2 1.9 %collective-permute-start = (f32[128,1024]{1,0:T(8,128)S(1)}, f32[128,1024]{1,0:T(8,128)S(1)}, u32[]{:S(2)}, u32[]{:S(2)}) collective-permute-start(f32[128,1024]{1,0:T(8,128)S(1)} %slice_select_fusion), channel_id=1, source_target_pairs={{0,64},{64,0},{1,65},{65,1},{2,66},{66,2},{3,67},{67,3},{4,68},{68... | collective-permute-start | bytes 1572872 | tf_op jit(solution)/shard_map/ppermute | solution.py:41
  7.2 1.9 %collective-permute-done = f32[128,1024]{1,0:T(8,128)S(1)} collective-permute-done((f32[128,1024]{1,0:T(8,128)S(1)}, f32[128,1024]{1,0:T(8,128)S(1)}, u32[]{:S(2)}, u32[]{:S(2)}) %collective-permute-start) | collective-permute-done | bytes 524320 | tf_op jit(solution)/shard_map/ppermute | solution.py:41
  9.0 0.9 %select_add_fusion = f32[128,1024]{1,0:T(8,128)} fusion(f32[128,1024]{1,0:T(8,128)S(1)} %collective-permute-done, f32[256,1024]{1,0:T(8,128)S(1)} %fusion.27, pred[]{:T(512)S(6)} %eq.78), kind=kLoop, calls=%fused_computation.16 | loop fusion | flops 262144 | bytes 2097153 | tf_op jit(solution)/shard_map/add | solution.py:41
  9.9 4.5 %all-to-all-start = ((f32[4,32,1024]{2,1,0:T(8,128)}), f32[4,32,1024]{2,1,0:T(8,128)S(1)}, u32[]{:S(2)}, u32[]{:S(2)}) async-start(f32[4,32,1024]{2,1,0:T(8,128)} %bitcast.3), calls=%async_computation | async-start | bytes 1048576 | tf_op jit(solution)/shard_map/all_to_all | solution.py:42
  14.4 0.3 reduce-window.9
  14.9 9.2 %all-to-all-done = f32[4,32,1024]{2,1,0:T(8,128)S(1)} async-done(((f32[4,32,1024]{2,1,0:T(8,128)}), f32[4,32,1024]{2,1,0:T(8,128)S(1)}, u32[]{:S(2)}, u32[]{:S(2)}) %all-to-all-start) | async-done | bytes 524320 | tf_op jit(solution)/shard_map/all_to_all | solution.py:42
  24.4 0.8 broadcast_in_dim.35
  25.3 3.5 %all-to-all-start.1 = ((f32[4,32,1024]{2,1,0:T(8,128)}), f32[4,32,1024]{2,1,0:T(8,128)S(1)}, u32[]{:S(2)}, u32[]{:S(2)}) async-start(f32[4,32,1024]{2,1,0:T(8,128)} %broadcast_in_dim.35), calls=%async_computation.1 | async-start | bytes 1048576 | tf_op jit(solution)/shard_map/all_to_all | solution.py:46
  29.1 0.7 dynamic_slice.11
  29.8 0.6 dynamic_slice.10
  30.4 7.3 %all-to-all-done.1 = f32[4,32,1024]{2,1,0:T(8,128)S(1)} async-done(((f32[4,32,1024]{2,1,0:T(8,128)}), f32[4,32,1024]{2,1,0:T(8,128)S(1)}, u32[]{:S(2)}, u32[]{:S(2)}) %all-to-all-start.1) | async-done | bytes 524320 | tf_op jit(solution)/shard_map/all_to_all | solution.py:46
  37.6 1.9 %collective-permute-start.1 = (f32[128,1024]{1,0:T(8,128)S(1)}, f32[128,1024]{1,0:T(8,128)S(1)}, u32[]{:S(2)}, u32[]{:S(2)}) collective-permute-start(f32[128,1024]{1,0:T(8,128)S(1)} %bitcast.13), channel_id=1, source_target_pairs={{0,64},{64,0},{1,65},{65,1},{2,66},{66,2},{3,67},{67,3},{4,68},{68... | collective-permute-start | bytes 1572872 | tf_op jit(solution)/shard_map/ppermute | solution.py:49
  39.8 1.3 %broadcast_compare_fusion = (pred[256]{0:T(512)(128)(4,1)S(1)}, pred[256]{0:T(512)(128)(4,1)S(1)}) fusion(s32[256]{0:T(256)S(1)} %convert_reduce_fusion.1, s32[]{:T(128)} %bitcast.6, s32[]{:T(128)} %bitcast.5), kind=kLoop, calls=%fused_computation.45 | loop fusion | flops 512 | bytes 1544 | tf_op jit(solution)/shard_map/eq | solution.py:70
  41.0 0.4 collective-permute-done.1
  41.7 0.9 %broadcast_select_fusion = f32[64,1,1024]{2,1,0:T(1,128)} fusion(pred[64]{0:T(512)(128)(4,1)S(1)} %iota_compare_fusion, f32[1024]{0:T(1024)S(1)} %get-tuple-element.6, f32[1024]{0:T(1024)S(1)} %get-tuple-element.5), kind=kLoop, calls=%fused_computation.18 | loop fusion | flops 65536 | bytes 270400 | tf_op jit(solution)/shard_map/jit(_where)/select_n | solution.py:72
  42.6 18.6 %all-to-all-start.2 = ((f32[64,1,1024]{2,1,0:T(1,128)}), f32[64,1,1024]{2,1,0:T(1,128)S(1)}, u32[]{:S(2)}, u32[]{:S(2)}) async-start(f32[64,1,1024]{2,1,0:T(1,128)} %broadcast_select_fusion), calls=%async_computation.2 | async-start | bytes 524288 | tf_op jit(solution)/shard_map/all_to_all | solution.py:73
  61.4 21.5 %all-to-all-done.2 = f32[64,1,1024]{2,1,0:T(1,128)S(1)} async-done(((f32[64,1,1024]{2,1,0:T(1,128)}), f32[64,1,1024]{2,1,0:T(1,128)S(1)}, u32[]{:S(2)}, u32[]{:S(2)}) %all-to-all-start.2) | async-done | bytes 262176 | tf_op jit(solution)/shard_map/all_to_all | solution.py:73
  83.0 0.5 fusion.11
  83.4 0.7 multiply_reduce_fusion.1
  84.1 1.1 %fusion.2 = f32[512,256]{1,0:T(8,128)S(1)} fusion(f32[512,1024]{1,0:T(8,128)S(1)} %copy-done, f32[256,1024]{1,0:T(8,128)S(1)} %get-tuple-element.12, f32[512]{0:T(512)S(1)} %add_rsqrt_fusion, f32[256]{0:T(256)S(1)} %add_rsqrt_fusion.1), kind=kOutput, calls=%fused_computation.4 | convolution fusion | flops 806092800 | bytes 3673088 | tf_op jit(solution)/shard_map/dot_general | solution.py:94
  85.3 1.9 %fusion.4 = f32[512,256]{1,0:T(8,128)} fusion(f32[512,256]{1,0:T(8,128)S(1)} %fusion.2, f32[512,1024]{1,0:T(8,128)S(1)} %copy-done, f32[512]{0:T(512)S(1)} %add_rsqrt_fusion, f32[128,1024]{1,0:T(8,128)S(1)} %collective-permute-done.1, f32[128,1024]{1,0:T(8,128)S(1)} %bitcast.16, pred[]{:T(512)S(6)} %eq.78), kind=kOutput, calls=%fused_computation.7 | convolution fusion | flops 806748160 | bytes 4196353 | tf_op jit(solution)/shard_map/dot_general | solution.py:76
  (24 shorter events, 1.6 us)
Async XLA Ops:
  5.1 9.2 %copy-start.1 = (s32[512]{0:T(512)S(1)}, s32[512]{0:T(512)}, u32[]{:S(2)}) copy-start(s32[512]{0:T(512)} %param.7) | copy-start | bytes 6148
  5.2 3.8 %collective-permute-start = (f32[128,1024]{1,0:T(8,128)S(1)}, f32[128,1024]{1,0:T(8,128)S(1)}, u32[]{:S(2)}, u32[]{:S(2)}) collective-permute-start(f32[128,1024]{1,0:T(8,128)S(1)} %slice_select_fusion), channel_id=1, source_target_pairs={{0,64},{64,0},{1,65},{65,1},{2,66},{66,2},{3,67},{67,3},{4,68},{68... | collective-permute-start | bytes 1572872 | tf_op jit(solution)/shard_map/ppermute | solution.py:41
  9.9 14.2 %all-to-all-start = ((f32[4,32,1024]{2,1,0:T(8,128)}), f32[4,32,1024]{2,1,0:T(8,128)S(1)}, u32[]{:S(2)}, u32[]{:S(2)}) async-start(f32[4,32,1024]{2,1,0:T(8,128)} %bitcast.3), calls=%async_computation | async-start | bytes 1048576 | tf_op jit(solution)/shard_map/all_to_all | solution.py:42
  24.2 37.0 %copy-start = (f32[512,1024]{1,0:T(8,128)S(1)}, f32[512,1024]{1,0:T(8,128)}, u32[]{:S(2)}) copy-start(f32[512,1024]{1,0:T(8,128)} %param.4) | copy-start | bytes 6291460
  25.3 12.4 %all-to-all-start.1 = ((f32[4,32,1024]{2,1,0:T(8,128)}), f32[4,32,1024]{2,1,0:T(8,128)S(1)}, u32[]{:S(2)}, u32[]{:S(2)}) async-start(f32[4,32,1024]{2,1,0:T(8,128)} %broadcast_in_dim.35), calls=%async_computation.1 | async-start | bytes 1048576 | tf_op jit(solution)/shard_map/all_to_all | solution.py:46
  37.6 3.8 %collective-permute-start.1 = (f32[128,1024]{1,0:T(8,128)S(1)}, f32[128,1024]{1,0:T(8,128)S(1)}, u32[]{:S(2)}, u32[]{:S(2)}) collective-permute-start(f32[128,1024]{1,0:T(8,128)S(1)} %bitcast.13), channel_id=1, source_target_pairs={{0,64},{64,0},{1,65},{65,1},{2,66},{66,2},{3,67},{67,3},{4,68},{68... | collective-permute-start | bytes 1572872 | tf_op jit(solution)/shard_map/ppermute | solution.py:49
  42.6 40.4 %all-to-all-start.2 = ((f32[64,1,1024]{2,1,0:T(1,128)}), f32[64,1,1024]{2,1,0:T(1,128)S(1)}, u32[]{:S(2)}, u32[]{:S(2)}) async-start(f32[64,1,1024]{2,1,0:T(1,128)} %broadcast_select_fusion), calls=%async_computation.2 | async-start | bytes 524288 | tf_op jit(solution)/shard_map/all_to_all | solution.py:73

commit v15 on v14

--- a/solution.py
+++ b/solution.py
@@ -70,7 +70,10 @@
     first_sum = jnp.sum(jnp.where((cluster_ids == first_id[here])[:, None], label_rows, 0.0), axis=0)
     last_sum = jnp.sum(jnp.where((cluster_ids == last_id[here])[:, None], label_rows, 0.0), axis=0)
     sending = jnp.where(above[:, None], last_sum[None, :], first_sum[None, :])
-    gathered = lax.all_to_all(sending, "label", 0, 0, tiled=True)
+    lanes = 128
+    gathered = lax.all_to_all(
+        sending.reshape(width, -1, lanes), "label", 0, 0, tiled=True
+    ).reshape(width, -1)
 
     doc_unit = unit_rows(features)
     row_scores = lax.dot_general(

time: 87.7 us -> 87.6 us (level)
  no operation moved by 1% of the time
where the time goes in v15:
time: 87.6 us; the launch traced here: 87.1 us
  waiting for transfers between devices  40.3 us (46%)
  starting transfers between devices  30.3 us (35%)
  matrix products  6.81 us (8%)
  other arithmetic  6.29 us (7%)
  local copies, waits for them, and re-layouts  3.13 us (4%)
    all_to_all x1, waiting for transfers between devices, shards(): lax.all_to_all(sending.reshape(width, -1, lanes), 'label', 0, 0, tiled=True)  21.5 us
    all_to_all x1, starting transfers between devices, shards(): lax.all_to_all(sending.reshape(width, -1, lanes), 'label', 0, 0, tiled=True)  18.6 us
    all_to_all x1, waiting for transfers between devices, shards(): lax.all_to_all(chip_half.reshape(chips, half // chips, depth), 'dy', 0, 0...  9.24 us
    all_to_all x1, waiting for transfers between devices, shards(): lax.all_to_all(jnp.broadcast_to(mine[None], (chips,) + mine.shape), 'dy',...  7.27 us
    all_to_all x1, starting transfers between devices, shards(): lax.all_to_all(chip_half.reshape(chips, half // chips, depth), 'dy', 0, 0...  4.47 us
    all_to_all x1, starting transfers between devices, shards(): lax.all_to_all(jnp.broadcast_to(mine[None], (chips,) + mine.shape), 'dy',...  3.47 us
    dot_general x1, matrix products, shards(): jnp.dot(incidence, features, precision=lax.Precision.HIGH, preferred_elem...  2.67 us
    ppermute x1, starting transfers between devices, shards(): chip_half = keep + lax.ppermute(give, 'dc', sibling)  1.92 us
  transfers between devices with their start and end apart: 5, of which 5 were waited for; matrix products, arithmetic and copies ran while one was open for 4% of the time, Pallas kernels for 0%

profile of v15, /device:TPU:6, one launch (start us, length us, event | category | flops | bytes accessed | tf_op | source)
XLA Modules:
  0.0 87.1 jit_solution(14274253654985635971)
XLA Ops:
  0.0 0.8 dynamic_slice.9
  0.8 1.7 %convert_reduce_fusion = f32[256,512]{1,0:T(8,128)S(1)} fusion(s32[16,512]{1,0:T(8,128)} %bitcast.21, s32[256]{0:T(256)S(1)} %dynamic_slice.9), kind=kLoop, calls=%fused_computation | loop fusion | flops 6160384 | bytes 558080 | tf_op jit(solution)/shard_map/reduce_sum | solution.py:27
  2.5 2.7 %fusion.27 = f32[256,1024]{1,0:T(8,128)S(1)} fusion(f32[256,512]{1,0:T(8,128)S(1)} %convert_reduce_fusion, f32[512,1024]{1,0:T(8,128)} %param.4), kind=kOutput, calls=%fused_computation.52 | convolution fusion | flops 805306368 | bytes 3670016 | tf_op jit(solution)/shard_map/dot_general | solution.py:30
  5.2 1.9 %collective-permute-start = (f32[128,1024]{1,0:T(8,128)S(1)}, f32[128,1024]{1,0:T(8,128)S(1)}, u32[]{:S(2)}, u32[]{:S(2)}) collective-permute-start(f32[128,1024]{1,0:T(8,128)S(1)} %slice_select_fusion), channel_id=1, source_target_pairs={{0,64},{64,0},{1,65},{65,1},{2,66},{66,2},{3,67},{67,3},{4,68},{68... | collective-permute-start | bytes 1572872 | tf_op jit(solution)/shard_map/ppermute | solution.py:41
  7.2 1.9 %collective-permute-done = f32[128,1024]{1,0:T(8,128)S(1)} collective-permute-done((f32[128,1024]{1,0:T(8,128)S(1)}, f32[128,1024]{1,0:T(8,128)S(1)}, u32[]{:S(2)}, u32[]{:S(2)}) %collective-permute-start) | collective-permute-done | bytes 524320 | tf_op jit(solution)/shard_map/ppermute | solution.py:41
  9.0 0.9 %select_add_fusion = f32[128,1024]{1,0:T(8,128)} fusion(f32[128,1024]{1,0:T(8,128)S(1)} %collective-permute-done, f32[256,1024]{1,0:T(8,128)S(1)} %fusion.27, pred[]{:T(512)S(6)} %eq.78), kind=kLoop, calls=%fused_computation.16 | loop fusion | flops 262144 | bytes 2097153 | tf_op jit(solution)/shard_map/add | solution.py:41
  9.9 4.5 %all-to-all-start = ((f32[4,32,1024]{2,1,0:T(8,128)}), f32[4,32,1024]{2,1,0:T(8,128)S(1)}, u32[]{:S(2)}, u32[]{:S(2)}) async-start(f32[4,32,1024]{2,1,0:T(8,128)} %bitcast.3), calls=%async_computation | async-start | bytes 1048576 | tf_op jit(solution)/shard_map/all_to_all | solution.py:42
  14.4 0.3 reduce-window.9
  14.9 9.2 %all-to-all-done = f32[4,32,1024]{2,1,0:T(8,128)S(1)} async-done(((f32[4,32,1024]{2,1,0:T(8,128)}), f32[4,32,1024]{2,1,0:T(8,128)S(1)}, u32[]{:S(2)}, u32[]{:S(2)}) %all-to-all-start) | async-done | bytes 524320 | tf_op jit(solution)/shard_map/all_to_all | solution.py:42
  24.4 0.8 broadcast_in_dim.48
  25.3 3.5 %all-to-all-start.1 = ((f32[4,32,1024]{2,1,0:T(8,128)}), f32[4,32,1024]{2,1,0:T(8,128)S(1)}, u32[]{:S(2)}, u32[]{:S(2)}) async-start(f32[4,32,1024]{2,1,0:T(8,128)} %broadcast_in_dim.48), calls=%async_computation.1 | async-start | bytes 1048576 | tf_op jit(solution)/shard_map/all_to_all | solution.py:46
  29.1 0.7 dynamic_slice.11
  29.8 0.6 dynamic_slice.10
  30.4 7.3 %all-to-all-done.1 = f32[4,32,1024]{2,1,0:T(8,128)S(1)} async-done(((f32[4,32,1024]{2,1,0:T(8,128)}), f32[4,32,1024]{2,1,0:T(8,128)S(1)}, u32[]{:S(2)}, u32[]{:S(2)}) %all-to-all-start.1) | async-done | bytes 524320 | tf_op jit(solution)/shard_map/all_to_all | solution.py:46
  37.6 1.9 %collective-permute-start.1 = (f32[128,1024]{1,0:T(8,128)S(1)}, f32[128,1024]{1,0:T(8,128)S(1)}, u32[]{:S(2)}, u32[]{:S(2)}) collective-permute-start(f32[128,1024]{1,0:T(8,128)S(1)} %bitcast.16), channel_id=1, source_target_pairs={{0,64},{64,0},{1,65},{65,1},{2,66},{66,2},{3,67},{67,3},{4,68},{68... | collective-permute-start | bytes 1572872 | tf_op jit(solution)/shard_map/ppermute | solution.py:49
  39.8 1.3 %broadcast_compare_fusion = (pred[256]{0:T(512)(128)(4,1)S(1)}, pred[256]{0:T(512)(128)(4,1)S(1)}) fusion(s32[256]{0:T(256)S(1)} %convert_reduce_fusion.1, s32[]{:T(128)} %bitcast.7, s32[]{:T(128)} %bitcast.5), kind=kLoop, calls=%fused_computation.45 | loop fusion | flops 512 | bytes 1544 | tf_op jit(solution)/shard_map/eq | solution.py:70
  41.0 0.4 collective-permute-done.1
  41.7 0.8 broadcast_select_fusion
  42.5 18.6 %all-to-all-start.2 = ((f32[64,8,128]{2,1,0:T(8,128)}), f32[64,8,128]{2,1,0:T(8,128)S(1)}, u32[]{:S(2)}, u32[]{:S(2)}) async-start(f32[64,8,128]{2,1,0:T(8,128)} %broadcast_select_fusion), calls=%async_computation.2 | async-start | bytes 524288 | tf_op jit(solution)/shard_map/all_to_all | solution.py:74
  61.3 21.5 %all-to-all-done.2 = f32[64,8,128]{2,1,0:T(8,128)S(1)} async-done(((f32[64,8,128]{2,1,0:T(8,128)}), f32[64,8,128]{2,1,0:T(8,128)S(1)}, u32[]{:S(2)}, u32[]{:S(2)}) %all-to-all-start.2) | async-done | bytes 262176 | tf_op jit(solution)/shard_map/all_to_all | solution.py:74
  82.9 0.5 fusion.11
  83.4 0.7 multiply_reduce_fusion.1
  84.0 1.1 %fusion.2 = f32[512,256]{1,0:T(8,128)S(1)} fusion(f32[512,1024]{1,0:T(8,128)S(1)} %copy-done, f32[256,1024]{1,0:T(8,128)S(1)} %get-tuple-element.12, f32[512]{0:T(512)S(1)} %add_rsqrt_fusion, f32[256]{0:T(256)S(1)} %add_rsqrt_fusion.1), kind=kOutput, calls=%fused_computation.4 | convolution fusion | flops 806092800 | bytes 3673088 | tf_op jit(solution)/shard_map/dot_general | solution.py:97
  85.2 1.9 %fusion.4 = f32[512,256]{1,0:T(8,128)} fusion(f32[512,256]{1,0:T(8,128)S(1)} %fusion.2, f32[512,1024]{1,0:T(8,128)S(1)} %copy-done, f32[512]{0:T(512)S(1)} %add_rsqrt_fusion, f32[128,1024]{1,0:T(8,128)S(1)} %collective-permute-done.1, f32[128,1024]{1,0:T(8,128)S(1)} %bitcast.19, pred[]{:T(512)S(6)} %eq.78), kind=kOutput, calls=%fused_computation.7 | convolution fusion | flops 806748160 | bytes 4196353 | tf_op jit(solution)/shard_map/dot_general | solution.py:79
  (24 shorter events, 1.6 us)
Async XLA Ops:
  5.1 9.2 %copy-start.1 = (s32[512]{0:T(512)S(1)}, s32[512]{0:T(512)}, u32[]{:S(2)}) copy-start(s32[512]{0:T(512)} %param.7) | copy-start | bytes 6148
  5.2 3.8 %collective-permute-start = (f32[128,1024]{1,0:T(8,128)S(1)}, f32[128,1024]{1,0:T(8,128)S(1)}, u32[]{:S(2)}, u32[]{:S(2)}) collective-permute-start(f32[128,1024]{1,0:T(8,128)S(1)} %slice_select_fusion), channel_id=1, source_target_pairs={{0,64},{64,0},{1,65},{65,1},{2,66},{66,2},{3,67},{67,3},{4,68},{68... | collective-permute-start | bytes 1572872 | tf_op jit(solution)/shard_map/ppermute | solution.py:41
  9.9 14.2 %all-to-all-start = ((f32[4,32,1024]{2,1,0:T(8,128)}), f32[4,32,1024]{2,1,0:T(8,128)S(1)}, u32[]{:S(2)}, u32[]{:S(2)}) async-start(f32[4,32,1024]{2,1,0:T(8,128)} %bitcast.3), calls=%async_computation | async-start | bytes 1048576 | tf_op jit(solution)/shard_map/all_to_all | solution.py:42
  24.2 36.9 %copy-start = (f32[512,1024]{1,0:T(8,128)S(1)}, f32[512,1024]{1,0:T(8,128)}, u32[]{:S(2)}) copy-start(f32[512,1024]{1,0:T(8,128)} %param.4) | copy-start | bytes 6291460
  25.3 12.4 %all-to-all-start.1 = ((f32[4,32,1024]{2,1,0:T(8,128)}), f32[4,32,1024]{2,1,0:T(8,128)S(1)}, u32[]{:S(2)}, u32[]{:S(2)}) async-start(f32[4,32,1024]{2,1,0:T(8,128)} %broadcast_in_dim.48), calls=%async_computation.1 | async-start | bytes 1048576 | tf_op jit(solution)/shard_map/all_to_all | solution.py:46
  37.6 3.8 %collective-permute-start.1 = (f32[128,1024]{1,0:T(8,128)S(1)}, f32[128,1024]{1,0:T(8,128)S(1)}, u32[]{:S(2)}, u32[]{:S(2)}) collective-permute-start(f32[128,1024]{1,0:T(8,128)S(1)} %bitcast.16), channel_id=1, source_target_pairs={{0,64},{64,0},{1,65},{65,1},{2,66},{66,2},{3,67},{67,3},{4,68},{68... | collective-permute-start | bytes 1572872 | tf_op jit(solution)/shard_map/ppermute | solution.py:49
  42.5 40.4 %all-to-all-start.2 = ((f32[64,8,128]{2,1,0:T(8,128)}), f32[64,8,128]{2,1,0:T(8,128)S(1)}, u32[]{:S(2)}, u32[]{:S(2)}) async-start(f32[64,8,128]{2,1,0:T(8,128)} %broadcast_select_fusion), calls=%async_computation.2 | async-start | bytes 524288 | tf_op jit(solution)/shard_map/all_to_all | solution.py:74

commit v16 on v14

--- a/solution.py
+++ b/solution.py
@@ -70,7 +70,15 @@
     first_sum = jnp.sum(jnp.where((cluster_ids == first_id[here])[:, None], label_rows, 0.0), axis=0)
     last_sum = jnp.sum(jnp.where((cluster_ids == last_id[here])[:, None], label_rows, 0.0), axis=0)
     sending = jnp.where(above[:, None], last_sum[None, :], first_sum[None, :])
-    gathered = lax.all_to_all(sending, "label", 0, 0, tiled=True)
+    lanes = lax.axis_size("dy") * 2
+    lane = lax.axis_index("dy") * 2 + core
+    slice_width = depth // lanes
+    mine_slice = lax.dynamic_slice_in_dim(sending, lane * slice_width, slice_width, axis=1)
+    got = lax.all_to_all(mine_slice, "label", 0, 0, tiled=True)
+    slices = lax.all_to_all(
+        jnp.broadcast_to(got[None], (lanes,) + got.shape), ("dy", "dc"), 0, 0, tiled=True
+    )
+    gathered = jnp.transpose(slices, (1, 0, 2)).reshape(width, depth)
 
     doc_unit = unit_rows(features)
     row_scores = lax.dot_general(

time: 87.7 us -> 92.4 us (1.054)
  the two profiles are of different devices: /device:TPU:6 before, /device:TPU:1 now
where the time goes in v16:
time: 92.4 us; the launch traced here: 91.8 us
  starting transfers between devices  38.5 us (42%)
  waiting for transfers between devices  36.2 us (39%)
  matrix products  6.81 us (7%)
  other arithmetic  6.14 us (7%)
  local copies, waits for them, and re-layouts  4 us (4%)
    all_to_all x1, starting transfers between devices, shards(): got = lax.all_to_all(mine_slice, 'label', 0, 0, tiled=True)  13.3 us
    all_to_all x1, waiting for transfers between devices, shards(): got = lax.all_to_all(mine_slice, 'label', 0, 0, tiled=True)  13.2 us
    ppermute x1, starting transfers between devices, shards(): chip_half = keep + lax.ppermute(give, 'dc', sibling)  8.79 us
    all_to_all x1, waiting for transfers between devices, shards(): lax.all_to_all(chip_half.reshape(chips, half // chips, depth), 'dy', 0, 0...  8.63 us
    all_to_all x1, waiting for transfers between devices, shards(): lax.all_to_all(jnp.broadcast_to(got[None], (lanes,) + got.shape), ('dy',...  6.51 us
    all_to_all x1, waiting for transfers between devices, shards(): lax.all_to_all(jnp.broadcast_to(mine[None], (chips,) + mine.shape), 'dy',...  6.38 us
    all_to_all x1, starting transfers between devices, shards(): lax.all_to_all(jnp.broadcast_to(got[None], (lanes,) + got.shape), ('dy',...  5.11 us
    ppermute x1, starting transfers between devices, shards(): other_half = lax.ppermute(own_half, 'dc', sibling)  4.31 us
  transfers between devices with their start and end apart: 6, of which 5 were waited for; matrix products, arithmetic and copies ran while one was open for 4% of the time, Pallas kernels for 0%

profile of v16, /device:TPU:1, one launch (start us, length us, event | category | flops | bytes accessed | tf_op | source)
XLA Modules:
  0.0 91.8 jit_solution(2672486610281961895)
XLA Ops:
  0.0 0.8 dynamic_slice.12
  0.8 1.7 %convert_reduce_fusion = f32[256,512]{1,0:T(8,128)S(1)} fusion(s32[16,512]{1,0:T(8,128)} %bitcast.25, s32[256]{0:T(256)S(1)} %dynamic_slice.12), kind=kLoop, calls=%fused_computation | loop fusion | flops 6160384 | bytes 558080 | tf_op jit(solution)/shard_map/reduce_sum | solution.py:27
  2.5 2.7 %fusion.27 = f32[256,1024]{1,0:T(8,128)S(1)} fusion(f32[256,512]{1,0:T(8,128)S(1)} %convert_reduce_fusion, f32[512,1024]{1,0:T(8,128)} %param.4), kind=kOutput, calls=%fused_computation.52 | convolution fusion | flops 805306368 | bytes 3670016 | tf_op jit(solution)/shard_map/dot_general | solution.py:30
  5.2 8.8 %collective-permute-start = (f32[128,1024]{1,0:T(8,128)S(1)}, f32[128,1024]{1,0:T(8,128)S(1)}, u32[]{:S(2)}, u32[]{:S(2)}) collective-permute-start(f32[128,1024]{1,0:T(8,128)S(1)} %slice_select_fusion), channel_id=1, source_target_pairs={{0,64},{64,0},{1,65},{65,1},{2,66},{66,2},{3,67},{67,3},{4,68},{68... | collective-permute-start | bytes 1572872 | tf_op jit(solution)/shard_map/ppermute | solution.py:41
  14.0 1.5 %collective-permute-done = f32[128,1024]{1,0:T(8,128)S(1)} collective-permute-done((f32[128,1024]{1,0:T(8,128)S(1)}, f32[128,1024]{1,0:T(8,128)S(1)}, u32[]{:S(2)}, u32[]{:S(2)}) %collective-permute-start) | collective-permute-done | bytes 524320 | tf_op jit(solution)/shard_map/ppermute | solution.py:41
  15.5 0.9 select_add_fusion
  16.4 3.5 %all-to-all-start = ((f32[4,32,1024]{2,1,0:T(8,128)}), f32[4,32,1024]{2,1,0:T(8,128)S(1)}, u32[]{:S(2)}, u32[]{:S(2)}) async-start(f32[4,32,1024]{2,1,0:T(8,128)} %bitcast.3), calls=%async_computation | async-start | bytes 1048576 | tf_op jit(solution)/shard_map/all_to_all | solution.py:42
  20.5 8.6 %all-to-all-done = f32[4,32,1024]{2,1,0:T(8,128)S(1)} async-done(((f32[4,32,1024]{2,1,0:T(8,128)}), f32[4,32,1024]{2,1,0:T(8,128)S(1)}, u32[]{:S(2)}, u32[]{:S(2)}) %all-to-all-start) | async-done | bytes 524320 | tf_op jit(solution)/shard_map/all_to_all | solution.py:42
  29.3 0.8 broadcast_in_dim.48
  30.2 3.5 %all-to-all-start.1 = ((f32[4,32,1024]{2,1,0:T(8,128)}), f32[4,32,1024]{2,1,0:T(8,128)S(1)}, u32[]{:S(2)}, u32[]{:S(2)}) async-start(f32[4,32,1024]{2,1,0:T(8,128)} %broadcast_in_dim.48), calls=%async_computation.1 | async-start | bytes 1048576 | tf_op jit(solution)/shard_map/all_to_all | solution.py:46
  34.0 0.7 dynamic_slice.14
  34.7 0.6 dynamic_slice.13
  35.3 6.4 %all-to-all-done.1 = f32[4,32,1024]{2,1,0:T(8,128)S(1)} async-done(((f32[4,32,1024]{2,1,0:T(8,128)}), f32[4,32,1024]{2,1,0:T(8,128)S(1)}, u32[]{:S(2)}, u32[]{:S(2)}) %all-to-all-start.1) | async-done | bytes 524320 | tf_op jit(solution)/shard_map/all_to_all | solution.py:46
  41.7 4.3 %collective-permute-start.1 = (f32[128,1024]{1,0:T(8,128)S(1)}, f32[128,1024]{1,0:T(8,128)S(1)}, u32[]{:S(2)}, u32[]{:S(2)}) collective-permute-start(f32[128,1024]{1,0:T(8,128)S(1)} %bitcast.20), channel_id=1, source_target_pairs={{0,64},{64,0},{1,65},{65,1},{2,66},{66,2},{3,67},{67,3},{4,68},{68... | collective-permute-start | bytes 1572872 | tf_op jit(solution)/shard_map/ppermute | solution.py:49
  46.2 1.3 %broadcast_compare_fusion = (pred[256]{0:T(512)(128)(4,1)S(1)}, pred[256]{0:T(512)(128)(4,1)S(1)}) fusion(s32[256]{0:T(256)S(1)} %convert_reduce_fusion.1, s32[]{:T(128)} %bitcast.6, s32[]{:T(128)} %bitcast.5), kind=kLoop, calls=%fused_computation.45 | loop fusion | flops 512 | bytes 1544 | tf_op jit(solution)/shard_map/eq | solution.py:70
  47.9 0.7 broadcast_select_fusion
  48.6 13.3 %all-to-all-start.2 = ((f32[64,1,128]{2,1,0:T(1,128)}), f32[64,1,128]{2,1,0:T(1,128)S(1)}, u32[]{:S(2)}, u32[]{:S(2)}) async-start(f32[64,1,128]{2,1,0:T(1,128)} %bitcast.7), calls=%async_computation.2 | async-start | bytes 65536 | tf_op jit(solution)/shard_map/all_to_all | solution.py:77
  62.1 13.2 %all-to-all-done.2 = f32[64,1,128]{2,1,0:T(1,128)S(1)} async-done(((f32[64,1,128]{2,1,0:T(1,128)}), f32[64,1,128]{2,1,0:T(1,128)S(1)}, u32[]{:S(2)}, u32[]{:S(2)}) %all-to-all-start.2) | async-done | bytes 32800 | tf_op jit(solution)/shard_map/all_to_all | solution.py:77
  75.3 0.7 broadcast_in_dim.56
  76.0 5.1 %all-to-all-start.3 = ((f32[8,64,128]{2,1,0:T(8,128)}), f32[8,64,128]{2,1,0:T(8,128)S(1)}, u32[]{:S(2)}, u32[]{:S(2)}) async-start(f32[8,64,128]{2,1,0:T(8,128)} %broadcast_in_dim.56), calls=%async_computation.3 | async-start | bytes 524288 | tf_op jit(solution)/shard_map/all_to_all | solution.py:78
  81.2 6.5 %all-to-all-done.3 = f32[8,64,128]{2,1,0:T(8,128)S(1)} async-done(((f32[8,64,128]{2,1,0:T(8,128)}), f32[8,64,128]{2,1,0:T(8,128)S(1)}, u32[]{:S(2)}, u32[]{:S(2)}) %all-to-all-start.3) | async-done | bytes 262176 | tf_op jit(solution)/shard_map/all_to_all | solution.py:78
  88.2 0.7 multiply_reduce_fusion.1
  88.8 1.1 %fusion.2 = f32[512,256]{1,0:T(8,128)S(1)} fusion(f32[512,1024]{1,0:T(8,128)S(1)} %copy-done, f32[256,1024]{1,0:T(8,128)S(1)} %get-tuple-element.12, f32[512]{0:T(512)S(1)} %add_rsqrt_fusion, f32[256]{0:T(256)S(1)} %add_rsqrt_fusion.1), kind=kOutput, calls=%fused_computation.4 | convolution fusion | flops 806092800 | bytes 3673088 | tf_op jit(solution)/shard_map/dot_general | solution.py:102
  90.0 1.9 %fusion.4 = f32[512,256]{1,0:T(8,128)} fusion(f32[512,256]{1,0:T(8,128)S(1)} %fusion.2, f32[512,1024]{1,0:T(8,128)S(1)} %copy-done, f32[512]{0:T(512)S(1)} %add_rsqrt_fusion, f32[128,1024]{1,0:T(8,128)S(1)} %collective-permute-done.1, f32[128,1024]{1,0:T(8,128)S(1)} %bitcast.23, pred[]{:T(512)S(6)} %eq.78), kind=kOutput, calls=%fused_computation.7 | convolution fusion | flops 806748160 | bytes 4196353 | tf_op jit(solution)/shard_map/dot_general | solution.py:84
  (29 shorter events, 2.5 us)
Async XLA Ops:
  5.1 14.8 %copy-start.1 = (s32[512]{0:T(512)S(1)}, s32[512]{0:T(512)}, u32[]{:S(2)}) copy-start(s32[512]{0:T(512)} %param.7) | copy-start | bytes 6148
  5.2 10.3 %collective-permute-start = (f32[128,1024]{1,0:T(8,128)S(1)}, f32[128,1024]{1,0:T(8,128)S(1)}, u32[]{:S(2)}, u32[]{:S(2)}) collective-permute-start(f32[128,1024]{1,0:T(8,128)S(1)} %slice_select_fusion), channel_id=1, source_target_pairs={{0,64},{64,0},{1,65},{65,1},{2,66},{66,2},{3,67},{67,3},{4,68},{68... | collective-permute-start | bytes 1572872 | tf_op jit(solution)/shard_map/ppermute | solution.py:41
  16.4 12.7 %all-to-all-start = ((f32[4,32,1024]{2,1,0:T(8,128)}), f32[4,32,1024]{2,1,0:T(8,128)S(1)}, u32[]{:S(2)}, u32[]{:S(2)}) async-start(f32[4,32,1024]{2,1,0:T(8,128)} %bitcast.3), calls=%async_computation | async-start | bytes 1048576 | tf_op jit(solution)/shard_map/all_to_all | solution.py:42
  19.9 42.0 %copy-start = (f32[512,1024]{1,0:T(8,128)S(1)}, f32[512,1024]{1,0:T(8,128)}, u32[]{:S(2)}) copy-start(f32[512,1024]{1,0:T(8,128)} %param.4) | copy-start | bytes 6291460
  30.2 11.5 %all-to-all-start.1 = ((f32[4,32,1024]{2,1,0:T(8,128)}), f32[4,32,1024]{2,1,0:T(8,128)S(1)}, u32[]{:S(2)}, u32[]{:S(2)}) async-start(f32[4,32,1024]{2,1,0:T(8,128)} %broadcast_in_dim.48), calls=%async_computation.1 | async-start | bytes 1048576 | tf_op jit(solution)/shard_map/all_to_all | solution.py:46
  41.7 5.8 %collective-permute-start.1 = (f32[128,1024]{1,0:T(8,128)S(1)}, f32[128,1024]{1,0:T(8,128)S(1)}, u32[]{:S(2)}, u32[]{:S(2)}) collective-permute-start(f32[128,1024]{1,0:T(8,128)S(1)} %bitcast.20), channel_id=1, source_target_pairs={{0,64},{64,0},{1,65},{65,1},{2,66},{66,2},{3,67},{67,3},{4,68},{68... | collective-permute-start | bytes 1572872 | tf_op jit(solution)/shard_map/ppermute | solution.py:49
  48.6 26.7 %all-to-all-start.2 = ((f32[64,1,128]{2,1,0:T(1,128)}), f32[64,1,128]{2,1,0:T(1,128)S(1)}, u32[]{:S(2)}, u32[]{:S(2)}) async-start(f32[64,1,128]{2,1,0:T(1,128)} %bitcast.7), calls=%async_computation.2 | async-start | bytes 65536 | tf_op jit(solution)/shard_map/all_to_all | solution.py:77
  76.0 11.6 %all-to-all-start.3 = ((f32[8,64,128]{2,1,0:T(8,128)}), f32[8,64,128]{2,1,0:T(8,128)S(1)}, u32[]{:S(2)}, u32[]{:S(2)}) async-start(f32[8,64,128]{2,1,0:T(8,128)} %broadcast_in_dim.56), calls=%async_computation.3 | async-start | bytes 524288 | tf_op jit(solution)/shard_map/all_to_all | solution.py:78

commit v17 on v15

--- a/solution.py
+++ b/solution.py
@@ -76,12 +76,20 @@
     ).reshape(width, -1)
 
     doc_unit = unit_rows(features)
-    row_scores = lax.dot_general(
-        doc_unit,
-        label_rows,
-        (((1,), (1,)), ((), ())),
-        precision=lax.Precision.HIGH,
-        preferred_element_type=jnp.float32,
+    own_scores, other_scores = (
+        lax.dot_general(
+            doc_unit,
+            rows,
+            (((1,), (1,)), ((), ())),
+            precision=lax.Precision.HIGH,
+            preferred_element_type=jnp.float32,
+        )
+        for rows in (own_half, other_half)
+    )
+    row_scores = jnp.where(
+        core == 0,
+        jnp.concatenate([own_scores, other_scores], axis=1),
+        jnp.concatenate([other_scores, own_scores], axis=1),
     )
     below = shard < here
     take_below = (last_id[None, :] == cluster_ids[:, None]) & below[None, :]

time: 87.6 us -> 87.6 us (level)
  waiting for transfers between devices: 40.3 us -> 37.5 us
  matrix products: 6.81 us -> 9.48 us
    all_to_all x1, waiting for transfers between devices: 21.5 us -> 18.7 us  [shards(): lax.all_to_all(sending.reshape(width, -1, lanes), 'label', 0, 0, tiled=True)]
    dot_general x1, matrix products: 0.48 us -> 1.47 us  [shards(): jnp.dot(weights.astype(jnp.float32), gathered, precision=lax.Precision.HI...]
    dot_general x1 -> x2, matrix products: 1.87 us -> 2.76 us  [shards(): lax.dot_general(doc_unit, rows, (((1,), (1,)), ((), ())), precision=lax.P...]
  transfers between devices with their start and end apart: 5 -> 5, of which waited for: 5 -> 5; matrix products, arithmetic and copies ran while one was open for 4% -> 8% of each run, Pallas kernels for 0% -> 0%
where the time goes in v17:
time: 87.6 us; the launch traced here: 87.1 us
  waiting for transfers between devices  37.5 us (43%)
  starting transfers between devices  30.5 us (35%)
  matrix products  9.48 us (11%)
  other arithmetic  6.29 us (7%)
  local copies, waits for them, and re-layouts  3.13 us (4%)
    all_to_all x1, starting transfers between devices, shards(): lax.all_to_all(sending.reshape(width, -1, lanes), 'label', 0, 0, tiled=True)  18.8 us
    all_to_all x1, waiting for transfers between devices, shards(): lax.all_to_all(sending.reshape(width, -1, lanes), 'label', 0, 0, tiled=True)  18.7 us
    all_to_all x1, waiting for transfers between devices, shards(): lax.all_to_all(chip_half.reshape(chips, half // chips, depth), 'dy', 0, 0...  9.24 us
    all_to_all x1, waiting for transfers between devices, shards(): lax.all_to_all(jnp.broadcast_to(mine[None], (chips,) + mine.shape), 'dy',...  7.27 us
    all_to_all x1, starting transfers between devices, shards(): lax.all_to_all(chip_half.reshape(chips, half // chips, depth), 'dy', 0, 0...  4.47 us
    all_to_all x1, starting transfers between devices, shards(): lax.all_to_all(jnp.broadcast_to(mine[None], (chips,) + mine.shape), 'dy',...  3.47 us
    dot_general x2, matrix products, shards(): lax.dot_general(doc_unit, rows, (((1,), (1,)), ((), ())), precision=lax.P...  2.76 us
    dot_general x1, matrix products, shards(): jnp.dot(incidence, features, precision=lax.Precision.HIGH, preferred_elem...  2.67 us
  transfers between devices with their start and end apart: 5, of which 5 were waited for; matrix products, arithmetic and copies ran while one was open for 8% of the time, Pallas kernels for 0%

profile of v17, /device:TPU:6, one launch (start us, length us, event | category | flops | bytes accessed | tf_op | source)
XLA Modules:
  0.0 87.1 jit_solution(14167324030754111441)
XLA Ops:
  0.0 0.8 dynamic_slice.9
  0.8 1.7 %convert_reduce_fusion = f32[256,512]{1,0:T(8,128)S(1)} fusion(s32[16,512]{1,0:T(8,128)} %bitcast.22, s32[256]{0:T(256)S(1)} %dynamic_slice.9), kind=kLoop, calls=%fused_computation | loop fusion | flops 6160384 | bytes 558080 | tf_op jit(solution)/shard_map/reduce_sum | solution.py:27
  2.5 2.7 %fusion.31 = f32[256,1024]{1,0:T(8,128)S(1)} fusion(f32[256,512]{1,0:T(8,128)S(1)} %convert_reduce_fusion, f32[512,1024]{1,0:T(8,128)} %param.4), kind=kOutput, calls=%fused_computation.57 | convolution fusion | flops 805306368 | bytes 3670016 | tf_op jit(solution)/shard_map/dot_general | solution.py:30
  5.2 1.9 %collective-permute-start = (f32[128,1024]{1,0:T(8,128)S(1)}, f32[128,1024]{1,0:T(8,128)S(1)}, u32[]{:S(2)}, u32[]{:S(2)}) collective-permute-start(f32[128,1024]{1,0:T(8,128)S(1)} %slice_select_fusion), channel_id=1, source_target_pairs={{0,64},{64,0},{1,65},{65,1},{2,66},{66,2},{3,67},{67,3},{4,68},{68... | collective-permute-start | bytes 1572872 | tf_op jit(solution)/shard_map/ppermute | solution.py:41
  7.2 1.9 %collective-permute-done = f32[128,1024]{1,0:T(8,128)S(1)} collective-permute-done((f32[128,1024]{1,0:T(8,128)S(1)}, f32[128,1024]{1,0:T(8,128)S(1)}, u32[]{:S(2)}, u32[]{:S(2)}) %collective-permute-start) | collective-permute-done | bytes 524320 | tf_op jit(solution)/shard_map/ppermute | solution.py:41
  9.0 0.9 %select_add_fusion = f32[128,1024]{1,0:T(8,128)} fusion(f32[128,1024]{1,0:T(8,128)S(1)} %collective-permute-done, f32[256,1024]{1,0:T(8,128)S(1)} %fusion.31, pred[]{:T(512)S(6)} %eq.79), kind=kLoop, calls=%fused_computation.20 | loop fusion | flops 262144 | bytes 2097153 | tf_op jit(solution)/shard_map/add | solution.py:41
  9.9 4.5 %all-to-all-start = ((f32[4,32,1024]{2,1,0:T(8,128)}), f32[4,32,1024]{2,1,0:T(8,128)S(1)}, u32[]{:S(2)}, u32[]{:S(2)}) async-start(f32[4,32,1024]{2,1,0:T(8,128)} %bitcast.3), calls=%async_computation | async-start | bytes 1048576 | tf_op jit(solution)/shard_map/all_to_all | solution.py:42
  14.9 9.2 %all-to-all-done = f32[4,32,1024]{2,1,0:T(8,128)S(1)} async-done(((f32[4,32,1024]{2,1,0:T(8,128)}), f32[4,32,1024]{2,1,0:T(8,128)S(1)}, u32[]{:S(2)}, u32[]{:S(2)}) %all-to-all-start) | async-done | bytes 524320 | tf_op jit(solution)/shard_map/all_to_all | solution.py:42
  24.4 0.8 broadcast_in_dim.48
  25.3 3.5 %all-to-all-start.1 = ((f32[4,32,1024]{2,1,0:T(8,128)}), f32[4,32,1024]{2,1,0:T(8,128)S(1)}, u32[]{:S(2)}, u32[]{:S(2)}) async-start(f32[4,32,1024]{2,1,0:T(8,128)} %broadcast_in_dim.48), calls=%async_computation.1 | async-start | bytes 1048576 | tf_op jit(solution)/shard_map/all_to_all | solution.py:46
  29.1 0.6 dynamic_slice.10
  29.7 0.7 dynamic_slice.11
  30.4 7.3 %all-to-all-done.1 = f32[4,32,1024]{2,1,0:T(8,128)S(1)} async-done(((f32[4,32,1024]{2,1,0:T(8,128)}), f32[4,32,1024]{2,1,0:T(8,128)S(1)}, u32[]{:S(2)}, u32[]{:S(2)}) %all-to-all-start.1) | async-done | bytes 524320 | tf_op jit(solution)/shard_map/all_to_all | solution.py:46
  37.6 1.9 %collective-permute-start.1 = (f32[128,1024]{1,0:T(8,128)S(1)}, f32[128,1024]{1,0:T(8,128)S(1)}, u32[]{:S(2)}, u32[]{:S(2)}) collective-permute-start(f32[128,1024]{1,0:T(8,128)S(1)} %bitcast.18), channel_id=1, source_target_pairs={{0,64},{64,0},{1,65},{65,1},{2,66},{66,2},{3,67},{67,3},{4,68},{68... | collective-permute-start | bytes 1572872 | tf_op jit(solution)/shard_map/ppermute | solution.py:49
  39.8 1.3 %broadcast_compare_fusion = (pred[256]{0:T(512)(128)(4,1)S(1)}, pred[256]{0:T(512)(128)(4,1)S(1)}) fusion(s32[256]{0:T(256)S(1)} %convert_reduce_fusion.1, s32[]{:T(128)} %bitcast.7, s32[]{:T(128)} %bitcast.5), kind=kLoop, calls=%fused_computation.49 | loop fusion | flops 512 | bytes 1544 | tf_op jit(solution)/shard_map/eq | solution.py:70
  41.0 0.4 collective-permute-done.1
  41.7 0.8 broadcast_select_fusion
  42.5 18.8 %all-to-all-start.2 = ((f32[64,8,128]{2,1,0:T(8,128)}), f32[64,8,128]{2,1,0:T(8,128)}, u32[]{:S(2)}, u32[]{:S(2)}) async-start(f32[64,8,128]{2,1,0:T(8,128)} %broadcast_select_fusion), calls=%async_computation.2 | async-start | bytes 524288 | tf_op jit(solution)/shard_map/all_to_all | solution.py:74
  61.5 1.0 %fusion.2 = f32[512,128]{1,0:T(8,128)S(1)} fusion(f32[128,1024]{1,0:T(8,128)S(1)} %bitcast.20, f32[512,1024]{1,0:T(8,128)S(1)} %copy-done, f32[512]{0:T(512)S(1)} %add_rsqrt_fusion), kind=kOutput, calls=%fused_computation.4 | convolution fusion | flops 403177472 | bytes 2885632 | tf_op jit(solution)/shard_map/dot_general | solution.py:80
  62.6 1.7 %fusion = f32[512,128]{1,0:T(8,128)} fusion(f32[128,1024]{1,0:T(8,128)S(1)} %collective-permute-done.1, f32[512,1024]{1,0:T(8,128)S(1)} %copy-done, f32[512]{0:T(512)S(1)} %add_rsqrt_fusion), kind=kOutput, calls=%fused_computation.2 | convolution fusion | flops 403177472 | bytes 2885632 | tf_op jit(solution)/shard_map/dot_general | solution.py:80
  64.3 18.7 %all-to-all-done.2 = f32[64,8,128]{2,1,0:T(8,128)} async-done(((f32[64,8,128]{2,1,0:T(8,128)}), f32[64,8,128]{2,1,0:T(8,128)}, u32[]{:S(2)}, u32[]{:S(2)}) %all-to-all-start.2) | async-done | bytes 262176 | tf_op jit(solution)/shard_map/all_to_all | solution.py:74
  83.0 1.5 %fusion.14 = f32[256,1024]{1,0:T(8,128)S(1)} fusion(f32[8,8,8,128]{3,2,1,0:T(8,128)} %bitcast.9, s32[64]{0:T(128)S(1)} %get-tuple-element.8, s32[64]{0:T(128)S(1)} %get-tuple-element.7, s32[256]{0:T(256)S(1)} %convert_reduce_fusion.1, pred[64]{0:T(512)(128)(4,1)S(1)} %iota_compare_fusion, pred[64]{0:T(512)(128)(4,1)S(1)} %iota_compare_fusion.1), kind=kOutput, calls=%fused_computation.23 | convolution fusion | flops 100745216 | bytes 1312384 | tf_op jit(solution)/shard_map/dot_general | solution.py:98
  84.5 0.7 multiply_reduce_fusion.1
  85.2 1.9 %fusion.6 = f32[512,256]{1,0:T(8,128)} fusion(f32[512,1024]{1,0:T(8,128)S(1)} %copy-done, f32[256,1024]{1,0:T(8,128)S(1)} %get-tuple-element.12, f32[512]{0:T(512)S(1)} %add_rsqrt_fusion, f32[512,128]{1,0:T(8,128)S(1)} %copy-done.1, f32[512,128]{1,0:T(8,128)S(1)} %fusion.2, f32[256]{0:T(256)S(1)} %add_rsqrt_fusion.1, pred[]{:T(512)S(6)} %eq.79), kind=kOutput, calls=%fused_computation.9 | convolution fusion | flops 806617088 | bytes 4197377 | tf_op jit(solution)/shard_map/dot_general | solution.py:105
  (27 shorter events, 1.9 us)
Async XLA Ops:
  5.1 9.2 %copy-start.2 = (s32[512]{0:T(512)S(1)}, s32[512]{0:T(512)}, u32[]{:S(2)}) copy-start(s32[512]{0:T(512)} %param.7) | copy-start | bytes 6148
  5.2 3.8 %collective-permute-start = (f32[128,1024]{1,0:T(8,128)S(1)}, f32[128,1024]{1,0:T(8,128)S(1)}, u32[]{:S(2)}, u32[]{:S(2)}) collective-permute-start(f32[128,1024]{1,0:T(8,128)S(1)} %slice_select_fusion), channel_id=1, source_target_pairs={{0,64},{64,0},{1,65},{65,1},{2,66},{66,2},{3,67},{67,3},{4,68},{68... | collective-permute-start | bytes 1572872 | tf_op jit(solution)/shard_map/ppermute | solution.py:41
  9.9 14.2 %all-to-all-start = ((f32[4,32,1024]{2,1,0:T(8,128)}), f32[4,32,1024]{2,1,0:T(8,128)S(1)}, u32[]{:S(2)}, u32[]{:S(2)}) async-start(f32[4,32,1024]{2,1,0:T(8,128)} %bitcast.3), calls=%async_computation | async-start | bytes 1048576 | tf_op jit(solution)/shard_map/all_to_all | solution.py:42
  24.2 37.1 %copy-start = (f32[512,1024]{1,0:T(8,128)S(1)}, f32[512,1024]{1,0:T(8,128)}, u32[]{:S(2)}) copy-start(f32[512,1024]{1,0:T(8,128)} %param.4) | copy-start | bytes 6291460
  25.3 12.4 %all-to-all-start.1 = ((f32[4,32,1024]{2,1,0:T(8,128)}), f32[4,32,1024]{2,1,0:T(8,128)S(1)}, u32[]{:S(2)}, u32[]{:S(2)}) async-start(f32[4,32,1024]{2,1,0:T(8,128)} %broadcast_in_dim.48), calls=%async_computation.1 | async-start | bytes 1048576 | tf_op jit(solution)/shard_map/all_to_all | solution.py:46
  37.6 3.8 %collective-permute-start.1 = (f32[128,1024]{1,0:T(8,128)S(1)}, f32[128,1024]{1,0:T(8,128)S(1)}, u32[]{:S(2)}, u32[]{:S(2)}) collective-permute-start(f32[128,1024]{1,0:T(8,128)S(1)} %bitcast.18), channel_id=1, source_target_pairs={{0,64},{64,0},{1,65},{65,1},{2,66},{66,2},{3,67},{67,3},{4,68},{68... | collective-permute-start | bytes 1572872 | tf_op jit(solution)/shard_map/ppermute | solution.py:49
  42.5 40.5 %all-to-all-start.2 = ((f32[64,8,128]{2,1,0:T(8,128)}), f32[64,8,128]{2,1,0:T(8,128)}, u32[]{:S(2)}, u32[]{:S(2)}) async-start(f32[64,8,128]{2,1,0:T(8,128)} %broadcast_select_fusion), calls=%async_computation.2 | async-start | bytes 524288 | tf_op jit(solution)/shard_map/all_to_all | solution.py:74
  83.0 2.2 %copy-start.1 = (f32[512,128]{1,0:T(8,128)S(1)}, f32[512,128]{1,0:T(8,128)}, u32[]{:S(2)}) copy-start(f32[512,128]{1,0:T(8,128)} %fusion) | copy-start | bytes 786436

commit v18 on v17

--- a/solution.py
+++ b/solution.py
@@ -59,12 +59,18 @@
     first_id = cluster_of(shard * L_DEV, starts)
     last_id = cluster_of(shard * L_DEV + (L_DEV - 1), starts)
 
-    same_cluster = (cluster_ids[:, None] == cluster_ids[None, :]).astype(jnp.float32)
-    local_sum = jnp.dot(
-        same_cluster,
-        label_rows,
-        precision=lax.Precision.HIGH,
-        preferred_element_type=jnp.float32,
+    half_ids = (
+        cluster_of(base + core * half + jnp.arange(half), starts),
+        cluster_of(base + (1 - core) * half + jnp.arange(half), starts),
+    )
+    local_sum = sum(
+        jnp.dot(
+            (cluster_ids[:, None] == ids[None, :]).astype(jnp.float32),
+            rows,
+            precision=lax.Precision.HIGH,
+            preferred_element_type=jnp.float32,
+        )
+        for ids, rows in zip(half_ids, (own_half, other_half))
     )
     above = shard > here
     first_sum = jnp.sum(jnp.where((cluster_ids == first_id[here])[:, None], label_rows, 0.0), axis=0)

time: 87.6 us -> 87.5 us (level)
  waiting for transfers between devices: 37.5 us -> 36 us
  matrix products: 9.48 us -> 10.5 us
    dot_general x1 -> x2, matrix products: 0.67 us -> 1.96 us  [shards(): jnp.dot((cluster_ids[:, None] == ids[None, :]).astype(jnp.float32), rows,...]
    all_to_all x1, waiting for transfers between devices: 7.27 us -> 8.43 us  [shards(): lax.all_to_all(jnp.broadcast_to(mine[None], (chips,) + mine.shape), 'dy',...]
    all_to_all x1, waiting for transfers between devices: 9.24 us -> 8.13 us  [shards(): lax.all_to_all(chip_half.reshape(chips, half // chips, depth), 'dy', 0, 0...]
    all_to_all x1, waiting for transfers between devices: 18.7 us -> 17.7 us  [shards(): lax.all_to_all(sending.reshape(width, -1, lanes), 'label', 0, 0, tiled=True)]
  transfers between devices with their start and end apart: 5 -> 5, of which waited for: 5 -> 5; matrix products, arithmetic and copies ran while one was open for 8% -> 9% of each run, Pallas kernels for 0% -> 0%
where the time goes in v18:
time: 87.5 us; the launch traced here: 87 us
  waiting for transfers between devices  36 us (41%)
  starting transfers between devices  30.7 us (35%)
  matrix products  10.5 us (12%)
  other arithmetic  6.49 us (7%)
  local copies, waits for them, and re-layouts  3.12 us (4%)
    all_to_all x1, starting transfers between devices, shards(): lax.all_to_all(sending.reshape(width, -1, lanes), 'label', 0, 0, tiled=True)  18.8 us
    all_to_all x1, waiting for transfers between devices, shards(): lax.all_to_all(sending.reshape(width, -1, lanes), 'label', 0, 0, tiled=True)  17.7 us
    all_to_all x1, waiting for transfers between devices, shards(): lax.all_to_all(jnp.broadcast_to(mine[None], (chips,) + mine.shape), 'dy',...  8.43 us
    all_to_all x1, waiting for transfers between devices, shards(): lax.all_to_all(chip_half.reshape(chips, half // chips, depth), 'dy', 0, 0...  8.13 us
    all_to_all x1, starting transfers between devices, shards(): lax.all_to_all(chip_half.reshape(chips, half // chips, depth), 'dy', 0, 0...  4.59 us
    all_to_all x1, starting transfers between devices, shards(): lax.all_to_all(jnp.broadcast_to(mine[None], (chips,) + mine.shape), 'dy',...  3.47 us
    dot_general x1, matrix products, shards(): jnp.dot(incidence, features, precision=lax.Precision.HIGH, preferred_elem...  2.67 us
    dot_general x2, matrix products, shards(): lax.dot_general(doc_unit, rows, (((1,), (1,)), ((), ())), precision=lax.P...  2.05 us
  transfers between devices with their start and end apart: 5, of which 5 were waited for; matrix products, arithmetic and copies ran while one was open for 9% of the time, Pallas kernels for 0%

profile of v18, /device:TPU:6, one launch (start us, length us, event | category | flops | bytes accessed | tf_op | source)
XLA Modules:
  0.0 87.0 jit_solution(13110903542704227145)
XLA Ops:
  0.0 0.8 dynamic_slice.9
  0.8 1.7 %convert_reduce_fusion = f32[256,512]{1,0:T(8,128)S(1)} fusion(s32[16,512]{1,0:T(8,128)} %bitcast.26, s32[256]{0:T(256)S(1)} %dynamic_slice.9), kind=kLoop, calls=%fused_computation | loop fusion | flops 6160384 | bytes 558080 | tf_op jit(solution)/shard_map/reduce_sum | solution.py:27
  2.5 2.7 %fusion.33 = f32[256,1024]{1,0:T(8,128)S(1)} fusion(f32[256,512]{1,0:T(8,128)S(1)} %convert_reduce_fusion, f32[512,1024]{1,0:T(8,128)} %param.4), kind=kOutput, calls=%fused_computation.64 | convolution fusion | flops 805306368 | bytes 3670016 | tf_op jit(solution)/shard_map/dot_general | solution.py:30
  5.2 1.9 %collective-permute-start = (f32[128,1024]{1,0:T(8,128)S(1)}, f32[128,1024]{1,0:T(8,128)S(1)}, u32[]{:S(2)}, u32[]{:S(2)}) collective-permute-start(f32[128,1024]{1,0:T(8,128)S(1)} %slice_select_fusion), channel_id=1, source_target_pairs={{0,64},{64,0},{1,65},{65,1},{2,66},{66,2},{3,67},{67,3},{4,68},{68... | collective-permute-start | bytes 1572872 | tf_op jit(solution)/shard_map/ppermute | solution.py:41
  7.8 1.2 %collective-permute-done = f32[128,1024]{1,0:T(8,128)S(1)} collective-permute-done((f32[128,1024]{1,0:T(8,128)S(1)}, f32[128,1024]{1,0:T(8,128)S(1)}, u32[]{:S(2)}, u32[]{:S(2)}) %collective-permute-start) | collective-permute-done | bytes 524320 | tf_op jit(solution)/shard_map/ppermute | solution.py:41
  9.0 0.9 %select_add_fusion = f32[128,1024]{1,0:T(8,128)} fusion(f32[128,1024]{1,0:T(8,128)S(1)} %collective-permute-done, f32[256,1024]{1,0:T(8,128)S(1)} %fusion.33, pred[]{:T(512)S(6)} %eq.90), kind=kLoop, calls=%fused_computation.21 | loop fusion | flops 262144 | bytes 2097153 | tf_op jit(solution)/shard_map/add | solution.py:41
  9.9 4.6 %all-to-all-start = ((f32[4,32,1024]{2,1,0:T(8,128)}), f32[4,32,1024]{2,1,0:T(8,128)S(1)}, u32[]{:S(2)}, u32[]{:S(2)}) async-start(f32[4,32,1024]{2,1,0:T(8,128)} %bitcast.3), calls=%async_computation | async-start | bytes 1048576 | tf_op jit(solution)/shard_map/all_to_all | solution.py:42
  14.7 0.6 dynamic_slice.10
  15.3 0.7 dynamic_slice.11
  16.2 8.1 %all-to-all-done = f32[4,32,1024]{2,1,0:T(8,128)S(1)} async-done(((f32[4,32,1024]{2,1,0:T(8,128)}), f32[4,32,1024]{2,1,0:T(8,128)S(1)}, u32[]{:S(2)}, u32[]{:S(2)}) %all-to-all-start) | async-done | bytes 524320 | tf_op jit(solution)/shard_map/all_to_all | solution.py:42
  24.5 0.8 broadcast_in_dim.39
  25.4 3.5 %all-to-all-start.1 = ((f32[4,32,1024]{2,1,0:T(8,128)}), f32[4,32,1024]{2,1,0:T(8,128)S(1)}, u32[]{:S(2)}, u32[]{:S(2)}) async-start(f32[4,32,1024]{2,1,0:T(8,128)} %broadcast_in_dim.39), calls=%async_computation.1 | async-start | bytes 1048576 | tf_op jit(solution)/shard_map/all_to_all | solution.py:46
  29.3 8.4 %all-to-all-done.1 = f32[4,32,1024]{2,1,0:T(8,128)S(1)} async-done(((f32[4,32,1024]{2,1,0:T(8,128)}), f32[4,32,1024]{2,1,0:T(8,128)S(1)}, u32[]{:S(2)}, u32[]{:S(2)}) %all-to-all-start.1) | async-done | bytes 524320 | tf_op jit(solution)/shard_map/all_to_all | solution.py:46
  37.7 1.9 %collective-permute-start.1 = (f32[128,1024]{1,0:T(8,128)S(1)}, f32[128,1024]{1,0:T(8,128)S(1)}, u32[]{:S(2)}, u32[]{:S(2)}) collective-permute-start(f32[128,1024]{1,0:T(8,128)S(1)} %bitcast.22), channel_id=1, source_target_pairs={{0,64},{64,0},{1,65},{65,1},{2,66},{66,2},{3,67},{67,3},{4,68},{68... | collective-permute-start | bytes 1572872 | tf_op jit(solution)/shard_map/ppermute | solution.py:49
  39.7 1.3 %broadcast_compare_fusion = (pred[256]{0:T(512)(128)(4,1)S(1)}, pred[256]{0:T(512)(128)(4,1)S(1)}) fusion(s32[256]{0:T(256)S(1)} %convert_reduce_fusion.1, s32[]{:T(128)} %bitcast.7, s32[]{:T(128)} %bitcast.5), kind=kLoop, calls=%fused_computation.55 | loop fusion | flops 512 | bytes 1544 | tf_op jit(solution)/shard_map/eq | solution.py:76
  40.9 0.6 collective-permute-done.1
  41.8 0.8 broadcast_select_fusion
  42.6 18.8 %all-to-all-start.2 = ((f32[64,8,128]{2,1,0:T(8,128)}), f32[64,8,128]{2,1,0:T(8,128)}, u32[]{:S(2)}, u32[]{:S(2)}) async-start(f32[64,8,128]{2,1,0:T(8,128)} %broadcast_select_fusion), calls=%async_computation.2 | async-start | bytes 524288 | tf_op jit(solution)/shard_map/all_to_all | solution.py:80
  61.9 1.0 %fusion.2 = f32[512,128]{1,0:T(8,128)S(1)} fusion(f32[128,1024]{1,0:T(8,128)S(1)} %bitcast.25, f32[512,1024]{1,0:T(8,128)S(1)} %copy-done, f32[512]{0:T(512)S(1)} %add_rsqrt_fusion), kind=kOutput, calls=%fused_computation.4 | convolution fusion | flops 403177472 | bytes 2885632 | tf_op jit(solution)/shard_map/dot_general | solution.py:86
  62.9 1.5 %convolution_add_fusion.1 = f32[256,1024]{1,0:T(8,128)} fusion(f32[256,1024]{1,0:T(8,128)S(1)} %fusion.22, f32[128,1024]{1,0:T(8,128)S(1)} %collective-permute-done.1, s32[128]{0:T(128)S(1)} %get-tuple-element.9, s32[256]{0:T(256)S(1)} %convert_reduce_fusion.1), kind=kOutput, calls=%fused_computation.9 | convolution fusion | flops 201621504 | bytes 2622976 | tf_op jit(solution)/shard_map/dot_general | solution.py:67
  64.4 1.0 %fusion = f32[512,128]{1,0:T(8,128)S(1)} fusion(f32[128,1024]{1,0:T(8,128)S(1)} %collective-permute-done.1, f32[512,1024]{1,0:T(8,128)S(1)} %copy-done, f32[512]{0:T(512)S(1)} %add_rsqrt_fusion), kind=kOutput, calls=%fused_computation.2 | convolution fusion | flops 403177472 | bytes 2885632 | tf_op jit(solution)/shard_map/dot_general | solution.py:86
  65.4 17.7 %all-to-all-done.2 = f32[64,8,128]{2,1,0:T(8,128)} async-done(((f32[64,8,128]{2,1,0:T(8,128)}), f32[64,8,128]{2,1,0:T(8,128)}, u32[]{:S(2)}, u32[]{:S(2)}) %all-to-all-start.2) | async-done | bytes 262176 | tf_op jit(solution)/shard_map/all_to_all | solution.py:80
  83.1 1.9 %multiply_reduce_fusion.1 = (f32[256]{0:T(256)S(1)}, f32[256,1024]{1,0:T(8,128)S(1)}) fusion(f32[256,1024]{1,0:T(8,128)} %convolution_add_fusion.1, f32[8,8,8,128]{3,2,1,0:T(8,128)} %bitcast.9, s32[64]{0:T(128)S(1)} %get-tuple-element.8, s32[64]{0:T(128)S(1)} %get-tuple-element.7, s32[256]{0:T(256)S(1)} %convert_reduce_fusion.1, ...), kind=kOutput, calls=%fused_computation.13 | convolution fusion | flops 101531392 | bytes 2361984 | tf_op jit(solution)/shard_map/dot_general | solution.py:104
  85.1 1.9 %fusion.6 = f32[512,256]{1,0:T(8,128)} fusion(f32[512,1024]{1,0:T(8,128)S(1)} %copy-done, f32[256,1024]{1,0:T(8,128)S(1)} %get-tuple-element.14, f32[512]{0:T(512)S(1)} %add_rsqrt_fusion, f32[512,128]{1,0:T(8,128)S(1)} %fusion, f32[512,128]{1,0:T(8,128)S(1)} %fusion.2, f32[256]{0:T(256)S(1)} %add_rsqrt_fusion.1, pred[]{:T(512)S(6)} %eq.90), kind=kOutput, calls=%fused_computation.10 | convolution fusion | flops 806617088 | bytes 4197377 | tf_op jit(solution)/shard_map/dot_general | solution.py:111
  (28 shorter events, 2.6 us)
Async XLA Ops:
  2.5 4.7 %copy-start.1 = (s32[512]{0:T(512)S(1)}, s32[512]{0:T(512)}, u32[]{:S(2)}) copy-start(s32[512]{0:T(512)} %param.7) | copy-start | bytes 6148
  5.2 3.8 %collective-permute-start = (f32[128,1024]{1,0:T(8,128)S(1)}, f32[128,1024]{1,0:T(8,128)S(1)}, u32[]{:S(2)}, u32[]{:S(2)}) collective-permute-start(f32[128,1024]{1,0:T(8,128)S(1)} %slice_select_fusion), channel_id=1, source_target_pairs={{0,64},{64,0},{1,65},{65,1},{2,66},{66,2},{3,67},{67,3},{4,68},{68... | collective-permute-start | bytes 1572872 | tf_op jit(solution)/shard_map/ppermute | solution.py:41
  9.9 19.2 %copy-start = (f32[512,1024]{1,0:T(8,128)S(1)}, f32[512,1024]{1,0:T(8,128)}, u32[]{:S(2)}) copy-start(f32[512,1024]{1,0:T(8,128)} %param.4) | copy-start | bytes 6291460
  9.9 14.4 %all-to-all-start = ((f32[4,32,1024]{2,1,0:T(8,128)}), f32[4,32,1024]{2,1,0:T(8,128)S(1)}, u32[]{:S(2)}, u32[]{:S(2)}) async-start(f32[4,32,1024]{2,1,0:T(8,128)} %bitcast.3), calls=%async_computation | async-start | bytes 1048576 | tf_op jit(solution)/shard_map/all_to_all | solution.py:42
  25.4 12.4 %all-to-all-start.1 = ((f32[4,32,1024]{2,1,0:T(8,128)}), f32[4,32,1024]{2,1,0:T(8,128)S(1)}, u32[]{:S(2)}, u32[]{:S(2)}) async-start(f32[4,32,1024]{2,1,0:T(8,128)} %broadcast_in_dim.39), calls=%async_computation.1 | async-start | bytes 1048576 | tf_op jit(solution)/shard_map/all_to_all | solution.py:46
  37.7 3.8 %collective-permute-start.1 = (f32[128,1024]{1,0:T(8,128)S(1)}, f32[128,1024]{1,0:T(8,128)S(1)}, u32[]{:S(2)}, u32[]{:S(2)}) collective-permute-start(f32[128,1024]{1,0:T(8,128)S(1)} %bitcast.22), channel_id=1, source_target_pairs={{0,64},{64,0},{1,65},{65,1},{2,66},{66,2},{3,67},{67,3},{4,68},{68... | collective-permute-start | bytes 1572872 | tf_op jit(solution)/shard_map/ppermute | solution.py:49
  42.6 40.5 %all-to-all-start.2 = ((f32[64,8,128]{2,1,0:T(8,128)}), f32[64,8,128]{2,1,0:T(8,128)}, u32[]{:S(2)}, u32[]{:S(2)}) async-start(f32[64,8,128]{2,1,0:T(8,128)} %broadcast_select_fusion), calls=%async_computation.2 | async-start | bytes 524288 | tf_op jit(solution)/shard_map/all_to_all | solution.py:80

commit v19 on v18

--- a/solution.py
+++ b/solution.py
@@ -23,22 +23,24 @@
     base = here * L_DEV
     slots = jnp.arange(L_DEV, dtype=jnp.int32)
 
-    own_perm = lax.dynamic_slice_in_dim(tree_perm, base, L_DEV)
-    incidence = jnp.sum(
-        (doc_labels.T[:, None, :] == own_perm[None, :, None]).astype(jnp.float32), axis=0
-    )
-    partial_value = jnp.dot(
-        incidence, features, precision=lax.Precision.HIGH, preferred_element_type=jnp.float32
-    )
     chips = lax.axis_size("dy")
     depth = features.shape[1]
     half = L_DEV // 2
     core = lax.axis_index("dc")
     sibling = [(0, 1), (1, 0)]
-    halves = partial_value.reshape(2, half, depth)
-    keep = jnp.where(core == 0, halves[0], halves[1])
-    give = jnp.where(core == 0, halves[1], halves[0])
-    chip_half = keep + lax.ppermute(give, "dc", sibling)
+
+    def partial_rows(start):
+        labels = lax.dynamic_slice_in_dim(tree_perm, start, half)
+        incidence = jnp.sum(
+            (doc_labels.T[:, None, :] == labels[None, :, None]).astype(jnp.float32), axis=0
+        )
+        return jnp.dot(
+            incidence, features, precision=lax.Precision.HIGH, preferred_element_type=jnp.float32
+        )
+
+    given = lax.ppermute(partial_rows(base + (1 - core) * half), "dc", sibling)
+    (kept,) = lax.optimization_barrier((partial_rows(base + core * half),))
+    chip_half = kept + given
     pieces = lax.all_to_all(
         chip_half.reshape(chips, half // chips, depth), "dy", 0, 0, tiled=True
     )

time: 87.5 us -> 88.2 us (level)
  matrix products: 10.5 us -> 11.7 us
    dot_general x1 -> x2, matrix products: 2.67 us -> 3.85 us  [partial_rows(): jnp.dot(incidence, features, precision=lax.Precision.HIGH, preferred_elem...]
  transfers between devices with their start and end apart: 5 -> 5, of which waited for: 5 -> 5; matrix products, arithmetic and copies ran while one was open for 9% -> 10% of each run, Pallas kernels for 0% -> 0%
where the time goes in v19:
time: 88.2 us; the launch traced here: 87.7 us
  waiting for transfers between devices  35.5 us (40%)
  starting transfers between devices  30.7 us (35%)
  matrix products  11.7 us (13%)
  other arithmetic  6.38 us (7%)
  local copies, waits for them, and re-layouts  3.29 us (4%)
    all_to_all x1, starting transfers between devices, shards(): lax.all_to_all(sending.reshape(width, -1, lanes), 'label', 0, 0, tiled=True)  18.8 us
    all_to_all x1, waiting for transfers between devices, shards(): lax.all_to_all(sending.reshape(width, -1, lanes), 'label', 0, 0, tiled=True)  17.7 us
    all_to_all x1, waiting for transfers between devices, shards(): lax.all_to_all(jnp.broadcast_to(mine[None], (chips,) + mine.shape), 'dy',...  8.44 us
    all_to_all x1, waiting for transfers between devices, shards(): lax.all_to_all(chip_half.reshape(chips, half // chips, depth), 'dy', 0, 0...  8.12 us
    all_to_all x1, starting transfers between devices, shards(): lax.all_to_all(chip_half.reshape(chips, half // chips, depth), 'dy', 0, 0...  4.46 us
    dot_general x2, matrix products, partial_rows(): jnp.dot(incidence, features, precision=lax.Precision.HIGH, preferred_elem...  3.85 us
    all_to_all x1, starting transfers between devices, shards(): lax.all_to_all(jnp.broadcast_to(mine[None], (chips,) + mine.shape), 'dy',...  3.47 us
    dot_general x2, matrix products, shards(): lax.dot_general(doc_unit, rows, (((1,), (1,)), ((), ())), precision=lax.P...  2.06 us
  transfers between devices with their start and end apart: 5, of which 5 were waited for; matrix products, arithmetic and copies ran while one was open for 10% of the time, Pallas kernels for 0%

profile of v19, /device:TPU:6, one launch (start us, length us, event | category | flops | bytes accessed | tf_op | source)
XLA Modules:
  0.0 87.7 jit_solution(4822442164075007401)
XLA Ops:
  0.0 0.9 %fusion.33 = (s32[128]{0:T(128)S(1)}, s32[128]{0:T(128)S(1)}) fusion(s32[16384]{0:T(1024)} %param.6, s32[]{:T(128)S(6)} %select_n.38, s32[]{:T(128)S(6)} %select_n.39), kind=kLoop, calls=%fused_computation.63 | loop fusion | bytes 2056 | tf_op jit(solution)/shard_map/dynamic_slice | solution.py:33
  0.9 1.7 %convert_reduce_fusion = (f32[128,512]{1,0:T(8,128)S(1)}, f32[128,512]{1,0:T(8,128)S(1)}) fusion(s32[16,512]{1,0:T(8,128)} %bitcast.28, s32[128]{0:T(128)S(1)} %get-tuple-element.14, s32[128]{0:T(128)S(1)} %get-tuple-element.13), kind=kLoop, calls=%fused_computation | loop fusion | flops 6160384 | bytes 558080 | tf_op jit(solution)/shard_map/reduce_sum | solution.py:34
  2.6 3.1 %fusion.35 = f32[128,1024]{1,0:T(8,128)} fusion(f32[128,512]{1,0:T(8,128)S(1)} %get-tuple-element.7, f32[512,1024]{1,0:T(8,128)} %param.4), kind=kOutput, calls=%fused_computation.65 | convolution fusion | flops 402653184 | bytes 2883584 | tf_op jit(solution)/shard_map/dot_general | solution.py:37
  5.7 2.0 %collective-permute-start = (f32[128,1024]{1,0:T(8,128)}, f32[128,1024]{1,0:T(8,128)S(1)}, u32[]{:S(2)}, u32[]{:S(2)}) collective-permute-start(f32[128,1024]{1,0:T(8,128)} %fusion.35), channel_id=1, source_target_pairs={{0,64},{64,0},{1,65},{65,1},{2,66},{66,2},{3,67},{67,3},{4,68},{68... | collective-permute-start | bytes 1572872 | tf_op jit(solution)/shard_map/ppermute | solution.py:41
  7.8 0.7 fusion.34
  9.2 0.6 collective-permute-done
  9.9 0.9 add.113
  10.7 4.5 %all-to-all-start = ((f32[4,32,1024]{2,1,0:T(8,128)}), f32[4,32,1024]{2,1,0:T(8,128)S(1)}, u32[]{:S(2)}, u32[]{:S(2)}) async-start(f32[4,32,1024]{2,1,0:T(8,128)} %bitcast.3), calls=%async_computation | async-start | bytes 1048576 | tf_op jit(solution)/shard_map/all_to_all | solution.py:44
  16.0 0.7 dynamic_slice.15
  16.9 8.1 %all-to-all-done = f32[4,32,1024]{2,1,0:T(8,128)S(1)} async-done(((f32[4,32,1024]{2,1,0:T(8,128)}), f32[4,32,1024]{2,1,0:T(8,128)S(1)}, u32[]{:S(2)}, u32[]{:S(2)}) %all-to-all-start) | async-done | bytes 524320 | tf_op jit(solution)/shard_map/all_to_all | solution.py:44
  25.2 0.8 broadcast_in_dim.39
  26.1 3.5 %all-to-all-start.1 = ((f32[4,32,1024]{2,1,0:T(8,128)}), f32[4,32,1024]{2,1,0:T(8,128)S(1)}, u32[]{:S(2)}, u32[]{:S(2)}) async-start(f32[4,32,1024]{2,1,0:T(8,128)} %broadcast_in_dim.39), calls=%async_computation.1 | async-start | bytes 1048576 | tf_op jit(solution)/shard_map/all_to_all | solution.py:48
  30.0 8.4 %all-to-all-done.1 = f32[4,32,1024]{2,1,0:T(8,128)S(1)} async-done(((f32[4,32,1024]{2,1,0:T(8,128)}), f32[4,32,1024]{2,1,0:T(8,128)S(1)}, u32[]{:S(2)}, u32[]{:S(2)}) %all-to-all-start.1) | async-done | bytes 524320 | tf_op jit(solution)/shard_map/all_to_all | solution.py:48
  38.4 1.9 %collective-permute-start.1 = (f32[128,1024]{1,0:T(8,128)S(1)}, f32[128,1024]{1,0:T(8,128)S(1)}, u32[]{:S(2)}, u32[]{:S(2)}) collective-permute-start(f32[128,1024]{1,0:T(8,128)S(1)} %bitcast.24), channel_id=1, source_target_pairs={{0,64},{64,0},{1,65},{65,1},{2,66},{66,2},{3,67},{67,3},{4,68},{68... | collective-permute-start | bytes 1572872 | tf_op jit(solution)/shard_map/ppermute | solution.py:51
  40.4 1.3 %broadcast_compare_fusion = (pred[256]{0:T(512)(128)(4,1)S(1)}, pred[256]{0:T(512)(128)(4,1)S(1)}) fusion(s32[256]{0:T(256)S(1)} %convert_reduce_fusion.2, s32[]{:T(128)} %bitcast.7, s32[]{:T(128)} %bitcast.5), kind=kLoop, calls=%fused_computation.54 | loop fusion | flops 512 | bytes 1544 | tf_op jit(solution)/shard_map/eq | solution.py:78
  41.6 0.6 collective-permute-done.1
  42.5 0.8 broadcast_select_fusion
  43.3 18.8 %all-to-all-start.2 = ((f32[64,8,128]{2,1,0:T(8,128)}), f32[64,8,128]{2,1,0:T(8,128)}, u32[]{:S(2)}, u32[]{:S(2)}) async-start(f32[64,8,128]{2,1,0:T(8,128)} %broadcast_select_fusion), calls=%async_computation.2 | async-start | bytes 524288 | tf_op jit(solution)/shard_map/all_to_all | solution.py:82
  62.6 1.0 %fusion.2 = f32[512,128]{1,0:T(8,128)S(1)} fusion(f32[128,1024]{1,0:T(8,128)S(1)} %bitcast.27, f32[512,1024]{1,0:T(8,128)S(1)} %copy-done, f32[512]{0:T(512)S(1)} %add_rsqrt_fusion), kind=kOutput, calls=%fused_computation.5 | convolution fusion | flops 403177472 | bytes 2885632 | tf_op jit(solution)/shard_map/dot_general | solution.py:88
  63.6 1.5 %convolution_add_fusion.1 = f32[256,1024]{1,0:T(8,128)} fusion(f32[256,1024]{1,0:T(8,128)S(1)} %fusion.22, f32[128,1024]{1,0:T(8,128)S(1)} %collective-permute-done.1, s32[128]{0:T(128)S(1)} %get-tuple-element.11, s32[256]{0:T(256)S(1)} %convert_reduce_fusion.2), kind=kOutput, calls=%fused_computation.10 | convolution fusion | flops 201621504 | bytes 2622976 | tf_op jit(solution)/shard_map/dot_general | solution.py:69
  65.1 1.0 %fusion = f32[512,128]{1,0:T(8,128)S(1)} fusion(f32[128,1024]{1,0:T(8,128)S(1)} %collective-permute-done.1, f32[512,1024]{1,0:T(8,128)S(1)} %copy-done, f32[512]{0:T(512)S(1)} %add_rsqrt_fusion), kind=kOutput, calls=%fused_computation.3 | convolution fusion | flops 403177472 | bytes 2885632 | tf_op jit(solution)/shard_map/dot_general | solution.py:88
  66.1 17.7 %all-to-all-done.2 = f32[64,8,128]{2,1,0:T(8,128)} async-done(((f32[64,8,128]{2,1,0:T(8,128)}), f32[64,8,128]{2,1,0:T(8,128)}, u32[]{:S(2)}, u32[]{:S(2)}) %all-to-all-start.2) | async-done | bytes 262176 | tf_op jit(solution)/shard_map/all_to_all | solution.py:82
  83.8 1.9 %multiply_reduce_fusion.1 = (f32[256]{0:T(256)S(1)}, f32[256,1024]{1,0:T(8,128)S(1)}) fusion(f32[256,1024]{1,0:T(8,128)} %convolution_add_fusion.1, f32[8,8,8,128]{3,2,1,0:T(8,128)} %bitcast.9, s32[64]{0:T(128)S(1)} %get-tuple-element.10, s32[64]{0:T(128)S(1)} %get-tuple-element.9, s32[256]{0:T(256)S(1)} %convert_reduce_fusion.2, ...), kind=kOutput, calls=%fused_computation.14 | convolution fusion | flops 101531392 | bytes 2361984 | tf_op jit(solution)/shard_map/dot_general | solution.py:106
  85.7 1.9 %fusion.6 = f32[512,256]{1,0:T(8,128)} fusion(f32[512,1024]{1,0:T(8,128)S(1)} %copy-done, f32[256,1024]{1,0:T(8,128)S(1)} %get-tuple-element.18, f32[512]{0:T(512)S(1)} %add_rsqrt_fusion, f32[512,128]{1,0:T(8,128)S(1)} %fusion, f32[512,128]{1,0:T(8,128)S(1)} %fusion.2, f32[256]{0:T(256)S(1)} %add_rsqrt_fusion.1, pred[]{:T(512)S(6)} %eq.113), kind=kOutput, calls=%fused_computation.11 | convolution fusion | flops 806617088 | bytes 4197377 | tf_op jit(solution)/shard_map/dot_general | solution.py:113
  (28 shorter events, 3.1 us)
Async XLA Ops:
  0.0 7.8 %copy-start = (f32[512,1024]{1,0:T(8,128)S(1)}, f32[512,1024]{1,0:T(8,128)}, u32[]{:S(2)}) copy-start(f32[512,1024]{1,0:T(8,128)} %param.4) | copy-start | bytes 6291460
  5.7 2.8 %copy-start.1 = (s32[512]{0:T(512)S(1)}, s32[512]{0:T(512)}, u32[]{:S(2)}) copy-start(s32[512]{0:T(512)} %param.7) | copy-start | bytes 6148
  5.7 4.1 %collective-permute-start = (f32[128,1024]{1,0:T(8,128)}, f32[128,1024]{1,0:T(8,128)S(1)}, u32[]{:S(2)}, u32[]{:S(2)}) collective-permute-start(f32[128,1024]{1,0:T(8,128)} %fusion.35), channel_id=1, source_target_pairs={{0,64},{64,0},{1,65},{65,1},{2,66},{66,2},{3,67},{67,3},{4,68},{68... | collective-permute-start | bytes 1572872 | tf_op jit(solution)/shard_map/ppermute | solution.py:41
  10.7 14.2 %all-to-all-start = ((f32[4,32,1024]{2,1,0:T(8,128)}), f32[4,32,1024]{2,1,0:T(8,128)S(1)}, u32[]{:S(2)}, u32[]{:S(2)}) async-start(f32[4,32,1024]{2,1,0:T(8,128)} %bitcast.3), calls=%async_computation | async-start | bytes 1048576 | tf_op jit(solution)/shard_map/all_to_all | solution.py:44
  26.1 12.4 %all-to-all-start.1 = ((f32[4,32,1024]{2,1,0:T(8,128)}), f32[4,32,1024]{2,1,0:T(8,128)S(1)}, u32[]{:S(2)}, u32[]{:S(2)}) async-start(f32[4,32,1024]{2,1,0:T(8,128)} %broadcast_in_dim.39), calls=%async_computation.1 | async-start | bytes 1048576 | tf_op jit(solution)/shard_map/all_to_all | solution.py:48
  38.4 3.8 %collective-permute-start.1 = (f32[128,1024]{1,0:T(8,128)S(1)}, f32[128,1024]{1,0:T(8,128)S(1)}, u32[]{:S(2)}, u32[]{:S(2)}) collective-permute-start(f32[128,1024]{1,0:T(8,128)S(1)} %bitcast.24), channel_id=1, source_target_pairs={{0,64},{64,0},{1,65},{65,1},{2,66},{66,2},{3,67},{67,3},{4,68},{68... | collective-permute-start | bytes 1572872 | tf_op jit(solution)/shard_map/ppermute | solution.py:51
  43.3 40.5 %all-to-all-start.2 = ((f32[64,8,128]{2,1,0:T(8,128)}), f32[64,8,128]{2,1,0:T(8,128)}, u32[]{:S(2)}, u32[]{:S(2)}) async-start(f32[64,8,128]{2,1,0:T(8,128)} %broadcast_select_fusion), calls=%async_computation.2 | async-start | bytes 524288 | tf_op jit(solution)/shard_map/all_to_all | solution.py:82

commit v20 on v18

--- a/solution.py
+++ b/solution.py
@@ -98,14 +98,14 @@
         jnp.concatenate([other_scores, own_scores], axis=1),
     )
     below = shard < here
-    take_below = (last_id[None, :] == cluster_ids[:, None]) & below[None, :]
-    take_above = (first_id[None, :] == cluster_ids[:, None]) & above[None, :]
-    weights = take_below | take_above
-    cluster_sum = local_sum + jnp.dot(
-        weights.astype(jnp.float32),
-        gathered,
-        precision=lax.Precision.HIGH,
-        preferred_element_type=jnp.float32,
+    extras = []
+    for target in (first_id[here], last_id[here]):
+        use = (below & (last_id == target)) | (above & (first_id == target))
+        extras.append(jnp.sum(jnp.where(use[:, None], gathered, 0.0), axis=0))
+    in_first = (cluster_ids == first_id[here])[:, None]
+    in_last = (cluster_ids == last_id[here])[:, None]
+    cluster_sum = local_sum + jnp.where(
+        in_first, extras[0][None, :], jnp.where(in_last, extras[1][None, :], 0.0)
     )
     centroid = unit_rows(cluster_sum)
     return lax.dot_general(

time: 87.5 us -> 88.8 us (1.015)
  other arithmetic: 6.49 us -> 8.9 us
    dot_general x1 -> x0, matrix products: 1.92 us -> none  [shards(): jnp.dot(weights.astype(jnp.float32), gathered, precision=lax.Precision.HI...]
    dot_general x2, matrix products: 1.96 us -> 3.43 us  [shards(): jnp.dot((cluster_ids[:, None] == ids[None, :]).astype(jnp.float32), rows,...]
    or x0 -> x1, other arithmetic: none -> 1.25 us  [shards(): use = below & (last_id == target) | above & (first_id == target)]
    reduce_sum x0 -> x1, other arithmetic: none -> 1.15 us  [shards(): extras.append(jnp.sum(jnp.where(use[:, None], gathered, 0.0), axis=0))]
  transfers between devices with their start and end apart: 5 -> 5, of which waited for: 5 -> 5; matrix products, arithmetic and copies ran while one was open for 9% -> 10% of each run, Pallas kernels for 0% -> 0%
where the time goes in v20:
time: 88.8 us; the launch traced here: 88.2 us
  waiting for transfers between devices  35.2 us (40%)
  starting transfers between devices  30.7 us (35%)
  matrix products  10.1 us (11%)
  other arithmetic  8.9 us (10%)
  local copies, waits for them, and re-layouts  3.12 us (4%)
    all_to_all x1, starting transfers between devices, shards(): lax.all_to_all(sending.reshape(width, -1, lanes), 'label', 0, 0, tiled=True)  18.8 us
    all_to_all x1, waiting for transfers between devices, shards(): lax.all_to_all(sending.reshape(width, -1, lanes), 'label', 0, 0, tiled=True)  16.9 us
    all_to_all x1, waiting for transfers between devices, shards(): lax.all_to_all(jnp.broadcast_to(mine[None], (chips,) + mine.shape), 'dy',...  8.43 us
    all_to_all x1, waiting for transfers between devices, shards(): lax.all_to_all(chip_half.reshape(chips, half // chips, depth), 'dy', 0, 0...  8.05 us
    all_to_all x1, starting transfers between devices, shards(): lax.all_to_all(chip_half.reshape(chips, half // chips, depth), 'dy', 0, 0...  4.59 us
    all_to_all x1, starting transfers between devices, shards(): lax.all_to_all(jnp.broadcast_to(mine[None], (chips,) + mine.shape), 'dy',...  3.47 us
    dot_general x2, matrix products, shards(): jnp.dot((cluster_ids[:, None] == ids[None, :]).astype(jnp.float32), rows,...  3.43 us
    dot_general x1, matrix products, shards(): jnp.dot(incidence, features, precision=lax.Precision.HIGH, preferred_elem...  2.67 us
  transfers between devices with their start and end apart: 5, of which 5 were waited for; matrix products, arithmetic and copies ran while one was open for 10% of the time, Pallas kernels for 0%

profile of v20, /device:TPU:6, one launch (start us, length us, event | category | flops | bytes accessed | tf_op | source)
XLA Modules:
  0.0 88.2 jit_solution(4857869941560349411)
XLA Ops:
  0.0 0.8 dynamic_slice.6
  0.8 1.7 %convert_reduce_fusion = f32[256,512]{1,0:T(8,128)S(1)} fusion(s32[16,512]{1,0:T(8,128)} %bitcast.22, s32[256]{0:T(256)S(1)} %dynamic_slice.6), kind=kLoop, calls=%fused_computation | loop fusion | flops 6160384 | bytes 558080 | tf_op jit(solution)/shard_map/reduce_sum | solution.py:27
  2.5 2.7 %fusion.22 = f32[256,1024]{1,0:T(8,128)S(1)} fusion(f32[256,512]{1,0:T(8,128)S(1)} %convert_reduce_fusion, f32[512,1024]{1,0:T(8,128)} %param.4), kind=kOutput, calls=%fused_computation.55 | convolution fusion | flops 805306368 | bytes 3670016 | tf_op jit(solution)/shard_map/dot_general | solution.py:30
  5.2 1.9 %collective-permute-start = (f32[128,1024]{1,0:T(8,128)S(1)}, f32[128,1024]{1,0:T(8,128)S(1)}, u32[]{:S(2)}, u32[]{:S(2)}) collective-permute-start(f32[128,1024]{1,0:T(8,128)S(1)} %slice_select_fusion), channel_id=1, source_target_pairs={{0,64},{64,0},{1,65},{65,1},{2,66},{66,2},{3,67},{67,3},{4,68},{68... | collective-permute-start | bytes 1572872 | tf_op jit(solution)/shard_map/ppermute | solution.py:41
  7.8 1.3 %collective-permute-done = f32[128,1024]{1,0:T(8,128)S(1)} collective-permute-done((f32[128,1024]{1,0:T(8,128)S(1)}, f32[128,1024]{1,0:T(8,128)S(1)}, u32[]{:S(2)}, u32[]{:S(2)}) %collective-permute-start) | collective-permute-done | bytes 524320 | tf_op jit(solution)/shard_map/ppermute | solution.py:41
  9.0 0.9 %select_add_fusion = f32[128,1024]{1,0:T(8,128)} fusion(f32[128,1024]{1,0:T(8,128)S(1)} %collective-permute-done, f32[256,1024]{1,0:T(8,128)S(1)} %fusion.22, pred[]{:T(512)S(6)} %eq.106), kind=kLoop, calls=%fused_computation.21 | loop fusion | flops 262144 | bytes 2097153 | tf_op jit(solution)/shard_map/add | solution.py:41
  9.9 4.6 %all-to-all-start = ((f32[4,32,1024]{2,1,0:T(8,128)}), f32[4,32,1024]{2,1,0:T(8,128)S(1)}, u32[]{:S(2)}, u32[]{:S(2)}) async-start(f32[4,32,1024]{2,1,0:T(8,128)} %bitcast.3), calls=%async_computation | async-start | bytes 1048576 | tf_op jit(solution)/shard_map/all_to_all | solution.py:42
  14.8 0.7 dynamic_slice.14
  16.2 8.0 %all-to-all-done = f32[4,32,1024]{2,1,0:T(8,128)S(1)} async-done(((f32[4,32,1024]{2,1,0:T(8,128)}), f32[4,32,1024]{2,1,0:T(8,128)S(1)}, u32[]{:S(2)}, u32[]{:S(2)}) %all-to-all-start) | async-done | bytes 524320 | tf_op jit(solution)/shard_map/all_to_all | solution.py:42
  24.5 0.8 broadcast_in_dim.134
  25.4 3.5 %all-to-all-start.1 = ((f32[4,32,1024]{2,1,0:T(8,128)}), f32[4,32,1024]{2,1,0:T(8,128)S(1)}, u32[]{:S(2)}, u32[]{:S(2)}) async-start(f32[4,32,1024]{2,1,0:T(8,128)} %broadcast_in_dim.134), calls=%async_computation.1 | async-start | bytes 1048576 | tf_op jit(solution)/shard_map/all_to_all | solution.py:46
  29.3 8.4 %all-to-all-done.1 = f32[4,32,1024]{2,1,0:T(8,128)S(1)} async-done(((f32[4,32,1024]{2,1,0:T(8,128)}), f32[4,32,1024]{2,1,0:T(8,128)S(1)}, u32[]{:S(2)}, u32[]{:S(2)}) %all-to-all-start.1) | async-done | bytes 524320 | tf_op jit(solution)/shard_map/all_to_all | solution.py:46
  37.7 1.9 %collective-permute-start.1 = (f32[128,1024]{1,0:T(8,128)S(1)}, f32[128,1024]{1,0:T(8,128)S(1)}, u32[]{:S(2)}, u32[]{:S(2)}) collective-permute-start(f32[128,1024]{1,0:T(8,128)S(1)} %bitcast.18), channel_id=1, source_target_pairs={{0,64},{64,0},{1,65},{65,1},{2,66},{66,2},{3,67},{67,3},{4,68},{68... | collective-permute-start | bytes 1572872 | tf_op jit(solution)/shard_map/ppermute | solution.py:49
  39.7 1.3 %broadcast_compare_fusion.1 = (pred[256]{0:T(512)(128)(4,1)S(1)}, pred[256]{0:T(512)(128)(4,1)S(1)}) fusion(s32[256]{0:T(256)S(1)} %convert_reduce_fusion.1, s32[]{:T(128)} %bitcast.5, s32[]{:T(128)} %bitcast.6), kind=kLoop, calls=%fused_computation.49 | loop fusion | flops 512 | bytes 1544 | tf_op jit(solution)/shard_map/eq | solution.py:105
  41.8 0.8 broadcast_select_fusion
  42.6 18.8 %all-to-all-start.2 = ((f32[64,8,128]{2,1,0:T(8,128)}), f32[64,8,128]{2,1,0:T(8,128)}, u32[]{:S(2)}, u32[]{:S(2)}) async-start(f32[64,8,128]{2,1,0:T(8,128)} %broadcast_select_fusion), calls=%async_computation.2 | async-start | bytes 524288 | tf_op jit(solution)/shard_map/all_to_all | solution.py:80
  61.4 1.3 %and_or_fusion = (pred[64]{0:T(512)(128)(4,1)S(1)}, pred[64]{0:T(512)(128)(4,1)S(1)}) fusion(s32[64]{0:T(128)S(1)} %get-tuple-element.12, s32[64]{0:T(128)S(1)} %get-tuple-element.11, s32[]{:T(128)} %bitcast.6, s32[]{:T(128)S(6)} %axis_index.22, s32[]{:T(128)} %bitcast.5), kind=kLoop, calls=%fused_computation.43 | loop fusion | flops 768 | bytes 652 | tf_op jit(solution)/shard_map/or | solution.py:103
  62.7 1.5 %fusion.16 = f32[256,1024]{1,0:T(8,128)} fusion(f32[128,1024]{1,0:T(8,128)S(1)} %bitcast.20, s32[128]{0:T(128)S(1)} %get-tuple-element.10, s32[256]{0:T(256)S(1)} %convert_reduce_fusion.1), kind=kOutput, calls=%fused_computation.33 | convolution fusion | flops 201359360 | bytes 1574400 | tf_op jit(solution)/shard_map/dot_general | solution.py:67
  64.2 1.0 %fusion.2 = f32[512,128]{1,0:T(8,128)S(1)} fusion(f32[128,1024]{1,0:T(8,128)S(1)} %bitcast.21, f32[512,1024]{1,0:T(8,128)S(1)} %copy-done, f32[512]{0:T(512)S(1)} %add_rsqrt_fusion), kind=kOutput, calls=%fused_computation.4 | convolution fusion | flops 403177472 | bytes 2885632 | tf_op jit(solution)/shard_map/dot_general | solution.py:86
  65.2 1.0 %fusion = f32[512,128]{1,0:T(8,128)S(1)} fusion(f32[128,1024]{1,0:T(8,128)S(1)} %collective-permute-done.1, f32[512,1024]{1,0:T(8,128)S(1)} %copy-done, f32[512]{0:T(512)S(1)} %add_rsqrt_fusion), kind=kOutput, calls=%fused_computation.2 | convolution fusion | flops 403177472 | bytes 2885632 | tf_op jit(solution)/shard_map/dot_general | solution.py:86
  66.2 16.9 %all-to-all-done.2 = f32[64,8,128]{2,1,0:T(8,128)} async-done(((f32[64,8,128]{2,1,0:T(8,128)}), f32[64,8,128]{2,1,0:T(8,128)}, u32[]{:S(2)}, u32[]{:S(2)}) %all-to-all-start.2) | async-done | bytes 262176 | tf_op jit(solution)/shard_map/all_to_all | solution.py:80
  83.1 1.2 %select_reduce_fusion.3 = (f32[8,128]{1,0:T(8,128)S(1)}, f32[8,128]{1,0:T(8,128)S(1)}) fusion(f32[64,8,128]{2,1,0:T(8,128)} %all-to-all-done.2, pred[64]{0:T(512)(128)(4,1)S(1)} %get-tuple-element.14, pred[64]{0:T(512)(128)(4,1)S(1)} %get-tuple-element.13), kind=kLoop, calls=%fused_computation.25 | loop fusion | flops 260096 | bytes 270464 | tf_op jit(solution)/shard_map/reduce_sum | solution.py:104
  84.3 2.0 %multiply_reduce_fusion.1 = (f32[256]{0:T(256)S(1)}, f32[256,1024]{1,0:T(8,128)S(1)}) fusion(f32[1024]{0:T(1024)S(1)} %bitcast.24, pred[256]{0:T(512)(128)(4,1)S(1)} %get-tuple-element.16, f32[1024]{0:T(1024)S(1)} %bitcast.23, pred[256]{0:T(512)(128)(4,1)S(1)} %get-tuple-element.15, f32[256,1024]{1,0:T(8,128)} %fusion.16, ...), kind=kOutput, calls=%fused_computation.13 | convolution fusion | flops 202931968 | bytes 2632704 | tf_op jit(solution)/shard_map/dot_general | solution.py:67
  86.2 1.9 %fusion.7 = f32[512,256]{1,0:T(8,128)} fusion(f32[512,1024]{1,0:T(8,128)S(1)} %copy-done, f32[256,1024]{1,0:T(8,128)S(1)} %get-tuple-element.18, f32[512]{0:T(512)S(1)} %add_rsqrt_fusion, f32[512,128]{1,0:T(8,128)S(1)} %fusion, f32[512,128]{1,0:T(8,128)S(1)} %fusion.2, f32[256]{0:T(256)S(1)} %add_rsqrt_fusion.1, pred[]{:T(512)S(6)} %eq.106), kind=kOutput, calls=%fused_computation.10 | convolution fusion | flops 806617088 | bytes 4197377 | tf_op jit(solution)/shard_map/dot_general | solution.py:111
  (28 shorter events, 3.3 us)
Async XLA Ops:
  2.5 4.7 %copy-start.1 = (s32[512]{0:T(512)S(1)}, s32[512]{0:T(512)}, u32[]{:S(2)}) copy-start(s32[512]{0:T(512)} %param.7) | copy-start | bytes 6148
  5.2 3.8 %collective-permute-start = (f32[128,1024]{1,0:T(8,128)S(1)}, f32[128,1024]{1,0:T(8,128)S(1)}, u32[]{:S(2)}, u32[]{:S(2)}) collective-permute-start(f32[128,1024]{1,0:T(8,128)S(1)} %slice_select_fusion), channel_id=1, source_target_pairs={{0,64},{64,0},{1,65},{65,1},{2,66},{66,2},{3,67},{67,3},{4,68},{68... | collective-permute-start | bytes 1572872 | tf_op jit(solution)/shard_map/ppermute | solution.py:41
  9.9 19.2 %copy-start = (f32[512,1024]{1,0:T(8,128)S(1)}, f32[512,1024]{1,0:T(8,128)}, u32[]{:S(2)}) copy-start(f32[512,1024]{1,0:T(8,128)} %param.4) | copy-start | bytes 6291460
  9.9 14.4 %all-to-all-start = ((f32[4,32,1024]{2,1,0:T(8,128)}), f32[4,32,1024]{2,1,0:T(8,128)S(1)}, u32[]{:S(2)}, u32[]{:S(2)}) async-start(f32[4,32,1024]{2,1,0:T(8,128)} %bitcast.3), calls=%async_computation | async-start | bytes 1048576 | tf_op jit(solution)/shard_map/all_to_all | solution.py:42
  25.4 12.4 %all-to-all-start.1 = ((f32[4,32,1024]{2,1,0:T(8,128)}), f32[4,32,1024]{2,1,0:T(8,128)S(1)}, u32[]{:S(2)}, u32[]{:S(2)}) async-start(f32[4,32,1024]{2,1,0:T(8,128)} %broadcast_in_dim.134), calls=%async_computation.1 | async-start | bytes 1048576 | tf_op jit(solution)/shard_map/all_to_all | solution.py:46
  37.7 3.8 %collective-permute-start.1 = (f32[128,1024]{1,0:T(8,128)S(1)}, f32[128,1024]{1,0:T(8,128)S(1)}, u32[]{:S(2)}, u32[]{:S(2)}) collective-permute-start(f32[128,1024]{1,0:T(8,128)S(1)} %bitcast.18), channel_id=1, source_target_pairs={{0,64},{64,0},{1,65},{65,1},{2,66},{66,2},{3,67},{67,3},{4,68},{68... | collective-permute-start | bytes 1572872 | tf_op jit(solution)/shard_map/ppermute | solution.py:49
  42.6 40.5 %all-to-all-start.2 = ((f32[64,8,128]{2,1,0:T(8,128)}), f32[64,8,128]{2,1,0:T(8,128)}, u32[]{:S(2)}, u32[]{:S(2)}) async-start(f32[64,8,128]{2,1,0:T(8,128)} %broadcast_select_fusion), calls=%async_computation.2 | async-start | bytes 524288 | tf_op jit(solution)/shard_map/all_to_all | solution.py:80

commit v21 on v18

--- a/solution.py
+++ b/solution.py
@@ -97,25 +97,35 @@
         jnp.concatenate([own_scores, other_scores], axis=1),
         jnp.concatenate([other_scores, own_scores], axis=1),
     )
-    below = shard < here
-    take_below = (last_id[None, :] == cluster_ids[:, None]) & below[None, :]
-    take_above = (first_id[None, :] == cluster_ids[:, None]) & above[None, :]
-    weights = take_below | take_above
-    cluster_sum = local_sum + jnp.dot(
-        weights.astype(jnp.float32),
-        gathered,
+    local_scores = lax.dot_general(
+        doc_unit,
+        unit_rows(local_sum),
+        (((1,), (1,)), ((), ())),
         precision=lax.Precision.HIGH,
         preferred_element_type=jnp.float32,
     )
-    centroid = unit_rows(cluster_sum)
-    return lax.dot_general(
+    (local_scores,) = lax.optimization_barrier((local_scores,))
+    below = shard < here
+    targets = (first_id[here], last_id[here])
+    use = jnp.stack(
+        [(below & (last_id == t)) | (above & (first_id == t)) for t in targets]
+    ).astype(jnp.float32)
+    end_sums = jnp.stack([local_sum[0], local_sum[-1]]) + jnp.dot(
+        use, gathered, precision=lax.Precision.HIGH, preferred_element_type=jnp.float32
+    )
+    end_scores = lax.dot_general(
         doc_unit,
-        centroid,
+        unit_rows(end_sums),
         (((1,), (1,)), ((), ())),
         precision=lax.Precision.HIGH,
         preferred_element_type=jnp.float32,
-    ) + row_scores
-
+    )
+    in_first = (cluster_ids == targets[0])[None, :]
+    in_last = (cluster_ids == targets[1])[None, :]
+    centroid_scores = jnp.where(
+        in_first, end_scores[:, :1], jnp.where(in_last, end_scores[:, 1:], local_scores)
+    )
+    return centroid_scores + row_scores
 
 def solution(mesh):
     doc = mesh.shape["doc"]

time: 87.5 us -> 90.6 us (1.035)
  other arithmetic: 6.49 us -> 8.77 us
  matrix products: 10.5 us -> 12.1 us
    dot_general x2, matrix products: 1.96 us -> 3.3 us  [shards(): jnp.dot((cluster_ids[:, None] == ids[None, :]).astype(jnp.float32), rows,...]
    or x0 -> x1, other arithmetic: none -> 1.26 us  [shards(): below & (last_id == t) | above & (first_id == t)]
    ppermute x1, waiting for transfers between devices: 1.17 us -> 0.01 us  [shards(): chip_half = keep + lax.ppermute(give, 'dc', sibling)]
    add x0 -> x1, other arithmetic: none -> 1 us  [shards(): return centroid_scores + row_scores]
    dot_general x2 -> x3, matrix products: 3.85 us -> 3.38 us  [the longest x1 1.25 us: shards(): jnp.dot(use, gathered, precision=lax.Precision.HIGH, preferred_element_ty...]
  transfers between devices with their start and end apart: 5 -> 5, of which waited for: 5 -> 3; matrix products, arithmetic and copies ran while one was open for 9% -> 14% of each run, Pallas kernels for 0% -> 0%
where the time goes in v21:
time: 90.6 us; the launch traced here: 90 us
  waiting for transfers between devices  35.1 us (39%)
  starting transfers between devices  30.7 us (34%)
  matrix products  12.1 us (13%)
  other arithmetic  8.77 us (10%)
  local copies, waits for them, and re-layouts  3.16 us (3%)
    all_to_all x1, starting transfers between devices, shards(): lax.all_to_all(sending.reshape(width, -1, lanes), 'label', 0, 0, tiled=True)  18.8 us
    all_to_all x1, waiting for transfers between devices, shards(): lax.all_to_all(sending.reshape(width, -1, lanes), 'label', 0, 0, tiled=True)  17.3 us
    all_to_all x1, waiting for transfers between devices, shards(): lax.all_to_all(jnp.broadcast_to(mine[None], (chips,) + mine.shape), 'dy',...  9.05 us
    all_to_all x1, waiting for transfers between devices, shards(): lax.all_to_all(chip_half.reshape(chips, half // chips, depth), 'dy', 0, 0...  8.67 us
    all_to_all x1, starting transfers between devices, shards(): lax.all_to_all(chip_half.reshape(chips, half // chips, depth), 'dy', 0, 0...  4.59 us
    all_to_all x1, starting transfers between devices, shards(): lax.all_to_all(jnp.broadcast_to(mine[None], (chips,) + mine.shape), 'dy',...  3.47 us
    dot_general x2, matrix products, shards(): jnp.dot((cluster_ids[:, None] == ids[None, :]).astype(jnp.float32), rows,...  3.3 us
    dot_general x2, matrix products, shards(): lax.dot_general(doc_unit, rows, (((1,), (1,)), ((), ())), precision=lax.P...  2.74 us
  transfers between devices with their start and end apart: 5, of which 3 were waited for; matrix products, arithmetic and copies ran while one was open for 14% of the time, Pallas kernels for 0%

profile of v21, /device:TPU:6, one launch (start us, length us, event | category | flops | bytes accessed | tf_op | source)
XLA Modules:
  0.0 90.0 jit_solution(4813603280182020879)
XLA Ops:
  0.0 0.8 dynamic_slice.12
  0.8 1.7 %convert_reduce_fusion = f32[256,512]{1,0:T(8,128)S(1)} fusion(s32[16,512]{1,0:T(8,128)} %bitcast.46, s32[256]{0:T(256)S(1)} %dynamic_slice.12), kind=kLoop, calls=%fused_computation | loop fusion | flops 6160384 | bytes 558080 | tf_op jit(solution)/shard_map/reduce_sum | solution.py:27
  2.5 2.7 %fusion.39 = f32[256,1024]{1,0:T(8,128)S(1)} fusion(f32[256,512]{1,0:T(8,128)S(1)} %convert_reduce_fusion, f32[512,1024]{1,0:T(8,128)} %param.4), kind=kOutput, calls=%fused_computation.73 | convolution fusion | flops 805306368 | bytes 3670016 | tf_op jit(solution)/shard_map/dot_general | solution.py:30
  5.2 1.9 %collective-permute-start = (f32[128,1024]{1,0:T(8,128)S(1)}, f32[128,1024]{1,0:T(8,128)S(1)}, u32[]{:S(2)}, u32[]{:S(2)}) collective-permute-start(f32[128,1024]{1,0:T(8,128)S(1)} %slice_select_fusion), channel_id=1, source_target_pairs={{0,64},{64,0},{1,65},{65,1},{2,66},{66,2},{3,67},{67,3},{4,68},{68... | collective-permute-start | bytes 1572872 | tf_op jit(solution)/shard_map/ppermute | solution.py:41
  9.5 1.3 %fusion.35 = (pred[1,64]{1,0:T(4,128)(4,1)S(1)}, pred[1,64]{1,0:T(4,128)(4,1)S(1)}) fusion(s32[64]{0:T(128)S(1)} %get-tuple-element.8, s32[64]{0:T(128)S(1)} %get-tuple-element.7, s32[]{:T(128)} %bitcast.2, s32[]{:T(128)S(6)} %axis_index.22, s32[]{:T(128)} %bitcast.8), kind=kLoop, calls=%fused_computation.57 | loop fusion | flops 768 | bytes 652 | tf_op jit(solution)/shard_map/or | solution.py:111
  10.8 0.9 select_add_fusion
  11.7 4.6 %all-to-all-start = ((f32[4,32,1024]{2,1,0:T(8,128)}), f32[4,32,1024]{2,1,0:T(8,128)S(1)}, u32[]{:S(2)}, u32[]{:S(2)}) async-start(f32[4,32,1024]{2,1,0:T(8,128)} %bitcast.4), calls=%async_computation | async-start | bytes 1048576 | tf_op jit(solution)/shard_map/all_to_all | solution.py:42
  16.5 1.3 %broadcast_compare_fusion.1 = (pred[256]{0:T(512)(128)(4,1)S(1)}, pred[256]{0:T(512)(128)(4,1)S(1)}) fusion(s32[256]{0:T(256)S(1)} %convert_reduce_fusion.1, s32[]{:T(128)} %bitcast.2, s32[]{:T(128)} %bitcast.8), kind=kLoop, calls=%fused_computation.67 | loop fusion | flops 512 | bytes 1544 | tf_op jit(solution)/shard_map/eq | solution.py:123
  17.7 8.7 %all-to-all-done = f32[4,32,1024]{2,1,0:T(8,128)S(1)} async-done(((f32[4,32,1024]{2,1,0:T(8,128)}), f32[4,32,1024]{2,1,0:T(8,128)S(1)}, u32[]{:S(2)}, u32[]{:S(2)}) %all-to-all-start) | async-done | bytes 524320 | tf_op jit(solution)/shard_map/all_to_all | solution.py:42
  26.7 0.8 broadcast_in_dim.110
  27.5 3.5 %all-to-all-start.1 = ((f32[4,32,1024]{2,1,0:T(8,128)}), f32[4,32,1024]{2,1,0:T(8,128)S(1)}, u32[]{:S(2)}, u32[]{:S(2)}) async-start(f32[4,32,1024]{2,1,0:T(8,128)} %broadcast_in_dim.110), calls=%async_computation.1 | async-start | bytes 1048576 | tf_op jit(solution)/shard_map/all_to_all | solution.py:46
  31.2 9.1 %all-to-all-done.1 = f32[4,32,1024]{2,1,0:T(8,128)S(1)} async-done(((f32[4,32,1024]{2,1,0:T(8,128)}), f32[4,32,1024]{2,1,0:T(8,128)S(1)}, u32[]{:S(2)}, u32[]{:S(2)}) %all-to-all-start.1) | async-done | bytes 524320 | tf_op jit(solution)/shard_map/all_to_all | solution.py:46
  40.3 1.9 %collective-permute-start.1 = (f32[128,1024]{1,0:T(8,128)S(1)}, f32[128,1024]{1,0:T(8,128)S(1)}, u32[]{:S(2)}, u32[]{:S(2)}) collective-permute-start(f32[128,1024]{1,0:T(8,128)S(1)} %bitcast.42), channel_id=1, source_target_pairs={{0,64},{64,0},{1,65},{65,1},{2,66},{66,2},{3,67},{67,3},{4,68},{68... | collective-permute-start | bytes 1572872 | tf_op jit(solution)/shard_map/ppermute | solution.py:49
  42.2 1.5 %fusion.19 = f32[256,1024]{1,0:T(8,128)} fusion(f32[128,1024]{1,0:T(8,128)S(1)} %bitcast.43, s32[128]{0:T(128)S(1)} %get-tuple-element.10, s32[256]{0:T(256)S(1)} %convert_reduce_fusion.1), kind=kOutput, calls=%fused_computation.36 | convolution fusion | flops 201359360 | bytes 1574400 | tf_op jit(solution)/shard_map/dot_general | solution.py:67
  43.7 1.0 %fusion.2 = f32[512,128]{1,0:T(8,128)S(1)} fusion(f32[128,1024]{1,0:T(8,128)S(1)} %bitcast.44, f32[512,1024]{1,0:T(8,128)S(1)} %copy-done, f32[512]{0:T(512)S(1)} %add_rsqrt_fusion), kind=kOutput, calls=%fused_computation.4 | convolution fusion | flops 403177472 | bytes 2885632 | tf_op jit(solution)/shard_map/dot_general | solution.py:86
  45.0 0.9 broadcast_select_fusion
  45.8 18.8 %all-to-all-start.2 = ((f32[64,8,128]{2,1,0:T(8,128)}), f32[64,8,128]{2,1,0:T(8,128)}, u32[]{:S(2)}, u32[]{:S(2)}) async-start(f32[64,8,128]{2,1,0:T(8,128)} %broadcast_select_fusion), calls=%async_computation.2 | async-start | bytes 524288 | tf_op jit(solution)/shard_map/all_to_all | solution.py:80
  64.6 1.8 %multiply_reduce_fusion.1 = (f32[256]{0:T(256)S(1)}, f32[256,1024]{1,0:T(8,128)S(1)}) fusion(f32[256,1024]{1,0:T(8,128)} %fusion.19, f32[128,1024]{1,0:T(8,128)S(1)} %collective-permute-done.1, s32[128]{0:T(128)S(1)} %get-tuple-element.9, s32[256]{0:T(256)S(1)} %convert_reduce_fusion.1), kind=kOutput, calls=%fused_computation.13 | convolution fusion | flops 202145536 | bytes 2624000 | tf_op jit(solution)/shard_map/dot_general | solution.py:67
  66.5 1.1 %fusion.4 = f32[512,256]{1,0:T(8,128)S(1)} fusion(f32[512,1024]{1,0:T(8,128)S(1)} %copy-done, f32[256,1024]{1,0:T(8,128)S(1)} %get-tuple-element.22, f32[512]{0:T(512)S(1)} %add_rsqrt_fusion, f32[256]{0:T(256)S(1)} %add_rsqrt_fusion.1), kind=kOutput, calls=%fused_computation.6 | convolution fusion | flops 806092800 | bytes 3673088 | tf_op jit(solution)/shard_map/dot_general | solution.py:100
  67.6 1.7 %fusion = f32[512,128]{1,0:T(8,128)} fusion(f32[128,1024]{1,0:T(8,128)S(1)} %collective-permute-done.1, f32[512,1024]{1,0:T(8,128)S(1)} %copy-done, f32[512]{0:T(512)S(1)} %add_rsqrt_fusion), kind=kOutput, calls=%fused_computation.2 | convolution fusion | flops 403177472 | bytes 2885632 | tf_op jit(solution)/shard_map/dot_general | solution.py:86
  69.3 17.3 %all-to-all-done.2 = f32[64,8,128]{2,1,0:T(8,128)} async-done(((f32[64,8,128]{2,1,0:T(8,128)}), f32[64,8,128]{2,1,0:T(8,128)}, u32[]{:S(2)}, u32[]{:S(2)}) %all-to-all-start.2) | async-done | bytes 262176 | tf_op jit(solution)/shard_map/all_to_all | solution.py:80
  86.7 1.3 %multiply_reduce_fusion.3 = (f32[2]{0:T(128)S(1)}, f32[2,1024]{1,0:T(2,128)S(1)}) fusion(f32[8,8,8,128]{3,2,1,0:T(8,128)} %bitcast.15, pred[1,64]{1,0:T(4,128)(4,1)S(1)} %get-tuple-element.16, pred[1,64]{1,0:T(4,128)(4,1)S(1)} %get-tuple-element.15, f32[1,1024]{1,0:T(1,128)S(1)} %get-tuple-element.12, f32[1,1024]{1,0:T(1,128)S(1)} %get-tuple-element.11), kind=kOutput, calls=%fused_computation.45 | convolution fusion | flops 794750 | bytes 278664 | tf_op jit(solution)/shard_map/dot_general | solution.py:113
  87.9 1.0 %fusion.6 = f32[512,2]{0,1:T(2,128)S(1)} fusion(f32[512,1024]{1,0:T(8,128)S(1)} %copy-done, f32[512]{0:T(512)S(1)} %add_rsqrt_fusion, f32[2,1024]{1,0:T(2,128)S(1)} %get-tuple-element.20, f32[2]{0:T(128)S(1)} %add_rsqrt_fusion.2), kind=kOutput, calls=%fused_computation.8 | convolution fusion | flops 6817792 | bytes 2111496 | tf_op jit(solution)/shard_map/dot_general | solution.py:116
  89.0 1.0 %fusion.13 = f32[512,256]{1,0:T(8,128)} fusion(f32[512,128]{1,0:T(8,128)S(1)} %copy-done.1, f32[512,128]{1,0:T(8,128)S(1)} %fusion.2, f32[512,256]{1,0:T(8,128)S(1)} %fusion.4, f32[512]{0:T(512)S(1)} %bitcast.50, f32[512]{0:T(512)S(1)} %bitcast.49, pred[]{:T(512)S(6)} %eq.140, pred[256]{0:T(512)(128)(4,1)S(1)} %get-tuple-element.18, ...), kind=kLoop, calls=%fused_computation.21 | loop fusion | flops 786432 | bytes 1577473 | tf_op jit(solution)/shard_map/add | solution.py:128
  (35 shorter events, 3.4 us)
Async XLA Ops:
  2.5 4.7 %copy-start.2 = (s32[512]{0:T(512)S(1)}, s32[512]{0:T(512)}, u32[]{:S(2)}) copy-start(s32[512]{0:T(512)} %param.7) | copy-start | bytes 6148
  5.2 5.6 %collective-permute-start = (f32[128,1024]{1,0:T(8,128)S(1)}, f32[128,1024]{1,0:T(8,128)S(1)}, u32[]{:S(2)}, u32[]{:S(2)}) collective-permute-start(f32[128,1024]{1,0:T(8,128)S(1)} %slice_select_fusion), channel_id=1, source_target_pairs={{0,64},{64,0},{1,65},{65,1},{2,66},{66,2},{3,67},{67,3},{4,68},{68... | collective-permute-start | bytes 1572872 | tf_op jit(solution)/shard_map/ppermute | solution.py:41
  11.7 19.3 %copy-start = (f32[512,1024]{1,0:T(8,128)S(1)}, f32[512,1024]{1,0:T(8,128)}, u32[]{:S(2)}) copy-start(f32[512,1024]{1,0:T(8,128)} %param.4) | copy-start | bytes 6291460
  11.7 14.7 %all-to-all-start = ((f32[4,32,1024]{2,1,0:T(8,128)}), f32[4,32,1024]{2,1,0:T(8,128)S(1)}, u32[]{:S(2)}, u32[]{:S(2)}) async-start(f32[4,32,1024]{2,1,0:T(8,128)} %bitcast.4), calls=%async_computation | async-start | bytes 1048576 | tf_op jit(solution)/shard_map/all_to_all | solution.py:42
  27.5 12.8 %all-to-all-start.1 = ((f32[4,32,1024]{2,1,0:T(8,128)}), f32[4,32,1024]{2,1,0:T(8,128)S(1)}, u32[]{:S(2)}, u32[]{:S(2)}) async-start(f32[4,32,1024]{2,1,0:T(8,128)} %broadcast_in_dim.110), calls=%async_computation.1 | async-start | bytes 1048576 | tf_op jit(solution)/shard_map/all_to_all | solution.py:46
  40.3 4.4 %collective-permute-start.1 = (f32[128,1024]{1,0:T(8,128)S(1)}, f32[128,1024]{1,0:T(8,128)S(1)}, u32[]{:S(2)}, u32[]{:S(2)}) collective-permute-start(f32[128,1024]{1,0:T(8,128)S(1)} %bitcast.42), channel_id=1, source_target_pairs={{0,64},{64,0},{1,65},{65,1},{2,66},{66,2},{3,67},{67,3},{4,68},{68... | collective-permute-start | bytes 1572872 | tf_op jit(solution)/shard_map/ppermute | solution.py:49
  45.8 40.8 %all-to-all-start.2 = ((f32[64,8,128]{2,1,0:T(8,128)}), f32[64,8,128]{2,1,0:T(8,128)}, u32[]{:S(2)}, u32[]{:S(2)}) async-start(f32[64,8,128]{2,1,0:T(8,128)} %broadcast_select_fusion), calls=%async_computation.2 | async-start | bytes 524288 | tf_op jit(solution)/shard_map/all_to_all | solution.py:80
  69.3 19.6 %copy-start.1 = (f32[512,128]{1,0:T(8,128)S(1)}, f32[512,128]{1,0:T(8,128)}, u32[]{:S(2)}) copy-start(f32[512,128]{1,0:T(8,128)} %fusion) | copy-start | bytes 786436

commit v22 on v18

--- a/solution.py
+++ b/solution.py
@@ -35,9 +35,8 @@
     half = L_DEV // 2
     core = lax.axis_index("dc")
     sibling = [(0, 1), (1, 0)]
-    halves = partial_value.reshape(2, half, depth)
-    keep = jnp.where(core == 0, halves[0], halves[1])
-    give = jnp.where(core == 0, halves[1], halves[0])
+    keep = lax.dynamic_slice_in_dim(partial_value, core * half, half)
+    give = lax.dynamic_slice_in_dim(partial_value, (1 - core) * half, half)
     chip_half = keep + lax.ppermute(give, "dc", sibling)
     pieces = lax.all_to_all(
         chip_half.reshape(chips, half // chips, depth), "dy", 0, 0, tiled=True
@@ -47,11 +46,6 @@
         jnp.broadcast_to(mine[None], (chips,) + mine.shape), "dy", 0, 0, tiled=True
     ).reshape(half, depth)
     other_half = lax.ppermute(own_half, "dc", sibling)
-    label_rows = jnp.where(
-        core == 0,
-        jnp.concatenate([own_half, other_half]),
-        jnp.concatenate([other_half, own_half]),
-    )
 
     starts = jnp.cumsum(cluster_sizes) - cluster_sizes
     cluster_ids = cluster_of(base + slots, starts)
@@ -73,8 +67,13 @@
         for ids, rows in zip(half_ids, (own_half, other_half))
     )
     above = shard > here
-    first_sum = jnp.sum(jnp.where((cluster_ids == first_id[here])[:, None], label_rows, 0.0), axis=0)
-    last_sum = jnp.sum(jnp.where((cluster_ids == last_id[here])[:, None], label_rows, 0.0), axis=0)
+    first_sum, last_sum = (
+        sum(
+            jnp.sum(jnp.where((ids == target)[:, None], rows, 0.0), axis=0)
+            for ids, rows in zip(half_ids, (own_half, other_half))
+        )
+        for target in (first_id[here], last_id[here])
+    )
     sending = jnp.where(above[:, None], last_sum[None, :], first_sum[None, :])
     lanes = 128
     gathered = lax.all_to_all(

time: 87.5 us -> 87.4 us (level)
  waiting for transfers between devices: 36 us -> 34.4 us
  other arithmetic: 6.49 us -> 7.73 us
    eq x1 -> x2, other arithmetic: 1.25 us -> 2.51 us  [shards(): ids == target]
    all_to_all x1, waiting for transfers between devices: 8.43 us -> 7.22 us  [shards(): lax.all_to_all(jnp.broadcast_to(mine[None], (chips,) + mine.shape), 'dy',...]
    all_to_all x1, waiting for transfers between devices: 8.13 us -> 7.07 us  [shards(): lax.all_to_all(chip_half.reshape(chips, half // chips, depth), 'dy', 0, 0...]
    ppermute x1, waiting for transfers between devices: 0.59 us -> 1.48 us  [shards(): other_half = lax.ppermute(own_half, 'dc', sibling)]
  transfers between devices with their start and end apart: 5 -> 5, of which waited for: 5 -> 5; matrix products, arithmetic and copies ran while one was open for 9% -> 11% of each run, Pallas kernels for 0% -> 0%
where the time goes in v22:
time: 87.4 us; the launch traced here: 86.9 us
  waiting for transfers between devices  34.4 us (39%)
  starting transfers between devices  30.7 us (35%)
  matrix products  10.5 us (12%)
  other arithmetic  7.73 us (9%)
  local copies, waits for them, and re-layouts  3.34 us (4%)
    all_to_all x1, starting transfers between devices, shards(): lax.all_to_all(sending.reshape(width, -1, lanes), 'label', 0, 0, tiled=True)  18.8 us
    all_to_all x1, waiting for transfers between devices, shards(): lax.all_to_all(sending.reshape(width, -1, lanes), 'label', 0, 0, tiled=True)  17.7 us
    all_to_all x1, waiting for transfers between devices, shards(): lax.all_to_all(jnp.broadcast_to(mine[None], (chips,) + mine.shape), 'dy',...  7.22 us
    all_to_all x1, waiting for transfers between devices, shards(): lax.all_to_all(chip_half.reshape(chips, half // chips, depth), 'dy', 0, 0...  7.07 us
    all_to_all x1, starting transfers between devices, shards(): lax.all_to_all(chip_half.reshape(chips, half // chips, depth), 'dy', 0, 0...  4.59 us
    all_to_all x1, starting transfers between devices, shards(): lax.all_to_all(jnp.broadcast_to(mine[None], (chips,) + mine.shape), 'dy',...  3.47 us
    dot_general x1, matrix products, shards(): jnp.dot(incidence, features, precision=lax.Precision.HIGH, preferred_elem...  2.67 us
    eq x2, other arithmetic, shards(): ids == target  2.51 us
  transfers between devices with their start and end apart: 5, of which 5 were waited for; matrix products, arithmetic and copies ran while one was open for 11% of the time, Pallas kernels for 0%

profile of v22, /device:TPU:6, one launch (start us, length us, event | category | flops | bytes accessed | tf_op | source)
XLA Modules:
  0.0 86.9 jit_solution(13522458709529888022)
XLA Ops:
  0.0 0.8 dynamic_slice.15
  0.8 1.7 %convert_reduce_fusion = f32[256,512]{1,0:T(8,128)S(1)} fusion(s32[16,512]{1,0:T(8,128)} %bitcast.27, s32[256]{0:T(256)S(1)} %dynamic_slice.15), kind=kLoop, calls=%fused_computation | loop fusion | flops 6160384 | bytes 558080 | tf_op jit(solution)/shard_map/reduce_sum | solution.py:27
  2.5 2.7 %fusion.33 = f32[256,1024]{1,0:T(8,128)S(1)} fusion(f32[256,512]{1,0:T(8,128)S(1)} %convert_reduce_fusion, f32[512,1024]{1,0:T(8,128)} %param.4), kind=kOutput, calls=%fused_computation.69 | convolution fusion | flops 805306368 | bytes 3670016 | tf_op jit(solution)/shard_map/dot_general | solution.py:30
  5.2 1.9 %collective-permute-start = (f32[128,1024]{1,0:T(8,128)S(1)}, f32[128,1024]{1,0:T(8,128)S(1)}, u32[]{:S(2)}, u32[]{:S(2)}) collective-permute-start(f32[128,1024]{1,0:T(8,128)S(1)} %constant_dynamic-slice_fusion), channel_id=1, source_target_pairs={{0,64},{64,0},{1,65},{65,1},{2,66},{66,2},{3,67},{67,3},{4,68},{68... | collective-permute-start | bytes 1572872 | tf_op jit(solution)/shard_map/ppermute | solution.py:40
  8.1 0.9 %collective-permute-done = f32[128,1024]{1,0:T(8,128)S(1)} collective-permute-done((f32[128,1024]{1,0:T(8,128)S(1)}, f32[128,1024]{1,0:T(8,128)S(1)}, u32[]{:S(2)}, u32[]{:S(2)}) %collective-permute-start) | collective-permute-done | bytes 524320 | tf_op jit(solution)/shard_map/ppermute | solution.py:40
  9.0 0.9 dynamic-slice_add_fusion
  9.9 4.6 %all-to-all-start = ((f32[4,32,1024]{2,1,0:T(8,128)}), f32[4,32,1024]{2,1,0:T(8,128)S(1)}, u32[]{:S(2)}, u32[]{:S(2)}) async-start(f32[4,32,1024]{2,1,0:T(8,128)} %bitcast.3), calls=%async_computation | async-start | bytes 1048576 | tf_op jit(solution)/shard_map/all_to_all | solution.py:41
  15.0 0.7 dynamic_slice.19
  15.9 1.3 %broadcast_compare_fusion.1 = (pred[128]{0:T(512)(128)(4,1)S(1)}, pred[128]{0:T(512)(128)(4,1)S(1)}) fusion(s32[128]{0:T(128)S(1)} %get-tuple-element.12, s32[]{:T(128)} %bitcast.7, s32[]{:T(128)} %bitcast.5), kind=kLoop, calls=%fused_computation.65 | loop fusion | flops 256 | bytes 776 | tf_op jit(solution)/shard_map/eq | solution.py:72
  17.2 7.1 %all-to-all-done = f32[4,32,1024]{2,1,0:T(8,128)S(1)} async-done(((f32[4,32,1024]{2,1,0:T(8,128)}), f32[4,32,1024]{2,1,0:T(8,128)S(1)}, u32[]{:S(2)}, u32[]{:S(2)}) %all-to-all-start) | async-done | bytes 524320 | tf_op jit(solution)/shard_map/all_to_all | solution.py:41
  24.5 0.8 broadcast_in_dim.58
  25.3 3.5 %all-to-all-start.1 = ((f32[4,32,1024]{2,1,0:T(8,128)}), f32[4,32,1024]{2,1,0:T(8,128)S(1)}, u32[]{:S(2)}, u32[]{:S(2)}) async-start(f32[4,32,1024]{2,1,0:T(8,128)} %broadcast_in_dim.58), calls=%async_computation.1 | async-start | bytes 1048576 | tf_op jit(solution)/shard_map/all_to_all | solution.py:45
  29.2 1.3 %broadcast_compare_fusion = (pred[128]{0:T(512)(128)(4,1)S(1)}, pred[128]{0:T(512)(128)(4,1)S(1)}) fusion(s32[128]{0:T(128)S(1)} %get-tuple-element.11, s32[]{:T(128)} %bitcast.7, s32[]{:T(128)} %bitcast.5), kind=kLoop, calls=%fused_computation.64 | loop fusion | flops 256 | bytes 776 | tf_op jit(solution)/shard_map/eq | solution.py:72
  30.5 7.2 %all-to-all-done.1 = f32[4,32,1024]{2,1,0:T(8,128)S(1)} async-done(((f32[4,32,1024]{2,1,0:T(8,128)}), f32[4,32,1024]{2,1,0:T(8,128)S(1)}, u32[]{:S(2)}, u32[]{:S(2)}) %all-to-all-start.1) | async-done | bytes 524320 | tf_op jit(solution)/shard_map/all_to_all | solution.py:45
  37.7 1.9 %collective-permute-start.1 = (f32[128,1024]{1,0:T(8,128)S(1)}, f32[128,1024]{1,0:T(8,128)S(1)}, u32[]{:S(2)}, u32[]{:S(2)}) collective-permute-start(f32[128,1024]{1,0:T(8,128)S(1)} %bitcast.24), channel_id=1, source_target_pairs={{0,64},{64,0},{1,65},{65,1},{2,66},{66,2},{3,67},{67,3},{4,68},{68... | collective-permute-start | bytes 1572872 | tf_op jit(solution)/shard_map/ppermute | solution.py:48
  40.0 1.5 %collective-permute-done.1 = f32[128,1024]{1,0:T(8,128)S(1)} collective-permute-done((f32[128,1024]{1,0:T(8,128)S(1)}, f32[128,1024]{1,0:T(8,128)S(1)}, u32[]{:S(2)}, u32[]{:S(2)}) %collective-permute-start.1) | collective-permute-done | bytes 524320 | tf_op jit(solution)/shard_map/ppermute | solution.py:48
  41.7 0.8 broadcast_select_fusion
  42.5 18.8 %all-to-all-start.2 = ((f32[64,8,128]{2,1,0:T(8,128)}), f32[64,8,128]{2,1,0:T(8,128)}, u32[]{:S(2)}, u32[]{:S(2)}) async-start(f32[64,8,128]{2,1,0:T(8,128)} %broadcast_select_fusion), calls=%async_computation.2 | async-start | bytes 524288 | tf_op jit(solution)/shard_map/all_to_all | solution.py:79
  61.8 1.0 %fusion.2 = f32[512,128]{1,0:T(8,128)S(1)} fusion(f32[128,1024]{1,0:T(8,128)S(1)} %bitcast.26, f32[512,1024]{1,0:T(8,128)S(1)} %copy-done, f32[512]{0:T(512)S(1)} %add_rsqrt_fusion), kind=kOutput, calls=%fused_computation.4 | convolution fusion | flops 403177472 | bytes 2885632 | tf_op jit(solution)/shard_map/dot_general | solution.py:85
  62.8 1.5 %convolution_add_fusion.1 = f32[256,1024]{1,0:T(8,128)} fusion(f32[256,1024]{1,0:T(8,128)S(1)} %fusion.22, f32[128,1024]{1,0:T(8,128)S(1)} %collective-permute-done.1, s32[128]{0:T(128)S(1)} %get-tuple-element.11, s32[256]{0:T(256)S(1)} %convert_reduce_fusion.1), kind=kOutput, calls=%fused_computation.9 | convolution fusion | flops 201621504 | bytes 2622976 | tf_op jit(solution)/shard_map/dot_general | solution.py:61
  64.3 1.0 %fusion = f32[512,128]{1,0:T(8,128)S(1)} fusion(f32[128,1024]{1,0:T(8,128)S(1)} %collective-permute-done.1, f32[512,1024]{1,0:T(8,128)S(1)} %copy-done, f32[512]{0:T(512)S(1)} %add_rsqrt_fusion), kind=kOutput, calls=%fused_computation.2 | convolution fusion | flops 403177472 | bytes 2885632 | tf_op jit(solution)/shard_map/dot_general | solution.py:85
  65.3 17.7 %all-to-all-done.2 = f32[64,8,128]{2,1,0:T(8,128)} async-done(((f32[64,8,128]{2,1,0:T(8,128)}), f32[64,8,128]{2,1,0:T(8,128)}, u32[]{:S(2)}, u32[]{:S(2)}) %all-to-all-start.2) | async-done | bytes 262176 | tf_op jit(solution)/shard_map/all_to_all | solution.py:79
  83.0 1.9 %multiply_reduce_fusion.1 = (f32[256]{0:T(256)S(1)}, f32[256,1024]{1,0:T(8,128)S(1)}) fusion(f32[256,1024]{1,0:T(8,128)} %convolution_add_fusion.1, f32[8,8,8,128]{3,2,1,0:T(8,128)} %bitcast.9, s32[64]{0:T(128)S(1)} %get-tuple-element.10, s32[64]{0:T(128)S(1)} %get-tuple-element.9, s32[256]{0:T(256)S(1)} %convert_reduce_fusion.1, ...), kind=kOutput, calls=%fused_computation.12 | convolution fusion | flops 101531392 | bytes 2361984 | tf_op jit(solution)/shard_map/dot_general | solution.py:103
  84.9 1.9 %fusion.6 = f32[512,256]{1,0:T(8,128)} fusion(f32[512,1024]{1,0:T(8,128)S(1)} %copy-done, f32[256,1024]{1,0:T(8,128)S(1)} %get-tuple-element.18, f32[512]{0:T(512)S(1)} %add_rsqrt_fusion, f32[512,128]{1,0:T(8,128)S(1)} %fusion, f32[512,128]{1,0:T(8,128)S(1)} %fusion.2, f32[256]{0:T(256)S(1)} %add_rsqrt_fusion.1, pred[]{:T(512)S(6)} %eq.127), kind=kOutput, calls=%fused_computation.10 | convolution fusion | flops 806617088 | bytes 4197377 | tf_op jit(solution)/shard_map/dot_general | solution.py:110
  (35 shorter events, 3.4 us)
Async XLA Ops:
  2.5 4.7 %copy-start.1 = (s32[512]{0:T(512)S(1)}, s32[512]{0:T(512)}, u32[]{:S(2)}) copy-start(s32[512]{0:T(512)} %param.7) | copy-start | bytes 6148
  5.2 3.8 %collective-permute-start = (f32[128,1024]{1,0:T(8,128)S(1)}, f32[128,1024]{1,0:T(8,128)S(1)}, u32[]{:S(2)}, u32[]{:S(2)}) collective-permute-start(f32[128,1024]{1,0:T(8,128)S(1)} %constant_dynamic-slice_fusion), channel_id=1, source_target_pairs={{0,64},{64,0},{1,65},{65,1},{2,66},{66,2},{3,67},{67,3},{4,68},{68... | collective-permute-start | bytes 1572872 | tf_op jit(solution)/shard_map/ppermute | solution.py:40
  9.9 29.7 %copy-start = (f32[512,1024]{1,0:T(8,128)S(1)}, f32[512,1024]{1,0:T(8,128)}, u32[]{:S(2)}) copy-start(f32[512,1024]{1,0:T(8,128)} %param.4) | copy-start | bytes 6291460
  9.9 14.4 %all-to-all-start = ((f32[4,32,1024]{2,1,0:T(8,128)}), f32[4,32,1024]{2,1,0:T(8,128)S(1)}, u32[]{:S(2)}, u32[]{:S(2)}) async-start(f32[4,32,1024]{2,1,0:T(8,128)} %bitcast.3), calls=%async_computation | async-start | bytes 1048576 | tf_op jit(solution)/shard_map/all_to_all | solution.py:41
  25.3 12.4 %all-to-all-start.1 = ((f32[4,32,1024]{2,1,0:T(8,128)}), f32[4,32,1024]{2,1,0:T(8,128)S(1)}, u32[]{:S(2)}, u32[]{:S(2)}) async-start(f32[4,32,1024]{2,1,0:T(8,128)} %broadcast_in_dim.58), calls=%async_computation.1 | async-start | bytes 1048576 | tf_op jit(solution)/shard_map/all_to_all | solution.py:45
  37.7 3.8 %collective-permute-start.1 = (f32[128,1024]{1,0:T(8,128)S(1)}, f32[128,1024]{1,0:T(8,128)S(1)}, u32[]{:S(2)}, u32[]{:S(2)}) collective-permute-start(f32[128,1024]{1,0:T(8,128)S(1)} %bitcast.24), channel_id=1, source_target_pairs={{0,64},{64,0},{1,65},{65,1},{2,66},{66,2},{3,67},{67,3},{4,68},{68... | collective-permute-start | bytes 1572872 | tf_op jit(solution)/shard_map/ppermute | solution.py:48
  42.5 40.5 %all-to-all-start.2 = ((f32[64,8,128]{2,1,0:T(8,128)}), f32[64,8,128]{2,1,0:T(8,128)}, u32[]{:S(2)}, u32[]{:S(2)}) async-start(f32[64,8,128]{2,1,0:T(8,128)} %broadcast_select_fusion), calls=%async_computation.2 | async-start | bytes 524288 | tf_op jit(solution)/shard_map/all_to_all | solution.py:79

commit v23 on v18

--- a/solution.py
+++ b/solution.py
@@ -7,6 +7,16 @@
 
 
 EPS = 1e-06
+
+
+def exact_left_dot(a, b):
+    a = a.astype(jnp.bfloat16)
+    scaled = b * 65537.0
+    high = scaled - (scaled - b)
+    low = b - high
+    return jnp.dot(a, high.astype(jnp.bfloat16), preferred_element_type=jnp.float32) + jnp.dot(
+        a, low.astype(jnp.bfloat16), preferred_element_type=jnp.float32
+    )
 
 
 def unit_rows(matrix):
@@ -27,9 +37,7 @@
     incidence = jnp.sum(
         (doc_labels.T[:, None, :] == own_perm[None, :, None]).astype(jnp.float32), axis=0
     )
-    partial_value = jnp.dot(
-        incidence, features, precision=lax.Precision.HIGH, preferred_element_type=jnp.float32
-    )
+    partial_value = exact_left_dot(incidence, features)
     chips = lax.axis_size("dy")
     depth = features.shape[1]
     half = L_DEV // 2
@@ -101,12 +109,7 @@
     take_below = (last_id[None, :] == cluster_ids[:, None]) & below[None, :]
     take_above = (first_id[None, :] == cluster_ids[:, None]) & above[None, :]
     weights = take_below | take_above
-    cluster_sum = local_sum + jnp.dot(
-        weights.astype(jnp.float32),
-        gathered,
-        precision=lax.Precision.HIGH,
-        preferred_element_type=jnp.float32,
-    )
+    cluster_sum = local_sum + exact_left_dot(weights, gathered)
     centroid = unit_rows(cluster_sum)
     return lax.dot_general(
         doc_unit,

time: 87.5 us -> 89.5 us (1.023)
  other arithmetic: 6.49 us -> 8.25 us
    add x1, other arithmetic: 0.89 us -> 1.92 us  [shards(): chip_half = keep + lax.ppermute(give, 'dc', sibling)]
    dot_general x2 -> x4, matrix products: 4.59 us -> 4.59 us  [the longest x2 2.4 us: exact_left_dot(): jnp.dot(a, high.astype(jnp.bfloat16), preferred_element_type=jnp.float32)]
  transfers between devices with their start and end apart: 5 -> 5, of which waited for: 5 -> 5; matrix products, arithmetic and copies ran while one was open for 9% -> 10% of each run, Pallas kernels for 0% -> 0%
where the time goes in v23:
time: 89.5 us; the launch traced here: 89 us
  waiting for transfers between devices  35.7 us (40%)
  starting transfers between devices  30.3 us (34%)
  matrix products  11.2 us (13%)
  other arithmetic  8.25 us (9%)
  local copies, waits for them, and re-layouts  3.28 us (4%)
    all_to_all x1, starting transfers between devices, shards(): lax.all_to_all(sending.reshape(width, -1, lanes), 'label', 0, 0, tiled=True)  18.6 us
    all_to_all x1, waiting for transfers between devices, shards(): lax.all_to_all(sending.reshape(width, -1, lanes), 'label', 0, 0, tiled=True)  17 us
    all_to_all x1, waiting for transfers between devices, shards(): lax.all_to_all(jnp.broadcast_to(mine[None], (chips,) + mine.shape), 'dy',...  8.44 us
    all_to_all x1, waiting for transfers between devices, shards(): lax.all_to_all(chip_half.reshape(chips, half // chips, depth), 'dy', 0, 0...  8.12 us
    all_to_all x1, starting transfers between devices, shards(): lax.all_to_all(chip_half.reshape(chips, half // chips, depth), 'dy', 0, 0...  4.47 us
    all_to_all x1, starting transfers between devices, shards(): lax.all_to_all(jnp.broadcast_to(mine[None], (chips,) + mine.shape), 'dy',...  3.47 us
    dot_general x2, matrix products, shards(): lax.dot_general(doc_unit, rows, (((1,), (1,)), ((), ())), precision=lax.P...  2.78 us
    dot_general x2, matrix products, exact_left_dot(): jnp.dot(a, high.astype(jnp.bfloat16), preferred_element_type=jnp.float32)  2.4 us
  transfers between devices with their start and end apart: 5, of which 5 were waited for; matrix products, arithmetic and copies ran while one was open for 10% of the time, Pallas kernels for 0%

profile of v23, /device:TPU:6, one launch (start us, length us, event | category | flops | bytes accessed | tf_op | source)
XLA Modules:
  0.0 89.0 jit_solution(10535771844197280043)
XLA Ops:
  0.0 0.9 %dynamic_slice.9 = s32[256]{0:T(256)S(1)} dynamic-slice(s32[16384]{0:T(1024)} %param.6, s32[]{:T(128)S(6)} %select_n.48), dynamic_slice_sizes={256} | dynamic-slice | bytes 2052 | tf_op jit(solution)/shard_map/dynamic_slice | solution.py:36
  0.9 1.6 %convert_reduce_fusion = bf16[256,512]{1,0:T(8,128)(2,1)S(1)} fusion(s32[16,512]{1,0:T(8,128)} %bitcast.31, s32[256]{0:T(256)S(1)} %dynamic_slice.9), kind=kLoop, calls=%fused_computation | loop fusion | flops 6160384 | bytes 295936 | tf_op jit(solution)/shard_map/reduce_sum | solution.py:37
  2.6 2.1 %fusion.14 = f32[256,1024]{1,0:T(8,128)S(1)} fusion(f32[512,1024]{1,0:T(8,128)} %param.4, bf16[256,512]{1,0:T(8,128)(2,1)S(1)} %convert_reduce_fusion), kind=kOutput, calls=%fused_computation.17 | convolution fusion | flops 270532608 | bytes 3407872 | tf_op jit(solution)/shard_map/dot_general | solution.py:17
  5.2 0.9 slice_select_fusion
  6.0 1.9 %collective-permute-start = (f32[128,1024]{1,0:T(8,128)}, f32[128,1024]{1,0:T(8,128)}, u32[]{:S(2)}, u32[]{:S(2)}) collective-permute-start(f32[128,1024]{1,0:T(8,128)} %slice_select_fusion), channel_id=1, source_target_pairs={{0,64},{64,0},{1,65},{65,1},{2,66},{66,2},{3,67},{67,3},{4,68},{68... | collective-permute-start | bytes 1572872 | tf_op jit(solution)/shard_map/ppermute | solution.py:49
  8.6 1.5 %collective-permute-done = f32[128,1024]{1,0:T(8,128)} collective-permute-done((f32[128,1024]{1,0:T(8,128)}, f32[128,1024]{1,0:T(8,128)}, u32[]{:S(2)}, u32[]{:S(2)}) %collective-permute-start) | collective-permute-done | bytes 524320 | tf_op jit(solution)/shard_map/ppermute | solution.py:49
  10.2 1.9 %select_add_fusion = f32[128,1024]{1,0:T(8,128)} fusion(f32[128,1024]{1,0:T(8,128)} %collective-permute-done, f32[256,1024]{1,0:T(8,128)S(1)} %convolution_add_fusion.2, pred[]{:T(512)S(6)} %eq.90), kind=kLoop, calls=%fused_computation.30 | loop fusion | flops 262144 | bytes 2097153 | tf_op jit(solution)/shard_map/add | solution.py:49
  12.1 4.5 %all-to-all-start = ((f32[4,32,1024]{2,1,0:T(8,128)}), f32[4,32,1024]{2,1,0:T(8,128)S(1)}, u32[]{:S(2)}, u32[]{:S(2)}) async-start(f32[4,32,1024]{2,1,0:T(8,128)} %bitcast.30), calls=%async_computation | async-start | bytes 1048576 | tf_op jit(solution)/shard_map/all_to_all | solution.py:50
  16.8 0.7 dynamic_slice.11
  18.2 8.1 %all-to-all-done = f32[4,32,1024]{2,1,0:T(8,128)S(1)} async-done(((f32[4,32,1024]{2,1,0:T(8,128)}), f32[4,32,1024]{2,1,0:T(8,128)S(1)}, u32[]{:S(2)}, u32[]{:S(2)}) %all-to-all-start) | async-done | bytes 524320 | tf_op jit(solution)/shard_map/all_to_all | solution.py:50
  26.6 0.8 broadcast_in_dim.39
  27.4 3.5 %all-to-all-start.1 = ((f32[4,32,1024]{2,1,0:T(8,128)}), f32[4,32,1024]{2,1,0:T(8,128)S(1)}, u32[]{:S(2)}, u32[]{:S(2)}) async-start(f32[4,32,1024]{2,1,0:T(8,128)} %broadcast_in_dim.39), calls=%async_computation.1 | async-start | bytes 1048576 | tf_op jit(solution)/shard_map/all_to_all | solution.py:54
  31.3 8.4 %all-to-all-done.1 = f32[4,32,1024]{2,1,0:T(8,128)S(1)} async-done(((f32[4,32,1024]{2,1,0:T(8,128)}), f32[4,32,1024]{2,1,0:T(8,128)S(1)}, u32[]{:S(2)}, u32[]{:S(2)}) %all-to-all-start.1) | async-done | bytes 524320 | tf_op jit(solution)/shard_map/all_to_all | solution.py:54
  39.8 1.9 %collective-permute-start.1 = (f32[128,1024]{1,0:T(8,128)S(1)}, f32[128,1024]{1,0:T(8,128)S(1)}, u32[]{:S(2)}, u32[]{:S(2)}) collective-permute-start(f32[128,1024]{1,0:T(8,128)S(1)} %bitcast.24), channel_id=1, source_target_pairs={{0,64},{64,0},{1,65},{65,1},{2,66},{66,2},{3,67},{67,3},{4,68},{68... | collective-permute-start | bytes 1572872 | tf_op jit(solution)/shard_map/ppermute | solution.py:57
  41.7 1.3 %broadcast_compare_fusion = (pred[256]{0:T(512)(128)(4,1)S(1)}, pred[256]{0:T(512)(128)(4,1)S(1)}) fusion(s32[256]{0:T(256)S(1)} %convert_reduce_fusion.1, s32[]{:T(128)} %bitcast.7, s32[]{:T(128)} %bitcast.5), kind=kLoop, calls=%fused_computation.62 | loop fusion | flops 512 | bytes 1544 | tf_op jit(solution)/shard_map/eq | solution.py:84
  43.0 0.6 collective-permute-done.1
  43.8 0.8 broadcast_select_fusion
  44.7 18.6 %all-to-all-start.2 = ((f32[64,8,128]{2,1,0:T(8,128)}), f32[64,8,128]{2,1,0:T(8,128)S(1)}, u32[]{:S(2)}, u32[]{:S(2)}) async-start(f32[64,8,128]{2,1,0:T(8,128)} %broadcast_select_fusion), calls=%async_computation.2 | async-start | bytes 524288 | tf_op jit(solution)/shard_map/all_to_all | solution.py:88
  63.8 1.8 %fusion.5 = f32[512,128]{1,0:T(8,128)} fusion(f32[128,1024]{1,0:T(8,128)S(1)} %bitcast.27, f32[512,1024]{1,0:T(8,128)S(1)} %copy-done, f32[512]{0:T(512)S(1)} %add_rsqrt_fusion), kind=kOutput, calls=%fused_computation.8 | convolution fusion | flops 403177472 | bytes 2885632 | tf_op jit(solution)/shard_map/dot_general | solution.py:94
  65.5 1.5 %convolution_add_fusion.1 = f32[256,1024]{1,0:T(8,128)} fusion(f32[256,1024]{1,0:T(8,128)S(1)} %fusion.34, f32[128,1024]{1,0:T(8,128)S(1)} %collective-permute-done.1, s32[128]{0:T(128)S(1)} %get-tuple-element.9, s32[256]{0:T(256)S(1)} %convert_reduce_fusion.1), kind=kOutput, calls=%fused_computation.14 | convolution fusion | flops 201621504 | bytes 2622976 | tf_op jit(solution)/shard_map/dot_general | solution.py:75
  67.0 1.0 %fusion.3 = f32[512,128]{1,0:T(8,128)S(1)} fusion(f32[128,1024]{1,0:T(8,128)S(1)} %collective-permute-done.1, f32[512,1024]{1,0:T(8,128)S(1)} %copy-done, f32[512]{0:T(512)S(1)} %add_rsqrt_fusion), kind=kOutput, calls=%fused_computation.6 | convolution fusion | flops 403177472 | bytes 2885632 | tf_op jit(solution)/shard_map/dot_general | solution.py:94
  68.0 17.0 %all-to-all-done.2 = f32[64,8,128]{2,1,0:T(8,128)S(1)} async-done(((f32[64,8,128]{2,1,0:T(8,128)}), f32[64,8,128]{2,1,0:T(8,128)S(1)}, u32[]{:S(2)}, u32[]{:S(2)}) %all-to-all-start.2) | async-done | bytes 262176 | tf_op jit(solution)/shard_map/all_to_all | solution.py:88
  85.4 1.7 %multiply_reduce_fusion.1 = (f32[256]{0:T(256)S(1)}, f32[256,1024]{1,0:T(8,128)S(1)}) fusion(f32[256,1024]{1,0:T(8,128)} %convolution_add_fusion.1, f32[256,1024]{1,0:T(8,128)S(1)} %fusion.27, f32[8,8,8,128]{3,2,1,0:T(8,128)S(1)} %bitcast.29, s32[64]{0:T(128)S(1)} %get-tuple-element.8, s32[64]{0:T(128)S(1)} %get-tuple-element.7, ...), kind=kOutput, calls=%fused_computation.20 | convolution fusion | flops 35012352 | bytes 3410560 | tf_op jit(solution)/shard_map/dot_general | solution.py:17
  87.1 1.9 %fusion.10 = f32[512,256]{1,0:T(8,128)} fusion(f32[512,1024]{1,0:T(8,128)S(1)} %copy-done, f32[256,1024]{1,0:T(8,128)S(1)} %get-tuple-element.14, f32[512]{0:T(512)S(1)} %add_rsqrt_fusion, f32[512,128]{1,0:T(8,128)S(1)} %fusion.3, f32[512,128]{1,0:T(8,128)S(1)} %copy-done.1, f32[256]{0:T(256)S(1)} %add_rsqrt_fusion.1, pred[]{:T(512)S(6)} %eq.90), kind=kOutput, calls=%fused_computation.16 | convolution fusion | flops 806617088 | bytes 4197377 | tf_op jit(solution)/shard_map/dot_general | solution.py:114
  (32 shorter events, 4.0 us)
Async XLA Ops:
  0.0 4.6 %copy-start = (f32[512,1024]{1,0:T(8,128)S(1)}, f32[512,1024]{1,0:T(8,128)}, u32[]{:S(2)}) copy-start(f32[512,1024]{1,0:T(8,128)} %param.4) | copy-start | bytes 6291460
  4.6 3.3 %copy-start.2 = (s32[512]{0:T(512)S(1)}, s32[512]{0:T(512)}, u32[]{:S(2)}) copy-start(s32[512]{0:T(512)} %param.7) | copy-start | bytes 6148
  6.0 4.1 %collective-permute-start = (f32[128,1024]{1,0:T(8,128)}, f32[128,1024]{1,0:T(8,128)}, u32[]{:S(2)}, u32[]{:S(2)}) collective-permute-start(f32[128,1024]{1,0:T(8,128)} %slice_select_fusion), channel_id=1, source_target_pairs={{0,64},{64,0},{1,65},{65,1},{2,66},{66,2},{3,67},{67,3},{4,68},{68... | collective-permute-start | bytes 1572872 | tf_op jit(solution)/shard_map/ppermute | solution.py:49
  12.1 14.2 %all-to-all-start = ((f32[4,32,1024]{2,1,0:T(8,128)}), f32[4,32,1024]{2,1,0:T(8,128)S(1)}, u32[]{:S(2)}, u32[]{:S(2)}) async-start(f32[4,32,1024]{2,1,0:T(8,128)} %bitcast.30), calls=%async_computation | async-start | bytes 1048576 | tf_op jit(solution)/shard_map/all_to_all | solution.py:50
  27.4 12.4 %all-to-all-start.1 = ((f32[4,32,1024]{2,1,0:T(8,128)}), f32[4,32,1024]{2,1,0:T(8,128)S(1)}, u32[]{:S(2)}, u32[]{:S(2)}) async-start(f32[4,32,1024]{2,1,0:T(8,128)} %broadcast_in_dim.39), calls=%async_computation.1 | async-start | bytes 1048576 | tf_op jit(solution)/shard_map/all_to_all | solution.py:54
  39.8 3.8 %collective-permute-start.1 = (f32[128,1024]{1,0:T(8,128)S(1)}, f32[128,1024]{1,0:T(8,128)S(1)}, u32[]{:S(2)}, u32[]{:S(2)}) collective-permute-start(f32[128,1024]{1,0:T(8,128)S(1)} %bitcast.24), channel_id=1, source_target_pairs={{0,64},{64,0},{1,65},{65,1},{2,66},{66,2},{3,67},{67,3},{4,68},{68... | collective-permute-start | bytes 1572872 | tf_op jit(solution)/shard_map/ppermute | solution.py:57
  44.7 40.4 %all-to-all-start.2 = ((f32[64,8,128]{2,1,0:T(8,128)}), f32[64,8,128]{2,1,0:T(8,128)S(1)}, u32[]{:S(2)}, u32[]{:S(2)}) async-start(f32[64,8,128]{2,1,0:T(8,128)} %broadcast_select_fusion), calls=%async_computation.2 | async-start | bytes 524288 | tf_op jit(solution)/shard_map/all_to_all | solution.py:88
  85.1 2.0 %copy-start.1 = (f32[512,128]{1,0:T(8,128)S(1)}, f32[512,128]{1,0:T(8,128)}, u32[]{:S(2)}) copy-start(f32[512,128]{1,0:T(8,128)} %fusion.5) | copy-start | bytes 786436

commit v24 on v18

--- a/solution.py
+++ b/solution.py
@@ -77,9 +77,20 @@
     last_sum = jnp.sum(jnp.where((cluster_ids == last_id[here])[:, None], label_rows, 0.0), axis=0)
     sending = jnp.where(above[:, None], last_sum[None, :], first_sum[None, :])
     lanes = 128
-    gathered = lax.all_to_all(
-        sending.reshape(width, -1, lanes), "label", 0, 0, tiled=True
-    ).reshape(width, -1)
+    part = depth // 2
+    got = lax.all_to_all(
+        lax.dynamic_slice_in_dim(sending, core * part, part, axis=1).reshape(width, -1, lanes),
+        "label",
+        0,
+        0,
+        tiled=True,
+    ).reshape(width, part)
+    swapped = lax.ppermute(got, "dc", sibling)
+    gathered = jnp.where(
+        core == 0,
+        jnp.concatenate([got, swapped], axis=1),
+        jnp.concatenate([swapped, got], axis=1),
+    )
 
     doc_unit = unit_rows(features)
     own_scores, other_scores = (

time: 87.5 us -> 87.7 us (level)
  the two profiles are of different devices: /device:TPU:6 before, /device:TPU:1 now
where the time goes in v24:
time: 87.7 us; the launch traced here: 87.2 us
  starting transfers between devices  38.5 us (44%)
  waiting for transfers between devices  27 us (31%)
  matrix products  10.5 us (12%)
  other arithmetic  6.88 us (8%)
  local copies, waits for them, and re-layouts  4.01 us (5%)
    all_to_all x1, starting transfers between devices, shards(): lax.all_to_all(lax.dynamic_slice_in_dim(sending, core * part, part, axis=...  13.3 us
    all_to_all x1, waiting for transfers between devices, shards(): lax.all_to_all(lax.dynamic_slice_in_dim(sending, core * part, part, axis=...  13 us
    ppermute x1, starting transfers between devices, shards(): chip_half = keep + lax.ppermute(give, 'dc', sibling)  8.79 us
    all_to_all x1, waiting for transfers between devices, shards(): lax.all_to_all(chip_half.reshape(chips, half // chips, depth), 'dy', 0, 0...  6.98 us
    all_to_all x1, waiting for transfers between devices, shards(): lax.all_to_all(jnp.broadcast_to(mine[None], (chips,) + mine.shape), 'dy',...  6.5 us
    ppermute x1, starting transfers between devices, shards(): swapped = lax.ppermute(got, 'dc', sibling)  5.02 us
    ppermute x1, starting transfers between devices, shards(): other_half = lax.ppermute(own_half, 'dc', sibling)  4.31 us
    all_to_all x1, starting transfers between devices, shards(): lax.all_to_all(chip_half.reshape(chips, half // chips, depth), 'dy', 0, 0...  3.6 us
  transfers between devices with their start and end apart: 6, of which 4 were waited for; matrix products, arithmetic and copies ran while one was open for 12% of the time, Pallas kernels for 0%

profile of v24, /device:TPU:1, one launch (start us, length us, event | category | flops | bytes accessed | tf_op | source)
XLA Modules:
  0.0 87.2 jit_solution(9994015915433329334)
XLA Ops:
  0.0 0.8 dynamic_slice.12
  0.8 1.7 %convert_reduce_fusion = f32[256,512]{1,0:T(8,128)S(1)} fusion(s32[16,512]{1,0:T(8,128)} %bitcast.25, s32[256]{0:T(256)S(1)} %dynamic_slice.12), kind=kLoop, calls=%fused_computation | loop fusion | flops 6160384 | bytes 558080 | tf_op jit(solution)/shard_map/reduce_sum | solution.py:27
  2.5 2.7 %fusion.38 = f32[256,1024]{1,0:T(8,128)S(1)} fusion(f32[256,512]{1,0:T(8,128)S(1)} %convert_reduce_fusion, f32[512,1024]{1,0:T(8,128)} %param.4), kind=kOutput, calls=%fused_computation.71 | convolution fusion | flops 805306368 | bytes 3670016 | tf_op jit(solution)/shard_map/dot_general | solution.py:30
  5.2 8.8 %collective-permute-start = (f32[128,1024]{1,0:T(8,128)S(1)}, f32[128,1024]{1,0:T(8,128)S(1)}, u32[]{:S(2)}, u32[]{:S(2)}) collective-permute-start(f32[128,1024]{1,0:T(8,128)S(1)} %slice_select_fusion), channel_id=1, source_target_pairs={{0,64},{64,0},{1,65},{65,1},{2,66},{66,2},{3,67},{67,3},{4,68},{68... | collective-permute-start | bytes 1572872 | tf_op jit(solution)/shard_map/ppermute | solution.py:41
  15.5 0.9 %select_add_fusion = f32[128,1024]{1,0:T(8,128)} fusion(f32[128,1024]{1,0:T(8,128)S(1)} %collective-permute-done, f32[256,1024]{1,0:T(8,128)S(1)} %fusion.38, pred[]{:T(512)S(6)} %eq.91), kind=kLoop, calls=%fused_computation.21 | loop fusion | flops 262144 | bytes 2097153 | tf_op jit(solution)/shard_map/add | solution.py:41
  16.4 3.6 %all-to-all-start = ((f32[4,32,1024]{2,1,0:T(8,128)}), f32[4,32,1024]{2,1,0:T(8,128)S(1)}, u32[]{:S(2)}, u32[]{:S(2)}) async-start(f32[4,32,1024]{2,1,0:T(8,128)} %bitcast.3), calls=%async_computation | async-start | bytes 1048576 | tf_op jit(solution)/shard_map/all_to_all | solution.py:42
  20.6 0.7 dynamic_slice.14
  21.5 0.7 convert_reduce_fusion.2
  22.3 7.0 %all-to-all-done = f32[4,32,1024]{2,1,0:T(8,128)S(1)} async-done(((f32[4,32,1024]{2,1,0:T(8,128)}), f32[4,32,1024]{2,1,0:T(8,128)S(1)}, u32[]{:S(2)}, u32[]{:S(2)}) %all-to-all-start) | async-done | bytes 524320 | tf_op jit(solution)/shard_map/all_to_all | solution.py:42
  29.5 0.8 broadcast_in_dim.35
  30.3 3.5 %all-to-all-start.1 = ((f32[4,32,1024]{2,1,0:T(8,128)}), f32[4,32,1024]{2,1,0:T(8,128)S(1)}, u32[]{:S(2)}, u32[]{:S(2)}) async-start(f32[4,32,1024]{2,1,0:T(8,128)} %broadcast_in_dim.35), calls=%async_computation.1 | async-start | bytes 1048576 | tf_op jit(solution)/shard_map/all_to_all | solution.py:46
  34.0 1.3 %broadcast_compare_fusion = (pred[256]{0:T(512)(128)(4,1)S(1)}, pred[256]{0:T(512)(128)(4,1)S(1)}) fusion(s32[256]{0:T(256)S(1)} %convert_reduce_fusion.1, s32[]{:T(128)} %bitcast.6, s32[]{:T(128)} %bitcast.5), kind=kLoop, calls=%fused_computation.61 | loop fusion | flops 512 | bytes 1544 | tf_op jit(solution)/shard_map/eq | solution.py:76
  35.3 6.5 %all-to-all-done.1 = f32[4,32,1024]{2,1,0:T(8,128)S(1)} async-done(((f32[4,32,1024]{2,1,0:T(8,128)}), f32[4,32,1024]{2,1,0:T(8,128)S(1)}, u32[]{:S(2)}, u32[]{:S(2)}) %all-to-all-start.1) | async-done | bytes 524320 | tf_op jit(solution)/shard_map/all_to_all | solution.py:46
  41.8 4.3 %collective-permute-start.1 = (f32[128,1024]{1,0:T(8,128)S(1)}, f32[128,1024]{1,0:T(8,128)S(1)}, u32[]{:S(2)}, u32[]{:S(2)}) collective-permute-start(f32[128,1024]{1,0:T(8,128)S(1)} %bitcast.18), channel_id=1, source_target_pairs={{0,64},{64,0},{1,65},{65,1},{2,66},{66,2},{3,67},{67,3},{4,68},{68... | collective-permute-start | bytes 1572872 | tf_op jit(solution)/shard_map/ppermute | solution.py:49
  46.7 1.0 %fusion.2 = f32[512,128]{1,0:T(8,128)S(1)} fusion(f32[128,1024]{1,0:T(8,128)S(1)} %bitcast.19, f32[512,1024]{1,0:T(8,128)S(1)} %copy-done, f32[512]{0:T(512)S(1)} %add_rsqrt_fusion), kind=kOutput, calls=%fused_computation.4 | convolution fusion | flops 403177472 | bytes 2885632 | tf_op jit(solution)/shard_map/dot_general | solution.py:97
  48.3 0.7 reshape.115
  49.0 13.3 %all-to-all-start.2 = ((f32[64,4,128]{2,1,0:T(4,128)}), f32[64,4,128]{2,1,0:T(4,128)S(1)}, u32[]{:S(2)}, u32[]{:S(2)}) async-start(f32[64,4,128]{2,1,0:T(4,128)} %reshape.115), calls=%async_computation.2 | async-start | bytes 262144 | tf_op jit(solution)/shard_map/all_to_all | solution.py:81
  62.3 1.5 %fusion.26 = f32[256,1024]{1,0:T(8,128)} fusion(f32[128,1024]{1,0:T(8,128)S(1)} %bitcast.21, s32[128]{0:T(128)S(1)} %get-tuple-element.10, s32[256]{0:T(256)S(1)} %convert_reduce_fusion.1), kind=kOutput, calls=%fused_computation.43 | convolution fusion | flops 201359360 | bytes 1574400 | tf_op jit(solution)/shard_map/dot_general | solution.py:67
  63.8 1.0 %fusion = f32[512,128]{1,0:T(8,128)S(1)} fusion(f32[128,1024]{1,0:T(8,128)S(1)} %collective-permute-done.1, f32[512,1024]{1,0:T(8,128)S(1)} %copy-done, f32[512]{0:T(512)S(1)} %add_rsqrt_fusion), kind=kOutput, calls=%fused_computation.2 | convolution fusion | flops 403177472 | bytes 2885632 | tf_op jit(solution)/shard_map/dot_general | solution.py:97
  64.8 13.0 %all-to-all-done.2 = f32[64,4,128]{2,1,0:T(4,128)S(1)} async-done(((f32[64,4,128]{2,1,0:T(4,128)}), f32[64,4,128]{2,1,0:T(4,128)S(1)}, u32[]{:S(2)}, u32[]{:S(2)}) %all-to-all-start.2) | async-done | bytes 131104 | tf_op jit(solution)/shard_map/all_to_all | solution.py:81
  77.8 5.0 %collective-permute-start.2 = (f32[64,512]{1,0:T(8,128)S(1)}, f32[64,512]{1,0:T(8,128)S(1)}, u32[]{:S(2)}, u32[]{:S(2)}) collective-permute-start(f32[64,512]{1,0:T(8,128)S(1)} %bitcast.23), channel_id=1, source_target_pairs={{0,64},{64,0},{1,65},{65,1},{2,66},{66,2},{3,67},{67,3},{4,68},{68... | collective-permute-start | bytes 393224 | tf_op jit(solution)/shard_map/ppermute | solution.py:88
  82.9 1.8 %convolution_add_fusion.1 = f32[256,1024]{1,0:T(8,128)S(1)} fusion(f32[256,1024]{1,0:T(8,128)} %fusion.26, f32[128,1024]{1,0:T(8,128)S(1)} %collective-permute-done.1, s32[128]{0:T(128)S(1)} %copy-done.6, s32[256]{0:T(256)S(1)} %convert_reduce_fusion.1), kind=kOutput, calls=%fused_computation.9 | convolution fusion | flops 201621504 | bytes 2622976 | tf_op jit(solution)/shard_map/dot_general | solution.py:67
  84.7 0.6 multiply_reduce_fusion.1
  85.3 1.9 %fusion.6 = f32[512,256]{1,0:T(8,128)} fusion(f32[512,1024]{1,0:T(8,128)S(1)} %copy-done, f32[256,1024]{1,0:T(8,128)S(1)} %get-tuple-element.14, f32[512]{0:T(512)S(1)} %add_rsqrt_fusion, f32[512,128]{1,0:T(8,128)S(1)} %fusion, f32[512,128]{1,0:T(8,128)S(1)} %fusion.2, f32[256]{0:T(256)S(1)} %add_rsqrt_fusion.1, pred[]{:T(512)S(6)} %eq.91), kind=kOutput, calls=%fused_computation.10 | convolution fusion | flops 806617088 | bytes 4197377 | tf_op jit(solution)/shard_map/dot_general | solution.py:122
  (46 shorter events, 3.9 us)
Async XLA Ops:
  2.5 11.6 %copy-start.1 = (s32[512]{0:T(512)S(1)}, s32[512]{0:T(512)}, u32[]{:S(2)}) copy-start(s32[512]{0:T(512)} %param.7) | copy-start | bytes 6148
  5.2 10.3 %collective-permute-start = (f32[128,1024]{1,0:T(8,128)S(1)}, f32[128,1024]{1,0:T(8,128)S(1)}, u32[]{:S(2)}, u32[]{:S(2)}) collective-permute-start(f32[128,1024]{1,0:T(8,128)S(1)} %slice_select_fusion), channel_id=1, source_target_pairs={{0,64},{64,0},{1,65},{65,1},{2,66},{66,2},{3,67},{67,3},{4,68},{68... | collective-permute-start | bytes 1572872 | tf_op jit(solution)/shard_map/ppermute | solution.py:41
  14.9 6.4 %copy-start.2 = (s32[64]{0:T(128)}, s32[64]{0:T(128)S(1)}, u32[]{:S(2)}) copy-start(s32[64]{0:T(128)S(1)} %get-tuple-element.7) | copy-start | bytes 772
  14.9 6.4 %copy-start.4 = (s32[64]{0:T(128)}, s32[64]{0:T(128)S(1)}, u32[]{:S(2)}) copy-start(s32[64]{0:T(128)S(1)} %get-tuple-element.8) | copy-start | bytes 772
  16.4 17.4 %copy-start = (f32[512,1024]{1,0:T(8,128)S(1)}, f32[512,1024]{1,0:T(8,128)}, u32[]{:S(2)}) copy-start(f32[512,1024]{1,0:T(8,128)} %param.4) | copy-start | bytes 6291460
  16.4 12.8 %all-to-all-start = ((f32[4,32,1024]{2,1,0:T(8,128)}), f32[4,32,1024]{2,1,0:T(8,128)S(1)}, u32[]{:S(2)}, u32[]{:S(2)}) async-start(f32[4,32,1024]{2,1,0:T(8,128)} %bitcast.3), calls=%async_computation | async-start | bytes 1048576 | tf_op jit(solution)/shard_map/all_to_all | solution.py:42
  30.3 11.5 %all-to-all-start.1 = ((f32[4,32,1024]{2,1,0:T(8,128)}), f32[4,32,1024]{2,1,0:T(8,128)S(1)}, u32[]{:S(2)}, u32[]{:S(2)}) async-start(f32[4,32,1024]{2,1,0:T(8,128)} %broadcast_in_dim.35), calls=%async_computation.1 | async-start | bytes 1048576 | tf_op jit(solution)/shard_map/all_to_all | solution.py:46
  41.8 5.9 %collective-permute-start.1 = (f32[128,1024]{1,0:T(8,128)S(1)}, f32[128,1024]{1,0:T(8,128)S(1)}, u32[]{:S(2)}, u32[]{:S(2)}) collective-permute-start(f32[128,1024]{1,0:T(8,128)S(1)} %bitcast.18), channel_id=1, source_target_pairs={{0,64},{64,0},{1,65},{65,1},{2,66},{66,2},{3,67},{67,3},{4,68},{68... | collective-permute-start | bytes 1572872 | tf_op jit(solution)/shard_map/ppermute | solution.py:49
  49.0 28.8 %all-to-all-start.2 = ((f32[64,4,128]{2,1,0:T(4,128)}), f32[64,4,128]{2,1,0:T(4,128)S(1)}, u32[]{:S(2)}, u32[]{:S(2)}) async-start(f32[64,4,128]{2,1,0:T(4,128)} %reshape.115), calls=%async_computation.2 | async-start | bytes 262144 | tf_op jit(solution)/shard_map/all_to_all | solution.py:81
  63.8 19.1 %copy-start.6 = (s32[128]{0:T(128)S(1)}, s32[128]{0:T(128)}, u32[]{:S(2)}) copy-start(s32[128]{0:T(128)} %get-tuple-element.9) | copy-start | bytes 1540
  64.8 19.8 %copy-start.3 = (s32[64]{0:T(128)S(1)}, s32[64]{0:T(128)}, u32[]{:S(2)}) copy-start(s32[64]{0:T(128)} %copy-done.2) | copy-start | bytes 772
  64.8 19.8 %copy-start.7 = (pred[64]{0:T(512)(128)(4,1)S(1)}, pred[64]{0:T(512)(128)(4,1)}, u32[]{:S(2)}) copy-start(pred[64]{0:T(512)(128)(4,1)} %iota_compare_fusion.1) | copy-start | bytes 196
  77.8 6.9 %copy-start.5 = (s32[64]{0:T(128)S(1)}, s32[64]{0:T(128)}, u32[]{:S(2)}) copy-start(s32[64]{0:T(128)} %copy-done.4) | copy-start | bytes 772
  77.8 6.8 %collective-permute-start.2 = (f32[64,512]{1,0:T(8,128)S(1)}, f32[64,512]{1,0:T(8,128)S(1)}, u32[]{:S(2)}, u32[]{:S(2)}) collective-permute-start(f32[64,512]{1,0:T(8,128)S(1)} %bitcast.23), channel_id=1, source_target_pairs={{0,64},{64,0},{1,65},{65,1},{2,66},{66,2},{3,67},{67,3},{4,68},{68... | collective-permute-start | bytes 393224 | tf_op jit(solution)/shard_map/ppermute | solution.py:88

commit v25 on v18

--- a/solution.py
+++ b/solution.py
@@ -42,10 +42,10 @@
     pieces = lax.all_to_all(
         chip_half.reshape(chips, half // chips, depth), "dy", 0, 0, tiled=True
     )
-    mine = unit_rows(jnp.sum(pieces, axis=0))
-    own_half = lax.all_to_all(
-        jnp.broadcast_to(mine[None], (chips,) + mine.shape), "dy", 0, 0, tiled=True
-    ).reshape(half, depth)
+    summed = jnp.sum(pieces, axis=0)
+    scale = lax.rsqrt(jnp.sum(summed * summed, axis=1, keepdims=True) + EPS)
+    copies = jnp.broadcast_to(summed[None], pieces.shape) * jnp.broadcast_to(scale[None], (chips,) + scale.shape)
+    own_half = lax.all_to_all(copies, "dy", 0, 0, tiled=True).reshape(half, depth)
     other_half = lax.ppermute(own_half, "dc", sibling)
     label_rows = jnp.where(
         core == 0,

time: 87.5 us -> 87.5 us (level)
  no operation moved by 1% of the time
where the time goes in v25:
time: 87.5 us; the launch traced here: 86.9 us
  waiting for transfers between devices  36 us (41%)
  starting transfers between devices  30.7 us (35%)
  matrix products  10.5 us (12%)
  other arithmetic  7.31 us (8%)
  local copies, waits for them, and re-layouts  2.28 us (3%)
    all_to_all x1, starting transfers between devices, shards(): lax.all_to_all(sending.reshape(width, -1, lanes), 'label', 0, 0, tiled=True)  18.8 us
    all_to_all x1, waiting for transfers between devices, shards(): lax.all_to_all(sending.reshape(width, -1, lanes), 'label', 0, 0, tiled=True)  17.7 us
    all_to_all x1, waiting for transfers between devices, shards(): lax.all_to_all(copies, 'dy', 0, 0, tiled=True).reshape(half, depth)  8.43 us
    all_to_all x1, waiting for transfers between devices, shards(): lax.all_to_all(chip_half.reshape(chips, half // chips, depth), 'dy', 0, 0...  8.13 us
    all_to_all x1, starting transfers between devices, shards(): lax.all_to_all(chip_half.reshape(chips, half // chips, depth), 'dy', 0, 0...  4.59 us
    all_to_all x1, starting transfers between devices, shards(): lax.all_to_all(copies, 'dy', 0, 0, tiled=True).reshape(half, depth)  3.47 us
    dot_general x1, matrix products, shards(): jnp.dot(incidence, features, precision=lax.Precision.HIGH, preferred_elem...  2.67 us
    dot_general x2, matrix products, shards(): lax.dot_general(doc_unit, rows, (((1,), (1,)), ((), ())), precision=lax.P...  2.04 us
  transfers between devices with their start and end apart: 5, of which 5 were waited for; matrix products, arithmetic and copies ran while one was open for 9% of the time, Pallas kernels for 0%

profile of v25, /device:TPU:6, one launch (start us, length us, event | category | flops | bytes accessed | tf_op | source)
XLA Modules:
  0.0 86.9 jit_solution(5944471913649519809)
XLA Ops:
  0.0 0.8 dynamic_slice.9
  0.8 1.7 %convert_reduce_fusion = f32[256,512]{1,0:T(8,128)S(1)} fusion(s32[16,512]{1,0:T(8,128)} %bitcast.26, s32[256]{0:T(256)S(1)} %dynamic_slice.9), kind=kLoop, calls=%fused_computation | loop fusion | flops 6160384 | bytes 558080 | tf_op jit(solution)/shard_map/reduce_sum | solution.py:27
  2.5 2.7 %fusion.33 = f32[256,1024]{1,0:T(8,128)S(1)} fusion(f32[256,512]{1,0:T(8,128)S(1)} %convert_reduce_fusion, f32[512,1024]{1,0:T(8,128)} %param.4), kind=kOutput, calls=%fused_computation.64 | convolution fusion | flops 805306368 | bytes 3670016 | tf_op jit(solution)/shard_map/dot_general | solution.py:30
  5.2 1.9 %collective-permute-start = (f32[128,1024]{1,0:T(8,128)S(1)}, f32[128,1024]{1,0:T(8,128)S(1)}, u32[]{:S(2)}, u32[]{:S(2)}) collective-permute-start(f32[128,1024]{1,0:T(8,128)S(1)} %slice_select_fusion), channel_id=1, source_target_pairs={{0,64},{64,0},{1,65},{65,1},{2,66},{66,2},{3,67},{67,3},{4,68},{68... | collective-permute-start | bytes 1572872 | tf_op jit(solution)/shard_map/ppermute | solution.py:41
  7.8 1.2 %collective-permute-done = f32[128,1024]{1,0:T(8,128)S(1)} collective-permute-done((f32[128,1024]{1,0:T(8,128)S(1)}, f32[128,1024]{1,0:T(8,128)S(1)}, u32[]{:S(2)}, u32[]{:S(2)}) %collective-permute-start) | collective-permute-done | bytes 524320 | tf_op jit(solution)/shard_map/ppermute | solution.py:41
  9.0 0.9 %select_add_fusion = f32[128,1024]{1,0:T(8,128)} fusion(f32[128,1024]{1,0:T(8,128)S(1)} %collective-permute-done, f32[256,1024]{1,0:T(8,128)S(1)} %fusion.33, pred[]{:T(512)S(6)} %eq.90), kind=kLoop, calls=%fused_computation.21 | loop fusion | flops 262144 | bytes 2097153 | tf_op jit(solution)/shard_map/add | solution.py:41
  9.9 4.6 %all-to-all-start = ((f32[4,32,1024]{2,1,0:T(8,128)}), f32[4,32,1024]{2,1,0:T(8,128)S(1)}, u32[]{:S(2)}, u32[]{:S(2)}) async-start(f32[4,32,1024]{2,1,0:T(8,128)} %bitcast.3), calls=%async_computation | async-start | bytes 1048576 | tf_op jit(solution)/shard_map/all_to_all | solution.py:42
  14.7 0.6 dynamic_slice.10
  15.3 0.7 dynamic_slice.11
  16.2 8.1 %all-to-all-done = f32[4,32,1024]{2,1,0:T(8,128)S(1)} async-done(((f32[4,32,1024]{2,1,0:T(8,128)}), f32[4,32,1024]{2,1,0:T(8,128)S(1)}, u32[]{:S(2)}, u32[]{:S(2)}) %all-to-all-start) | async-done | bytes 524320 | tf_op jit(solution)/shard_map/all_to_all | solution.py:42
  24.4 0.9 %broadcast_multiply_fusion = f32[4,32,1024]{2,1,0:T(8,128)} fusion(f32[32]{0:T(128)S(1)} %add_rsqrt_fusion.2, f32[32,1024]{1,0:T(8,128)S(1)} %reduce_sum.112), kind=kLoop, calls=%fused_computation.27 | loop fusion | flops 131072 | bytes 655488 | tf_op jit(solution)/shard_map/mul | solution.py:47
  25.4 3.5 %all-to-all-start.1 = ((f32[4,32,1024]{2,1,0:T(8,128)}), f32[4,32,1024]{2,1,0:T(8,128)S(1)}, u32[]{:S(2)}, u32[]{:S(2)}) async-start(f32[4,32,1024]{2,1,0:T(8,128)} %broadcast_multiply_fusion), calls=%async_computation.1 | async-start | bytes 1048576 | tf_op jit(solution)/shard_map/all_to_all | solution.py:48
  29.3 8.4 %all-to-all-done.1 = f32[4,32,1024]{2,1,0:T(8,128)S(1)} async-done(((f32[4,32,1024]{2,1,0:T(8,128)}), f32[4,32,1024]{2,1,0:T(8,128)S(1)}, u32[]{:S(2)}, u32[]{:S(2)}) %all-to-all-start.1) | async-done | bytes 524320 | tf_op jit(solution)/shard_map/all_to_all | solution.py:48
  37.7 1.9 %collective-permute-start.1 = (f32[128,1024]{1,0:T(8,128)S(1)}, f32[128,1024]{1,0:T(8,128)S(1)}, u32[]{:S(2)}, u32[]{:S(2)}) collective-permute-start(f32[128,1024]{1,0:T(8,128)S(1)} %bitcast.22), channel_id=1, source_target_pairs={{0,64},{64,0},{1,65},{65,1},{2,66},{66,2},{3,67},{67,3},{4,68},{68... | collective-permute-start | bytes 1572872 | tf_op jit(solution)/shard_map/ppermute | solution.py:49
  39.6 1.3 %broadcast_compare_fusion = (pred[256]{0:T(512)(128)(4,1)S(1)}, pred[256]{0:T(512)(128)(4,1)S(1)}) fusion(s32[256]{0:T(256)S(1)} %convert_reduce_fusion.1, s32[]{:T(128)} %bitcast.7, s32[]{:T(128)} %bitcast.5), kind=kLoop, calls=%fused_computation.55 | loop fusion | flops 512 | bytes 1544 | tf_op jit(solution)/shard_map/eq | solution.py:76
  40.9 0.6 collective-permute-done.1
  41.8 0.8 broadcast_select_fusion
  42.6 18.8 %all-to-all-start.2 = ((f32[64,8,128]{2,1,0:T(8,128)}), f32[64,8,128]{2,1,0:T(8,128)}, u32[]{:S(2)}, u32[]{:S(2)}) async-start(f32[64,8,128]{2,1,0:T(8,128)} %broadcast_select_fusion), calls=%async_computation.2 | async-start | bytes 524288 | tf_op jit(solution)/shard_map/all_to_all | solution.py:80
  61.9 1.0 %fusion.2 = f32[512,128]{1,0:T(8,128)S(1)} fusion(f32[128,1024]{1,0:T(8,128)S(1)} %bitcast.25, f32[512,1024]{1,0:T(8,128)S(1)} %copy-done, f32[512]{0:T(512)S(1)} %add_rsqrt_fusion), kind=kOutput, calls=%fused_computation.4 | convolution fusion | flops 403177472 | bytes 2885632 | tf_op jit(solution)/shard_map/dot_general | solution.py:86
  62.9 1.5 %convolution_add_fusion.1 = f32[256,1024]{1,0:T(8,128)} fusion(f32[256,1024]{1,0:T(8,128)S(1)} %fusion.22, f32[128,1024]{1,0:T(8,128)S(1)} %collective-permute-done.1, s32[128]{0:T(128)S(1)} %get-tuple-element.9, s32[256]{0:T(256)S(1)} %convert_reduce_fusion.1), kind=kOutput, calls=%fused_computation.9 | convolution fusion | flops 201621504 | bytes 2622976 | tf_op jit(solution)/shard_map/dot_general | solution.py:67
  64.4 1.0 %fusion = f32[512,128]{1,0:T(8,128)S(1)} fusion(f32[128,1024]{1,0:T(8,128)S(1)} %collective-permute-done.1, f32[512,1024]{1,0:T(8,128)S(1)} %copy-done, f32[512]{0:T(512)S(1)} %add_rsqrt_fusion), kind=kOutput, calls=%fused_computation.2 | convolution fusion | flops 403177472 | bytes 2885632 | tf_op jit(solution)/shard_map/dot_general | solution.py:86
  65.4 17.7 %all-to-all-done.2 = f32[64,8,128]{2,1,0:T(8,128)} async-done(((f32[64,8,128]{2,1,0:T(8,128)}), f32[64,8,128]{2,1,0:T(8,128)}, u32[]{:S(2)}, u32[]{:S(2)}) %all-to-all-start.2) | async-done | bytes 262176 | tf_op jit(solution)/shard_map/all_to_all | solution.py:80
  83.1 1.9 %multiply_reduce_fusion.1 = (f32[256]{0:T(256)S(1)}, f32[256,1024]{1,0:T(8,128)S(1)}) fusion(f32[256,1024]{1,0:T(8,128)} %convolution_add_fusion.1, f32[8,8,8,128]{3,2,1,0:T(8,128)} %bitcast.9, s32[64]{0:T(128)S(1)} %get-tuple-element.8, s32[64]{0:T(128)S(1)} %get-tuple-element.7, s32[256]{0:T(256)S(1)} %convert_reduce_fusion.1, ...), kind=kOutput, calls=%fused_computation.13 | convolution fusion | flops 101531392 | bytes 2361984 | tf_op jit(solution)/shard_map/dot_general | solution.py:104
  85.0 1.9 %fusion.6 = f32[512,256]{1,0:T(8,128)} fusion(f32[512,1024]{1,0:T(8,128)S(1)} %copy-done, f32[256,1024]{1,0:T(8,128)S(1)} %get-tuple-element.14, f32[512]{0:T(512)S(1)} %add_rsqrt_fusion, f32[512,128]{1,0:T(8,128)S(1)} %fusion, f32[512,128]{1,0:T(8,128)S(1)} %fusion.2, f32[256]{0:T(256)S(1)} %add_rsqrt_fusion.1, pred[]{:T(512)S(6)} %eq.90), kind=kOutput, calls=%fused_computation.10 | convolution fusion | flops 806617088 | bytes 4197377 | tf_op jit(solution)/shard_map/dot_general | solution.py:111
  (27 shorter events, 2.5 us)
Async XLA Ops:
  2.5 4.7 %copy-start.1 = (s32[512]{0:T(512)S(1)}, s32[512]{0:T(512)}, u32[]{:S(2)}) copy-start(s32[512]{0:T(512)} %param.7) | copy-start | bytes 6148
  5.2 3.8 %collective-permute-start = (f32[128,1024]{1,0:T(8,128)S(1)}, f32[128,1024]{1,0:T(8,128)S(1)}, u32[]{:S(2)}, u32[]{:S(2)}) collective-permute-start(f32[128,1024]{1,0:T(8,128)S(1)} %slice_select_fusion), channel_id=1, source_target_pairs={{0,64},{64,0},{1,65},{65,1},{2,66},{66,2},{3,67},{67,3},{4,68},{68... | collective-permute-start | bytes 1572872 | tf_op jit(solution)/shard_map/ppermute | solution.py:41
  9.9 19.1 %copy-start = (f32[512,1024]{1,0:T(8,128)S(1)}, f32[512,1024]{1,0:T(8,128)}, u32[]{:S(2)}) copy-start(f32[512,1024]{1,0:T(8,128)} %param.4) | copy-start | bytes 6291460
  9.9 14.4 %all-to-all-start = ((f32[4,32,1024]{2,1,0:T(8,128)}), f32[4,32,1024]{2,1,0:T(8,128)S(1)}, u32[]{:S(2)}, u32[]{:S(2)}) async-start(f32[4,32,1024]{2,1,0:T(8,128)} %bitcast.3), calls=%async_computation | async-start | bytes 1048576 | tf_op jit(solution)/shard_map/all_to_all | solution.py:42
  25.4 12.4 %all-to-all-start.1 = ((f32[4,32,1024]{2,1,0:T(8,128)}), f32[4,32,1024]{2,1,0:T(8,128)S(1)}, u32[]{:S(2)}, u32[]{:S(2)}) async-start(f32[4,32,1024]{2,1,0:T(8,128)} %broadcast_multiply_fusion), calls=%async_computation.1 | async-start | bytes 1048576 | tf_op jit(solution)/shard_map/all_to_all | solution.py:48
  37.7 3.8 %collective-permute-start.1 = (f32[128,1024]{1,0:T(8,128)S(1)}, f32[128,1024]{1,0:T(8,128)S(1)}, u32[]{:S(2)}, u32[]{:S(2)}) collective-permute-start(f32[128,1024]{1,0:T(8,128)S(1)} %bitcast.22), channel_id=1, source_target_pairs={{0,64},{64,0},{1,65},{65,1},{2,66},{66,2},{3,67},{67,3},{4,68},{68... | collective-permute-start | bytes 1572872 | tf_op jit(solution)/shard_map/ppermute | solution.py:49
  42.6 40.5 %all-to-all-start.2 = ((f32[64,8,128]{2,1,0:T(8,128)}), f32[64,8,128]{2,1,0:T(8,128)}, u32[]{:S(2)}, u32[]{:S(2)}) async-start(f32[64,8,128]{2,1,0:T(8,128)} %broadcast_select_fusion), calls=%async_computation.2 | async-start | bytes 524288 | tf_op jit(solution)/shard_map/all_to_all | solution.py:80

commit v26 on v22

--- a/solution.py
+++ b/solution.py
@@ -41,10 +41,10 @@
     pieces = lax.all_to_all(
         chip_half.reshape(chips, half // chips, depth), "dy", 0, 0, tiled=True
     )
-    mine = unit_rows(jnp.sum(pieces, axis=0))
-    own_half = lax.all_to_all(
-        jnp.broadcast_to(mine[None], (chips,) + mine.shape), "dy", 0, 0, tiled=True
-    ).reshape(half, depth)
+    summed = jnp.sum(pieces, axis=0)
+    scale = lax.rsqrt(jnp.sum(summed * summed, axis=1, keepdims=True) + EPS)
+    copies = jnp.broadcast_to(summed[None], pieces.shape) * jnp.broadcast_to(scale[None], (chips,) + scale.shape)
+    own_half = lax.all_to_all(copies, "dy", 0, 0, tiled=True).reshape(half, depth)
     other_half = lax.ppermute(own_half, "dc", sibling)
 
     starts = jnp.cumsum(cluster_sizes) - cluster_sizes

time: 87.4 us -> 87.4 us (level)
  no operation moved by 1% of the time
where the time goes in v26:
time: 87.4 us; the launch traced here: 86.8 us
  waiting for transfers between devices  34.4 us (39%)
  starting transfers between devices  30.7 us (35%)
  matrix products  10.5 us (12%)
  other arithmetic  8.55 us (10%)
  local copies, waits for them, and re-layouts  2.49 us (3%)
    all_to_all x1, starting transfers between devices, shards(): lax.all_to_all(sending.reshape(width, -1, lanes), 'label', 0, 0, tiled=True)  18.8 us
    all_to_all x1, waiting for transfers between devices, shards(): lax.all_to_all(sending.reshape(width, -1, lanes), 'label', 0, 0, tiled=True)  17.7 us
    all_to_all x1, waiting for transfers between devices, shards(): lax.all_to_all(copies, 'dy', 0, 0, tiled=True).reshape(half, depth)  7.22 us
    all_to_all x1, waiting for transfers between devices, shards(): lax.all_to_all(chip_half.reshape(chips, half // chips, depth), 'dy', 0, 0...  7.07 us
    all_to_all x1, starting transfers between devices, shards(): lax.all_to_all(chip_half.reshape(chips, half // chips, depth), 'dy', 0, 0...  4.59 us
    all_to_all x1, starting transfers between devices, shards(): lax.all_to_all(copies, 'dy', 0, 0, tiled=True).reshape(half, depth)  3.47 us
    dot_general x1, matrix products, shards(): jnp.dot(incidence, features, precision=lax.Precision.HIGH, preferred_elem...  2.67 us
    eq x2, other arithmetic, shards(): ids == target  2.51 us
  transfers between devices with their start and end apart: 5, of which 5 were waited for; matrix products, arithmetic and copies ran while one was open for 11% of the time, Pallas kernels for 0%

profile of v26, /device:TPU:6, one launch (start us, length us, event | category | flops | bytes accessed | tf_op | source)
XLA Modules:
  0.0 86.8 jit_solution(6985834422030357741)
XLA Ops:
  0.0 0.8 dynamic_slice.15
  0.8 1.7 %convert_reduce_fusion = f32[256,512]{1,0:T(8,128)S(1)} fusion(s32[16,512]{1,0:T(8,128)} %bitcast.27, s32[256]{0:T(256)S(1)} %dynamic_slice.15), kind=kLoop, calls=%fused_computation | loop fusion | flops 6160384 | bytes 558080 | tf_op jit(solution)/shard_map/reduce_sum | solution.py:27
  2.5 2.7 %fusion.33 = f32[256,1024]{1,0:T(8,128)S(1)} fusion(f32[256,512]{1,0:T(8,128)S(1)} %convert_reduce_fusion, f32[512,1024]{1,0:T(8,128)} %param.4), kind=kOutput, calls=%fused_computation.69 | convolution fusion | flops 805306368 | bytes 3670016 | tf_op jit(solution)/shard_map/dot_general | solution.py:30
  5.2 1.9 %collective-permute-start = (f32[128,1024]{1,0:T(8,128)S(1)}, f32[128,1024]{1,0:T(8,128)S(1)}, u32[]{:S(2)}, u32[]{:S(2)}) collective-permute-start(f32[128,1024]{1,0:T(8,128)S(1)} %constant_dynamic-slice_fusion), channel_id=1, source_target_pairs={{0,64},{64,0},{1,65},{65,1},{2,66},{66,2},{3,67},{67,3},{4,68},{68... | collective-permute-start | bytes 1572872 | tf_op jit(solution)/shard_map/ppermute | solution.py:40
  8.1 0.9 %collective-permute-done = f32[128,1024]{1,0:T(8,128)S(1)} collective-permute-done((f32[128,1024]{1,0:T(8,128)S(1)}, f32[128,1024]{1,0:T(8,128)S(1)}, u32[]{:S(2)}, u32[]{:S(2)}) %collective-permute-start) | collective-permute-done | bytes 524320 | tf_op jit(solution)/shard_map/ppermute | solution.py:40
  9.0 0.9 dynamic-slice_add_fusion
  9.9 4.6 %all-to-all-start = ((f32[4,32,1024]{2,1,0:T(8,128)}), f32[4,32,1024]{2,1,0:T(8,128)S(1)}, u32[]{:S(2)}, u32[]{:S(2)}) async-start(f32[4,32,1024]{2,1,0:T(8,128)} %bitcast.3), calls=%async_computation | async-start | bytes 1048576 | tf_op jit(solution)/shard_map/all_to_all | solution.py:41
  15.0 0.7 dynamic_slice.19
  15.9 1.3 %broadcast_compare_fusion.1 = (pred[128]{0:T(512)(128)(4,1)S(1)}, pred[128]{0:T(512)(128)(4,1)S(1)}) fusion(s32[128]{0:T(128)S(1)} %get-tuple-element.12, s32[]{:T(128)} %bitcast.7, s32[]{:T(128)} %bitcast.5), kind=kLoop, calls=%fused_computation.65 | loop fusion | flops 256 | bytes 776 | tf_op jit(solution)/shard_map/eq | solution.py:72
  17.2 7.1 %all-to-all-done = f32[4,32,1024]{2,1,0:T(8,128)S(1)} async-done(((f32[4,32,1024]{2,1,0:T(8,128)}), f32[4,32,1024]{2,1,0:T(8,128)S(1)}, u32[]{:S(2)}, u32[]{:S(2)}) %all-to-all-start) | async-done | bytes 524320 | tf_op jit(solution)/shard_map/all_to_all | solution.py:41
  24.4 0.9 %broadcast_multiply_fusion = f32[4,32,1024]{2,1,0:T(8,128)} fusion(f32[32]{0:T(128)S(1)} %add_rsqrt_fusion.2, f32[32,1024]{1,0:T(8,128)S(1)} %reduce_sum.130), kind=kLoop, calls=%fused_computation.27 | loop fusion | flops 131072 | bytes 655488 | tf_op jit(solution)/shard_map/mul | solution.py:46
  25.3 3.5 %all-to-all-start.1 = ((f32[4,32,1024]{2,1,0:T(8,128)}), f32[4,32,1024]{2,1,0:T(8,128)S(1)}, u32[]{:S(2)}, u32[]{:S(2)}) async-start(f32[4,32,1024]{2,1,0:T(8,128)} %broadcast_multiply_fusion), calls=%async_computation.1 | async-start | bytes 1048576 | tf_op jit(solution)/shard_map/all_to_all | solution.py:47
  29.2 1.3 %broadcast_compare_fusion = (pred[128]{0:T(512)(128)(4,1)S(1)}, pred[128]{0:T(512)(128)(4,1)S(1)}) fusion(s32[128]{0:T(128)S(1)} %get-tuple-element.11, s32[]{:T(128)} %bitcast.7, s32[]{:T(128)} %bitcast.5), kind=kLoop, calls=%fused_computation.64 | loop fusion | flops 256 | bytes 776 | tf_op jit(solution)/shard_map/eq | solution.py:72
  30.4 7.2 %all-to-all-done.1 = f32[4,32,1024]{2,1,0:T(8,128)S(1)} async-done(((f32[4,32,1024]{2,1,0:T(8,128)}), f32[4,32,1024]{2,1,0:T(8,128)S(1)}, u32[]{:S(2)}, u32[]{:S(2)}) %all-to-all-start.1) | async-done | bytes 524320 | tf_op jit(solution)/shard_map/all_to_all | solution.py:47
  37.7 1.9 %collective-permute-start.1 = (f32[128,1024]{1,0:T(8,128)S(1)}, f32[128,1024]{1,0:T(8,128)S(1)}, u32[]{:S(2)}, u32[]{:S(2)}) collective-permute-start(f32[128,1024]{1,0:T(8,128)S(1)} %bitcast.24), channel_id=1, source_target_pairs={{0,64},{64,0},{1,65},{65,1},{2,66},{66,2},{3,67},{67,3},{4,68},{68... | collective-permute-start | bytes 1572872 | tf_op jit(solution)/shard_map/ppermute | solution.py:48
  40.0 1.5 %collective-permute-done.1 = f32[128,1024]{1,0:T(8,128)S(1)} collective-permute-done((f32[128,1024]{1,0:T(8,128)S(1)}, f32[128,1024]{1,0:T(8,128)S(1)}, u32[]{:S(2)}, u32[]{:S(2)}) %collective-permute-start.1) | collective-permute-done | bytes 524320 | tf_op jit(solution)/shard_map/ppermute | solution.py:48
  41.6 0.8 broadcast_select_fusion
  42.5 18.8 %all-to-all-start.2 = ((f32[64,8,128]{2,1,0:T(8,128)}), f32[64,8,128]{2,1,0:T(8,128)}, u32[]{:S(2)}, u32[]{:S(2)}) async-start(f32[64,8,128]{2,1,0:T(8,128)} %broadcast_select_fusion), calls=%async_computation.2 | async-start | bytes 524288 | tf_op jit(solution)/shard_map/all_to_all | solution.py:79
  61.8 1.0 %fusion.2 = f32[512,128]{1,0:T(8,128)S(1)} fusion(f32[128,1024]{1,0:T(8,128)S(1)} %bitcast.26, f32[512,1024]{1,0:T(8,128)S(1)} %copy-done, f32[512]{0:T(512)S(1)} %add_rsqrt_fusion), kind=kOutput, calls=%fused_computation.4 | convolution fusion | flops 403177472 | bytes 2885632 | tf_op jit(solution)/shard_map/dot_general | solution.py:85
  62.8 1.5 %convolution_add_fusion.1 = f32[256,1024]{1,0:T(8,128)} fusion(f32[256,1024]{1,0:T(8,128)S(1)} %fusion.22, f32[128,1024]{1,0:T(8,128)S(1)} %collective-permute-done.1, s32[128]{0:T(128)S(1)} %get-tuple-element.11, s32[256]{0:T(256)S(1)} %convert_reduce_fusion.1), kind=kOutput, calls=%fused_computation.9 | convolution fusion | flops 201621504 | bytes 2622976 | tf_op jit(solution)/shard_map/dot_general | solution.py:61
  64.3 1.0 %fusion = f32[512,128]{1,0:T(8,128)S(1)} fusion(f32[128,1024]{1,0:T(8,128)S(1)} %collective-permute-done.1, f32[512,1024]{1,0:T(8,128)S(1)} %copy-done, f32[512]{0:T(512)S(1)} %add_rsqrt_fusion), kind=kOutput, calls=%fused_computation.2 | convolution fusion | flops 403177472 | bytes 2885632 | tf_op jit(solution)/shard_map/dot_general | solution.py:85
  65.3 17.7 %all-to-all-done.2 = f32[64,8,128]{2,1,0:T(8,128)} async-done(((f32[64,8,128]{2,1,0:T(8,128)}), f32[64,8,128]{2,1,0:T(8,128)}, u32[]{:S(2)}, u32[]{:S(2)}) %all-to-all-start.2) | async-done | bytes 262176 | tf_op jit(solution)/shard_map/all_to_all | solution.py:79
  83.0 1.9 %multiply_reduce_fusion.1 = (f32[256]{0:T(256)S(1)}, f32[256,1024]{1,0:T(8,128)S(1)}) fusion(f32[256,1024]{1,0:T(8,128)} %convolution_add_fusion.1, f32[8,8,8,128]{3,2,1,0:T(8,128)} %bitcast.9, s32[64]{0:T(128)S(1)} %get-tuple-element.10, s32[64]{0:T(128)S(1)} %get-tuple-element.9, s32[256]{0:T(256)S(1)} %convert_reduce_fusion.1, ...), kind=kOutput, calls=%fused_computation.12 | convolution fusion | flops 101531392 | bytes 2361984 | tf_op jit(solution)/shard_map/dot_general | solution.py:103
  84.9 1.9 %fusion.6 = f32[512,256]{1,0:T(8,128)} fusion(f32[512,1024]{1,0:T(8,128)S(1)} %copy-done, f32[256,1024]{1,0:T(8,128)S(1)} %get-tuple-element.18, f32[512]{0:T(512)S(1)} %add_rsqrt_fusion, f32[512,128]{1,0:T(8,128)S(1)} %fusion, f32[512,128]{1,0:T(8,128)S(1)} %fusion.2, f32[256]{0:T(256)S(1)} %add_rsqrt_fusion.1, pred[]{:T(512)S(6)} %eq.127), kind=kOutput, calls=%fused_computation.10 | convolution fusion | flops 806617088 | bytes 4197377 | tf_op jit(solution)/shard_map/dot_general | solution.py:110
  (34 shorter events, 3.3 us)
Async XLA Ops:
  2.5 4.7 %copy-start.1 = (s32[512]{0:T(512)S(1)}, s32[512]{0:T(512)}, u32[]{:S(2)}) copy-start(s32[512]{0:T(512)} %param.7) | copy-start | bytes 6148
  5.2 3.8 %collective-permute-start = (f32[128,1024]{1,0:T(8,128)S(1)}, f32[128,1024]{1,0:T(8,128)S(1)}, u32[]{:S(2)}, u32[]{:S(2)}) collective-permute-start(f32[128,1024]{1,0:T(8,128)S(1)} %constant_dynamic-slice_fusion), channel_id=1, source_target_pairs={{0,64},{64,0},{1,65},{65,1},{2,66},{66,2},{3,67},{67,3},{4,68},{68... | collective-permute-start | bytes 1572872 | tf_op jit(solution)/shard_map/ppermute | solution.py:40
  9.9 29.7 %copy-start = (f32[512,1024]{1,0:T(8,128)S(1)}, f32[512,1024]{1,0:T(8,128)}, u32[]{:S(2)}) copy-start(f32[512,1024]{1,0:T(8,128)} %param.4) | copy-start | bytes 6291460
  9.9 14.4 %all-to-all-start = ((f32[4,32,1024]{2,1,0:T(8,128)}), f32[4,32,1024]{2,1,0:T(8,128)S(1)}, u32[]{:S(2)}, u32[]{:S(2)}) async-start(f32[4,32,1024]{2,1,0:T(8,128)} %bitcast.3), calls=%async_computation | async-start | bytes 1048576 | tf_op jit(solution)/shard_map/all_to_all | solution.py:41
  25.3 12.4 %all-to-all-start.1 = ((f32[4,32,1024]{2,1,0:T(8,128)}), f32[4,32,1024]{2,1,0:T(8,128)S(1)}, u32[]{:S(2)}, u32[]{:S(2)}) async-start(f32[4,32,1024]{2,1,0:T(8,128)} %broadcast_multiply_fusion), calls=%async_computation.1 | async-start | bytes 1048576 | tf_op jit(solution)/shard_map/all_to_all | solution.py:47
  37.7 3.8 %collective-permute-start.1 = (f32[128,1024]{1,0:T(8,128)S(1)}, f32[128,1024]{1,0:T(8,128)S(1)}, u32[]{:S(2)}, u32[]{:S(2)}) collective-permute-start(f32[128,1024]{1,0:T(8,128)S(1)} %bitcast.24), channel_id=1, source_target_pairs={{0,64},{64,0},{1,65},{65,1},{2,66},{66,2},{3,67},{67,3},{4,68},{68... | collective-permute-start | bytes 1572872 | tf_op jit(solution)/shard_map/ppermute | solution.py:48
  42.5 40.5 %all-to-all-start.2 = ((f32[64,8,128]{2,1,0:T(8,128)}), f32[64,8,128]{2,1,0:T(8,128)}, u32[]{:S(2)}, u32[]{:S(2)}) async-start(f32[64,8,128]{2,1,0:T(8,128)} %broadcast_select_fusion), calls=%async_computation.2 | async-start | bytes 524288 | tf_op jit(solution)/shard_map/all_to_all | solution.py:79
